TPU v7x, 32 devices: a whole 2x2x4 slice. The times are simulated.
32 devices in a mesh: dp: 8 (over z, x), tensor: 4 (over y, core).
Axes of the slice: x: 2, y: 2, z: 4, core: 2. Of those that a mesh axis runs over, the one named last changes fastest.
Arguments:
- layer_input: bfloat16 [5120, 2304], P(('dp', 'tensor')), may hold values from -6 to 6
- cotangent: bfloat16 [5120, 2304], P(('dp', 'tensor')), may hold values from -6 to 6
- norm_gains: bfloat16 [4, 2304], replicated, may hold values from 0.25 to 1.75
- w_query: bfloat16 [2304, 2048], P('dp', 'tensor'), may hold values from -0.125 to 0.125
- w_key: bfloat16 [2304, 1024], P('dp', 'tensor'), may hold values from -0.125 to 0.125
- w_value: bfloat16 [2304, 1024], P('dp', 'tensor'), may hold values from -0.125 to 0.125
- w_output: bfloat16 [2048, 2304], P('tensor', 'dp'), may hold values from -0.125 to 0.125
- w_gate: bfloat16 [2304, 9216], P('dp', 'tensor'), may hold values from -0.125 to 0.125
- w_up: bfloat16 [2304, 9216], P('dp', 'tensor'), may hold values from -0.125 to 0.125
- w_down: bfloat16 [9216, 2304], P('tensor', 'dp'), may hold values from -0.0625 to 0.0625
- query_shrink: bfloat16 [8, 16, 2304], replicated, may hold values from -0.125 to 0.125
- key_shrink: bfloat16 [8, 16, 2304], replicated, may hold values from -0.125 to 0.125
- value_shrink: bfloat16 [8, 16, 2304], replicated, may hold values from -0.125 to 0.125
- output_shrink: bfloat16 [8, 16, 2048], P(None, None, 'tensor'), may hold values from -0.125 to 0.125
- gate_shrink: bfloat16 [8, 16, 2304], replicated, may hold values from -0.125 to 0.125
- up_shrink: bfloat16 [8, 16, 2304], replicated, may hold values from -0.125 to 0.125
- down_shrink: bfloat16 [8, 16, 9216], P(None, None, 'tensor'), may hold values from -0.0625 to 0.0625
- query_expand: bfloat16 [8, 16, 2048], P(None, None, 'tensor'), may hold values from -0.75 to 0.75
- key_expand: bfloat16 [8, 16, 1024], P(None, None, 'tensor'), may hold values from -0.75 to 0.75
- value_expand: bfloat16 [8, 16, 1024], P(None, None, 'tensor'), may hold values from -0.75 to 0.75
- output_expand: bfloat16 [8, 16, 2304], replicated, may hold values from -0.75 to 0.75
- gate_expand: bfloat16 [8, 16, 9216], P(None, None, 'tensor'), may hold values from -0.75 to 0.75
- up_expand: bfloat16 [8, 16, 9216], P(None, None, 'tensor'), may hold values from -0.75 to 0.75
- down_expand: bfloat16 [8, 16, 2304], replicated, may hold values from -0.75 to 0.75
- adapter_ids: int32 [8], P('dp'), may hold values from 0 to 7
- parent_segments: int32 [8, 13], P('dp'), may hold values from 0 to 4, as said below
- segment_ids: int32 [5120], P('dp'), may hold values from 0 to 12, as said below
Outputs:
- layer_output: bfloat16 [5120, 2304], P(('dp', 'tensor'))
- input_grad: float32 [5120, 2304], P(('dp', 'tensor'))
- shrink_query: float32 [8, 16, 2304], replicated
- shrink_key: float32 [8, 16, 2304], replicated
- shrink_value: float32 [8, 16, 2304], replicated
- shrink_output: float32 [8, 16, 2048], P(None, None, 'tensor')
- shrink_gate: float32 [8, 16, 2304], replicated
- shrink_up: float32 [8, 16, 2304], replicated
- shrink_down: float32 [8, 16, 9216], P(None, None, 'tensor')
- expand_query: float32 [8, 16, 2048], P(None, None, 'tensor')
- expand_key: float32 [8, 16, 1024], P(None, None, 'tensor')
- expand_value: float32 [8, 16, 1024], P(None, None, 'tensor')
- expand_output: float32 [8, 16, 2304], replicated
- expand_gate: float32 [8, 16, 9216], P(None, None, 'tensor')
- expand_up: float32 [8, 16, 9216], P(None, None, 'tensor')
- expand_down: float32 [8, 16, 2304], replicated
Inputs may be any that keep to these rules, and one draw needn't show every extreme that they name: `parent_segments`: in each tree, segment 0 is the trunk and is its own parent; segments 1 to 4 have parent 0; each of the other segments has a branch (1 to 4) as parent, and every branch is the parent of exactly 2 of them. `segment_ids`: the first 256 tokens of each tree are segment 0; the rest are 12 contiguous runs of 32 tokens, one run for each other segment, in any order.
All inputs are finite; a program needn't handle non-finite values.
Results may differ from a plain program's by a relative error of at most 0.028.
Values may be sent and summed in bfloat16 or wider, within the bound.
No kernel may reach another device: no remote copies, remote signals or barrier semaphores. Data moves between devices by JAX's collectives and lax.ppermute only.
A program may use at most 256 MiB of HBM per device.

v0:
```python
import math

import jax
import jax.numpy as jnp
from jax import lax
from jax.sharding import PartitionSpec as P

HEAD_WIDTH = 256
ADAPTERS = 8


def rms_scale(value_rows, gain_row):
    inverse = lax.rsqrt(jnp.mean(value_rows * value_rows, axis=-1, keepdims=True) + 1e-06)
    return value_rows * inverse * gain_row


def rms_back(value_rows, gain_row, upstream):
    inverse = lax.rsqrt(jnp.mean(value_rows * value_rows, axis=-1, keepdims=True) + 1e-06)
    scaled = gain_row * upstream
    return inverse * scaled - value_rows * (inverse * inverse * inverse) * jnp.mean(
        value_rows * scaled, axis=-1, keepdims=True
    )


def pick_from(lookup, indices, labels):
    return jnp.sum(jnp.where(indices[:, None] == labels[None, :], lookup[None, :], 0), axis=1)


def tree_tables(segments, parents):
    count_seg = parents.shape[0]
    sequence_length = segments.shape[0]
    labels = jnp.arange(count_seg, dtype=jnp.int32)
    places = jnp.arange(sequence_length, dtype=jnp.int32)
    member = segments[None, :] == labels[:, None]
    starts = jnp.min(jnp.where(member, places[None, :], sequence_length), axis=1)
    counts = jnp.sum(member.astype(jnp.int32), axis=1)
    grands = pick_from(parents, parents, labels)
    offsets = jnp.where(parents != labels, pick_from(counts, parents, labels), 0) + jnp.where(
        grands != parents, pick_from(counts, grands, labels), 0
    )
    tok_start = pick_from(starts, segments, labels)
    tok_offset = pick_from(offsets, segments, labels)
    tok_parent = pick_from(parents, segments, labels)
    tok_grand = pick_from(grands, segments, labels)
    positions = (places - tok_start + tok_offset).astype(jnp.float32)
    same_seg = (segments[None, :] == segments[:, None]) & (places[None, :] <= places[:, None])
    from_parent = (segments[None, :] == tok_parent[:, None]) & (tok_parent != segments)[:, None]
    from_grand = (segments[None, :] == tok_grand[:, None]) & (tok_grand != tok_parent)[:, None]
    visible = same_seg | from_parent | from_grand
    inv_freq = jnp.exp(
        jnp.arange(HEAD_WIDTH // 2, dtype=jnp.float32) * (-2.0 * math.log(10000.0) / HEAD_WIDTH)
    )
    angles = positions[:, None] * inv_freq[None, :]
    return (visible, jnp.cos(angles), jnp.sin(angles))


def apply_rotary(value_rows, cos_rows, sin_rows):
    half_size = value_rows.shape[-1] // 2
    front_half = value_rows[..., :half_size]
    back_half = value_rows[..., half_size:]
    return jnp.concatenate(
        [
            front_half * cos_rows - back_half * sin_rows,
            back_half * cos_rows + front_half * sin_rows,
        ],
        axis=-1,
    )


def rotate_back(value_rows, cos_rows, sin_rows):
    half_size = value_rows.shape[-1] // 2
    front_half = value_rows[..., :half_size]
    back_half = value_rows[..., half_size:]
    return jnp.concatenate(
        [
            front_half * cos_rows + back_half * sin_rows,
            back_half * cos_rows - front_half * sin_rows,
        ],
        axis=-1,
    )


def product(former, latter):
    return jnp.dot(former, latter, preferred_element_type=jnp.float32)


def select(onehot, stacked):
    return jnp.einsum("e,erc->rc", onehot, stacked, preferred_element_type=jnp.float32).astype(
        jnp.bfloat16
    )


def project(inputs, weight, shrink, expand):
    inner_rank = jnp.einsum("li,ri->lr", inputs, shrink, preferred_element_type=jnp.float32)
    return (product(inputs, weight) + product(inner_rank, expand.astype(jnp.float32)), inner_rank)


def project_back(inputs, inner_rank, upstream, weight, shrink, expand):
    grad_expand = jnp.einsum("lr,lo->ro", inner_rank, upstream, preferred_element_type=jnp.float32)
    grad_inner = jnp.einsum("lo,ro->lr", upstream, expand, preferred_element_type=jnp.float32)
    grad_shrink = jnp.einsum("lr,li->ri", grad_inner, inputs, preferred_element_type=jnp.float32)
    grad_inputs = jnp.einsum(
        "lo,io->li", upstream, weight, preferred_element_type=jnp.float32
    ) + product(grad_inner, shrink.astype(jnp.float32))
    return (grad_inputs, grad_shrink, grad_expand)


def score_block(query_rows, rotated_keys, visible):
    scores = jnp.einsum(
        "qngd,knd->ngqk", query_rows, rotated_keys, preferred_element_type=jnp.float32
    )
    bounded = jnp.tanh(scores / 50.0)
    masked = jnp.where(visible[None, None], 50.0 * bounded, -1e30)
    return (bounded, masked)


def activate(gate_in, up_in):
    return jax.nn.gelu(gate_in, approximate=True) * up_in


def on_device(
    layer_input,
    cotangent,
    norm_gains,
    w_query,
    w_key,
    w_value,
    w_output,
    w_gate,
    w_up,
    w_down,
    query_shrink,
    key_shrink,
    value_shrink,
    output_shrink,
    gate_shrink,
    up_shrink,
    down_shrink,
    query_expand,
    key_expand,
    value_expand,
    output_expand,
    gate_expand,
    up_expand,
    down_expand,
    adapter_ids,
    parent_segments,
    segment_ids,
):
    norm_gain = norm_gains.astype(jnp.float32)
    w_query, w_key, w_value, w_output, w_gate, w_up, w_down = (
        lax.all_gather(w_query, "dp", axis=0, tiled=True),
        lax.all_gather(w_key, "dp", axis=0, tiled=True),
        lax.all_gather(w_value, "dp", axis=0, tiled=True),
        lax.all_gather(w_output, "dp", axis=1, tiled=True),
        lax.all_gather(w_gate, "dp", axis=0, tiled=True),
        lax.all_gather(w_up, "dp", axis=0, tiled=True),
        lax.all_gather(w_down, "dp", axis=1, tiled=True),
    )
    labels = jnp.arange(ADAPTERS, dtype=jnp.int32)
    onehot = (labels == adapter_ids[0]).astype(jnp.bfloat16)
    chosen = [
        select(onehot, stacked)
        for stacked in (
            query_shrink,
            key_shrink,
            value_shrink,
            output_shrink,
            gate_shrink,
            up_shrink,
            down_shrink,
            query_expand,
            key_expand,
            value_expand,
            output_expand,
            gate_expand,
            up_expand,
            down_expand,
        )
    ]
    s_query, s_key, s_value, s_output, s_gate, s_up, s_down = chosen[:7]
    e_query, e_key, e_value, e_output, e_gate, e_up, e_down = chosen[7:]
    visible, cos_rows, sin_rows = tree_tables(segment_ids, parent_segments[0])
    cosine_per_head = cos_rows[:, None, :]
    sine_per_head = sin_rows[:, None, :]
    own_rows = layer_input.astype(jnp.float32)
    normed = rms_scale(own_rows, norm_gain[0]).astype(jnp.bfloat16)
    normed_all = lax.all_gather(normed, "tensor", axis=0, tiled=True)
    sequence_length = normed_all.shape[0]
    query_pre, query_inner = project(normed_all, w_query, s_query, e_query)
    key_before_rotation, key_inner = project(normed_all, w_key, s_key, e_key)
    value_projected, value_inner = project(normed_all, w_value, s_value, e_value)
    heads_q = query_pre.shape[1] // HEAD_WIDTH
    heads_kv = key_before_rotation.shape[1] // HEAD_WIDTH
    head_groups = heads_q // heads_kv
    query_rows = (
        (
            apply_rotary(
                query_pre.reshape(sequence_length, heads_q, HEAD_WIDTH),
                cosine_per_head,
                sine_per_head,
            )
            * HEAD_WIDTH ** (-0.5)
        )
        .astype(jnp.bfloat16)
        .reshape(sequence_length, heads_kv, head_groups, HEAD_WIDTH)
    )
    rotated_keys = apply_rotary(
        key_before_rotation.reshape(sequence_length, heads_kv, HEAD_WIDTH),
        cosine_per_head,
        sine_per_head,
    ).astype(jnp.bfloat16)
    value_rows = value_projected.astype(jnp.bfloat16).reshape(sequence_length, heads_kv, HEAD_WIDTH)
    bounded, masked = score_block(query_rows, rotated_keys, visible)
    row_max = jnp.max(masked, axis=-1, keepdims=True)
    exponent = jnp.exp(masked - row_max)
    row_total = jnp.sum(exponent, axis=-1, keepdims=True)
    log_total = row_max + jnp.log(row_total)
    probs_low = (exponent / row_total).astype(jnp.bfloat16)
    mixed_heads = (
        jnp.einsum("ngqk,knd->qngd", probs_low, value_rows, preferred_element_type=jnp.float32)
        .reshape(sequence_length, heads_q * HEAD_WIDTH)
        .astype(jnp.bfloat16)
    )
    attn_part, output_inner = project(mixed_heads, w_output, s_output, e_output)
    attended = lax.psum_scatter(
        attn_part.astype(jnp.bfloat16), "tensor", scatter_dimension=0, tiled=True
    ).astype(jnp.float32)
    residual = own_rows + rms_scale(attended, norm_gain[1])
    normed_ffn = rms_scale(residual, norm_gain[2]).astype(jnp.bfloat16)
    ffn_rows = lax.all_gather(normed_ffn, "tensor", axis=0, tiled=True)
    gate_pre, gate_inner = project(ffn_rows, w_gate, s_gate, e_gate)
    up_pre, up_inner = project(ffn_rows, w_up, s_up, e_up)
    hidden_full, act_back = jax.vjp(activate, gate_pre, up_pre)
    hidden = hidden_full.astype(jnp.bfloat16)
    ffn_part, down_inner = project(hidden, w_down, s_down, e_down)
    ffn_out = lax.psum_scatter(
        ffn_part.astype(jnp.bfloat16), "tensor", scatter_dimension=0, tiled=True
    ).astype(jnp.float32)
    layer_output = (residual + rms_scale(ffn_out, norm_gain[3])).astype(jnp.bfloat16)
    grad_out = cotangent.astype(jnp.float32)
    grad_ffn = rms_back(ffn_out, norm_gain[3], grad_out).astype(jnp.bfloat16)
    grad_ffn_all = lax.all_gather(grad_ffn, "tensor", axis=0, tiled=True)
    down_back = project_back(hidden, down_inner, grad_ffn_all, w_down, s_down, e_down)
    grad_gate, grad_up = act_back(down_back[0])
    grad_gate = grad_gate.astype(jnp.bfloat16)
    grad_up = grad_up.astype(jnp.bfloat16)
    gate_back = project_back(ffn_rows, gate_inner, grad_gate, w_gate, s_gate, e_gate)
    up_back = project_back(ffn_rows, up_inner, grad_up, w_up, s_up, e_up)
    grad_normed_ffn = lax.psum_scatter(
        (gate_back[0] + up_back[0]).astype(jnp.bfloat16), "tensor", scatter_dimension=0, tiled=True
    ).astype(jnp.float32)
    grad_resid = grad_out + rms_back(residual, norm_gain[2], grad_normed_ffn)
    grad_attn = rms_back(attended, norm_gain[1], grad_resid).astype(jnp.bfloat16)
    grad_attn_all = lax.all_gather(grad_attn, "tensor", axis=0, tiled=True)
    output_back = project_back(
        mixed_heads, output_inner, grad_attn_all, w_output, s_output, e_output
    )
    grad_mixed = (
        output_back[0]
        .astype(jnp.bfloat16)
        .reshape(sequence_length, heads_kv, head_groups, HEAD_WIDTH)
    )
    bounded, masked = score_block(query_rows, rotated_keys, visible)
    attn_probs = jnp.exp(masked - log_total)
    probs_low = attn_probs.astype(jnp.bfloat16)
    grad_values = (
        jnp.einsum("ngqk,qngd->knd", probs_low, grad_mixed, preferred_element_type=jnp.float32)
        .reshape(sequence_length, heads_kv * HEAD_WIDTH)
        .astype(jnp.bfloat16)
    )
    grad_probs = jnp.einsum(
        "qngd,knd->ngqk", grad_mixed, value_rows, preferred_element_type=jnp.float32
    )
    grad_capped = attn_probs * (
        grad_probs - jnp.sum(attn_probs * grad_probs, axis=-1, keepdims=True)
    )
    grad_scores = (grad_capped * (1.0 - bounded * bounded)).astype(jnp.bfloat16)
    grad_queries = jnp.einsum(
        "ngqk,knd->qngd", grad_scores, rotated_keys, preferred_element_type=jnp.float32
    ).reshape(sequence_length, heads_q, HEAD_WIDTH)
    grad_keys = jnp.einsum(
        "ngqk,qngd->knd", grad_scores, query_rows, preferred_element_type=jnp.float32
    )
    grad_qpre = (
        rotate_back(grad_queries * HEAD_WIDTH ** (-0.5), cosine_per_head, sine_per_head)
        .reshape(sequence_length, heads_q * HEAD_WIDTH)
        .astype(jnp.bfloat16)
    )
    grad_kpre = (
        rotate_back(grad_keys, cosine_per_head, sine_per_head)
        .reshape(sequence_length, heads_kv * HEAD_WIDTH)
        .astype(jnp.bfloat16)
    )
    query_back = project_back(normed_all, query_inner, grad_qpre, w_query, s_query, e_query)
    key_back = project_back(normed_all, key_inner, grad_kpre, w_key, s_key, e_key)
    value_back = project_back(normed_all, value_inner, grad_values, w_value, s_value, e_value)
    grad_normed = lax.psum_scatter(
        (query_back[0] + key_back[0] + value_back[0]).astype(jnp.bfloat16),
        "tensor",
        scatter_dimension=0,
        tiled=True,
    ).astype(jnp.float32)
    input_grad = grad_resid + rms_back(own_rows, norm_gain[0], grad_normed)
    hot_rows = onehot.astype(jnp.float32)[:, None, None]
    split_sums = (
        lax.psum((hot_rows * query_back[2][None]).astype(jnp.bfloat16), "dp").astype(jnp.float32),
        lax.psum((hot_rows * key_back[2][None]).astype(jnp.bfloat16), "dp").astype(jnp.float32),
        lax.psum((hot_rows * value_back[2][None]).astype(jnp.bfloat16), "dp").astype(jnp.float32),
        lax.psum((hot_rows * output_back[1][None]).astype(jnp.bfloat16), "dp").astype(jnp.float32),
        lax.psum((hot_rows * gate_back[2][None]).astype(jnp.bfloat16), "dp").astype(jnp.float32),
        lax.psum((hot_rows * up_back[2][None]).astype(jnp.bfloat16), "dp").astype(jnp.float32),
        lax.psum((hot_rows * down_back[1][None]).astype(jnp.bfloat16), "dp").astype(jnp.float32),
    )
    shared_sums = lax.psum(
        (
            hot_rows * query_back[1][None],
            hot_rows * key_back[1][None],
            hot_rows * value_back[1][None],
            hot_rows * output_back[2][None],
            hot_rows * gate_back[1][None],
            hot_rows * up_back[1][None],
            hot_rows * down_back[2][None],
        ),
        ("dp", "tensor"),
    )
    return (
        layer_output,
        input_grad,
        shared_sums[0],
        shared_sums[1],
        shared_sums[2],
        split_sums[3],
        shared_sums[4],
        shared_sums[5],
        split_sums[6],
        split_sums[0],
        split_sums[1],
        split_sums[2],
        shared_sums[3],
        split_sums[4],
        split_sums[5],
        shared_sums[6],
    )


def solution(mesh):
    placed = (
        P(("dp", "tensor"), None),
        P(("dp", "tensor"), None),
        P(),
        P("dp", "tensor"),
        P("dp", "tensor"),
        P("dp", "tensor"),
        P("tensor", "dp"),
        P("dp", "tensor"),
        P("dp", "tensor"),
        P("tensor", "dp"),
        P(),
        P(),
        P(),
        P(None, None, "tensor"),
        P(),
        P(),
        P(None, None, "tensor"),
        P(None, None, "tensor"),
        P(None, None, "tensor"),
        P(None, None, "tensor"),
        P(),
        P(None, None, "tensor"),
        P(None, None, "tensor"),
        P(),
        P("dp"),
        P("dp", None),
        P("dp"),
    )
    return jax.shard_map(
        on_device,
        mesh=mesh,
        in_specs=placed,
        out_specs=(
            P(("dp", "tensor"), None),
            P(("dp", "tensor"), None),
            P(),
            P(),
            P(),
            P(None, None, "tensor"),
            P(),
            P(),
            P(None, None, "tensor"),
            P(None, None, "tensor"),
            P(None, None, "tensor"),
            P(None, None, "tensor"),
            P(),
            P(None, None, "tensor"),
            P(None, None, "tensor"),
            P(),
        ),
        check_vma=False,
    )
```

profile of v0, /device:TPU:0, one launch (start us, length us, event | category | flops | bytes accessed | tf_op | source)
XLA Modules:
  0.0 1369.6 jit_solution(2153370588222020406)
XLA Ops:
  10.8 2.3 fusion.42
  24.3 2.1 multiply_cosine_fusion
  26.4 17.0 %all-gather.12.cloned.1.call-done = bf16[640,2304]{1,0:T(8,128)(2,1)} async-done(((bf16[160,2304]{1,0:T(8,128)(2,1)}), bf16[640,2304]{1,0:T(8,128)(2,1)}) %all-gather.12.cloned.1.call-update) | async-done | bytes 2949136 | tf_op jit(solution)/shard_map/all_gather | solution.py:188
  43.4 2.8 fusion.129
  46.2 51.4 %all-gather.18.cloned.1.call-done = bf16[2304,512]{1,0:T(8,128)(2,1)} async-done(((bf16[288,512]{1,0:T(8,128)(2,1)}), bf16[2304,512]{1,0:T(8,128)(2,1)}) %all-gather.18.cloned.1.call-update) | async-done | bytes 2359312 | tf_op jit(solution)/shard_map/all_gather | solution.py:152
  97.7 3.7 fusion.192
  102.9 2.2 copy.118
  105.1 2.2 copy.117
  107.3 1.8 fusion.127
  109.0 30.4 %all-gather.16.cloned.1.call-done = bf16[2304,256]{1,0:T(8,128)(2,1)} async-done(((bf16[288,256]{1,0:T(8,128)(2,1)}), bf16[2304,256]{1,0:T(8,128)(2,1)}) %all-gather.16.cloned.1.call-update) | async-done | bytes 1179664 | tf_op jit(solution)/shard_map/all_gather | solution.py:153
  139.5 2.4 fusion.191
  143.9 37.5 %all-gather.14.cloned.1.call-done = bf16[2304,256]{1,0:T(8,128)(2,1)} async-done(((bf16[288,256]{1,0:T(8,128)(2,1)}), bf16[2304,256]{1,0:T(8,128)(2,1)}) %all-gather.14.cloned.1.call-update) | async-done | bytes 1179664 | tf_op jit(solution)/shard_map/all_gather | solution.py:154
  181.4 2.3 fusion.190
  184.1 1.9 fusion.112
  190.3 44.0 %all-gather.20.cloned.1.call-done = bf16[512,2304]{0,1:T(8,128)(2,1)} async-done(((bf16[512,288]{0,1:T(8,128)(2,1)}), bf16[512,2304]{0,1:T(8,128)(2,1)}) %all-gather.20.cloned.1.call-update) | async-done | bytes 2359312 | tf_op jit(solution)/shard_map/all_gather | solution.py:155
  234.3 3.4 fusion.193
  237.7 2.6 add_convert_fusion.3
  240.4 35.4 %reduce-scatter.5.cloned.1.call-done = bf16[160,2304]{1,0:T(8,128)(2,1)} async-done(((bf16[640,2304]{1,0:T(8,128)(2,1)}), bf16[160,2304]{1,0:T(8,128)(2,1)}) %reduce-scatter.5.cloned.1.call-update) | async-done | bytes 737296 | tf_op jit(solution)/shard_map/reduce_scatter | solution.py:226
  280.0 2.5 multiply_convert_fusion.2
  287.9 22.2 %all-gather.22.cloned.1.call-done = bf16[640,2304]{1,0:T(8,128)(2,1)} async-done(((bf16[160,2304]{1,0:T(8,128)(2,1)}), bf16[640,2304]{1,0:T(8,128)(2,1)}) %all-gather.22.cloned.1.call-update) | async-done | bytes 2949136 | tf_op jit(solution)/shard_map/all_gather | solution.py:231
  310.1 3.5 fusion.134
  313.5 2.4 fusion.132
  315.9 149.0 %all-gather.24.cloned.1.call-done = bf16[2304,2304]{1,0:T(8,128)(2,1)} async-done(((bf16[288,2304]{1,0:T(8,128)(2,1)}), bf16[2304,2304]{1,0:T(8,128)(2,1)}) %all-gather.24.cloned.1.call-update) | async-done | bytes 10616848 | tf_op jit(solution)/shard_map/all_gather | solution.py:156
  465.0 9.6 fusion.194
  474.5 3.4 convolution_add_fusion.2
  478.0 140.1 %all-gather.26.cloned.1.call-done = bf16[2304,2304]{1,0:T(8,128)(2,1)} async-done(((bf16[288,2304]{1,0:T(8,128)(2,1)}), bf16[2304,2304]{1,0:T(8,128)(2,1)}) %all-gather.26.cloned.1.call-update) | async-done | bytes 10616848 | tf_op jit(solution)/shard_map/all_gather | solution.py:157
  618.0 9.5 fusion.195
  627.6 4.2 multiply_convert_fusion.1
  634.9 136.1 %all-gather.28.cloned.1.call-done = bf16[2304,2304]{0,1:T(8,128)(2,1)} async-done(((bf16[2304,288]{0,1:T(8,128)(2,1)}), bf16[2304,2304]{0,1:T(8,128)(2,1)}) %all-gather.28.cloned.1.call-update) | async-done | bytes 10616848 | tf_op jit(solution)/shard_map/all_gather | solution.py:158
  771.0 10.4 fusion.196
  781.4 2.6 add_convert_fusion.2
  784.1 35.0 %reduce-scatter.7.cloned.1.call-done = bf16[160,2304]{1,0:T(8,128)(2,1)} async-done(((bf16[640,2304]{1,0:T(8,128)(2,1)}), bf16[160,2304]{1,0:T(8,128)(2,1)}) %reduce-scatter.7.cloned.1.call-update) | async-done | bytes 737296 | tf_op jit(solution)/shard_map/reduce_scatter | solution.py:237
  819.2 1.8 fusion.39
  820.9 2.6 fusion.27
  823.6 27.5 %all-gather.30.cloned.1.call-done = bf16[640,2304]{1,0:T(8,128)(2,1)} async-done(((bf16[160,2304]{1,0:T(8,128)(2,1)}), bf16[640,2304]{1,0:T(8,128)(2,1)}) %all-gather.30.cloned.1.call-update) | async-done | bytes 2949136 | tf_op jit(solution)/shard_map/all_gather | solution.py:243
  851.1 11.4 fusion.197
  863.5 8.0 fusion.6
  874.5 12.2 fusion.199
  886.7 12.2 fusion.198
  898.8 7.3 add_convert_fusion.1
  906.7 36.3 %reduce-scatter.9.cloned.1.call-done = bf16[160,2304]{1,0:T(8,128)(2,1)} async-done(((bf16[640,2304]{1,0:T(8,128)(2,1)}), bf16[160,2304]{1,0:T(8,128)(2,1)}) %reduce-scatter.9.cloned.1.call-update) | async-done | bytes 737296 | tf_op jit(solution)/shard_map/reduce_scatter | solution.py:250
  943.1 2.1 multiply_reduce_fusion
  945.2 4.2 fusion.33
  952.6 3.3 fusion.208
  961.7 17.8 %all-gather.32.cloned.1.call-done = bf16[640,2304]{1,0:T(8,128)(2,1)} async-done(((bf16[160,2304]{1,0:T(8,128)(2,1)}), bf16[640,2304]{1,0:T(8,128)(2,1)}) %all-gather.32.cloned.1.call-update) | async-done | bytes 2949136 | tf_op jit(solution)/shard_map/all_gather | solution.py:255
  979.5 2.8 fusion.130
  982.7 3.8 fusion.200
  988.8 2.2 fusion.8
  994.4 1.6 fusion.107
  998.7 2.2 copy.74
  1003.6 3.6 fusion.128
  1007.2 3.4 fusion.126
  1010.6 3.5 fusion.124
  1017.9 4.0 multiply_convert_fusion.3
  1024.9 1.8 fusion.201
  1026.7 10.2 add_convert_fusion
  1037.5 90.8 %all-reduce.7.cloned.1.call-done = (bf16[8,16,512]{2,1,0:T(8,128)(2,1)}, bf16[8,16,2304]{2,1,0:T(8,128)(2,1)}, bf16[8,16,512]{2,1,0:T(8,128)(2,1)}, bf16[8,16,25...) async-done(((bf16[8,16,512]{2,1,0:T(8,128)(2,1)}, bf16[8,16,2304]{2,1,0:T(8,128)(2,1)}, ...) | async-done | bytes 2162704 | tf_op jit(solution)/shard_map/psum | solution.py:310
  1128.3 1.7 convert_element_type.291
  1133.1 1.6 convert_element_type.295
  1134.8 2.2 convert_element_type.293
  1139.2 27.3 %reduce-scatter.11.cloned.1.call-done = bf16[160,2304]{1,0:T(8,128)(2,1)} async-done(((bf16[640,2304]{1,0:T(8,128)(2,1)}), bf16[160,2304]{1,0:T(8,128)(2,1)}) %reduce-scatter.11.cloned.1.call-update) | async-done | bytes 737296 | tf_op jit(solution)/shard_map/reduce_scatter | solution.py:298
  1168.0 2.7 fusion.45
  1170.7 183.6 %all-reduce.5.cloned.1.call-done = (f32[8,16,2304]{2,1,0:T(8,128)}, f32[8,16,2304]{2,1,0:T(8,128)}, f32[8,16,2304]{2,1,0:T(8,128)}, f32[8,16,2304]{2,1,0:T(8,128...) async-done(((f32[8,16,2304]{2,1,0:T(8,128)}, f32[8,16,2304]{2,1,0:T(8,128)}, f32[8,16,2304]{2,1,0:T(8,128)}, f32[8,16,2304]{2,1,0:T(8,128)}, ...) | async-done | bytes 8257552 | tf_op jit(solution)/shard_map/psum | solution.py:315
  1354.2 2.5 copy.208
  (406 shorter events, 79.1 us)
Async XLA Ops:
  7.2 13.1 copy-start
  7.2 9.3 copy-start.110
  7.2 9.4 copy-start.133
  7.2 10.0 copy-start.116
  7.2 10.7 copy-start.117
  7.2 11.5 copy-start.107
  7.3 12.3 copy-start.108
  7.3 14.0 %copy-start.58 = (bf16[8,16,2304]{2,1,0:T(8,128)(2,1)S(1)}, bf16[8,16,2304]{2,1,0:T(8,128)(2,1)}, u32[]{:S(2)}) copy-start(bf16[8,16,2304]{2,1,0:T(8,128)(2,1)} %param.38) | copy-start | bytes 1769476
  7.3 15.0 %copy-start.59 = (bf16[8,16,2304]{2,1,0:T(8,128)(2,1)S(1)}, bf16[8,16,2304]{2,1,0:T(8,128)(2,1)}, u32[]{:S(2)}) copy-start(bf16[8,16,2304]{2,1,0:T(8,128)(2,1)} %param.39) | copy-start | bytes 1769476
  7.3 36.1 %all-gather.12.cloned.1.call-start = ((), (), s32[]{:S(2)}) async-start(), calls=%async_computation.4 | async-start | bytes 3686400 | tf_op jit(solution)/shard_map/all_gather | solution.py:188
  10.8 11.8 copy-start.94
  10.8 269.1 %copy-start.78 = (f32[2304]{0:T(1024)}, f32[2304]{0:T(1024)S(1)}, u32[]{:S(2)}) copy-start(f32[2304]{0:T(1024)S(1)} %get-tuple-element.20) | copy-start | bytes 27652
  10.8 11.8 copy-start.60
  13.1 84.6 %all-gather.18.cloned.1.call-start = ((), (), s32[]{:S(2)}) async-start(), calls=%async_computation.7 | async-start | bytes 2654208 | tf_op jit(solution)/shard_map/all_gather | solution.py:152
  13.9 125.6 %all-gather.16.cloned.1.call-start = ((), (), s32[]{:S(2)}) async-start(), calls=%async_computation.6 | async-start | bytes 1327104 | tf_op jit(solution)/shard_map/all_gather | solution.py:153
  14.6 166.8 %all-gather.14.cloned.1.call-start = ((), (), s32[]{:S(2)}) async-start(), calls=%async_computation.5 | async-start | bytes 1327104 | tf_op jit(solution)/shard_map/all_gather | solution.py:154
  15.2 219.1 %all-gather.20.cloned.1.call-start = ((), (), s32[]{:S(2)}) async-start(), calls=%async_computation.8 | async-start | bytes 2654208 | tf_op jit(solution)/shard_map/all_gather | solution.py:155
  15.8 260.0 %reduce-scatter.5.cloned.1.call-start = ((), (), s32[]{:S(2)}) async-start(), calls=%async_computation.9 | async-start | bytes 3686400 | tf_op jit(solution)/shard_map/reduce_scatter | solution.py:226
  15.8 10.5 copy-start.134
  17.1 166.9 %copy-start.112 = (f32[640]{0:T(1024)}, f32[640]{0:T(1024)S(1)}, u32[]{:S(2)}) copy-start(f32[640]{0:T(1024)S(1)} %add_convert_fusion.5) | copy-start | bytes 7684
  22.6 120.5 %copy-start.73 = (bf16[1,16,2304]{2,0,1:T(2,128)(2,1)}, bf16[1,16,2304]{2,0,1:T(2,128)(2,1)S(1)}, u32[]{:S(2)}) copy-start(bf16[1,16,2304]{2,0,1:T(2,128)(2,1)S(1)} %fusion.92) | copy-start | bytes 221188
  24.3 164.2 %copy-start.24 = (pred[640,640]{0,1:T(8,128)(4,1)}, pred[640,640]{0,1:T(8,128)(4,1)S(1)}, u32[]{:S(2)}) copy-start(pred[640,640]{0,1:T(8,128)(4,1)S(1)} %fusion.25) | copy-start | bytes 1228804
  43.4 54.3 %copy-start.2 = (bf16[640,2304]{1,0:T(8,128)(2,1)S(1)}, bf16[640,2304]{1,0:T(8,128)(2,1)}, u32[]{:S(2)}) copy-start(bf16[640,2304]{1,0:T(8,128)(2,1)} %all-gather.12.cloned.1.call-done) | copy-start | bytes 8847364
  46.2 55.2 %copy-start.92 = (bf16[640,16]{0,1:T(8,128)(2,1)}, bf16[640,16]{0,1:T(8,128)(2,1)S(1)}, u32[]{:S(2)}) copy-start(bf16[640,16]{0,1:T(8,128)(2,1)S(1)} %fusion.129) | copy-start | bytes 61444
  109.0 32.9 %copy-start.103 = (bf16[640,16]{0,1:T(8,128)(2,1)}, bf16[640,16]{0,1:T(8,128)(2,1)S(1)}, u32[]{:S(2)}) copy-start(bf16[640,16]{0,1:T(8,128)(2,1)S(1)} %fusion.127) | copy-start | bytes 61444
  143.9 39.8 %copy-start.90 = (bf16[640,16]{0,1:T(8,128)(2,1)}, bf16[640,16]{0,1:T(8,128)(2,1)S(1)}, u32[]{:S(2)}) copy-start(bf16[640,16]{0,1:T(8,128)(2,1)S(1)} %fusion.125) | copy-start | bytes 61444
  143.9 39.9 %copy-start.114 = (bf16[1,16,256]{2,0,1:T(2,128)(2,1)S(1)}, bf16[1,16,256]{2,0,1:T(2,128)(2,1)}, u32[]{:S(2)}) copy-start(bf16[1,16,256]{2,0,1:T(2,128)(2,1)} %fusion.122) | copy-start | bytes 24580
  143.9 40.2 %copy-start.135 = (f32[128]{0:T(128)S(1)}, f32[128]{0:T(128)}, u32[]{:S(2)}) copy-start(f32[128]{0:T(128)} %copy-done.134) | copy-start | bytes 1540
  190.0 47.7 %copy-start.22 = (bf16[256,2,640]{2,0,1:T(8,128)(2,1)}, bf16[256,2,640]{2,0,1:T(8,128)(2,1)S(1)}, u32[]{:S(2)}) copy-start(bf16[256,2,640]{2,0,1:T(8,128)(2,1)S(1)} %fusion.54) | copy-start | bytes 1966084
  190.3 47.5 %copy-start.99 = (bf16[640,16]{0,1:T(8,128)(2,1)}, bf16[640,16]{0,1:T(8,128)(2,1)S(1)}, u32[]{:S(2)}) copy-start(bf16[640,16]{0,1:T(8,128)(2,1)S(1)} %fusion.141) | copy-start | bytes 61444
  190.3 47.5 %copy-start.54 = (bf16[1,16,2304]{2,0,1:T(2,128)(2,1)S(1)}, bf16[1,16,2304]{2,0,1:T(2,128)(2,1)}, u32[]{:S(2)}) copy-start(bf16[1,16,2304]{2,0,1:T(2,128)(2,1)} %fusion.86) | copy-start | bytes 221188
  240.3 37.4 %copy-start.5 = (bf16[160,2304]{1,0:T(8,128)(2,1)S(1)}, bf16[160,2304]{1,0:T(8,128)(2,1)}, u32[]{:S(2)}) copy-start(bf16[160,2304]{1,0:T(8,128)(2,1)} %param.27) | copy-start | bytes 2211844
  240.3 39.6 %copy-start.97 = (f32[2304]{0:T(1024)S(1)}, f32[2304]{0:T(1024)}, u32[]{:S(2)}) copy-start(f32[2304]{0:T(1024)} %get-tuple-element.19) | copy-start | bytes 27652
  240.4 69.7 %all-gather.22.cloned.1.call-start = ((), (), s32[]{:S(2)}) async-start(), calls=%async_computation.10 | async-start | bytes 3686400 | tf_op jit(solution)/shard_map/all_gather | solution.py:231
  282.5 182.5 %all-gather.24.cloned.1.call-start = ((), (), s32[]{:S(2)}) async-start(), calls=%async_computation.11 | async-start | bytes 11943936 | tf_op jit(solution)/shard_map/all_gather | solution.py:156
  283.3 334.8 %all-gather.26.cloned.1.call-start = ((), (), s32[]{:S(2)}) async-start(), calls=%async_computation.12 | async-start | bytes 11943936 | tf_op jit(solution)/shard_map/all_gather | solution.py:157
  284.0 487.0 %all-gather.28.cloned.1.call-start = ((), (), s32[]{:S(2)}) async-start(), calls=%async_computation.13 | async-start | bytes 11943936 | tf_op jit(solution)/shard_map/all_gather | solution.py:158
  284.6 534.6 %reduce-scatter.7.cloned.1.call-start = ((), (), s32[]{:S(2)}) async-start(), calls=%async_computation.14 | async-start | bytes 3686400 | tf_op jit(solution)/shard_map/reduce_scatter | solution.py:237
  464.9 9.6 copy-start.86
  618.0 9.6 copy-start.9
  618.0 9.6 copy-start.84
  771.0 10.4 copy-start.88
  784.0 35.1 %copy-start.96 = (f32[2304]{0:T(1024)S(1)}, f32[2304]{0:T(1024)}, u32[]{:S(2)}) copy-start(f32[2304]{0:T(1024)} %get-tuple-element.18) | copy-start | bytes 27652
  784.1 67.1 %all-gather.30.cloned.1.call-start = ((), (), s32[]{:S(2)}) async-start(), calls=%async_computation.15 | async-start | bytes 3686400 | tf_op jit(solution)/shard_map/all_gather | solution.py:243
  823.6 119.5 %reduce-scatter.9.cloned.1.call-start = ((), (), s32[]{:S(2)}) async-start(), calls=%async_computation.16 | async-start | bytes 3686400 | tf_op jit(solution)/shard_map/reduce_scatter | solution.py:250
  851.1 11.4 copy-start.11
  871.5 15.2 %copy-start.15 = (bf16[640,2304]{1,0:T(8,128)(2,1)}, bf16[640,2304]{1,0:T(8,128)(2,1)S(1)}, u32[]{:S(2)}) copy-start(bf16[640,2304]{1,0:T(8,128)(2,1)S(1)} %get-tuple-element.46) | copy-start | bytes 8847364
  906.1 36.9 %copy-start.79 = (f32[2304]{0:T(1024)S(1)}, f32[2304]{0:T(1024)}, u32[]{:S(2)}) copy-start(f32[2304]{0:T(1024)} %copy-done.78) | copy-start | bytes 27652
  906.2 36.9 %copy-start.98 = (f32[2304]{0:T(1024)S(1)}, f32[2304]{0:T(1024)}, u32[]{:S(2)}) copy-start(f32[2304]{0:T(1024)} %get-tuple-element.19) | copy-start | bytes 27652
  906.2 36.9 %copy-start.121 = (f32[160]{0:T(256)S(1)}, f32[160]{0:T(256)}, u32[]{:S(2)}) copy-start(f32[160]{0:T(256)} %copy-done.120) | copy-start | bytes 1924
  906.2 39.0 %copy-start.130 = (f32[160]{0:T(256)S(1)}, f32[160]{0:T(256)}, u32[]{:S(2)}) copy-start(f32[160]{0:T(256)} %copy-done.129) | copy-start | bytes 1924
  906.2 39.0 %copy-start.140 = (f32[160]{0:T(256)S(1)}, f32[160]{0:T(256)}, u32[]{:S(2)}) copy-start(f32[160]{0:T(256)} %get-tuple-element.67) | copy-start | bytes 1924
  906.2 73.3 %all-gather.32.cloned.1.call-start = ((), (), s32[]{:S(2)}) async-start(), calls=%async_computation.17 | async-start | bytes 3686400 | tf_op jit(solution)/shard_map/all_gather | solution.py:255
  951.9 176.5 %all-reduce.7.cloned.1.call-start = ((), (), s32[]{:S(2)}) async-start(), calls=%async_computation.20 | async-start | bytes 4325376 | tf_op jit(solution)/shard_map/psum | solution.py:310
  952.5 34.4 %copy-start.126 = (f32[2,640]{1,0:T(2,128)}, f32[2,640]{1,0:T(2,128)S(1)}, u32[]{:S(2)}) copy-start(f32[2,640]{1,0:T(2,128)S(1)} %log_add_fusion) | copy-start | bytes 15364
  959.4 20.1 %copy-start.55 = (bf16[1,16,2304]{2,0,1:T(2,128)(2,1)S(1)}, bf16[1,16,2304]{2,0,1:T(2,128)(2,1)}, u32[]{:S(2)}) copy-start(bf16[1,16,2304]{2,0,1:T(2,128)(2,1)} %fusion.86) | copy-start | bytes 221188
  1021.9 144.6 %reduce-scatter.11.cloned.1.call-start = ((), (), s32[]{:S(2)}) async-start(), calls=%async_computation.18 | async-start | bytes 3686400 | tf_op jit(solution)/shard_map/reduce_scatter | solution.py:298
  1036.9 317.3 %all-reduce.5.cloned.1.call-start = ((), (), s32[]{:S(2)}) async-start(), calls=%async_computation.19 | async-start | bytes 16515072 | tf_op jit(solution)/shard_map/psum | solution.py:315
  1128.3 9.8 copy-start.56
  1131.6 35.0 %copy-start.6 = (bf16[160,2304]{1,0:T(8,128)(2,1)S(1)}, bf16[160,2304]{1,0:T(8,128)(2,1)}, u32[]{:S(2)}) copy-start(bf16[160,2304]{1,0:T(8,128)(2,1)} %param.27) | copy-start | bytes 2211844
  1131.6 35.0 %copy-start.95 = (f32[2304]{0:T(1024)S(1)}, f32[2304]{0:T(1024)}, u32[]{:S(2)}) copy-start(f32[2304]{0:T(1024)} %copy-done.94) | copy-start | bytes 27652
  1137.0 31.0 %copy-start.18 = (f32[160,2304]{1,0:T(8,128)S(1)}, f32[160,2304]{1,0:T(8,128)}, u32[]{:S(2)}) copy-start(f32[160,2304]{1,0:T(8,128)} %copy-done.17) | copy-start | bytes 4423684
  1137.0 31.0 %copy-start.132 = (f32[160]{0:T(256)S(1)}, f32[160]{0:T(256)}, u32[]{:S(2)}) copy-start(f32[160]{0:T(256)} %copy-done.131) | copy-start | bytes 1924
  1137.0 31.0 %copy-start.139 = (f32[160]{0:T(256)S(1)}, f32[160]{0:T(256)}, u32[]{:S(2)}) copy-start(f32[160]{0:T(256)} %get-tuple-element.63) | copy-start | bytes 1924
  (94 other events, 289.3 us)
Sparse Core Ops, SparseCore 0:
  13.2 30.1 all-gather.11
  45.6 52.0 all-gather.17
  99.9 39.5 all-gather.15
  141.5 39.8 all-gather.13
  183.4 50.8 all-gather.19
  240.5 35.2 reduce-scatter.4
  282.6 27.4 all-gather.21
  312.5 152.4 all-gather.23
  467.4 150.6 all-gather.25
  620.3 150.6 all-gather.27
  784.2 34.9 reduce-scatter.6
  823.7 27.4 all-gather.29
  906.3 36.6 reduce-scatter.8
  952.0 27.4 all-gather.31
  1022.0 106.2 all-reduce.6
  1130.9 35.5 reduce-scatter.10
  1173.9 180.2 all-reduce.4
where the time goes:
time: 1380 us; the launch traced here: 1370 us
  waiting for transfers between devices  1090 us (79%)
  matrix products  187 us (14%)
  other arithmetic  55.4 us (4%)
  local copies, waits for them, and re-layouts  22.7 us (2%)
  between operations  16.2 us (1%)
    psum x1, waiting for transfers between devices, on_device(): lax.psum((hot_rows * query_back[1][None], hot_rows * key_back[1][None], h...  184 us
    all_gather x1, waiting for transfers between devices, on_device(): lax.all_gather(w_gate, 'dp', axis=0, tiled=True)  149 us
    all_gather x1, waiting for transfers between devices, on_device(): lax.all_gather(w_up, 'dp', axis=0, tiled=True)  140 us
    all_gather x1, waiting for transfers between devices, on_device(): lax.all_gather(w_down, 'dp', axis=1, tiled=True)  136 us
    psum x1, waiting for transfers between devices, on_device(): lax.psum((hot_rows * output_back[1][None]).astype(jnp.bfloat16), 'dp')  90.8 us
    dot_general x21, matrix products, product(): return jnp.dot(former, latter, preferred_element_type=jnp.float32)  83.2 us
    dot_general x7, matrix products, project_back(): jnp.einsum('lo,io->li', upstream, weight, preferred_element_type=jnp.floa...  52.5 us
    all_gather x1, waiting for transfers between devices, on_device(): lax.all_gather(w_query, 'dp', axis=0, tiled=True)  51.4 us
  transfers between devices with their start and end apart: 17, of which 17 were waited for; matrix products, arithmetic and copies ran while one was open for 8% of the time, Pallas kernels for 0%

commit v1 on v0

v1 whole, which is shorter than its diff:
```python
import math

import jax
import jax.numpy as jnp
from jax import lax
from jax.experimental import pallas as pl
from jax.experimental.pallas import tpu as pltpu
from jax.sharding import PartitionSpec as P

HEAD_WIDTH = 256
ADAPTERS = 8


def rms_scale(value_rows, gain_row):
    inverse = lax.rsqrt(jnp.mean(value_rows * value_rows, axis=-1, keepdims=True) + 1e-06)
    return value_rows * inverse * gain_row


def rms_back(value_rows, gain_row, upstream):
    inverse = lax.rsqrt(jnp.mean(value_rows * value_rows, axis=-1, keepdims=True) + 1e-06)
    scaled = gain_row * upstream
    return inverse * scaled - value_rows * (inverse * inverse * inverse) * jnp.mean(
        value_rows * scaled, axis=-1, keepdims=True
    )


def pick_from(lookup, indices, labels):
    return jnp.sum(jnp.where(indices[:, None] == labels[None, :], lookup[None, :], 0), axis=1)


def tree_tables(segments, parents, order):
    count_seg = parents.shape[0]
    sequence_length = segments.shape[0]
    blocks = order.shape[0]
    labels = jnp.arange(count_seg, dtype=jnp.int32)
    ordered_places = jnp.arange(sequence_length, dtype=jnp.int32)
    member = segments[None, :] == labels[:, None]
    starts = jnp.min(jnp.where(member, ordered_places[None, :], sequence_length), axis=1)
    counts = jnp.sum(member.astype(jnp.int32), axis=1)
    grands = pick_from(parents, parents, labels)
    offsets = jnp.where(parents != labels, pick_from(counts, parents, labels), 0) + jnp.where(
        grands != parents, pick_from(counts, grands, labels), 0
    )
    block_rows = sequence_length // blocks
    chosen = order[:, None] == jnp.arange(blocks, dtype=jnp.int32)[None, :]
    segments = jnp.sum(
        jnp.where(chosen[:, :, None], segments.reshape(1, blocks, block_rows), 0), axis=1
    ).reshape(sequence_length)
    places = (
        order[:, None] * block_rows + jnp.arange(block_rows, dtype=jnp.int32)[None, :]
    ).reshape(sequence_length)
    tok_start = pick_from(starts, segments, labels)
    tok_offset = pick_from(offsets, segments, labels)
    tok_parent = pick_from(parents, segments, labels)
    tok_grand = pick_from(grands, segments, labels)
    positions = (places - tok_start + tok_offset).astype(jnp.float32)
    same_seg = (segments[None, :] == segments[:, None]) & (places[None, :] <= places[:, None])
    from_parent = (segments[None, :] == tok_parent[:, None]) & (tok_parent != segments)[:, None]
    from_grand = (segments[None, :] == tok_grand[:, None]) & (tok_grand != tok_parent)[:, None]
    visible = same_seg | from_parent | from_grand
    inv_freq = jnp.exp(
        jnp.arange(HEAD_WIDTH // 2, dtype=jnp.float32) * (-2.0 * math.log(10000.0) / HEAD_WIDTH)
    )
    angles = positions[:, None] * inv_freq[None, :]
    return (visible, jnp.cos(angles), jnp.sin(angles))


def apply_rotary(value_rows, cos_rows, sin_rows):
    half_size = value_rows.shape[-1] // 2
    front_half = value_rows[..., :half_size]
    back_half = value_rows[..., half_size:]
    return jnp.concatenate(
        [
            front_half * cos_rows - back_half * sin_rows,
            back_half * cos_rows + front_half * sin_rows,
        ],
        axis=-1,
    )


def rotate_back(value_rows, cos_rows, sin_rows):
    return apply_rotary(value_rows, cos_rows, -sin_rows)


def product(former, latter):
    return jnp.dot(former, latter, preferred_element_type=jnp.float32)


def times_rows(former, latter):
    return lax.dot_general(
        former, latter, (((1,), (1,)), ((), ())), preferred_element_type=jnp.float32
    )


def over_rows(former, latter):
    return lax.dot_general(
        former, latter, (((0,), (0,)), ((), ())), preferred_element_type=jnp.float32
    )


def low(values):
    return values.astype(jnp.bfloat16)


def select(onehot, stacked):
    return low(jnp.einsum("e,erc->rc", onehot, stacked, preferred_element_type=jnp.float32))


def score_block(query_rows, rotated_keys, visible):
    scores = jnp.einsum(
        "qngd,knd->ngqk", query_rows, rotated_keys, preferred_element_type=jnp.float32
    )
    bounded = jnp.tanh(scores / 50.0)
    masked = jnp.where(visible[None, None], 50.0 * bounded, -1e30)
    return (bounded, masked)


def activate(gate_in, up_in):
    return jax.nn.gelu(gate_in, approximate=True) * up_in


def flip(values, axis_name, bit):
    size = lax.axis_size(axis_name)
    return lax.ppermute(values, axis_name, [(i, i ^ bit) for i in range(size)])


def gather_blocks(pieces, columns_z):
    along_z, stacks, along_x = [], [], []
    for i, (mine, other) in enumerate(pieces):
        needs = []
        if i >= 1:
            needs += along_z[i - 1]
        if i >= 2:
            needs.append(along_x[i - 2])
        if needs:
            mine, other, *_ = lax.optimization_barrier((mine, other, *needs))
        got = [flip(other if k % 2 else mine, "dp", 2 * k) for k in range(1, columns_z)]
        along_z.append(got)
        stack = jnp.stack([mine] + got)
        stacks.append(stack)
        if i >= 1:
            stack, _ = lax.optimization_barrier((stack, along_x[i - 1]))
        along_x.append(flip(stack, "dp", 1))
    return stacks, along_x


def assemble(stacks, crossed, slots):
    columns_z, _, columns = stacks[0].shape
    rows = sum(stack.shape[1] for stack in stacks)
    count = len(stacks)

    def kernel(slots_ref, *refs):
        out_ref, sems = refs[2 * count], refs[2 * count + 1]
        copies = []
        for side in range(2):
            first = 0
            for i in range(count):
                source = refs[side * count + i]
                height = source.shape[1]
                for k in range(columns_z):
                    slot = slots_ref[side * columns_z + k]
                    copies.append(
                        pltpu.make_async_copy(
                            source.at[k],
                            out_ref.at[slot, pl.ds(first, height)],
                            sems.at[len(copies)],
                        )
                    )
                first += height
        for copy in copies:
            copy.start()
        for copy in copies:
            copy.wait()

    out = pl.pallas_call(
        kernel,
        out_shape=jax.ShapeDtypeStruct((2 * columns_z, rows, columns), stacks[0].dtype),
        in_specs=[pl.BlockSpec(memory_space=pltpu.SMEM)]
        + [pl.BlockSpec(memory_space=pl.ANY)] * (2 * count),
        out_specs=pl.BlockSpec(memory_space=pl.ANY),
        scratch_shapes=[pltpu.SemaphoreType.DMA((2 * count * columns_z,))],
        cost_estimate=pl.CostEstimate(
            flops=0,
            transcendentals=0,
            bytes_accessed=4 * 2 * columns_z * rows * columns,
        ),
    )(slots, *stacks, *crossed)
    return out.reshape(2 * columns_z * rows, columns)


def gather_pair(own):
    pair = jnp.concatenate([own, flip(own, "tensor", 2)])
    return jnp.concatenate([pair, flip(pair, "tensor", 1)])


def scatter_pair(part):
    rows = part.shape[0] // 4
    part = low(part)
    got = flip(part[2 * rows :], "tensor", 1).astype(jnp.float32)
    kept = part[: 2 * rows].astype(jnp.float32) + got
    last = flip(low(kept[rows:]), "tensor", 2)
    return kept[:rows] + last.astype(jnp.float32)


def gather_square(own):
    half = own.shape[0] // 2
    from_y = flip(own, "tensor", 2)
    from_z = flip(own, "dp", 2)
    three = jnp.concatenate([own, from_y, from_z])
    three_core = flip(three, "tensor", 1)
    diagonal = jnp.concatenate(
        [flip(from_y[:half], "dp", 2), flip(from_z[half:], "tensor", 2)]
    )
    diagonal_core = flip(diagonal, "tensor", 1)
    return jnp.concatenate([three, diagonal, three_core, diagonal_core])


def scatter_square(part):
    rows = part.shape[0] // 8
    half = rows // 2
    part = low(part)
    got = flip(part[4 * rows :], "tensor", 1).astype(jnp.float32)
    kept = part[: 4 * rows].astype(jnp.float32) + got
    kept_low = low(kept)
    mine, to_y, to_z, to_zy = (kept[i * rows : (i + 1) * rows] for i in range(4))
    low_y, low_z, low_zy = (kept_low[i * rows : (i + 1) * rows] for i in range(1, 4))
    got_y = flip(jnp.concatenate([low_y[:half], low_zy[:half]]), "tensor", 2)
    got_z = flip(jnp.concatenate([low_z[half:], low_zy[half:]]), "dp", 2)
    got_y, got_z = got_y.astype(jnp.float32), got_z.astype(jnp.float32)
    last_y = flip(low(to_y[half:] + got_z[half:]), "tensor", 2).astype(jnp.float32)
    last_z = flip(low(to_z[:half] + got_y[half:]), "dp", 2).astype(jnp.float32)
    return jnp.concatenate(
        [mine[:half] + got_y[:half] + last_z, mine[half:] + got_z[:half] + last_y]
    )


def on_device(
    layer_input,
    cotangent,
    norm_gains,
    w_query,
    w_key,
    w_value,
    w_output,
    w_gate,
    w_up,
    w_down,
    query_shrink,
    key_shrink,
    value_shrink,
    output_shrink,
    gate_shrink,
    up_shrink,
    down_shrink,
    query_expand,
    key_expand,
    value_expand,
    output_expand,
    gate_expand,
    up_expand,
    down_expand,
    adapter_ids,
    parent_segments,
    segment_ids,
):
    trees = lax.axis_size("dp")
    columns_z = trees // 2
    my_tree = lax.axis_index("dp")
    my_z, my_x = my_tree // 2, my_tree % 2
    my_part = lax.axis_index("tensor")
    odd = my_z % 2 == 1
    norm_gain = norm_gains.astype(jnp.float32)

    def my_half(values):
        half = values.shape[-1] // 2
        return jnp.where(odd, values[..., half:], values[..., :half])

    def other_half(values):
        half = values.shape[-1] // 2
        return jnp.where(odd, values[..., :half], values[..., half:])

    own_rows = layer_input.astype(jnp.float32)
    normed = low(rms_scale(own_rows, norm_gain[0]))
    normed_all = gather_pair(normed)

    w_qkv = jnp.concatenate([w_query, w_key, w_value], axis=1)
    w_out_t = w_output.T
    w_down_t = w_down.T
    depth = w_qkv.shape[0]
    cut = depth // 2 // 16 * 16
    pieces = [(w_qkv[:cut],) * 2, (w_qkv[cut:],) * 2, (w_out_t,) * 2]
    for matrix in (w_gate, w_up, w_down_t):
        mine, other = my_half(matrix), other_half(matrix)
        pieces += [(mine[:cut], other[:cut]), (mine[cut:], other[cut:])]
    stacks, crossed = gather_blocks(pieces, columns_z)
    slots = jnp.stack(
        [(my_z ^ k) * 2 + my_x for k in range(columns_z)]
        + [(my_z ^ k) * 2 + 1 - my_x for k in range(columns_z)]
    ).astype(jnp.int32)
    full_qkv = assemble(stacks[0:2], crossed[0:2], slots)
    full_out_t = assemble(stacks[2:3], crossed[2:3], slots)
    full_gate = assemble(stacks[3:5], crossed[3:5], slots)
    full_up = assemble(stacks[5:7], crossed[5:7], slots)
    full_down_t = assemble(stacks[7:9], crossed[7:9], slots)

    all_ids = lax.all_gather(adapter_ids, "dp", axis=0, tiled=True)
    labels = jnp.arange(ADAPTERS, dtype=jnp.int32)
    onehots = low(all_ids[:, None] == labels[None, :])
    onehot = low(labels == adapter_ids[0])
    near_id = jnp.sum(
        jnp.where(jnp.arange(trees, dtype=jnp.int32) == my_tree ^ 2, all_ids, 0)
    )
    onehot_near = low(labels == near_id)

    def both(stacked):
        return jnp.concatenate([select(onehot, stacked), select(onehot_near, stacked)])

    s_qkv = jnp.concatenate(
        [select(onehot, stacked) for stacked in (query_shrink, key_shrink, value_shrink)]
    )
    e_parts = [select(onehot, stacked) for stacked in (query_expand, key_expand, value_expand)]
    rank = e_parts[0].shape[0]
    widths = [part.shape[1] for part in e_parts]
    e_qkv = jnp.concatenate(
        [
            jnp.pad(part, ((0, 0), (sum(widths[:i]), sum(widths[i + 1 :]))))
            for i, part in enumerate(e_parts)
        ]
    )
    s_output, e_output = select(onehot, output_shrink), select(onehot, output_expand)
    s_gate_up = jnp.concatenate([both(gate_shrink), both(up_shrink)])
    e_gate, e_up = my_half(both(gate_expand)), my_half(both(up_expand))
    s_down, e_down = my_half(both(down_shrink)), both(down_expand)

    sequence_length = normed_all.shape[0]
    order = jnp.stack([my_part, my_part ^ 2, my_part ^ 1, my_part ^ 3]).astype(jnp.int32)
    visible, cos_rows, sin_rows = tree_tables(segment_ids, parent_segments[0], order)
    cosine_per_head = cos_rows[:, None, :]
    sine_per_head = sin_rows[:, None, :]
    inner_qkv = low(times_rows(normed_all, s_qkv))
    qkv_pre = product(normed_all, full_qkv) + product(inner_qkv, e_qkv)
    query_pre = qkv_pre[:, : widths[0]]
    key_before_rotation = qkv_pre[:, widths[0] : widths[0] + widths[1]]
    value_projected = qkv_pre[:, widths[0] + widths[1] :]
    heads_q = widths[0] // HEAD_WIDTH
    heads_kv = widths[1] // HEAD_WIDTH
    head_groups = heads_q // heads_kv
    query_rows = low(
        apply_rotary(
            query_pre.reshape(sequence_length, heads_q, HEAD_WIDTH),
            cosine_per_head,
            sine_per_head,
        )
        * HEAD_WIDTH ** (-0.5)
    ).reshape(sequence_length, heads_kv, head_groups, HEAD_WIDTH)
    rotated_keys = low(
        apply_rotary(
            key_before_rotation.reshape(sequence_length, heads_kv, HEAD_WIDTH),
            cosine_per_head,
            sine_per_head,
        )
    )
    value_rows = low(value_projected).reshape(sequence_length, heads_kv, HEAD_WIDTH)
    bounded, masked = score_block(query_rows, rotated_keys, visible)
    row_max = jnp.max(masked, axis=-1, keepdims=True)
    exponent = jnp.exp(masked - row_max)
    row_total = jnp.sum(exponent, axis=-1, keepdims=True)
    log_total = row_max + jnp.log(row_total)
    probs_low = low(exponent / row_total)
    mixed_heads = low(
        jnp.einsum(
            "ngqk,knd->qngd", probs_low, value_rows, preferred_element_type=jnp.float32
        ).reshape(sequence_length, heads_q * HEAD_WIDTH)
    )
    inner_output = low(times_rows(mixed_heads, s_output))
    attn_part = times_rows(mixed_heads, full_out_t) + product(inner_output, e_output)
    attended = scatter_pair(attn_part)
    residual = own_rows + rms_scale(attended, norm_gain[1])

    ffn_rows = gather_square(low(rms_scale(residual, norm_gain[2])))
    block_rows = residual.shape[0]
    row_block = jnp.arange(8 * block_rows, dtype=jnp.int32) // block_rows
    row_near = (row_block // 2 % 2)[:, None]
    rank_near = (jnp.arange(4 * rank, dtype=jnp.int32) // rank % 2)[None, :]
    keep_four = row_near == rank_near
    keep_two = keep_four[:, : 2 * rank]
    inner_gate_up = low(jnp.where(keep_four, times_rows(ffn_rows, s_gate_up), 0.0))
    inner_gate, inner_up = inner_gate_up[:, : 2 * rank], inner_gate_up[:, 2 * rank :]
    gate_pre = product(ffn_rows, full_gate) + product(inner_gate, e_gate)
    up_pre = product(ffn_rows, full_up) + product(inner_up, e_up)
    hidden_full, act_back = jax.vjp(activate, gate_pre, up_pre)
    hidden = low(hidden_full)
    inner_down = low(jnp.where(keep_two, times_rows(hidden, s_down), 0.0))
    ffn_part = times_rows(hidden, full_down_t) + product(inner_down, e_down)
    ffn_out = scatter_square(ffn_part)
    layer_output = low(residual + rms_scale(ffn_out, norm_gain[3]))

    grad_out = cotangent.astype(jnp.float32)
    grad_ffn = gather_square(low(rms_back(ffn_out, norm_gain[3], grad_out)))
    grad_inner_down = low(jnp.where(keep_two, times_rows(grad_ffn, e_down), 0.0))
    grad_hidden = product(grad_ffn, full_down_t) + product(grad_inner_down, s_down)
    grad_gate, grad_up = (low(grad) for grad in act_back(grad_hidden))
    grad_inner_gate = low(jnp.where(keep_two, times_rows(grad_gate, e_gate), 0.0))
    grad_inner_up = low(jnp.where(keep_two, times_rows(grad_up, e_up), 0.0))
    grad_inner_gate_up = jnp.concatenate([grad_inner_gate, grad_inner_up], axis=1)
    grad_normed_part = (
        times_rows(grad_gate, full_gate)
        + times_rows(grad_up, full_up)
        + product(grad_inner_gate_up, s_gate_up)
    )
    grad_normed_ffn = scatter_square(grad_normed_part)
    grad_expand_down = over_rows(inner_down, grad_ffn)
    grad_shrink_down = over_rows(grad_inner_down, hidden)
    grad_expand_gate = over_rows(inner_gate, grad_gate)
    grad_expand_up = over_rows(inner_up, grad_up)
    grad_shrink_gate_up = over_rows(grad_inner_gate_up, ffn_rows)

    grad_resid = grad_out + rms_back(residual, norm_gain[2], grad_normed_ffn)
    grad_attn = gather_pair(low(rms_back(attended, norm_gain[1], grad_resid)))

    grad_inner_output = low(times_rows(grad_attn, e_output))
    grad_mixed = low(
        product(grad_attn, full_out_t) + product(grad_inner_output, s_output)
    ).reshape(sequence_length, heads_kv, head_groups, HEAD_WIDTH)
    grad_expand_output = over_rows(inner_output, grad_attn)
    grad_shrink_output = over_rows(grad_inner_output, mixed_heads)
    bounded, masked = score_block(query_rows, rotated_keys, visible)
    attn_probs = jnp.exp(masked - log_total)
    probs_low = low(attn_probs)
    grad_values = low(
        jnp.einsum("ngqk,qngd->knd", probs_low, grad_mixed, preferred_element_type=jnp.float32)
    ).reshape(sequence_length, heads_kv * HEAD_WIDTH)
    grad_probs = jnp.einsum(
        "qngd,knd->ngqk", grad_mixed, value_rows, preferred_element_type=jnp.float32
    )
    grad_capped = attn_probs * (
        grad_probs - jnp.sum(attn_probs * grad_probs, axis=-1, keepdims=True)
    )
    grad_scores = low(grad_capped * (1.0 - bounded * bounded))
    grad_queries = jnp.einsum(
        "ngqk,knd->qngd", grad_scores, rotated_keys, preferred_element_type=jnp.float32
    ).reshape(sequence_length, heads_q, HEAD_WIDTH)
    grad_keys = jnp.einsum(
        "ngqk,qngd->knd", grad_scores, query_rows, preferred_element_type=jnp.float32
    )
    grad_qpre = low(
        rotate_back(grad_queries * HEAD_WIDTH ** (-0.5), cosine_per_head, sine_per_head)
    ).reshape(sequence_length, heads_q * HEAD_WIDTH)
    grad_kpre = low(rotate_back(grad_keys, cosine_per_head, sine_per_head)).reshape(
        sequence_length, heads_kv * HEAD_WIDTH
    )
    grad_qkv = jnp.concatenate([grad_qpre, grad_kpre, grad_values], axis=1)
    grad_inner_qkv = low(times_rows(grad_qkv, e_qkv))
    grad_normed = scatter_pair(
        times_rows(grad_qkv, full_qkv) + product(grad_inner_qkv, s_qkv)
    )
    grad_expand_qkv = over_rows(inner_qkv, grad_qkv)
    grad_shrink_qkv = over_rows(grad_inner_qkv, normed_all)
    input_grad = grad_resid + rms_back(own_rows, norm_gain[0], grad_normed)

    def by_adapter(hot, gathered):
        return lax.dot_general(
            hot, gathered, (((0,), (0,)), ((), ())), preferred_element_type=jnp.float32
        )

    local = low(
        jnp.concatenate([grad_expand_gate, grad_expand_up, grad_shrink_down], axis=1)
    )
    width = local.shape[1] // 3
    local_all = lax.all_gather(local, "dp", axis=0, tiled=False)
    local_all = local_all.reshape(columns_z // 2, 2, 2, 2, rank, 3 * width)
    hot_grid = onehots.reshape(columns_z // 2, 2, 2, ADAPTERS)
    sums = []
    for parity in range(2):
        hot = jnp.stack([hot_grid[:, parity], hot_grid[:, 1 - parity]], axis=2)
        sums.append(
            by_adapter(
                hot.reshape(2 * trees // 2, ADAPTERS),
                local_all[:, parity].reshape(2 * trees // 2, rank, 3 * width),
            )
        )
    out_expand_gate, out_expand_up, out_shrink_down = (
        jnp.concatenate([part[:, :, i * width : (i + 1) * width] for part in sums], axis=2)
        for i in range(3)
    )

    shared = low(
        jnp.concatenate([grad_shrink_gate_up, grad_expand_down]).reshape(3, 2, rank, -1)
    )
    shared = shared[:, 0].astype(jnp.float32) + flip(shared[:, 1], "dp", 2).astype(jnp.float32)
    shared = low(shared).reshape(3 * rank, -1)
    shared = lax.psum_scatter(shared, "tensor", scatter_dimension=0, tiled=True)
    shared_all = lax.all_gather(shared, ("dp", "tensor"), axis=0, tiled=True)
    shared_all = by_adapter(onehots, shared_all.reshape(trees, 3 * rank, -1))
    out_shrink_gate, out_shrink_up, out_expand_down = (
        shared_all[:, i * rank : (i + 1) * rank] for i in range(3)
    )

    starts = [sum(widths[:i]) for i in range(3)]
    local = low(
        jnp.concatenate(
            [
                grad_expand_qkv[i * rank : (i + 1) * rank, starts[i] : starts[i] + widths[i]]
                for i in range(3)
            ]
            + [grad_shrink_output],
            axis=1,
        )
    )
    local_all = by_adapter(onehots, lax.all_gather(local, "dp", axis=0, tiled=False))
    out_expand_query, out_expand_key, out_expand_value = (
        local_all[:, :, starts[i] : starts[i] + widths[i]] for i in range(3)
    )
    out_shrink_output = local_all[:, :, sum(widths) :]

    shared = low(jnp.concatenate([grad_shrink_qkv, grad_expand_output]))
    shared = lax.psum_scatter(shared, "tensor", scatter_dimension=0, tiled=True)
    shared_all = lax.all_gather(shared, ("dp", "tensor"), axis=0, tiled=True)
    shared_all = by_adapter(onehots, shared_all.reshape(trees, 4 * rank, -1))
    out_shrink_query, out_shrink_key, out_shrink_value, out_expand_output = (
        shared_all[:, i * rank : (i + 1) * rank] for i in range(4)
    )
    return (
        layer_output,
        input_grad,
        out_shrink_query,
        out_shrink_key,
        out_shrink_value,
        out_shrink_output,
        out_shrink_gate,
        out_shrink_up,
        out_shrink_down,
        out_expand_query,
        out_expand_key,
        out_expand_value,
        out_expand_output,
        out_expand_gate,
        out_expand_up,
        out_expand_down,
    )


def solution(mesh):
    placed = (
        P(("dp", "tensor"), None),
        P(("dp", "tensor"), None),
        P(),
        P("dp", "tensor"),
        P("dp", "tensor"),
        P("dp", "tensor"),
        P("tensor", "dp"),
        P("dp", "tensor"),
        P("dp", "tensor"),
        P("tensor", "dp"),
        P(),
        P(),
        P(),
        P(None, None, "tensor"),
        P(),
        P(),
        P(None, None, "tensor"),
        P(None, None, "tensor"),
        P(None, None, "tensor"),
        P(None, None, "tensor"),
        P(),
        P(None, None, "tensor"),
        P(None, None, "tensor"),
        P(),
        P("dp"),
        P("dp", None),
        P("dp"),
    )
    return jax.shard_map(
        on_device,
        mesh=mesh,
        in_specs=placed,
        out_specs=(
            P(("dp", "tensor"), None),
            P(("dp", "tensor"), None),
            P(),
            P(),
            P(),
            P(None, None, "tensor"),
            P(),
            P(),
            P(None, None, "tensor"),
            P(None, None, "tensor"),
            P(None, None, "tensor"),
            P(None, None, "tensor"),
            P(),
            P(None, None, "tensor"),
            P(None, None, "tensor"),
            P(),
        ),
        check_vma=False,
    )
```

time: 1380 us -> 1530 us (1.11)
  waiting for transfers between devices: 1090 us -> 318 us
  Pallas kernels: 0 us -> 706 us
  starting transfers between devices: 1.14 us -> 76.7 us
  local copies, waits for them, and re-layouts: 22.7 us -> 84.1 us
  blocking collectives: 0 us -> 56.7 us
    pallas_call x0 -> x5, Pallas kernels: none -> 706 us  [assemble(): pl.pallas_call(kernel, out_shape=jax.ShapeDtypeStruct((2 * columns_z, row...]
    all_gather x11 -> x3, waiting for transfers between devices: 673 us -> 14.1 us  [the longest x2 14.1 us: on_device(): shared_all = lax.all_gather(shared, ('dp', 'tensor'), axis=0, tiled=True)]
    ppermute x0 -> x67, waiting for transfers between devices: none -> 294 us  [flip(): return lax.ppermute(values, axis_name, [(i, i ^ bit) for i in range(size)])]
    psum x2 -> x0, waiting for transfers between devices: 274 us -> none  [the longest x1 184 us: on_device(): lax.psum((hot_rows * query_back[1][None], hot_rows * key_back[1][None], h...]
    reduce_scatter x4 -> x1, waiting for transfers between devices: 134 us -> 9.53 us  [on_device(): shared = lax.psum_scatter(shared, 'tensor', scatter_dimension=0, tiled=True)]
    ppermute x0 -> x67, starting transfers between devices: none -> 75.2 us  [flip(): return lax.ppermute(values, axis_name, [(i, i ^ bit) for i in range(size)])]
    all_gather x0 -> x1, blocking collectives: none -> 32.1 us  [on_device(): lax.all_gather(local, 'dp', axis=0, tiled=False)]
    unnamed x291 -> x421, local copies, waits for them, and re-layouts: 18.8 us -> 46.6 us
  transfers between devices with their start and end apart: 17 -> 72, of which waited for: 17 -> 29; matrix products, arithmetic and copies ran while one was open for 8% -> 15% of each run, Pallas kernels for 0% -> 21%
where the time goes in v1:
time: 1530 us; the launch traced here: 1520 us
  Pallas kernels  706 us (46%)
  waiting for transfers between devices  318 us (21%)
  matrix products  200 us (13%)
  local copies, waits for them, and re-layouts  84.1 us (5%)
  starting transfers between devices  76.7 us (5%)
  other arithmetic  60.1 us (4%)
  blocking collectives  56.7 us (4%)
  between operations  18.7 us (1%)
    pallas_call x5, Pallas kernels, assemble(): pl.pallas_call(kernel, out_shape=jax.ShapeDtypeStruct((2 * columns_z, row...  706 us
    ppermute x67, waiting for transfers between devices, flip(): return lax.ppermute(values, axis_name, [(i, i ^ bit) for i in range(size)])  294 us
    dot_general x14, matrix products, product(): return jnp.dot(former, latter, preferred_element_type=jnp.float32)  83.2 us
    ppermute x67, starting transfers between devices, flip(): return lax.ppermute(values, axis_name, [(i, i ^ bit) for i in range(size)])  75.2 us
    dot_general x14, matrix products, times_rows(): lax.dot_general(former, latter, (((1,), (1,)), ((), ())), preferred_eleme...  70.6 us
    unnamed x421, local copies, waits for them, and re-layouts  46.6 us
    all_gather x1, blocking collectives, on_device(): lax.all_gather(local, 'dp', axis=0, tiled=False)  32.1 us
  transfers between devices with their start and end apart: 72, of which 29 were waited for; matrix products, arithmetic and copies ran while one was open for 15% of the time, Pallas kernels for 21%

profile of v1, /device:TPU:0, one launch (start us, length us, event | category | flops | bytes accessed | tf_op | source)
XLA Modules:
  0.0 1520.1 jit_solution(10537965768816302531)
XLA Ops:
  11.2 4.0 collective-permute-start.3
  26.6 15.0 all-reduce.3
  76.6 3.5 collective-permute-start.7
  83.3 22.1 %collective-permute-done.6 = bf16[144,1024]{1,0:T(8,128)(2,1)S(1)} collective-permute-done((bf16[144,1024]{1,0:T(8,128)(2,1)}, bf16[144,1024]{1,0:T(8,128)(2,1)S(1)}, u32[]{:S(2)}, u32[]{:S(2)}) %collective-permute-start.6) | collective-permute-done | bytes 294944 | tf_op jit(solution)/shard_map/ppermute | solution.py:124
  110.3 3.2 collective-permute-start.11
  115.1 19.7 %collective-permute-done.11 = bf16[288,512]{1,0:T(8,128)(2,1)S(1)} collective-permute-done((bf16[288,512]{1,0:T(8,128)(2,1)}, bf16[288,512]{1,0:T(8,128)(2,1)S(1)}, u32[]{:S(2)}, u32[]{:S(2)}) %collective-permute-start.11) | collective-permute-done | bytes 294944 | tf_op jit(solution)/shard_map/ppermute | solution.py:124
  137.0 2.7 convolution_convert_fusion.9
  141.8 145.0 %shard_map.378 = bf16[8,288,1024]{2,1,0:T(8,128)(2,1)} custom-call(s32[8]{0:T(128)} %stack.191.slots_ref, bf16[4,144,1024]{2,1,0:T(8,128)(2,1)} %copy-done.29, bf16[4,144,1024]{2,1,0:T(8,128)(2,1)} %pad_maximum_fusion.15.refs_1_, bf16[4,144,1024]{2,1,0:T(8,128)(2,1)} %copy-done.66, bf16[4,144,1024]{2,1,0:T(8,128)(2,1)} %collective-permute-done.9.refs_3_), custom_call_target="tpu_custom_call" | custom-call | bytes 9437184 | tf_op jit(solution)/shard_map/pallas_call | solution.py:175
  286.8 7.0 convolution_add_fusion.5
  307.4 3.5 fusion.179
  310.9 11.5 collective-permute-done.13.refs_1_
  322.5 73.3 %shard_map.379 = bf16[8,288,512]{2,1,0:T(8,128)(2,1)} custom-call(s32[8]{0:T(128)} %stack.191.slots_ref, bf16[4,288,512]{2,1,0:T(8,128)(2,1)} %pad_maximum_fusion.16.refs_0_, bf16[4,288,512]{2,1,0:T(8,128)(2,1)} %collective-permute-done.13.refs_1_), custom_call_target="tpu_custom_call" | custom-call | bytes 4718592 | tf_op jit(solution)/shard_map/pallas_call | solution.py:175
  395.8 5.1 add_convert_fusion.1
  407.8 24.5 %collective-permute-done.23 = bf16[144,1152]{1,0:T(8,128)(2,1)S(1)} collective-permute-done((bf16[144,1152]{1,0:T(8,128)(2,1)S(1)}, bf16[144,1152]{1,0:T(8,128)(2,1)S(1)}, u32[]{:S(2)}, u32[]{:S(2)}) %collective-permute-start.23) | collective-permute-done | bytes 331808 | tf_op jit(solution)/shard_map/ppermute | solution.py:124
  434.3 2.7 collective-permute-start.26
  441.3 19.5 %collective-permute-done.26 = bf16[144,1152]{1,0:T(8,128)(2,1)S(1)} collective-permute-done((bf16[144,1152]{1,0:T(8,128)(2,1)S(1)}, bf16[144,1152]{1,0:T(8,128)(2,1)S(1)}, u32[]{:S(2)}, u32[]{:S(2)}) %collective-permute-start.26) | collective-permute-done | bytes 331808 | tf_op jit(solution)/shard_map/ppermute | solution.py:124
  461.1 5.0 collective-permute-done.28.refs_2_
  469.3 2.7 collective-permute-start.31
  475.5 18.8 %collective-permute-done.31 = bf16[144,1152]{1,0:T(8,128)(2,1)S(1)} collective-permute-done((bf16[144,1152]{1,0:T(8,128)(2,1)S(1)}, bf16[144,1152]{1,0:T(8,128)(2,1)S(1)}, u32[]{:S(2)}, u32[]{:S(2)}) %collective-permute-start.31) | collective-permute-done | bytes 331808 | tf_op jit(solution)/shard_map/ppermute | solution.py:124
  500.7 162.7 %shard_map.380 = bf16[8,288,1152]{2,1,0:T(8,128)(2,1)} custom-call(s32[8]{0:T(128)} %stack.191.slots_ref, bf16[4,144,1152]{2,1,0:T(8,128)(2,1)} %copy-done.24, bf16[4,144,1152]{2,1,0:T(8,128)(2,1)} %copy-done.26, bf16[4,144,1152]{2,1,0:T(8,128)(2,1)} %copy-done.60, bf16[4,144,1152]{2,1,0:T(8,128)(2,1)} %copy-done.61), custom_call_target="tpu_custom_call" | custom-call | bytes 10616832 | tf_op jit(solution)/shard_map/pallas_call | solution.py:175
  671.9 6.4 collective-permute-done.19
  679.9 11.1 collective-permute-done.36.refs_2_
  692.6 2.8 collective-permute-start.39
  696.2 21.0 %collective-permute-done.39 = bf16[144,1152]{1,0:T(8,128)(2,1)S(1)} collective-permute-done((bf16[144,1152]{1,0:T(8,128)(2,1)S(1)}, bf16[144,1152]{1,0:T(8,128)(2,1)S(1)}, u32[]{:S(2)}, u32[]{:S(2)}) %collective-permute-start.39) | collective-permute-done | bytes 331808 | tf_op jit(solution)/shard_map/ppermute | solution.py:124
  721.4 5.2 fusion.18
  727.6 18.9 %collective-permute-done.37.refs_3_ = bf16[4,144,1152]{2,1,0:T(8,128)(2,1)S(1)} collective-permute-done((bf16[4,144,1152]{2,1,0:T(8,128)(2,1)S(1)}, bf16[4,144,1152]{2,1,0:T(8,128)(2,1)S(1)}, u32[]{:S(2)}, u32[]{:S(2)}) %collective-permute-start.37) | collective-permute-done | bytes 1327136 | tf_op jit(solution)/shard_map/ppermute | solution.py:124
  748.0 9.6 convolution_add_fusion.4
  758.9 3.1 collective-permute-start.42
  762.0 3.5 fusion.170
  765.5 162.7 %shard_map.381 = bf16[8,288,1152]{2,1,0:T(8,128)(2,1)} custom-call(s32[8]{0:T(128)} %stack.191.slots_ref, bf16[4,144,1152]{2,1,0:T(8,128)(2,1)} %copy-done.23, bf16[4,144,1152]{2,1,0:T(8,128)(2,1)} %copy-done.25, bf16[4,144,1152]{2,1,0:T(8,128)(2,1)} %copy-done.59, bf16[4,144,1152]{2,1,0:T(8,128)(2,1)} %copy-done.62), custom_call_target="tpu_custom_call" | custom-call | bytes 10616832 | tf_op jit(solution)/shard_map/pallas_call | solution.py:175
  930.8 15.9 %multiply_convert_fusion.1 = (bf16[1280,1152]{1,0:T(8,128)(2,1)S(1)}, f32[1280,1152]{1,0:T(8,128)}) fusion(f32[1280,1152]{1,0:T(8,128)} %convolution_add_fusion.4, f32[1280,1152]{1,0:T(8,128)} %fusion.170, bf16[1280,2304]{1,0:T(8,128)(2,1)} %constant_dynamic-update-slice_fusion.3, bf16[2304,1152]{1,0:T(8,128)(2,1)} %bitcast.418), kind=kOutput, calls=%fused_computation.21 | convolution fusion | flops 6810992640 | bytes 31850496 | tf_op jit(solution)/shard_map/dot_general | solution.py:86
  947.7 6.1 fusion.158
  956.1 162.7 %shard_map.382 = bf16[8,288,1152]{2,1,0:T(8,128)(2,1)} custom-call(s32[8]{0:T(128)} %stack.191.slots_ref, bf16[4,144,1152]{2,1,0:T(8,128)(2,1)} %copy-done.27, bf16[4,144,1152]{2,1,0:T(8,128)(2,1)} %copy-done.28, bf16[4,144,1152]{2,1,0:T(8,128)(2,1)} %copy-done.63, bf16[4,144,1152]{2,1,0:T(8,128)(2,1)} %collective-permute-done.45.refs_3_), custom_call_target="tpu_custom_call" | custom-call | bytes 10616832 | tf_op jit(solution)/shard_map/pallas_call | solution.py:175
  1118.8 12.3 fusion.2
  1131.4 5.4 collective-permute-done.46
  1138.1 18.1 %collective-permute-done.49 = bf16[160,2304]{1,0:T(8,128)(2,1)S(1)} collective-permute-done((bf16[160,2304]{1,0:T(8,128)(2,1)S(1)}, bf16[160,2304]{1,0:T(8,128)(2,1)S(1)}, u32[]{:S(2)}, u32[]{:S(2)}) %collective-permute-start.49) | collective-permute-done | bytes 737312 | tf_op jit(solution)/shard_map/ppermute | solution.py:124
  1158.7 7.8 collective-permute-done.48
  1170.5 15.2 %collective-permute-done.52 = bf16[160,2304]{1,0:T(8,128)(2,1)S(1)} collective-permute-done((bf16[160,2304]{1,0:T(8,128)(2,1)S(1)}, bf16[160,2304]{1,0:T(8,128)(2,1)S(1)}, u32[]{:S(2)}, u32[]{:S(2)}) %collective-permute-start.52) | collective-permute-done | bytes 737312 | tf_op jit(solution)/shard_map/ppermute | solution.py:124
  1195.5 5.1 collective-permute-done.54
  1204.0 3.2 constant_dynamic-update-slice_fusion.11
  1208.1 4.7 fusion.19
  1215.5 3.5 fusion.283
  1219.0 17.4 %fusion.10 = (bf16[1280,1152]{1,0:T(8,128)(2,1)S(1)}, bf16[1280,1152]{1,0:T(8,128)(2,1)S(1)}) fusion(f32[1280,1152]{1,0:T(8,128)} %convolution_add_fusion.4, f32[1280,1152]{1,0:T(8,128)} %get-tuple-element.247, f32[1280,1152]{1,0:T(8,128)} %fusion.283, bf16[1280,2304]{1,0:T(8,128)(2,1)S(1)} %copy-done.4, bf16[2304,1152]{1,0:T(8,128)(2,1)} %bitcast.423), kind=kOutput, calls=%fused_computation.16 | convolution fusion | flops 6831636480 | bytes 34799616 | tf_op jit(solution)/shard_map/dot_general | solution.py:86
  1240.3 10.6 fusion.284
  1251.8 6.1 fusion.154
  1257.9 15.7 %fusion.3 = bf16[1280,2304]{1,0:T(8,128)(2,1)} fusion(f32[1280,2304]{1,0:T(8,128)} %fusion.154, f32[1280,2304]{1,0:T(8,128)} %fusion.284, bf16[1280,1152]{1,0:T(8,128)(2,1)S(1)} %get-tuple-element.152, bf16[2304,1152]{1,0:T(8,128)(2,1)} %bitcast.414), kind=kOutput, calls=%fused_computation.4 | convolution fusion | flops 6803619840 | bytes 37748736 | tf_op jit(solution)/shard_map/dot_general | solution.py:90
  1273.6 3.6 slice.551
  1277.9 3.8 convolution_convert_fusion
  1285.2 12.2 collective-permute-done.66
  1299.0 9.5 fusion
  1311.8 5.1 convert_add_fusion
  1318.0 4.6 collective-permute-start.58
  1324.8 11.9 collective-permute-done.60
  1343.2 11.1 collective-permute-done.59
  1360.2 19.9 %collective-permute-done.62 = bf16[160,2304]{1,0:T(8,128)(2,1)S(1)} collective-permute-done((bf16[160,2304]{1,0:T(8,128)(2,1)S(1)}, bf16[160,2304]{1,0:T(8,128)(2,1)S(1)}, u32[]{:S(2)}, u32[]{:S(2)}) %collective-permute-start.62) | collective-permute-done | bytes 737312 | tf_op jit(solution)/shard_map/ppermute | solution.py:124
  1385.8 4.0 reshape.877
  1389.8 4.1 fusion.26
  1396.7 3.6 fusion.60
  1414.2 3.5 fusion.159
  1422.7 7.4 add_convert_fusion
  1433.5 9.5 reduce-scatter.4.cloned.1.call-done
  1452.0 32.1 %all_gather.19 = bf16[8,16,1536]{2,1,0:T(8,128)(2,1)S(1)} all-gather(bf16[1,16,1536]{2,1,0:T(8,128)(2,1)S(1)} %pad_maximum_fusion.45), channel_id=1, replica_groups=mesh['dp'=8,'tensor'=4] {'dp'}, dimensions={0}, use_global_device_ids=true | all-gather | bytes 442368 | tf_op jit(solution)/shard_map/all_gather | solution.py:510
  1489.7 14.1 all-gather.5.cloned.1.call-done
  1503.8 3.3 fusion.16
  (736 shorter events, 232.1 us)
Async XLA Ops:
  7.2 1315.3 %all-gather.7.cloned.1.call-start = ((), (), s32[]{:S(2)}) async-start(), calls=%async_computation.3 | async-start | bytes 1990656 | tf_op jit(solution)/shard_map/all_gather | solution.py:470
  11.2 59.8 %collective-permute-start.3 = (bf16[144,1024]{1,0:T(8,128)(2,1)}, bf16[144,1024]{1,0:T(8,128)(2,1)}, u32[]{:S(2)}, u32[]{:S(2)}) collective-permute-start(bf16[144,1024]{1,0:T(8,128)(2,1)} %get-tuple-element.224), channel_id=1, source_target_pairs={{0,16},{4,20},{8,24},{12,28},{16,0},{20,4},{24,8},{28,12},{1,17},{... | collective-permute-start | bytes 884744 | tf_op jit(solution)/shard_map/ppermute | solution.py:124
  15.2 55.8 %collective-permute-start.2 = (bf16[144,1024]{1,0:T(8,128)(2,1)}, bf16[144,1024]{1,0:T(8,128)(2,1)}, u32[]{:S(2)}, u32[]{:S(2)}) collective-permute-start(bf16[144,1024]{1,0:T(8,128)(2,1)} %get-tuple-element.224), channel_id=1, source_target_pairs={{0,8},{4,12},{8,0},{12,4},{16,24},{20,28},{24,16},{28,20},{1,9},{5... | collective-permute-start | bytes 884744 | tf_op jit(solution)/shard_map/ppermute | solution.py:124
  16.8 54.2 %collective-permute-start.4 = (bf16[144,1024]{1,0:T(8,128)(2,1)}, bf16[144,1024]{1,0:T(8,128)(2,1)}, u32[]{:S(2)}, u32[]{:S(2)}) collective-permute-start(bf16[144,1024]{1,0:T(8,128)(2,1)} %get-tuple-element.224), channel_id=1, source_target_pairs={{0,24},{4,28},{8,16},{12,20},{16,8},{20,12},{24,0},{28,4},{1,25},{... | collective-permute-start | bytes 884744 | tf_op jit(solution)/shard_map/ppermute | solution.py:124
  19.2 54.8 %collective-permute-start = (bf16[160,2304]{1,0:T(8,128)(2,1)S(1)}, bf16[160,2304]{1,0:T(8,128)(2,1)}, u32[]{:S(2)}, u32[]{:S(2)}) collective-permute-start(bf16[160,2304]{1,0:T(8,128)(2,1)S(1)} %fusion.45), channel_id=1, source_target_pairs={{0,2},{1,3},{2,0},{3,1},{4,6},{5,7},{6,4},{7,5},{8,10},{9,11},{10,... | collective-permute-start | bytes 2211848 | tf_op jit(solution)/shard_map/ppermute | solution.py:124
  72.4 35.1 %collective-permute-start.8 = (bf16[4,144,1024]{2,1,0:T(8,128)(2,1)S(1)}, bf16[4,144,1024]{2,1,0:T(8,128)(2,1)S(1)}, u32[]{:S(2)}, u32[]{:S(2)}) collective-permute-start(bf16[4,144,1024]{2,1,0:T(8,128)(2,1)S(1)} %pad_maximum_fusion.14.refs_0_), channel_id=1, source_target_pairs={{0,4},{4,0},{8,12},{12,8},{16,20},{20,16},{24,28},{28,24},{1,5},{5... | collective-permute-start | bytes 3538952 | tf_op jit(solution)/shard_map/ppermute | solution.py:124
  76.3 60.6 %collective-permute-start.1 = (bf16[320,2304]{1,0:T(8,128)(2,1)}, bf16[320,2304]{1,0:T(8,128)(2,1)}, u32[]{:S(2)}, u32[]{:S(2)}) collective-permute-start(bf16[320,2304]{1,0:T(8,128)(2,1)} %pad_maximum_fusion.4), channel_id=1, source_target_pairs={{0,1},{1,0},{2,3},{3,2},{4,5},{5,4},{6,7},{7,6},{8,9},{9,8},{10,11... | collective-permute-start | bytes 4423688 | tf_op jit(solution)/shard_map/ppermute | solution.py:124
  76.6 28.8 %collective-permute-start.7 = (bf16[144,1024]{1,0:T(8,128)(2,1)}, bf16[144,1024]{1,0:T(8,128)(2,1)S(1)}, u32[]{:S(2)}, u32[]{:S(2)}) collective-permute-start(bf16[144,1024]{1,0:T(8,128)(2,1)} %get-tuple-element.40), channel_id=1, source_target_pairs={{0,24},{4,28},{8,16},{12,20},{16,8},{20,12},{24,0},{28,4},{1,25},{... | collective-permute-start | bytes 884744 | tf_op jit(solution)/shard_map/ppermute | solution.py:124
  80.1 25.3 %collective-permute-start.5 = (bf16[144,1024]{1,0:T(8,128)(2,1)}, bf16[144,1024]{1,0:T(8,128)(2,1)S(1)}, u32[]{:S(2)}, u32[]{:S(2)}) collective-permute-start(bf16[144,1024]{1,0:T(8,128)(2,1)} %get-tuple-element.40), channel_id=1, source_target_pairs={{0,8},{4,12},{8,0},{12,4},{16,24},{20,28},{24,16},{28,20},{1,9},{5... | collective-permute-start | bytes 884744 | tf_op jit(solution)/shard_map/ppermute | solution.py:124
  80.1 25.3 %collective-permute-start.6 = (bf16[144,1024]{1,0:T(8,128)(2,1)}, bf16[144,1024]{1,0:T(8,128)(2,1)S(1)}, u32[]{:S(2)}, u32[]{:S(2)}) collective-permute-start(bf16[144,1024]{1,0:T(8,128)(2,1)} %get-tuple-element.40), channel_id=1, source_target_pairs={{0,16},{4,20},{8,24},{12,28},{16,0},{20,4},{24,8},{28,12},{1,17},{... | collective-permute-start | bytes 884744 | tf_op jit(solution)/shard_map/ppermute | solution.py:124
  108.5 33.3 %collective-permute-start.9 = (bf16[4,144,1024]{2,1,0:T(8,128)(2,1)}, bf16[4,144,1024]{2,1,0:T(8,128)(2,1)}, u32[]{:S(2)}, u32[]{:S(2)}) collective-permute-start(bf16[4,144,1024]{2,1,0:T(8,128)(2,1)} %pad_maximum_fusion.15.refs_1_), channel_id=1, source_target_pairs={{0,4},{4,0},{8,12},{12,8},{16,20},{20,16},{24,28},{28,24},{1,5},{5... | collective-permute-start | bytes 3538952 | tf_op jit(solution)/shard_map/ppermute | solution.py:124
  109.0 25.7 %collective-permute-start.12 = (bf16[288,512]{1,0:T(8,128)(2,1)}, bf16[288,512]{1,0:T(8,128)(2,1)S(1)}, u32[]{:S(2)}, u32[]{:S(2)}) collective-permute-start(bf16[288,512]{1,0:T(8,128)(2,1)} %bitcast.50), channel_id=1, source_target_pairs={{0,24},{4,28},{8,16},{12,20},{16,8},{20,12},{24,0},{28,4},{1,25},{... | collective-permute-start | bytes 884744 | tf_op jit(solution)/shard_map/ppermute | solution.py:124
  110.3 24.5 %collective-permute-start.10 = (bf16[288,512]{1,0:T(8,128)(2,1)}, bf16[288,512]{1,0:T(8,128)(2,1)S(1)}, u32[]{:S(2)}, u32[]{:S(2)}) collective-permute-start(bf16[288,512]{1,0:T(8,128)(2,1)} %bitcast.50), channel_id=1, source_target_pairs={{0,8},{4,12},{8,0},{12,4},{16,24},{20,28},{24,16},{28,20},{1,9},{5... | collective-permute-start | bytes 884744 | tf_op jit(solution)/shard_map/ppermute | solution.py:124
  110.3 24.4 %collective-permute-start.11 = (bf16[288,512]{1,0:T(8,128)(2,1)}, bf16[288,512]{1,0:T(8,128)(2,1)S(1)}, u32[]{:S(2)}, u32[]{:S(2)}) collective-permute-start(bf16[288,512]{1,0:T(8,128)(2,1)} %bitcast.50), channel_id=1, source_target_pairs={{0,16},{4,20},{8,24},{12,28},{16,0},{20,4},{24,8},{28,12},{1,17},{... | collective-permute-start | bytes 884744 | tf_op jit(solution)/shard_map/ppermute | solution.py:124
  295.4 27.0 %collective-permute-start.13 = (bf16[4,288,512]{2,1,0:T(8,128)(2,1)}, bf16[4,288,512]{2,1,0:T(8,128)(2,1)}, u32[]{:S(2)}, u32[]{:S(2)}) collective-permute-start(bf16[4,288,512]{2,1,0:T(8,128)(2,1)} %pad_maximum_fusion.16.refs_0_), channel_id=1, source_target_pairs={{0,4},{4,0},{8,12},{12,8},{16,20},{20,16},{24,28},{28,24},{1,5},{5... | collective-permute-start | bytes 3538952 | tf_op jit(solution)/shard_map/ppermute | solution.py:124
  401.1 37.4 %collective-permute-start.14 = (bf16[320,2304]{1,0:T(8,128)(2,1)S(1)}, bf16[320,2304]{1,0:T(8,128)(2,1)S(1)}, u32[]{:S(2)}, u32[]{:S(2)}) collective-permute-start(bf16[320,2304]{1,0:T(8,128)(2,1)S(1)} %slice.503), channel_id=1, source_target_pairs={{0,1},{1,0},{2,3},{3,2},{4,5},{5,4},{6,7},{7,6},{8,9},{9,8},{10,11... | collective-permute-start | bytes 4423688 | tf_op jit(solution)/shard_map/ppermute | solution.py:124
  402.6 29.7 %collective-permute-start.24 = (bf16[144,1152]{1,0:T(8,128)(2,1)S(1)}, bf16[144,1152]{1,0:T(8,128)(2,1)S(1)}, u32[]{:S(2)}, u32[]{:S(2)}) collective-permute-start(bf16[144,1152]{1,0:T(8,128)(2,1)S(1)} %copy-done.99), channel_id=1, source_target_pairs={{0,24},{4,28},{8,16},{12,20},{16,8},{20,12},{24,0},{28,4},{1,25},{... | collective-permute-start | bytes 995336 | tf_op jit(solution)/shard_map/ppermute | solution.py:124
  404.8 27.6 %collective-permute-start.22 = (bf16[144,1152]{1,0:T(8,128)(2,1)S(1)}, bf16[144,1152]{1,0:T(8,128)(2,1)S(1)}, u32[]{:S(2)}, u32[]{:S(2)}) collective-permute-start(bf16[144,1152]{1,0:T(8,128)(2,1)S(1)} %copy-done.99), channel_id=1, source_target_pairs={{0,8},{4,12},{8,0},{12,4},{16,24},{20,28},{24,16},{28,20},{1,9},{5... | collective-permute-start | bytes 995336 | tf_op jit(solution)/shard_map/ppermute | solution.py:124
  404.8 27.5 %collective-permute-start.23 = (bf16[144,1152]{1,0:T(8,128)(2,1)S(1)}, bf16[144,1152]{1,0:T(8,128)(2,1)S(1)}, u32[]{:S(2)}, u32[]{:S(2)}) collective-permute-start(bf16[144,1152]{1,0:T(8,128)(2,1)S(1)} %copy-done.65), channel_id=1, source_target_pairs={{0,16},{4,20},{8,24},{12,28},{16,0},{20,4},{24,8},{28,12},{1,17},{... | collective-permute-start | bytes 995336 | tf_op jit(solution)/shard_map/ppermute | solution.py:124
  432.6 28.3 %collective-permute-start.27 = (bf16[144,1152]{1,0:T(8,128)(2,1)S(1)}, bf16[144,1152]{1,0:T(8,128)(2,1)S(1)}, u32[]{:S(2)}, u32[]{:S(2)}) collective-permute-start(bf16[144,1152]{1,0:T(8,128)(2,1)S(1)} %copy-done.98), channel_id=1, source_target_pairs={{0,24},{4,28},{8,16},{12,20},{16,8},{20,12},{24,0},{28,4},{1,25},{... | collective-permute-start | bytes 995336 | tf_op jit(solution)/shard_map/ppermute | solution.py:124
  434.3 26.6 %collective-permute-start.25 = (bf16[144,1152]{1,0:T(8,128)(2,1)S(1)}, bf16[144,1152]{1,0:T(8,128)(2,1)S(1)}, u32[]{:S(2)}, u32[]{:S(2)}) collective-permute-start(bf16[144,1152]{1,0:T(8,128)(2,1)S(1)} %copy-done.98), channel_id=1, source_target_pairs={{0,8},{4,12},{8,0},{12,4},{16,24},{20,28},{24,16},{28,20},{1,9},{5... | collective-permute-start | bytes 995336 | tf_op jit(solution)/shard_map/ppermute | solution.py:124
  434.3 26.6 %collective-permute-start.26 = (bf16[144,1152]{1,0:T(8,128)(2,1)S(1)}, bf16[144,1152]{1,0:T(8,128)(2,1)S(1)}, u32[]{:S(2)}, u32[]{:S(2)}) collective-permute-start(bf16[144,1152]{1,0:T(8,128)(2,1)S(1)} %copy-done.64), channel_id=1, source_target_pairs={{0,16},{4,20},{8,24},{12,28},{16,0},{20,4},{24,8},{28,12},{1,17},{... | collective-permute-start | bytes 995336 | tf_op jit(solution)/shard_map/ppermute | solution.py:124
  437.0 29.1 %collective-permute-start.28 = (bf16[4,144,1152]{2,1,0:T(8,128)(2,1)S(1)}, bf16[4,144,1152]{2,1,0:T(8,128)(2,1)S(1)}, u32[]{:S(2)}, u32[]{:S(2)}) collective-permute-start(bf16[4,144,1152]{2,1,0:T(8,128)(2,1)S(1)} %pad_maximum_fusion.7.refs_0_), channel_id=1, source_target_pairs={{0,4},{4,0},{8,12},{12,8},{16,20},{20,16},{24,28},{28,24},{1,5},{5... | collective-permute-start | bytes 3981320 | tf_op jit(solution)/shard_map/ppermute | solution.py:124
  439.0 33.1 %collective-permute-start.15 = (bf16[160,2304]{1,0:T(8,128)(2,1)S(1)}, bf16[160,2304]{1,0:T(8,128)(2,1)S(1)}, u32[]{:S(2)}, u32[]{:S(2)}) collective-permute-start(bf16[160,2304]{1,0:T(8,128)(2,1)S(1)} %slice.754), channel_id=1, source_target_pairs={{0,2},{1,3},{2,0},{3,1},{4,6},{5,7},{6,4},{7,5},{8,10},{9,11},{10,... | collective-permute-start | bytes 2211848 | tf_op jit(solution)/shard_map/ppermute | solution.py:124
  466.1 29.9 %collective-permute-start.32 = (bf16[144,1152]{1,0:T(8,128)(2,1)S(1)}, bf16[144,1152]{1,0:T(8,128)(2,1)S(1)}, u32[]{:S(2)}, u32[]{:S(2)}) collective-permute-start(bf16[144,1152]{1,0:T(8,128)(2,1)S(1)} %get-tuple-element.53), channel_id=1, source_target_pairs={{0,24},{4,28},{8,16},{12,20},{16,8},{20,12},{24,0},{28,4},{1,25},{... | collective-permute-start | bytes 995336 | tf_op jit(solution)/shard_map/ppermute | solution.py:124
  467.8 28.2 %collective-permute-start.30 = (bf16[144,1152]{1,0:T(8,128)(2,1)S(1)}, bf16[144,1152]{1,0:T(8,128)(2,1)S(1)}, u32[]{:S(2)}, u32[]{:S(2)}) collective-permute-start(bf16[144,1152]{1,0:T(8,128)(2,1)S(1)} %get-tuple-element.53), channel_id=1, source_target_pairs={{0,8},{4,12},{8,0},{12,4},{16,24},{20,28},{24,16},{28,20},{1,9},{5... | collective-permute-start | bytes 995336 | tf_op jit(solution)/shard_map/ppermute | solution.py:124
  467.8 28.4 %collective-permute-start.29 = (bf16[4,144,1152]{2,1,0:T(8,128)(2,1)S(1)}, bf16[4,144,1152]{2,1,0:T(8,128)(2,1)S(1)}, u32[]{:S(2)}, u32[]{:S(2)}) collective-permute-start(bf16[4,144,1152]{2,1,0:T(8,128)(2,1)S(1)} %pad_maximum_fusion.8.refs_1_), channel_id=1, source_target_pairs={{0,4},{4,0},{8,12},{12,8},{16,20},{20,16},{24,28},{28,24},{1,5},{5... | collective-permute-start | bytes 3981320 | tf_op jit(solution)/shard_map/ppermute | solution.py:124
  469.3 25.0 %collective-permute-start.31 = (bf16[144,1152]{1,0:T(8,128)(2,1)S(1)}, bf16[144,1152]{1,0:T(8,128)(2,1)S(1)}, u32[]{:S(2)}, u32[]{:S(2)}) collective-permute-start(bf16[144,1152]{1,0:T(8,128)(2,1)S(1)} %copy-done.58), channel_id=1, source_target_pairs={{0,16},{4,20},{8,24},{12,28},{16,0},{20,4},{24,8},{28,12},{1,17},{... | collective-permute-start | bytes 995336 | tf_op jit(solution)/shard_map/ppermute | solution.py:124
  475.5 188.0 %collective-permute-start.17 = (bf16[160,2304]{1,0:T(8,128)(2,1)}, bf16[160,2304]{1,0:T(8,128)(2,1)S(1)}, u32[]{:S(2)}, u32[]{:S(2)}) collective-permute-start(bf16[160,2304]{1,0:T(8,128)(2,1)} %get-tuple-element.147), channel_id=1, source_target_pairs={{0,8},{4,12},{8,0},{12,4},{16,24},{20,28},{24,16},{28,20},{1,9},{5... | collective-permute-start | bytes 2211848 | tf_op jit(solution)/shard_map/ppermute | solution.py:124
  494.3 170.7 %collective-permute-start.16 = (bf16[160,2304]{1,0:T(8,128)(2,1)}, bf16[160,2304]{1,0:T(8,128)(2,1)S(1)}, u32[]{:S(2)}, u32[]{:S(2)}) collective-permute-start(bf16[160,2304]{1,0:T(8,128)(2,1)} %get-tuple-element.147), channel_id=1, source_target_pairs={{0,2},{1,3},{2,0},{3,1},{4,6},{5,7},{6,4},{7,5},{8,10},{9,11},{10,... | collective-permute-start | bytes 2211848 | tf_op jit(solution)/shard_map/ppermute | solution.py:124
  496.3 172.0 %collective-permute-start.35 = (bf16[144,1152]{1,0:T(8,128)(2,1)}, bf16[144,1152]{1,0:T(8,128)(2,1)}, u32[]{:S(2)}, u32[]{:S(2)}) collective-permute-start(bf16[144,1152]{1,0:T(8,128)(2,1)} %get-tuple-element.55), channel_id=1, source_target_pairs={{0,24},{4,28},{8,16},{12,20},{16,8},{20,12},{24,0},{28,4},{1,25},{... | collective-permute-start | bytes 995336 | tf_op jit(solution)/shard_map/ppermute | solution.py:124
  498.0 172.3 %collective-permute-start.33 = (bf16[144,1152]{1,0:T(8,128)(2,1)}, bf16[144,1152]{1,0:T(8,128)(2,1)}, u32[]{:S(2)}, u32[]{:S(2)}) collective-permute-start(bf16[144,1152]{1,0:T(8,128)(2,1)} %get-tuple-element.55), channel_id=1, source_target_pairs={{0,8},{4,12},{8,0},{12,4},{16,24},{20,28},{24,16},{28,20},{1,9},{5... | collective-permute-start | bytes 995336 | tf_op jit(solution)/shard_map/ppermute | solution.py:124
  498.7 168.7 %collective-permute-start.34 = (bf16[144,1152]{1,0:T(8,128)(2,1)S(1)}, bf16[144,1152]{1,0:T(8,128)(2,1)}, u32[]{:S(2)}, u32[]{:S(2)}) collective-permute-start(bf16[144,1152]{1,0:T(8,128)(2,1)S(1)} %copy-done.56), channel_id=1, source_target_pairs={{0,16},{4,20},{8,24},{12,28},{16,0},{20,4},{24,8},{28,12},{1,17},{... | collective-permute-start | bytes 995336 | tf_op jit(solution)/shard_map/ppermute | solution.py:124
  663.5 27.5 %collective-permute-start.36 = (bf16[4,144,1152]{2,1,0:T(8,128)(2,1)S(1)}, bf16[4,144,1152]{2,1,0:T(8,128)(2,1)S(1)}, u32[]{:S(2)}, u32[]{:S(2)}) collective-permute-start(bf16[4,144,1152]{2,1,0:T(8,128)(2,1)S(1)} %pad_maximum_fusion.9.refs_0_), channel_id=1, source_target_pairs={{0,4},{4,0},{8,12},{12,8},{16,20},{20,16},{24,28},{28,24},{1,5},{5... | collective-permute-start | bytes 3981320 | tf_op jit(solution)/shard_map/ppermute | solution.py:124
  666.3 52.6 %collective-permute-start.20 = (bf16[480,2304]{1,0:T(8,128)(2,1)S(1)}, bf16[480,2304]{1,0:T(8,128)(2,1)S(1)}, u32[]{:S(2)}, u32[]{:S(2)}) collective-permute-start(bf16[480,2304]{1,0:T(8,128)(2,1)S(1)} %pad_maximum_fusion.2), channel_id=1, source_target_pairs={{0,1},{1,0},{2,3},{3,2},{4,5},{5,4},{6,7},{7,6},{8,9},{9,8},{10,11... | collective-permute-start | bytes 6635528 | tf_op jit(solution)/shard_map/ppermute | solution.py:124
  679.0 41.4 %collective-permute-start.21 = (bf16[160,2304]{1,0:T(8,128)(2,1)S(1)}, bf16[160,2304]{1,0:T(8,128)(2,1)S(1)}, u32[]{:S(2)}, u32[]{:S(2)}) collective-permute-start(bf16[160,2304]{1,0:T(8,128)(2,1)S(1)} %pad_maximum_fusion.20), channel_id=1, source_target_pairs={{0,1},{1,0},{2,3},{3,2},{4,5},{5,4},{6,7},{7,6},{8,9},{9,8},{10,11... | collective-permute-start | bytes 2211848 | tf_op jit(solution)/shard_map/ppermute | solution.py:124
  691.0 27.6 %collective-permute-start.40 = (bf16[144,1152]{1,0:T(8,128)(2,1)S(1)}, bf16[144,1152]{1,0:T(8,128)(2,1)S(1)}, u32[]{:S(2)}, u32[]{:S(2)}) collective-permute-start(bf16[144,1152]{1,0:T(8,128)(2,1)S(1)} %copy-done.97), channel_id=1, source_target_pairs={{0,24},{4,28},{8,16},{12,20},{16,8},{20,12},{24,0},{28,4},{1,25},{... | collective-permute-start | bytes 995336 | tf_op jit(solution)/shard_map/ppermute | solution.py:124
  692.6 26.1 %collective-permute-start.38 = (bf16[144,1152]{1,0:T(8,128)(2,1)S(1)}, bf16[144,1152]{1,0:T(8,128)(2,1)S(1)}, u32[]{:S(2)}, u32[]{:S(2)}) collective-permute-start(bf16[144,1152]{1,0:T(8,128)(2,1)S(1)} %copy-done.97), channel_id=1, source_target_pairs={{0,8},{4,12},{8,0},{12,4},{16,24},{20,28},{24,16},{28,20},{1,9},{5... | collective-permute-start | bytes 995336 | tf_op jit(solution)/shard_map/ppermute | solution.py:124
  692.6 24.6 %collective-permute-start.39 = (bf16[144,1152]{1,0:T(8,128)(2,1)S(1)}, bf16[144,1152]{1,0:T(8,128)(2,1)S(1)}, u32[]{:S(2)}, u32[]{:S(2)}) collective-permute-start(bf16[144,1152]{1,0:T(8,128)(2,1)S(1)} %copy-done.55), channel_id=1, source_target_pairs={{0,16},{4,20},{8,24},{12,28},{16,0},{20,4},{24,8},{28,12},{1,17},{... | collective-permute-start | bytes 995336 | tf_op jit(solution)/shard_map/ppermute | solution.py:124
  717.2 29.3 %collective-permute-start.37 = (bf16[4,144,1152]{2,1,0:T(8,128)(2,1)S(1)}, bf16[4,144,1152]{2,1,0:T(8,128)(2,1)S(1)}, u32[]{:S(2)}, u32[]{:S(2)}) collective-permute-start(bf16[4,144,1152]{2,1,0:T(8,128)(2,1)S(1)} %pad_maximum_fusion.10.refs_1_), channel_id=1, source_target_pairs={{0,4},{4,0},{8,12},{12,8},{16,20},{20,16},{24,28},{28,24},{1,5},{5... | collective-permute-start | bytes 3981320 | tf_op jit(solution)/shard_map/ppermute | solution.py:124
  746.5 183.2 %collective-permute-start.44 = (bf16[4,144,1152]{2,1,0:T(8,128)(2,1)S(1)}, bf16[4,144,1152]{2,1,0:T(8,128)(2,1)S(1)}, u32[]{:S(2)}, u32[]{:S(2)}) collective-permute-start(bf16[4,144,1152]{2,1,0:T(8,128)(2,1)S(1)} %pad_maximum_fusion.11.refs_0_), channel_id=1, source_target_pairs={{0,4},{4,0},{8,12},{12,8},{16,20},{20,16},{24,28},{28,24},{1,5},{5... | collective-permute-start | bytes 3981320 | tf_op jit(solution)/shard_map/ppermute | solution.py:124
  757.6 170.7 %collective-permute-start.43 = (bf16[144,1152]{1,0:T(8,128)(2,1)}, bf16[144,1152]{1,0:T(8,128)(2,1)}, u32[]{:S(2)}, u32[]{:S(2)}) collective-permute-start(bf16[144,1152]{1,0:T(8,128)(2,1)} %get-tuple-element.61), channel_id=1, source_target_pairs={{0,24},{4,28},{8,16},{12,20},{16,8},{20,12},{24,0},{28,4},{1,25},{... | collective-permute-start | bytes 995336 | tf_op jit(solution)/shard_map/ppermute | solution.py:124
  758.9 169.4 %collective-permute-start.41 = (bf16[144,1152]{1,0:T(8,128)(2,1)}, bf16[144,1152]{1,0:T(8,128)(2,1)}, u32[]{:S(2)}, u32[]{:S(2)}) collective-permute-start(bf16[144,1152]{1,0:T(8,128)(2,1)} %get-tuple-element.61), channel_id=1, source_target_pairs={{0,8},{4,12},{8,0},{12,4},{16,24},{20,28},{24,16},{28,20},{1,9},{5... | collective-permute-start | bytes 995336 | tf_op jit(solution)/shard_map/ppermute | solution.py:124
  758.9 169.3 %collective-permute-start.42 = (bf16[144,1152]{1,0:T(8,128)(2,1)S(1)}, bf16[144,1152]{1,0:T(8,128)(2,1)}, u32[]{:S(2)}, u32[]{:S(2)}) collective-permute-start(bf16[144,1152]{1,0:T(8,128)(2,1)S(1)} %copy-done.54), channel_id=1, source_target_pairs={{0,16},{4,20},{8,24},{12,28},{16,0},{20,4},{24,8},{28,12},{1,17},{... | collective-permute-start | bytes 995336 | tf_op jit(solution)/shard_map/ppermute | solution.py:124
  929.7 26.4 %collective-permute-start.45 = (bf16[4,144,1152]{2,1,0:T(8,128)(2,1)S(1)}, bf16[4,144,1152]{2,1,0:T(8,128)(2,1)}, u32[]{:S(2)}, u32[]{:S(2)}) collective-permute-start(bf16[4,144,1152]{2,1,0:T(8,128)(2,1)S(1)} %pad_maximum_fusion.12.refs_1_), channel_id=1, source_target_pairs={{0,4},{4,0},{8,12},{12,8},{16,20},{20,16},{24,28},{28,24},{1,5},{5... | collective-permute-start | bytes 3981320 | tf_op jit(solution)/shard_map/ppermute | solution.py:124
  1137.7 18.6 %collective-permute-start.49 = (bf16[160,2304]{1,0:T(8,128)(2,1)S(1)}, bf16[160,2304]{1,0:T(8,128)(2,1)S(1)}, u32[]{:S(2)}, u32[]{:S(2)}) collective-permute-start(bf16[160,2304]{1,0:T(8,128)(2,1)S(1)} %pad_maximum_fusion.22), channel_id=1, source_target_pairs={{0,8},{4,12},{8,0},{12,4},{16,24},{20,28},{24,16},{28,20},{1,9},{5... | collective-permute-start | bytes 2211848 | tf_op jit(solution)/shard_map/ppermute | solution.py:124
  1138.1 18.3 %collective-permute-start.47 = (bf16[160,2304]{1,0:T(8,128)(2,1)S(1)}, bf16[160,2304]{1,0:T(8,128)(2,1)S(1)}, u32[]{:S(2)}, u32[]{:S(2)}) collective-permute-start(bf16[160,2304]{1,0:T(8,128)(2,1)S(1)} %pad_maximum_fusion.21), channel_id=1, source_target_pairs={{0,2},{1,3},{2,0},{3,1},{4,6},{5,7},{6,4},{7,5},{8,10},{9,11},{10,... | collective-permute-start | bytes 2211848 | tf_op jit(solution)/shard_map/ppermute | solution.py:124
  1169.6 16.2 %collective-permute-start.52 = (bf16[160,2304]{1,0:T(8,128)(2,1)S(1)}, bf16[160,2304]{1,0:T(8,128)(2,1)S(1)}, u32[]{:S(2)}, u32[]{:S(2)}) collective-permute-start(bf16[160,2304]{1,0:T(8,128)(2,1)S(1)} %get-tuple-element.145), channel_id=1, source_target_pairs={{0,8},{4,12},{8,0},{12,4},{16,24},{20,28},{24,16},{28,20},{1,9},{5... | collective-permute-start | bytes 2211848 | tf_op jit(solution)/shard_map/ppermute | solution.py:124
  1170.2 16.2 %collective-permute-start.51 = (bf16[160,2304]{1,0:T(8,128)(2,1)S(1)}, bf16[160,2304]{1,0:T(8,128)(2,1)S(1)}, u32[]{:S(2)}, u32[]{:S(2)}) collective-permute-start(bf16[160,2304]{1,0:T(8,128)(2,1)S(1)} %get-tuple-element.145), channel_id=1, source_target_pairs={{0,2},{1,3},{2,0},{3,1},{4,6},{5,7},{6,4},{7,5},{8,10},{9,11},{10,... | collective-permute-start | bytes 2211848 | tf_op jit(solution)/shard_map/ppermute | solution.py:124
  1188.3 15.7 %collective-permute-start.55 = (bf16[480,2304]{1,0:T(8,128)(2,1)}, bf16[480,2304]{1,0:T(8,128)(2,1)}, u32[]{:S(2)}, u32[]{:S(2)}) collective-permute-start(bf16[480,2304]{1,0:T(8,128)(2,1)} %pad_maximum_fusion.3), channel_id=1, source_target_pairs={{0,1},{1,0},{2,3},{3,2},{4,5},{5,4},{6,7},{7,6},{8,9},{9,8},{10,11... | collective-permute-start | bytes 6635528 | tf_op jit(solution)/shard_map/ppermute | solution.py:124
  1189.5 11.1 collective-permute-start.54
  1251.7 134.1 %all-gather.9.cloned.1.call-start = ((), (), s32[]{:S(2)}) async-start(), calls=%async_computation.4 | async-start | bytes 2433024 | tf_op jit(solution)/shard_map/all_gather | solution.py:493
  1277.3 34.5 %collective-permute-start.57 = (bf16[640,2304]{1,0:T(8,128)(2,1)}, bf16[640,2304]{1,0:T(8,128)(2,1)S(1)}, u32[]{:S(2)}, u32[]{:S(2)}) collective-permute-start(bf16[640,2304]{1,0:T(8,128)(2,1)} %slice.551), channel_id=1, source_target_pairs={{0,1},{1,0},{2,3},{3,2},{4,5},{5,4},{6,7},{7,6},{8,9},{9,8},{10,11... | collective-permute-start | bytes 8847368 | tf_op jit(solution)/shard_map/ppermute | solution.py:124
  1282.4 14.9 collective-permute-start.66
  1311.7 131.3 %reduce-scatter.4.cloned.1.call-start = ((), (), s32[]{:S(2)}) async-start(), calls=%async_computation.1 | async-start | bytes 368640 | tf_op jit(solution)/shard_map/reduce_scatter | solution.py:517
  1317.0 19.7 %collective-permute-start.60 = (bf16[160,2304]{1,0:T(8,128)(2,1)S(1)}, bf16[160,2304]{1,0:T(8,128)(2,1)}, u32[]{:S(2)}, u32[]{:S(2)}) collective-permute-start(bf16[160,2304]{1,0:T(8,128)(2,1)S(1)} %pad_maximum_fusion.25), channel_id=1, source_target_pairs={{0,8},{4,12},{8,0},{12,4},{16,24},{20,28},{24,16},{28,20},{1,9},{5... | collective-permute-start | bytes 2211848 | tf_op jit(solution)/shard_map/ppermute | solution.py:124
  1318.0 21.6 %collective-permute-start.58 = (bf16[160,2304]{1,0:T(8,128)(2,1)}, bf16[160,2304]{1,0:T(8,128)(2,1)}, u32[]{:S(2)}, u32[]{:S(2)}) collective-permute-start(bf16[160,2304]{1,0:T(8,128)(2,1)} %pad_maximum_fusion.24), channel_id=1, source_target_pairs={{0,2},{1,3},{2,0},{3,1},{4,6},{5,7},{6,4},{7,5},{8,10},{9,11},{10,... | collective-permute-start | bytes 2211848 | tf_op jit(solution)/shard_map/ppermute | solution.py:124
  1341.0 13.3 collective-permute-start.59
  1342.8 11.5 collective-permute-start.61
  1359.4 20.7 %collective-permute-start.62 = (bf16[160,2304]{1,0:T(8,128)(2,1)S(1)}, bf16[160,2304]{1,0:T(8,128)(2,1)S(1)}, u32[]{:S(2)}, u32[]{:S(2)}) collective-permute-start(bf16[160,2304]{1,0:T(8,128)(2,1)S(1)} %subtract_convert_fusion), channel_id=1, source_target_pairs={{0,2},{1,3},{2,0},{3,1},{4,6},{5,7},{6,4},{7,5},{8,10},{9,11},{10,... | collective-permute-start | bytes 2211848 | tf_op jit(solution)/shard_map/ppermute | solution.py:124
  1381.4 12.4 collective-permute-start.63
  1422.7 81.1 %all-gather.5.cloned.1.call-start = ((), (), s32[]{:S(2)}) async-start(), calls=%async_computation.2 | async-start | bytes 2433024 | tf_op jit(solution)/shard_map/all_gather | solution.py:518
  1433.0 17.3 %collective-permute-start.64 = (bf16[320,2304]{1,0:T(8,128)(2,1)}, bf16[320,2304]{1,0:T(8,128)(2,1)S(1)}, u32[]{:S(2)}, u32[]{:S(2)}) collective-permute-start(bf16[320,2304]{1,0:T(8,128)(2,1)} %slice.569), channel_id=1, source_target_pairs={{0,1},{1,0},{2,3},{3,2},{4,5},{5,4},{6,7},{7,6},{8,9},{9,8},{10,11... | collective-permute-start | bytes 4423688 | tf_op jit(solution)/shard_map/ppermute | solution.py:124
  1451.7 36.0 %collective-permute-start.65 = (bf16[160,2304]{1,0:T(8,128)(2,1)S(1)}, bf16[160,2304]{1,0:T(8,128)(2,1)S(1)}, u32[]{:S(2)}, u32[]{:S(2)}) collective-permute-start(bf16[160,2304]{1,0:T(8,128)(2,1)S(1)} %slice.753), channel_id=1, source_target_pairs={{0,2},{1,3},{2,0},{3,1},{4,6},{5,7},{6,4},{7,5},{8,10},{9,11},{10,... | collective-permute-start | bytes 2211848 | tf_op jit(solution)/shard_map/ppermute | solution.py:124
  (202 other events, 4374.6 us)
Sparse Core Ops, SparseCore 0:
  1251.8 46.2 all-gather.6
  1311.8 64.0 all-gather.8
  1422.8 20.1 reduce-scatter.3
  1446.2 57.5 all-gather.4

commit v2 on v1

v2 whole, which is shorter than its diff:
```python
import functools
import math

import jax
import jax.numpy as jnp
from jax import lax
from jax.experimental import pallas as pl
from jax.experimental.pallas import tpu as pltpu
from jax.sharding import PartitionSpec as P

HEAD_WIDTH = 256
ADAPTERS = 8
TINY = pl.CostEstimate(flops=1, transcendentals=0, bytes_accessed=1)


def rms_scale(value_rows, gain_row):
    inverse = lax.rsqrt(jnp.mean(value_rows * value_rows, axis=-1, keepdims=True) + 1e-06)
    return value_rows * inverse * gain_row


def rms_back(value_rows, gain_row, upstream):
    inverse = lax.rsqrt(jnp.mean(value_rows * value_rows, axis=-1, keepdims=True) + 1e-06)
    scaled = gain_row * upstream
    return inverse * scaled - value_rows * (inverse * inverse * inverse) * jnp.mean(
        value_rows * scaled, axis=-1, keepdims=True
    )


def pick_from(lookup, indices, labels):
    return jnp.sum(jnp.where(indices[:, None] == labels[None, :], lookup[None, :], 0), axis=1)


def tree_tables(segments, parents, order):
    count_seg = parents.shape[0]
    sequence_length = segments.shape[0]
    blocks = order.shape[0]
    labels = jnp.arange(count_seg, dtype=jnp.int32)
    ordered_places = jnp.arange(sequence_length, dtype=jnp.int32)
    member = segments[None, :] == labels[:, None]
    starts = jnp.min(jnp.where(member, ordered_places[None, :], sequence_length), axis=1)
    counts = jnp.sum(member.astype(jnp.int32), axis=1)
    grands = pick_from(parents, parents, labels)
    offsets = jnp.where(parents != labels, pick_from(counts, parents, labels), 0) + jnp.where(
        grands != parents, pick_from(counts, grands, labels), 0
    )
    block_rows = sequence_length // blocks
    chosen = order[:, None] == jnp.arange(blocks, dtype=jnp.int32)[None, :]
    segments = jnp.sum(
        jnp.where(chosen[:, :, None], segments.reshape(1, blocks, block_rows), 0), axis=1
    ).reshape(sequence_length)
    places = (
        order[:, None] * block_rows + jnp.arange(block_rows, dtype=jnp.int32)[None, :]
    ).reshape(sequence_length)
    tok_start = pick_from(starts, segments, labels)
    tok_offset = pick_from(offsets, segments, labels)
    tok_parent = pick_from(parents, segments, labels)
    tok_grand = pick_from(grands, segments, labels)
    positions = (places - tok_start + tok_offset).astype(jnp.float32)
    same_seg = (segments[None, :] == segments[:, None]) & (places[None, :] <= places[:, None])
    from_parent = (segments[None, :] == tok_parent[:, None]) & (tok_parent != segments)[:, None]
    from_grand = (segments[None, :] == tok_grand[:, None]) & (tok_grand != tok_parent)[:, None]
    visible = same_seg | from_parent | from_grand
    inv_freq = jnp.exp(
        jnp.arange(HEAD_WIDTH // 2, dtype=jnp.float32) * (-2.0 * math.log(10000.0) / HEAD_WIDTH)
    )
    angles = positions[:, None] * inv_freq[None, :]
    return (visible, jnp.cos(angles), jnp.sin(angles))


def product(former, latter):
    return jnp.dot(former, latter, preferred_element_type=jnp.float32)


def times_rows(former, latter):
    return lax.dot_general(
        former, latter, (((1,), (1,)), ((), ())), preferred_element_type=jnp.float32
    )


def over_rows(former, latter):
    return lax.dot_general(
        former, latter, (((0,), (0,)), ((), ())), preferred_element_type=jnp.float32
    )


def low(values):
    return values.astype(jnp.bfloat16)


def flip(values, axis_name, bit):
    size = lax.axis_size(axis_name)
    return lax.ppermute(values, axis_name, [(i, i ^ bit) for i in range(size)])


def settle(*groups):
    flat, tree = jax.tree.flatten(groups)
    return jax.tree.unflatten(tree, lax.optimization_barrier(flat))


def along_z(blocks, columns_z):
    kinds = blocks.shape[0]
    lines = [[2 * z + x for z in range(columns_z)] for x in range(2)]
    sent = jnp.concatenate([blocks] * (columns_z // kinds))
    return lax.all_to_all(sent, "dp", 0, 0, axis_index_groups=lines)


def assemble(parts, place):
    columns_z, rows, columns = parts[0].shape

    def kernel(place_ref, mine_ref, cross_ref, core_ref, core_cross_ref, out_ref):
        my_x = place_ref[0]
        out_ref[my_x, :, :columns] = mine_ref[0]
        out_ref[my_x, :, columns:] = core_ref[0]
        out_ref[1 - my_x, :, :columns] = cross_ref[0]
        out_ref[1 - my_x, :, columns:] = core_cross_ref[0]

    out = pl.pallas_call(
        kernel,
        out_shape=jax.ShapeDtypeStruct((2 * columns_z, rows, 2 * columns), parts[0].dtype),
        grid_spec=pltpu.PrefetchScalarGridSpec(
            num_scalar_prefetch=1,
            grid=(columns_z,),
            in_specs=[pl.BlockSpec((1, rows, columns), lambda k, place_ref: (k, 0, 0))] * 4,
            out_specs=pl.BlockSpec((2, rows, 2 * columns), lambda k, place_ref: (k, 0, 0)),
        ),
        compiler_params=pltpu.CompilerParams(vmem_limit_bytes=32 << 20),
        cost_estimate=TINY,
    )(place, *parts)
    return out.reshape(2 * columns_z * rows, 2 * columns)


def beside(first, second):
    return jnp.concatenate([first, second], axis=1)


def pick_adapters(ids, whole, halved):
    rank = whole[0][0].shape[1]

    def kernel(ids_ref, *refs):
        count = len(refs) // 2
        for i in range(count):
            refs[count + i][...] = refs[i][0]

    in_specs, out_specs, shapes, stacks = [], [], [], []
    for entries, parity in ((whole, False), (halved, True)):
        for stack, near in entries:
            columns = stack.shape[2] // (2 if parity else 1)
            in_specs.append(
                pl.BlockSpec(
                    (1, rank, columns),
                    functools.partial(
                        lambda near, parity, i, ids_ref: (
                            ids_ref[1 if near else 0],
                            0,
                            ids_ref[2] if parity else 0,
                        ),
                        near,
                        parity,
                    ),
                )
            )
            out_specs.append(pl.BlockSpec((rank, columns), lambda i, ids_ref: (0, 0)))
            shapes.append(jax.ShapeDtypeStruct((rank, columns), stack.dtype))
            stacks.append(stack)
    return pl.pallas_call(
        kernel,
        out_shape=shapes,
        grid_spec=pltpu.PrefetchScalarGridSpec(
            num_scalar_prefetch=1, grid=(1,), in_specs=in_specs, out_specs=out_specs
        ),
        cost_estimate=TINY,
    )(ids, *stacks)


def fdot(former, latter, dims=((1,), (0,))):
    return lax.dot_general(former, latter, (dims, ((), ())), preferred_element_type=jnp.float32)


def turn(values, cosine, sine):
    half = values.shape[1] // 2
    front, back = values[:, :half], values[:, half:]
    return jnp.concatenate(
        [front * cosine - back * sine, back * cosine + front * sine], axis=1
    )


def project_heads(rows, weight, inner, expand, cosine, sine, queries):
    count, depth = rows.shape
    kinds = queries + 2

    def kernel(rows_ref, weight_ref, inner_ref, expand_ref, cosine_ref, sine_ref, out_ref):
        kind = pl.program_id(0) % kinds
        values = fdot(rows_ref[...], weight_ref[...]) + fdot(inner_ref[...], expand_ref[...])

        @pl.when(kind == kinds - 1)
        def _():
            out_ref[...] = low(values)

        @pl.when(kind < kinds - 1)
        def _():
            scale = jnp.where(kind < queries, HEAD_WIDTH ** (-0.5), 1.0)
            out_ref[...] = low(turn(values, cosine_ref[...], sine_ref[...]) * scale)

    whole = lambda array: pl.BlockSpec(array.shape, lambda j: (0, 0))
    return pl.pallas_call(
        kernel,
        out_shape=jax.ShapeDtypeStruct((count, weight.shape[1]), jnp.bfloat16),
        grid=(weight.shape[1] // HEAD_WIDTH,),
        in_specs=[
            whole(rows),
            pl.BlockSpec((depth, HEAD_WIDTH), lambda j: (0, j)),
            whole(inner),
            pl.BlockSpec((expand.shape[0], HEAD_WIDTH), lambda j: (0, j)),
            whole(cosine),
            whole(sine),
        ],
        out_specs=pl.BlockSpec((count, HEAD_WIDTH), lambda j: (0, j)),
        compiler_params=pltpu.CompilerParams(vmem_limit_bytes=40 << 20),
        cost_estimate=TINY,
    )(rows, weight, inner, expand, cosine, sine)


def soft_scores(query, keys, keep):
    bounded = jnp.tanh(fdot(query, keys, ((1,), (1,))) * (1.0 / 50.0))
    masked = jnp.where(keep, 50.0 * bounded, -1e30)
    exponent = jnp.exp(masked - jnp.max(masked, axis=1, keepdims=True))
    return bounded, exponent / jnp.sum(exponent, axis=1, keepdims=True)


def attend(projected, received, visible, queries):
    count = projected.shape[0]
    wide, pair = (queries + 2) * HEAD_WIDTH, 2 * HEAD_WIDTH

    def kernel(mine_ref, got_ref, visible_ref, out_ref):
        first = queries * HEAD_WIDTH
        mine = mine_ref[:, first:]
        got = got_ref[...]
        keys = jnp.concatenate([mine[:, :HEAD_WIDTH], got[:, :HEAD_WIDTH]])
        values = jnp.concatenate([mine[:, HEAD_WIDTH:], got[:, HEAD_WIDTH:]])
        keep = visible_ref[...] > 0
        for h in range(queries):
            columns = slice(h * HEAD_WIDTH, (h + 1) * HEAD_WIDTH)
            _, probs = soft_scores(mine_ref[:, columns], keys, keep)
            out_ref[:, columns] = low(fdot(low(probs), values))

    return pl.pallas_call(
        kernel,
        out_shape=jax.ShapeDtypeStruct((count, 2 * queries * HEAD_WIDTH), jnp.bfloat16),
        grid=(2,),
        in_specs=[
            pl.BlockSpec((count, wide), lambda j: (0, j)),
            pl.BlockSpec((count, pair), lambda j: (0, j)),
            pl.BlockSpec(visible.shape, lambda j: (0, 0)),
        ],
        out_specs=pl.BlockSpec((count, queries * HEAD_WIDTH), lambda j: (0, j)),
        compiler_params=pltpu.CompilerParams(vmem_limit_bytes=40 << 20),
        cost_estimate=TINY,
    )(projected, received, visible)


def attend_back(projected, received, visible, grad_mixed, cosine, sine, queries):
    count = projected.shape[0]
    wide, pair = (queries + 2) * HEAD_WIDTH, 2 * HEAD_WIDTH

    def kernel(mine_ref, got_ref, visible_ref, grad_ref, cos_ref, sin_ref, query_ref, pair_ref):
        first = queries * HEAD_WIDTH
        mine = mine_ref[:, first:]
        got = got_ref[...]
        keys = jnp.concatenate([mine[:, :HEAD_WIDTH], got[:, :HEAD_WIDTH]])
        values = jnp.concatenate([mine[:, HEAD_WIDTH:], got[:, HEAD_WIDTH:]])
        keep = visible_ref[...] > 0
        grad_keys, grad_values = 0.0, 0.0
        for h in range(queries):
            columns = slice(h * HEAD_WIDTH, (h + 1) * HEAD_WIDTH)
            query, grad = mine_ref[:, columns], grad_ref[:, columns]
            bounded, probs = soft_scores(query, keys, keep)
            grad_values = grad_values + fdot(low(probs), grad, ((0,), (0,)))
            grad_probs = fdot(grad, values, ((1,), (1,)))
            inner = jnp.sum(probs * grad_probs, axis=1, keepdims=True)
            grad_scores = low(probs * (grad_probs - inner) * (1.0 - bounded * bounded))
            grad_query = fdot(grad_scores, keys) * HEAD_WIDTH ** (-0.5)
            query_ref[:, columns] = low(turn(grad_query, cos_ref[...], -sin_ref[...]))
            grad_keys = grad_keys + fdot(grad_scores, query, ((0,), (0,)))
        pair_ref[:, :HEAD_WIDTH] = grad_keys
        pair_ref[:, HEAD_WIDTH:] = grad_values

    whole = lambda array: pl.BlockSpec(array.shape, lambda j: (0, 0))
    return pl.pallas_call(
        kernel,
        out_shape=[
            jax.ShapeDtypeStruct((count, 2 * queries * HEAD_WIDTH), jnp.bfloat16),
            jax.ShapeDtypeStruct((2 * count, 2 * pair), jnp.float32),
        ],
        grid=(2,),
        in_specs=[
            pl.BlockSpec((count, wide), lambda j: (0, j)),
            pl.BlockSpec((count, pair), lambda j: (0, j)),
            whole(visible),
            pl.BlockSpec((count, queries * HEAD_WIDTH), lambda j: (0, j)),
            whole(cosine),
            whole(sine),
        ],
        out_specs=[
            pl.BlockSpec((count, queries * HEAD_WIDTH), lambda j: (0, j)),
            pl.BlockSpec((2 * count, pair), lambda j: (0, j)),
        ],
        compiler_params=pltpu.CompilerParams(vmem_limit_bytes=48 << 20),
        cost_estimate=TINY,
    )(projected, received, visible, grad_mixed, cosine, sine)


GELU_A = math.sqrt(2.0 / math.pi)
GELU_B = 0.044715


def gate_and_up(rows, w_gate, w_up, inner, e_gate, e_up):
    count, depth = rows.shape
    units, tile = w_gate.shape[1], 256
    half = inner.shape[1] // 2

    def kernel(rows_ref, gate_w, up_w, inner_ref, gate_e, up_e, gate_ref, up_ref, hidden_ref):
        inner_rows = inner_ref[...]
        gate = fdot(rows_ref[...], gate_w[...]) + fdot(inner_rows[:, :half], gate_e[...])
        up = fdot(rows_ref[...], up_w[...]) + fdot(inner_rows[:, half:], up_e[...])
        bend = jnp.tanh(GELU_A * (gate + GELU_B * (gate * gate * gate)))
        gate_ref[...] = gate
        up_ref[...] = up
        hidden_ref[...] = low(0.5 * gate * (1.0 + bend) * up)

    whole = lambda array: pl.BlockSpec(array.shape, lambda j: (0, 0))
    column = lambda array: pl.BlockSpec((array.shape[0], tile), lambda j: (0, j))
    result = lambda dtype: jax.ShapeDtypeStruct((count, units), dtype)
    return pl.pallas_call(
        kernel,
        out_shape=[result(jnp.float32), result(jnp.float32), result(jnp.bfloat16)],
        grid=(units // tile,),
        in_specs=[whole(rows), column(w_gate), column(w_up), whole(inner), column(e_gate),
                  column(e_up)],
        out_specs=[pl.BlockSpec((count, tile), lambda j: (0, j))] * 3,
        compiler_params=pltpu.CompilerParams(vmem_limit_bytes=48 << 20),
        cost_estimate=TINY,
    )(rows, w_gate, w_up, inner, e_gate, e_up)


def feed_forward_back(grad_rows, grad_inner, inner_t, grad_inner_t, s_gate_up, keep, chunks):
    count, depth = grad_rows.shape
    tile = 256
    tiles = [chunk[0].shape[1] // tile for chunk in chunks]
    firsts = [sum(tiles[:i]) for i in range(len(tiles))]
    total = sum(tiles)
    twice = grad_inner.shape[1]
    each = len(chunks[0])

    def kernel(grad_ref, inner_grad_ref, inner_t_ref, inner_grad_t_ref, s_ref, keep_ref, *refs):
        ins, (rows_ref, inner_ref, units_ref, total_ref, sums_ref) = refs[:-5], refs[-5:]
        step = pl.program_id(0)

        @pl.when(step == 0)
        def _():
            total_ref[...] = jnp.zeros_like(total_ref)
            sums_ref[...] = jnp.zeros_like(sums_ref)

        def one(down, gate_w, up_w, gate_in, up_in, hidden, s_down, e_gate, e_up):
            grad = fdot(grad_ref[...], down[...]) + fdot(inner_grad_ref[...], s_down[...])
            gate, up = gate_in[...], up_in[...]
            square = gate * gate
            bend = jnp.tanh(GELU_A * gate * (1.0 + GELU_B * square))
            half_up = 0.5 * (1.0 + bend)
            slope = half_up + 0.5 * gate * (1.0 - bend * bend) * (
                GELU_A * (1.0 + 3.0 * GELU_B * square)
            )
            grad_gate = low(grad * up * slope)
            grad_up = low(grad * (gate * half_up))
            total_ref[...] += fdot(grad_gate, gate_w[...], ((1,), (1,))) + fdot(
                grad_up, up_w[...], ((1,), (1,))
            )
            sums_ref[:, :twice] += fdot(grad_gate, e_gate[...], ((1,), (1,)))
            sums_ref[:, twice:] += fdot(grad_up, e_up[...], ((1,), (1,)))
            units_ref[:twice] = fdot(inner_t_ref[:twice], grad_gate)
            units_ref[twice : 2 * twice] = fdot(inner_t_ref[twice:], grad_up)
            units_ref[2 * twice :] = fdot(inner_grad_t_ref[...], hidden[...])

        for i in range(len(chunks)):
            within = (step >= firsts[i]) & (step < firsts[i] + tiles[i])
            pl.when(within)(functools.partial(one, *ins[i * each : (i + 1) * each]))

        @pl.when(step == total - 1)
        def _():
            kept = low(sums_ref[...] * keep_ref[...])
            inner_ref[...] = kept
            rows_ref[...] = low(total_ref[...] + fdot(kept, s_ref[...]))

    whole = lambda array: pl.BlockSpec(array.shape, lambda j: (0, 0))

    def column(i, array):
        return pl.BlockSpec(
            (array.shape[0], tile),
            lambda j: (0, jnp.clip(j - firsts[i], 0, tiles[i] - 1)),
        )

    fixed = [grad_rows, grad_inner, inner_t, grad_inner_t, s_gate_up, keep]
    return pl.pallas_call(
        kernel,
        out_shape=[
            jax.ShapeDtypeStruct((count, depth), jnp.bfloat16),
            jax.ShapeDtypeStruct((count, 2 * twice), jnp.bfloat16),
            jax.ShapeDtypeStruct((3 * twice, total * tile), jnp.float32),
        ],
        grid=(total,),
        in_specs=[whole(array) for array in fixed]
        + [column(i, array) for i, chunk in enumerate(chunks) for array in chunk],
        out_specs=[
            pl.BlockSpec((count, depth), lambda j: (0, 0)),
            pl.BlockSpec((count, 2 * twice), lambda j: (0, 0)),
            pl.BlockSpec((3 * twice, tile), lambda j: (0, j)),
        ],
        scratch_shapes=[
            pltpu.VMEM((count, depth), jnp.float32),
            pltpu.VMEM((count, 2 * twice), jnp.float32),
        ],
        compiler_params=pltpu.CompilerParams(vmem_limit_bytes=60 << 20),
        cost_estimate=TINY,
    )(*fixed, *[array for chunk in chunks for array in chunk])


def scatter_pair(part):
    rows = part.shape[0] // 2
    got = flip(low(part[rows:]), "tensor", 2)
    return part[:rows] + got.astype(jnp.float32)


def gather_pair(own):
    return jnp.concatenate([own, flip(own, "tensor", 2)])


def gather_square(own):
    half = own.shape[0] // 2
    from_y = flip(own, "tensor", 2)
    from_z = flip(own, "dp", 2)
    diagonal = [flip(from_y[:half], "dp", 2), flip(from_z[half:], "tensor", 2)]
    return jnp.concatenate([own, from_y, from_z] + diagonal)


def scatter_square(part):
    rows = part.shape[0] // 4
    half = rows // 2
    mine, to_y, to_z, to_zy = (part[i * rows : (i + 1) * rows] for i in range(4))
    got_y = flip(low(jnp.concatenate([to_y[:half], to_zy[:half]])), "tensor", 2)
    got_z = flip(low(jnp.concatenate([to_z[half:], to_zy[half:]])), "dp", 2)
    got_y, got_z = got_y.astype(jnp.float32), got_z.astype(jnp.float32)
    last_y = flip(low(to_y[half:] + got_z[half:]), "tensor", 2).astype(jnp.float32)
    last_z = flip(low(to_z[:half] + got_y[half:]), "dp", 2).astype(jnp.float32)
    return jnp.concatenate(
        [mine[:half] + got_y[:half] + last_z, mine[half:] + got_z[:half] + last_y]
    )


def gather_trees(values, trees):
    values = values[None]
    bits = [1 << b for b in range(1, trees.bit_length() - 1)][::-1] + [1]
    for bit in bits:
        values = jnp.concatenate([values, flip(values, "dp", bit)])
    index = [0]
    for bit in bits:
        index += [i ^ bit for i in index]
    return values, index


def on_device(
    layer_input,
    cotangent,
    norm_gains,
    w_query,
    w_key,
    w_value,
    w_output,
    w_gate,
    w_up,
    w_down,
    query_shrink,
    key_shrink,
    value_shrink,
    output_shrink,
    gate_shrink,
    up_shrink,
    down_shrink,
    query_expand,
    key_expand,
    value_expand,
    output_expand,
    gate_expand,
    up_expand,
    down_expand,
    adapter_ids,
    parent_segments,
    segment_ids,
):
    trees = lax.axis_size("dp")
    columns_z = trees // 2
    my_tree = lax.axis_index("dp")
    my_z, my_x = my_tree // 2, my_tree % 2
    my_part = lax.axis_index("tensor")
    odd = my_z % 2 == 1
    norm_gain = norm_gains.astype(jnp.float32)
    place = my_x.astype(jnp.int32)[None]

    def halves(values):
        half = values.shape[-1] // 2
        return jnp.stack([values[:, :half], values[:, half:]])

    def on_core(values):
        return flip(values, "tensor", 1)

    w_qkv = jnp.concatenate([w_query, w_key, w_value], axis=1)
    cut = w_qkv.shape[0] // 2 // 16 * 16
    gate_halves, up_halves, down_halves = halves(w_gate), halves(w_up), halves(w_down.T)
    units = gate_halves.shape[2]
    first_units = (units // 128 + 1) // 2 * 128
    waiting = [
        w_qkv[None, :cut],
        w_qkv[None, cut:],
        w_output.T[None],
        gate_halves[:, :, first_units:],
        up_halves[:, :, first_units:],
        gate_halves[:, :, :first_units],
        up_halves[:, :, :first_units],
        down_halves[:, :, :first_units],
        down_halves[:, :, first_units:],
    ]
    count = len(waiting)
    near, cross = {}, {}

    near_core, cross_core = {}, {}

    def transfers(step):
        if step < count:
            near[step] = along_z(waiting[step], columns_z)
        if 0 <= step - 1 < count:
            cross[step - 1] = flip(near[step - 1], "dp", 1)
            near_core[step - 1] = on_core(near[step - 1])
        if 0 <= step - 2 < count:
            cross_core[step - 2] = on_core(cross[step - 2])

    def close(step, *values):
        moved = [
            (store, key)
            for store, key in (
                (near, step),
                (cross, step - 1),
                (near_core, step - 1),
                (cross_core, step - 2),
            )
            if key in store
        ]
        following = [waiting[step + 1]] if step + 1 < count else []
        moved_values, following, values = settle(
            [store[key] for store, key in moved], following, values
        )
        for (store, key), value in zip(moved, moved_values):
            store[key] = value
        if following:
            waiting[step + 1] = following[0]
        return values

    def matrix(*keys):
        parts = [
            jnp.concatenate([store[key] for key in keys], axis=1) if len(keys) > 1 else store[keys[0]]
            for store in (near, cross, near_core, cross_core)
        ]
        return assemble(parts, place)

    transfers(0)
    own_rows = layer_input.astype(jnp.float32)
    normed = low(rms_scale(own_rows, norm_gain[0]))
    normed_all = gather_pair(normed)
    near_ids = flip(adapter_ids, "dp", 2)
    labels = jnp.arange(ADAPTERS, dtype=jnp.int32)
    order = jnp.stack([my_part, my_part ^ 2, my_part ^ 1, my_part ^ 3]).astype(jnp.int32)
    visible, cos_rows, sin_rows = tree_tables(segment_ids, parent_segments[0], order)
    row_count = normed_all.shape[0]
    visible = low(visible[:row_count])
    cos_rows, sin_rows = cos_rows[:row_count], sin_rows[:row_count]
    normed_all, near_ids, visible, cos_rows, sin_rows = close(
        0, normed_all, near_ids, visible, cos_rows, sin_rows
    )

    transfers(1)
    picked = pick_adapters(
        jnp.concatenate([adapter_ids, near_ids, (my_z % 2).astype(jnp.int32)[None]]),
        [
            (stack, False)
            for stack in (
                query_shrink,
                key_shrink,
                value_shrink,
                query_expand,
                key_expand,
                value_expand,
                output_shrink,
                output_expand,
            )
        ]
        + [
            (stack, near_tree)
            for stack in (gate_shrink, up_shrink, down_expand)
            for near_tree in (False, True)
        ],
        [
            (stack, near_tree)
            for stack in (gate_expand, up_expand, down_shrink)
            for near_tree in (False, True)
        ],
    )
    s_qkv = jnp.concatenate(picked[0:3])
    e_parts = picked[3:6]
    rank = e_parts[0].shape[0]
    widths = [part.shape[1] for part in e_parts]
    attn_mine = jnp.concatenate(picked[3:7], axis=1)
    e_output = picked[7]
    s_gate_up = jnp.concatenate(picked[8:12])
    e_down = jnp.concatenate(picked[12:14])
    ffn_mine = jnp.concatenate(picked[14:20])
    inner_qkv = low(times_rows(normed_all, s_qkv))
    attn_mine, e_output, s_gate_up, e_down, ffn_mine, s_qkv, inner_qkv = close(
        1, attn_mine, e_output, s_gate_up, e_down, ffn_mine, s_qkv, inner_qkv
    )

    transfers(2)
    attn_other = on_core(attn_mine)
    ffn_other = on_core(ffn_mine)
    attn_other, ffn_other = close(2, attn_other, ffn_other)

    transfers(3)
    heads_here = sum(widths)
    queries = widths[0] // HEAD_WIDTH
    e_mine = attn_mine[:, :heads_here]
    e_other = attn_other[:, :heads_here]
    s_output = beside(attn_mine[:, heads_here:], attn_other[:, heads_here:])
    starts = [sum(widths[:i]) for i in range(4)]
    column_kind = sum(
        (jnp.arange(heads_here, dtype=jnp.int32) >= start).astype(jnp.int32)
        for start in starts[1:3]
    )
    kind_mask = (
        jnp.arange(3 * rank, dtype=jnp.int32)[:, None] // rank
        == jnp.concatenate([column_kind, column_kind])[None, :]
    )
    e_qkv = low(jnp.where(kind_mask, jnp.tile(beside(e_mine, e_other), (3, 1)), 0.0))
    tree_ids, tree_index = gather_trees(adapter_ids, trees)
    units_a = beside(ffn_mine[:, :first_units], ffn_other[:, :first_units])
    units_b = beside(ffn_mine[:, first_units:], ffn_other[:, first_units:])
    adapters_ab = [
        [block[i * 2 * rank : (i + 1) * 2 * rank] for i in range(3)] for block in (units_a, units_b)
    ]
    tree_ids, e_qkv, s_output, adapters_ab = close(3, tree_ids, e_qkv, s_output, adapters_ab)

    transfers(4)
    full_qkv = matrix(0, 1)
    projected = project_heads(
        normed_all, full_qkv, inner_qkv, e_qkv, cos_rows, sin_rows, queries
    )
    received = on_core(
        beside(projected[:, heads_here + starts[1] :], projected[:, starts[1] : heads_here])
    )
    full_qkv, projected, received = close(4, full_qkv, projected, received)

    transfers(5)
    full_out_t = matrix(2)
    mixed_heads = attend(projected, received, visible, queries)
    inner_output = low(times_rows(mixed_heads, s_output))
    attn_part = times_rows(mixed_heads, full_out_t) + product(inner_output, e_output)
    mixed_heads, full_out_t, inner_output, attn_part = close(
        5, mixed_heads, full_out_t, inner_output, attn_part
    )

    transfers(6)
    attended = scatter_pair(attn_part)
    full_gate_b = matrix(3)
    residual = own_rows + rms_scale(attended, norm_gain[1])
    normed_ffn = low(rms_scale(residual, norm_gain[2]))
    residual, attended, normed_ffn, full_gate_b = close(
        6, residual, attended, normed_ffn, full_gate_b
    )

    transfers(7)
    normed_y = flip(normed_ffn, "tensor", 2)
    full_up_b = matrix(4)
    normed_y, full_up_b = close(7, normed_y, full_up_b)

    transfers(8)
    normed_z = flip(normed_ffn, "dp", 2)
    full_gate_a = matrix(5)
    normed_z, full_gate_a = close(8, normed_z, full_gate_a)

    transfers(9)
    normed_zy = flip(normed_z, "tensor", 2)
    full_up_a = matrix(6)
    ffn_rows = jnp.concatenate([normed_ffn, normed_y, normed_z, normed_zy])
    block_rows = residual.shape[0]
    row_block = jnp.arange(4 * block_rows, dtype=jnp.int32) // block_rows
    row_near = (row_block // 2)[:, None]
    rank_near = (jnp.arange(4 * rank, dtype=jnp.int32) // rank % 2)[None, :]
    keep_four = (row_near == rank_near).astype(jnp.float32)
    keep_two = keep_four[:, : 2 * rank]
    inner_gate_up = low(keep_four * times_rows(ffn_rows, s_gate_up))
    chunk_out = [
        gate_and_up(ffn_rows, full_gate, full_up, inner_gate_up, e_gate, e_up)
        for full_gate, full_up, (e_gate, e_up, _) in (
            (full_gate_a, full_up_a, adapters_ab[0]),
            (full_gate_b, full_up_b, adapters_ab[1]),
        )
    ]
    chunk_out, full_gate_a, full_up_a, full_gate_b, full_up_b = close(
        9, chunk_out, full_gate_a, full_up_a, full_gate_b, full_up_b
    )

    cross_core[8] = on_core(cross[8])
    full_down_a = matrix(7)
    hidden = [parts[2] for parts in chunk_out]
    inner_down = low(
        keep_two
        * (times_rows(hidden[0], adapters_ab[0][2]) + times_rows(hidden[1], adapters_ab[1][2]))
    )
    ffn_first = times_rows(hidden[0], full_down_a) + product(inner_down, e_down)
    full_down_b = matrix(8)
    ffn_part = ffn_first + times_rows(hidden[1], full_down_b)
    ffn_out = scatter_square(ffn_part)
    layer_output = low(residual + rms_scale(ffn_out, norm_gain[3]))

    grad_out = cotangent.astype(jnp.float32)
    grad_ffn = gather_square(low(rms_back(ffn_out, norm_gain[3], grad_out)))
    grad_inner_down = low(keep_two * times_rows(grad_ffn, e_down))
    grad_normed_part, grad_inner_gate_up, grad_units = feed_forward_back(
        grad_ffn,
        grad_inner_down,
        inner_gate_up.T,
        grad_inner_down.T,
        s_gate_up,
        keep_four,
        [
            (full_down, full_gate, full_up, *parts, adapters[2], adapters[0], adapters[1])
            for full_down, full_gate, full_up, parts, adapters in (
                (full_down_a, full_gate_a, full_up_a, chunk_out[0], adapters_ab[0]),
                (full_down_b, full_gate_b, full_up_b, chunk_out[1], adapters_ab[1]),
            )
        ],
    )
    grad_normed_ffn = scatter_square(grad_normed_part)
    grad_expand_down = over_rows(inner_down, grad_ffn)
    grad_shrink_gate_up = over_rows(grad_inner_gate_up, ffn_rows)

    grad_resid = grad_out + rms_back(residual, norm_gain[2], grad_normed_ffn)
    grad_attn = gather_pair(low(rms_back(attended, norm_gain[1], grad_resid)))

    grad_inner_output = low(times_rows(grad_attn, e_output))
    grad_mixed = low(
        product(grad_attn, full_out_t) + product(grad_inner_output, s_output)
    )
    grad_expand_output = over_rows(inner_output, grad_attn)
    grad_shrink_output = over_rows(grad_inner_output, mixed_heads)
    grad_queries, grad_pairs = attend_back(
        projected, received, visible, grad_mixed, cos_rows, sin_rows, queries
    )
    pair = 2 * HEAD_WIDTH
    to_core = low(beside(grad_pairs[row_count:, pair:], grad_pairs[row_count:, :pair]))
    grad_pairs = grad_pairs[:row_count] + on_core(to_core).astype(jnp.float32)
    grad_sides = []
    for side in range(2):
        keys_values = grad_pairs[:, side * pair : (side + 1) * pair]
        grad_sides += [
            grad_queries[:, side * widths[0] : (side + 1) * widths[0]],
            low(turn(keys_values[:, :HEAD_WIDTH], cos_rows, -sin_rows)),
            low(keys_values[:, HEAD_WIDTH:]),
        ]
    grad_qkv = jnp.concatenate(grad_sides, axis=1)
    grad_inner_qkv = low(times_rows(grad_qkv, e_qkv))
    grad_expand_qkv = over_rows(inner_qkv, grad_qkv)
    grad_shrink_qkv = over_rows(grad_inner_qkv, normed_all)
    grad_normed = scatter_pair(
        times_rows(grad_qkv, full_qkv) + product(grad_inner_qkv, s_qkv)
    )
    input_grad = grad_resid + rms_back(own_rows, norm_gain[0], grad_normed)

    tree_ids = tree_ids.reshape(trees)
    hot_near = low(tree_ids[:, None] == labels[None, :])

    def by_adapter(hot, gathered):
        return lax.dot_general(
            hot, gathered, (((0,), (0,)), ((), ())), preferred_element_type=jnp.float32
        )

    def from_other_core(mine, other):
        return low(mine + on_core(low(other)).astype(jnp.float32))

    rest = units - first_units
    cuts = [0, first_units, 2 * first_units, 2 * first_units + rest, 2 * units]
    quarters = [grad_units[:, cuts[i] : cuts[i + 1]] for i in range(4)]
    mine, other = beside(quarters[0], quarters[2]), beside(quarters[1], quarters[3])
    local = from_other_core(mine, other)
    local_all, _ = gather_trees(local, trees)
    local_all = local_all.reshape(trees, 3, 2, rank, units)
    same, crossed, same_hot, crossed_hot = [], [], [], []
    where_is = {tree: i for i, tree in enumerate(tree_index)}
    for j in range(trees):
        for near in range(2):
            target = (crossed if (j // 2) % 2 else same)
            hots = (crossed_hot if (j // 2) % 2 else same_hot)
            target.append(local_all[where_is[j], :, near])
            hots.append(hot_near[where_is[j ^ (2 * near)]])
    mine_sum = by_adapter(jnp.stack(same_hot), jnp.stack(same))
    other_sum = by_adapter(jnp.stack(crossed_hot), jnp.stack(crossed))
    low_half = jnp.where(odd, other_sum, mine_sum)
    high_half = jnp.where(odd, mine_sum, other_sum)
    both_halves = jnp.concatenate([low_half, high_half], axis=-1)
    out_expand_gate, out_expand_up, out_shrink_down = (both_halves[:, i] for i in range(3))

    def share(blocks):
        blocks = low(blocks)
        swapped = jnp.where(my_part % 2 == 1, blocks.reshape(2, 2, rank, -1)[:, ::-1], blocks.reshape(2, 2, rank, -1))
        swapped = jnp.where(my_part // 2 == 1, swapped[::-1], swapped)
        kept = swapped[:, 0].astype(jnp.float32) + on_core(swapped[:, 1]).astype(jnp.float32)
        kept = kept[0] + flip(low(kept[1]), "tensor", 2).astype(jnp.float32)
        gathered, _ = gather_trees(low(kept), trees)
        total = low(by_adapter(hot_near, gathered))[None]
        total = jnp.concatenate([total, flip(total, "tensor", 2)])
        total = jnp.stack([total, on_core(total)], axis=1)
        total = jnp.where(my_part // 2 == 1, total[::-1], total)
        total = jnp.where(my_part % 2 == 1, total[:, ::-1], total)
        return total.reshape((4,) + total.shape[2:]).astype(jnp.float32)

    shared = jnp.concatenate([grad_shrink_gate_up, grad_expand_down]).reshape(3, 2, rank, -1)
    shared = shared[:, 0] + flip(low(shared[:, 1]), "dp", 2).astype(jnp.float32)
    shared = share(jnp.concatenate([shared, grad_expand_output[None]]))
    out_shrink_gate, out_shrink_up, out_expand_down, out_expand_output = (
        shared[i] for i in range(4)
    )

    pieces = []
    for side in range(2):
        for i in range(3):
            first = side * heads_here + starts[i]
            pieces.append(grad_expand_qkv[i * rank : (i + 1) * rank, first : first + widths[i]])
        pieces.append(grad_shrink_output[:, side * widths[0] : (side + 1) * widths[0]])
    local = from_other_core(
        jnp.concatenate(pieces[:4], axis=1), jnp.concatenate(pieces[4:], axis=1)
    )
    local_all, _ = gather_trees(local, trees)
    local_all = by_adapter(hot_near, local_all)
    out_expand_query, out_expand_key, out_expand_value = (
        local_all[:, :, starts[i] : starts[i] + widths[i]] for i in range(3)
    )
    out_shrink_output = local_all[:, :, heads_here:]

    shared = grad_shrink_qkv.reshape(3, rank, -1)
    shared = share(jnp.concatenate([shared, jnp.zeros_like(shared[:1])]))
    out_shrink_query, out_shrink_key, out_shrink_value = (shared[i] for i in range(3))
    return (
        layer_output,
        input_grad,
        out_shrink_query,
        out_shrink_key,
        out_shrink_value,
        out_shrink_output,
        out_shrink_gate,
        out_shrink_up,
        out_shrink_down,
        out_expand_query,
        out_expand_key,
        out_expand_value,
        out_expand_output,
        out_expand_gate,
        out_expand_up,
        out_expand_down,
    )


def solution(mesh):
    placed = (
        P(("dp", "tensor"), None),
        P(("dp", "tensor"), None),
        P(),
        P("dp", "tensor"),
        P("dp", "tensor"),
        P("dp", "tensor"),
        P("tensor", "dp"),
        P("dp", "tensor"),
        P("dp", "tensor"),
        P("tensor", "dp"),
        P(),
        P(),
        P(),
        P(None, None, "tensor"),
        P(),
        P(),
        P(None, None, "tensor"),
        P(None, None, "tensor"),
        P(None, None, "tensor"),
        P(None, None, "tensor"),
        P(),
        P(None, None, "tensor"),
        P(None, None, "tensor"),
        P(),
        P("dp"),
        P("dp", None),
        P("dp"),
    )
    return jax.shard_map(
        on_device,
        mesh=mesh,
        in_specs=placed,
        out_specs=(
            P(("dp", "tensor"), None),
            P(("dp", "tensor"), None),
            P(),
            P(),
            P(),
            P(None, None, "tensor"),
            P(),
            P(),
            P(None, None, "tensor"),
            P(None, None, "tensor"),
            P(None, None, "tensor"),
            P(None, None, "tensor"),
            P(),
            P(None, None, "tensor"),
            P(None, None, "tensor"),
            P(),
        ),
        check_vma=False,
    )
```

time: 1530 us -> 794 us (0.52)
  Pallas kernels: 706 us -> 112 us
  matrix products: 200 us -> 48.9 us
  blocking collectives: 56.7 us -> 0 us
  local copies, waits for them, and re-layouts: 84.1 us -> 119 us
  waiting for transfers between devices: 318 us -> 341 us
  starting transfers between devices: 76.7 us -> 99.1 us
    pallas_call x5 -> x8, Pallas kernels: 706 us -> 14.8 us  [assemble(): pl.pallas_call(kernel, out_shape=jax.ShapeDtypeStruct((2 * columns_z, row...]
    pallas_call x0 -> x7, Pallas kernels: none -> 96.8 us  [the longest x1 52.4 us: feed_forward_back(): pl.pallas_call(kernel, out_shape=[jax.ShapeDtypeStruct((count, depth), jn...]
    dot_general x14 -> x5, matrix products: 83.2 us -> 8.32 us  [product(): return jnp.dot(former, latter, preferred_element_type=jnp.float32)]
    all_to_all x0 -> x9, starting transfers between devices: none -> 41.4 us  [along_z(): return lax.all_to_all(sent, 'dp', 0, 0, axis_index_groups=lines)]
    dot_general x14 -> x12, matrix products: 70.6 us -> 29.8 us  [times_rows(): lax.dot_general(former, latter, (((1,), (1,)), ((), ())), preferred_eleme...]
    all_gather x1 -> x0, blocking collectives: 32.1 us -> none  [on_device(): lax.all_gather(local, 'dp', axis=0, tiled=False)]
    all_to_all x0 -> x9, waiting for transfers between devices: none -> 28.9 us  [along_z(): return lax.all_to_all(sent, 'dp', 0, 0, axis_index_groups=lines)]
    another operation x4 -> x27, local copies, waits for them, and re-layouts: 1.25 us -> 27.1 us  [the longest x13 13.6 us: on_device(): mine_sum = by_adapter(jnp.stack(same_hot), jnp.stack(same))]
  transfers between devices with their start and end apart: 72 -> 86, of which waited for: 29 -> 40; matrix products, arithmetic and copies ran while one was open for 15% -> 16% of each run, Pallas kernels for 21% -> 7%
where the time goes in v2:
time: 794 us; the launch traced here: 784 us
  waiting for transfers between devices  341 us (43%)
  local copies, waits for them, and re-layouts  119 us (15%)
  Pallas kernels  112 us (14%)
  starting transfers between devices  99.1 us (12%)
  other arithmetic  59.8 us (8%)
  matrix products  48.9 us (6%)
    ppermute x77, waiting for transfers between devices, flip(): return lax.ppermute(values, axis_name, [(i, i ^ bit) for i in range(size)])  312 us
    unnamed x355, local copies, waits for them, and re-layouts  67.9 us
    ppermute x77, starting transfers between devices, flip(): return lax.ppermute(values, axis_name, [(i, i ^ bit) for i in range(size)])  57.7 us
    pallas_call x1, Pallas kernels, feed_forward_back(): pl.pallas_call(kernel, out_shape=[jax.ShapeDtypeStruct((count, depth), jn...  52.4 us
    all_to_all x9, starting transfers between devices, along_z(): return lax.all_to_all(sent, 'dp', 0, 0, axis_index_groups=lines)  41.4 us
    dot_general x12, matrix products, times_rows(): lax.dot_general(former, latter, (((1,), (1,)), ((), ())), preferred_eleme...  29.8 us
    all_to_all x9, waiting for transfers between devices, along_z(): return lax.all_to_all(sent, 'dp', 0, 0, axis_index_groups=lines)  28.9 us
    pallas_call x2, Pallas kernels, gate_and_up(): pl.pallas_call(kernel, out_shape=[result(jnp.float32), result(jnp.float32...  25.4 us
  transfers between devices with their start and end apart: 86, of which 40 were waited for; matrix products, arithmetic and copies ran while one was open for 16% of the time, Pallas kernels for 7%

profile of v2, /device:TPU:0, one launch (start us, length us, event | category | flops | bytes accessed | tf_op | source)
XLA Modules:
  0.0 783.7 jit_solution(4822819368415775685)
XLA Ops:
  5.4 3.0 collective-permute-start
  10.5 5.0 all-to-all-start
  22.1 2.9 collective-permute-done
  26.3 8.2 %collective-permute-done.1 = s32[1]{0:T(128)} collective-permute-done((s32[1]{0:T(128)}, s32[1]{0:T(128)}, u32[]{:S(2)}, u32[]{:S(2)}) %collective-permute-start.1) | collective-permute-done | bytes 36 | tf_op jit(solution)/shard_map/ppermute | solution.py:92
  34.5 9.3 %all-to-all-done = bf16[4,144,1024]{2,1,0:T(8,128)(2,1)S(1)} async-done(((bf16[4,144,1024]{2,1,0:T(8,128)(2,1)}), bf16[4,144,1024]{2,1,0:T(8,128)(2,1)S(1)}, u32[]{:S(2)}, u32[]{:S(2)}) %all-to-all-start) | async-done | bytes 1179680 | tf_op jit(solution)/shard_map/all_to_all | solution.py:104
  46.4 3.0 shard_map.378
  52.4 4.4 all-to-all-start.1
  60.7 10.1 %collective-permute-done.2 = bf16[4,144,1024]{2,1,0:T(8,128)(2,1)} collective-permute-done((bf16[4,144,1024]{2,1,0:T(8,128)(2,1)S(1)}, bf16[4,144,1024]{2,1,0:T(8,128)(2,1)}, u32[]{:S(2)}, u32[]{:S(2)}) %collective-permute-start.2) | collective-permute-done | bytes 1179680 | tf_op jit(solution)/shard_map/ppermute | solution.py:92
  70.8 15.6 %all-to-all-done.1 = bf16[4,144,1024]{2,1,0:T(8,128)(2,1)} async-done(((bf16[4,144,1024]{2,1,0:T(8,128)(2,1)}), bf16[4,144,1024]{2,1,0:T(8,128)(2,1)}, u32[]{:S(2)}, u32[]{:S(2)}) %all-to-all-start.1) | async-done | bytes 1179680 | tf_op jit(solution)/shard_map/all_to_all | solution.py:104
  88.4 3.5 all-to-all-start.2
  97.5 2.8 collective-permute-start.12
  100.3 19.5 %collective-permute-done.4 = bf16[4,144,1024]{2,1,0:T(8,128)(2,1)S(1)} collective-permute-done((bf16[4,144,1024]{2,1,0:T(8,128)(2,1)}, bf16[4,144,1024]{2,1,0:T(8,128)(2,1)S(1)}, u32[]{:S(2)}, u32[]{:S(2)}) %collective-permute-start.4) | collective-permute-done | bytes 1179680 | tf_op jit(solution)/shard_map/ppermute | solution.py:92
  123.0 4.7 all-to-all-start.3
  133.8 12.1 %collective-permute-done.13 = s32[2,1]{0,1:T(1,128)S(1)} collective-permute-done((s32[2,1]{0,1:T(1,128)S(1)}, s32[2,1]{0,1:T(1,128)S(1)}, u32[]{:S(2)}, u32[]{:S(2)}) %collective-permute-start.13) | collective-permute-done | bytes 40 | tf_op jit(solution)/shard_map/ppermute | solution.py:92
  147.1 10.7 %collective-permute-done.14 = s32[4,1]{0,1:T(1,128)S(1)} collective-permute-done((s32[4,1]{0,1:T(1,128)S(1)}, s32[4,1]{0,1:T(1,128)S(1)}, u32[]{:S(2)}, u32[]{:S(2)}) %collective-permute-start.14) | collective-permute-done | bytes 48 | tf_op jit(solution)/shard_map/ppermute | solution.py:92
  167.3 5.2 all-to-all-start.4
  180.2 6.5 shard_map.380.mine_ref
  189.1 15.0 %collective-permute-done.15.cross_ref = bf16[4,288,512]{2,1,0:T(8,128)(2,1)} collective-permute-done((bf16[4,288,512]{2,1,0:T(8,128)(2,1)}, bf16[4,288,512]{2,1,0:T(8,128)(2,1)}, u32[]{:S(2)}, u32[]{:S(2)}) %collective-permute-start.15) | collective-permute-done | bytes 1179680 | tf_op jit(solution)/shard_map/ppermute | solution.py:92
  207.4 5.0 all-to-all-start.5
  220.5 3.0 shard_map.381
  224.4 3.3 convolution_add_fusion.1
  227.8 10.7 %collective-permute-done.19.cross_ref = bf16[4,288,512]{2,1,0:T(8,128)(2,1)S(1)} collective-permute-done((bf16[4,288,512]{2,1,0:T(8,128)(2,1)}, bf16[4,288,512]{2,1,0:T(8,128)(2,1)S(1)}, u32[]{:S(2)}, u32[]{:S(2)}) %collective-permute-start.19) | collective-permute-done | bytes 1179680 | tf_op jit(solution)/shard_map/ppermute | solution.py:92
  241.5 4.1 all-to-all-done.5.mine_ref
  249.7 3.6 all-to-all-start.6
  256.9 2.5 shard_map.383
  261.5 4.1 collective-permute-done.25
  270.5 18.3 %collective-permute-done.22.cross_ref = bf16[4,288,640]{2,1,0:T(8,128)(2,1)S(1)} collective-permute-done((bf16[4,288,640]{2,1,0:T(8,128)(2,1)S(1)}, bf16[4,288,640]{2,1,0:T(8,128)(2,1)S(1)}, u32[]{:S(2)}, u32[]{:S(2)}) %collective-permute-start.22) | collective-permute-done | bytes 1474592 | tf_op jit(solution)/shard_map/ppermute | solution.py:92
  291.0 3.1 pad_maximum_fusion.9
  294.2 4.8 all-to-all-start.7
  310.3 8.2 %collective-permute-done.29 = bf16[160,2304]{1,0:T(8,128)(2,1)S(1)} collective-permute-done((bf16[160,2304]{1,0:T(8,128)(2,1)}, bf16[160,2304]{1,0:T(8,128)(2,1)S(1)}, u32[]{:S(2)}, u32[]{:S(2)}) %collective-permute-start.29) | collective-permute-done | bytes 737312 | tf_op jit(solution)/shard_map/ppermute | solution.py:92
  318.6 12.0 %collective-permute-done.26.cross_ref = bf16[4,288,640]{2,1,0:T(8,128)(2,1)S(1)} collective-permute-done((bf16[4,288,640]{2,1,0:T(8,128)(2,1)S(1)}, bf16[4,288,640]{2,1,0:T(8,128)(2,1)S(1)}, u32[]{:S(2)}, u32[]{:S(2)}) %collective-permute-start.26) | collective-permute-done | bytes 1474592 | tf_op jit(solution)/shard_map/ppermute | solution.py:92
  336.4 5.2 all-to-all-start.8
  351.5 24.1 %collective-permute-done.33 = bf16[160,2304]{1,0:T(8,128)(2,1)S(1)} collective-permute-done((bf16[160,2304]{1,0:T(8,128)(2,1)}, bf16[160,2304]{1,0:T(8,128)(2,1)S(1)}, u32[]{:S(2)}, u32[]{:S(2)}) %collective-permute-start.33) | collective-permute-done | bytes 737312 | tf_op jit(solution)/shard_map/ppermute | solution.py:92
  389.2 6.1 collective-permute-done.37
  397.5 11.5 %shard_map.388 = (f32[640,1024]{1,0:T(8,128)S(1)}, f32[640,1024]{1,0:T(8,128)}, bf16[640,1024]{1,0:T(8,128)(2,1)S(1)}) custom-call(bf16[640,2304]{1,0:T(8,128)(2,1)} %copy-done, bf16[2304,1024]{1,0:T(8,128)(2,1)} %bitcast.286, bf16[2304,1024]{1,0:T(8,128)(2,1)} %bitcast.288, bf16[640,64]{1,0:T(8,128)(2,1)S(1)} %fusion.55.inner_ref, ...), custom_call_target="tpu_custom_call" | custom-call | flops 1 | bytes 1 | tf_op jit(solution)/shard_map/pallas_call | solution.py:333
  409.1 13.9 %shard_map.387 = (f32[640,1280]{1,0:T(8,128)}, f32[640,1280]{1,0:T(8,128)}, bf16[640,1280]{1,0:T(8,128)(2,1)S(1)}) custom-call(bf16[640,2304]{1,0:T(8,128)(2,1)S(1)} %copy-done.1, bf16[2304,1280]{1,0:T(8,128)(2,1)} %bitcast.282, bf16[2304,1280]{1,0:T(8,128)(2,1)} %bitcast.284, bf16[640,64]{1,0:T(8,128)(2,1)S(1)} %fusion.55.inner_ref, ...), custom_call_target="tpu_custom_call" | custom-call | flops 1 | bytes 1 | tf_op jit(solution)/shard_map/pallas_call | solution.py:333
  425.6 3.1 shard_map.389
  429.8 3.5 fusion.120
  433.4 5.8 fusion.118
  439.2 2.8 shard_map.390
  442.0 8.1 %fusion.105 = (bf16[640,2304]{1,0:T(8,128)(2,1)S(1)}, f32[640,2304]{1,0:T(8,128)S(1)}) fusion(f32[640,2304]{1,0:T(8,128)} %fusion.118, f32[640,2304]{1,0:T(8,128)} %fusion.120, bf16[640,1024]{1,0:T(8,128)(2,1)S(1)} %get-tuple-element.235.refs_14_, bf16[2304,1024]{1,0:T(8,128)(2,1)S(1)} %bitcast.290), kind=kOutput, calls=%fused_computation.370 | convolution fusion | flops 3024322560 | bytes 26673152 | tf_op jit(solution)/shard_map/dot_general | solution.py:75
  452.1 15.9 %collective-permute-done.41 = bf16[160,2304]{1,0:T(8,128)(2,1)S(1)} collective-permute-done((bf16[160,2304]{1,0:T(8,128)(2,1)S(1)}, bf16[160,2304]{1,0:T(8,128)(2,1)S(1)}, u32[]{:S(2)}, u32[]{:S(2)}) %collective-permute-start.41) | collective-permute-done | bytes 737312 | tf_op jit(solution)/shard_map/ppermute | solution.py:92
  471.7 5.5 collective-permute-done.40
  483.0 13.1 %collective-permute-done.43 = bf16[160,2304]{1,0:T(8,128)(2,1)} collective-permute-done((bf16[160,2304]{1,0:T(8,128)(2,1)}, bf16[160,2304]{1,0:T(8,128)(2,1)}, u32[]{:S(2)}, u32[]{:S(2)}) %collective-permute-start.43) | collective-permute-done | bytes 737312 | tf_op jit(solution)/shard_map/ppermute | solution.py:92
  508.3 3.4 fusion.26.inner_grad_ref
  513.3 52.4 %shard_map.391 = (bf16[640,2304]{1,0:T(8,128)(2,1)}, bf16[640,64]{1,0:T(8,128)(2,1)}, f32[96,2304]{1,0:T(8,128)}) custom-call(bf16[640,2304]{1,0:T(8,128)(2,1)} %constant_dynamic-update-slice_fusion.16.grad_ref, bf16[640,32]{1,0:T(8,128)(2,1)} %fusion.26.inner_grad_ref, bf16[64,640]{1,0:T(8,128)(2,1)} %get-tuple-element.448.inner_t_ref, ...), custom_call_target="tpu_custom_call" | custom-call | flops 1 | bytes 1 | tf_op jit(solution)/shard_map/pallas_call | solution.py:402
  575.3 8.3 %collective-permute-done.65 = bf16[3,16,2304]{2,1,0:T(8,128)(2,1)S(1)} collective-permute-done((bf16[3,16,2304]{2,1,0:T(8,128)(2,1)S(1)}, bf16[3,16,2304]{2,1,0:T(8,128)(2,1)S(1)}, u32[]{:S(2)}, u32[]{:S(2)}) %collective-permute-start.65) | collective-permute-done | bytes 221216 | tf_op jit(solution)/shard_map/ppermute | solution.py:92
  585.4 11.7 %collective-permute-done.74 = bf16[1,96,1152]{2,1,0:T(8,128)(2,1)S(1)} collective-permute-done((bf16[1,96,1152]{2,1,0:T(8,128)(2,1)S(1)}, bf16[1,96,1152]{2,1,0:T(8,128)(2,1)S(1)}, u32[]{:S(2)}, u32[]{:S(2)}) %collective-permute-start.74) | collective-permute-done | bytes 221216 | tf_op jit(solution)/shard_map/ppermute | solution.py:92
  597.2 2.9 collective-permute-start.75
  602.1 8.9 %collective-permute-done.75 = bf16[2,96,1152]{2,1,0:T(8,128)(2,1)S(1)} collective-permute-done((bf16[2,96,1152]{2,1,0:T(8,128)(2,1)S(1)}, bf16[2,96,1152]{2,1,0:T(8,128)(2,1)S(1)}, u32[]{:S(2)}, u32[]{:S(2)}) %collective-permute-start.75) | collective-permute-done | bytes 442400 | tf_op jit(solution)/shard_map/ppermute | solution.py:92
  612.0 6.0 collective-permute-done.48
  622.9 4.9 collective-permute-done.50
  638.4 4.8 stack.93
  644.8 6.5 stack.95
  662.2 3.2 fusion.18.grad_ref
  665.6 6.5 shard_map.392
  675.3 3.6 collective-permute-done.67
  681.2 7.3 collective-permute-done.68
  689.0 5.1 collective-permute-done.69
  699.5 3.3 convolution_add_fusion
  709.5 26.4 %collective-permute-done.55 = bf16[16,2304]{1,0:T(8,128)(2,1)S(1)} collective-permute-done((bf16[16,2304]{1,0:T(8,128)(2,1)S(1)}, bf16[16,2304]{1,0:T(8,128)(2,1)S(1)}, u32[]{:S(2)}, u32[]{:S(2)}) %collective-permute-start.55) | collective-permute-done | bytes 73760 | tf_op jit(solution)/shard_map/ppermute | solution.py:92
  738.1 6.8 collective-permute-done.56
  753.6 6.2 collective-permute-done.58
  763.3 10.8 %collective-permute-done.59 = bf16[1,8,16,2304]{3,1,2,0:T(8,128)(2,1)S(1)} collective-permute-done((bf16[1,8,16,2304]{3,1,2,0:T(8,128)(2,1)S(1)}, bf16[1,8,16,2304]{3,1,2,0:T(8,128)(2,1)S(1)}, u32[]{:S(2)}, u32[]{:S(2)}) %collective-permute-start.59) | collective-permute-done | bytes 589856 | tf_op jit(solution)/shard_map/ppermute | solution.py:92
  (730 shorter events, 247.2 us)
Async XLA Ops:
  5.4 19.6 %collective-permute-start = (bf16[160,2304]{1,0:T(8,128)(2,1)S(1)}, bf16[160,2304]{1,0:T(8,128)(2,1)}, u32[]{:S(2)}, u32[]{:S(2)}) collective-permute-start(bf16[160,2304]{1,0:T(8,128)(2,1)S(1)} %fusion.12), channel_id=1, source_target_pairs={{0,2},{1,3},{2,0},{3,1},{4,6},{5,7},{6,4},{7,5},{8,10},{9,11},{10,... | collective-permute-start | bytes 2211848 | tf_op jit(solution)/shard_map/ppermute | solution.py:92
  10.5 33.3 %all-to-all-start = ((bf16[4,144,1024]{2,1,0:T(8,128)(2,1)}), bf16[4,144,1024]{2,1,0:T(8,128)(2,1)S(1)}, u32[]{:S(2)}, u32[]{:S(2)}) async-start(bf16[4,144,1024]{2,1,0:T(8,128)(2,1)} %concatenate.222), calls=%async_computation | async-start | bytes 2359296 | tf_op jit(solution)/shard_map/all_to_all | solution.py:104
  15.5 19.0 %collective-permute-start.1 = (s32[1]{0:T(128)}, s32[1]{0:T(128)}, u32[]{:S(2)}, u32[]{:S(2)}) collective-permute-start(s32[1]{0:T(128)} %param.51), channel_id=1, source_target_pairs={{0,8},{4,12},{8,0},{12,4},{16,24},{20,28},{24,16},{28,20},{1,9},{5... | collective-permute-start | bytes 20 | tf_op jit(solution)/shard_map/ppermute | solution.py:92
  43.7 27.0 %collective-permute-start.2 = (bf16[4,144,1024]{2,1,0:T(8,128)(2,1)S(1)}, bf16[4,144,1024]{2,1,0:T(8,128)(2,1)}, u32[]{:S(2)}, u32[]{:S(2)}) collective-permute-start(bf16[4,144,1024]{2,1,0:T(8,128)(2,1)S(1)} %all-to-all-done), channel_id=1, source_target_pairs={{0,4},{4,0},{8,12},{12,8},{16,20},{20,16},{24,28},{28,24},{1,5},{5... | collective-permute-start | bytes 3538952 | tf_op jit(solution)/shard_map/ppermute | solution.py:92
  45.2 25.5 %collective-permute-start.3 = (bf16[4,144,1024]{2,1,0:T(8,128)(2,1)S(1)}, bf16[4,144,1024]{2,1,0:T(8,128)(2,1)}, u32[]{:S(2)}, u32[]{:S(2)}) collective-permute-start(bf16[4,144,1024]{2,1,0:T(8,128)(2,1)S(1)} %all-to-all-done), channel_id=1, source_target_pairs={{0,1},{1,0},{2,3},{3,2},{4,5},{5,4},{6,7},{7,6},{8,9},{9,8},{10,11... | collective-permute-start | bytes 3538952 | tf_op jit(solution)/shard_map/ppermute | solution.py:92
  52.4 34.0 %all-to-all-start.1 = ((bf16[4,144,1024]{2,1,0:T(8,128)(2,1)}), bf16[4,144,1024]{2,1,0:T(8,128)(2,1)}, u32[]{:S(2)}, u32[]{:S(2)}) async-start(bf16[4,144,1024]{2,1,0:T(8,128)(2,1)} %concatenate.224), calls=%async_computation.1 | async-start | bytes 2359296 | tf_op jit(solution)/shard_map/all_to_all | solution.py:104
  88.4 33.4 %all-to-all-start.2 = ((bf16[4,288,512]{2,1,0:T(8,128)(2,1)}), bf16[4,288,512]{2,1,0:T(8,128)(2,1)S(1)}, u32[]{:S(2)}, u32[]{:S(2)}) async-start(bf16[4,288,512]{2,1,0:T(8,128)(2,1)} %concatenate.231), calls=%async_computation.2 | async-start | bytes 2359296 | tf_op jit(solution)/shard_map/all_to_all | solution.py:104
  91.9 27.9 %collective-permute-start.4 = (bf16[4,144,1024]{2,1,0:T(8,128)(2,1)}, bf16[4,144,1024]{2,1,0:T(8,128)(2,1)S(1)}, u32[]{:S(2)}, u32[]{:S(2)}) collective-permute-start(bf16[4,144,1024]{2,1,0:T(8,128)(2,1)} %all-to-all-done.1), channel_id=1, source_target_pairs={{0,4},{4,0},{8,12},{12,8},{16,20},{20,16},{24,28},{28,24},{1,5},{5... | collective-permute-start | bytes 3538952 | tf_op jit(solution)/shard_map/ppermute | solution.py:92
  92.5 27.3 %collective-permute-start.5 = (bf16[4,144,1024]{2,1,0:T(8,128)(2,1)}, bf16[4,144,1024]{2,1,0:T(8,128)(2,1)S(1)}, u32[]{:S(2)}, u32[]{:S(2)}) collective-permute-start(bf16[4,144,1024]{2,1,0:T(8,128)(2,1)} %all-to-all-done.1), channel_id=1, source_target_pairs={{0,1},{1,0},{2,3},{3,2},{4,5},{5,4},{6,7},{7,6},{8,9},{9,8},{10,11... | collective-permute-start | bytes 3538952 | tf_op jit(solution)/shard_map/ppermute | solution.py:92
  92.5 29.3 %collective-permute-start.6 = (bf16[4,144,1024]{2,1,0:T(8,128)(2,1)}, bf16[4,144,1024]{2,1,0:T(8,128)(2,1)}, u32[]{:S(2)}, u32[]{:S(2)}) collective-permute-start(bf16[4,144,1024]{2,1,0:T(8,128)(2,1)} %collective-permute-done.2), channel_id=1, source_target_pairs={{0,1},{1,0},{2,3},{3,2},{4,5},{5,4},{6,7},{7,6},{8,9},{9,8},{10,11... | collective-permute-start | bytes 3538952 | tf_op jit(solution)/shard_map/ppermute | solution.py:92
  97.5 33.6 %collective-permute-start.12 = (s32[1,1]{0,1:T(1,128)}, s32[1,1]{0,1:T(1,128)}, u32[]{:S(2)}, u32[]{:S(2)}) collective-permute-start(s32[1,1]{0,1:T(1,128)} %bitcast.19), channel_id=1, source_target_pairs={{0,16},{4,20},{8,24},{12,28},{16,0},{20,4},{24,8},{28,12},{1,17},{... | collective-permute-start | bytes 20 | tf_op jit(solution)/shard_map/ppermute | solution.py:92
  123.0 41.8 %all-to-all-start.3 = ((bf16[4,288,512]{2,1,0:T(8,128)(2,1)}), bf16[4,288,512]{2,1,0:T(8,128)(2,1)}, u32[]{:S(2)}, u32[]{:S(2)}) async-start(bf16[4,288,512]{2,1,0:T(8,128)(2,1)} %pad_maximum_fusion.13), calls=%async_computation.3 | async-start | bytes 2359296 | tf_op jit(solution)/shard_map/all_to_all | solution.py:104
  129.3 33.5 %collective-permute-start.10 = (bf16[4,288,512]{2,1,0:T(8,128)(2,1)S(1)}, bf16[4,288,512]{2,1,0:T(8,128)(2,1)S(1)}, u32[]{:S(2)}, u32[]{:S(2)}) collective-permute-start(bf16[4,288,512]{2,1,0:T(8,128)(2,1)S(1)} %all-to-all-done.2.mine_ref), channel_id=1, source_target_pairs={{0,1},{1,0},{2,3},{3,2},{4,5},{5,4},{6,7},{7,6},{8,9},{9,8},{10,11... | collective-permute-start | bytes 3538952 | tf_op jit(solution)/shard_map/ppermute | solution.py:92
  129.4 35.5 %collective-permute-start.9 = (bf16[4,288,512]{2,1,0:T(8,128)(2,1)S(1)}, bf16[4,288,512]{2,1,0:T(8,128)(2,1)}, u32[]{:S(2)}, u32[]{:S(2)}) collective-permute-start(bf16[4,288,512]{2,1,0:T(8,128)(2,1)S(1)} %all-to-all-done.2.mine_ref), channel_id=1, source_target_pairs={{0,4},{4,0},{8,12},{12,8},{16,20},{20,16},{24,28},{28,24},{1,5},{5... | collective-permute-start | bytes 3538952 | tf_op jit(solution)/shard_map/ppermute | solution.py:92
  130.0 33.8 %collective-permute-start.11 = (bf16[4,144,1024]{2,1,0:T(8,128)(2,1)S(1)}, bf16[4,144,1024]{2,1,0:T(8,128)(2,1)S(1)}, u32[]{:S(2)}, u32[]{:S(2)}) collective-permute-start(bf16[4,144,1024]{2,1,0:T(8,128)(2,1)S(1)} %copy-done.98), channel_id=1, source_target_pairs={{0,1},{1,0},{2,3},{3,2},{4,5},{5,4},{6,7},{7,6},{8,9},{9,8},{10,11... | collective-permute-start | bytes 3538952 | tf_op jit(solution)/shard_map/ppermute | solution.py:92
  131.7 14.1 %collective-permute-start.13 = (s32[2,1]{0,1:T(1,128)S(1)}, s32[2,1]{0,1:T(1,128)S(1)}, u32[]{:S(2)}, u32[]{:S(2)}) collective-permute-start(s32[2,1]{0,1:T(1,128)S(1)} %pad_add_fusion.3), channel_id=1, source_target_pairs={{0,8},{4,12},{8,0},{12,4},{16,24},{20,28},{24,16},{28,20},{1,9},{5... | collective-permute-start | bytes 32 | tf_op jit(solution)/shard_map/ppermute | solution.py:92
  146.6 11.3 %collective-permute-start.14 = (s32[4,1]{0,1:T(1,128)S(1)}, s32[4,1]{0,1:T(1,128)S(1)}, u32[]{:S(2)}, u32[]{:S(2)}) collective-permute-start(s32[4,1]{0,1:T(1,128)S(1)} %pad_add_fusion.4), channel_id=1, source_target_pairs={{0,4},{4,0},{8,12},{12,8},{16,20},{20,16},{24,28},{28,24},{1,5},{5... | collective-permute-start | bytes 56 | tf_op jit(solution)/shard_map/ppermute | solution.py:92
  167.3 38.8 %all-to-all-start.4 = ((bf16[4,288,512]{2,1,0:T(8,128)(2,1)}), bf16[4,288,512]{2,1,0:T(8,128)(2,1)}, u32[]{:S(2)}, u32[]{:S(2)}) async-start(bf16[4,288,512]{2,1,0:T(8,128)(2,1)} %pad_maximum_fusion.14), calls=%async_computation.4 | async-start | bytes 2359296 | tf_op jit(solution)/shard_map/all_to_all | solution.py:104
  176.5 27.6 %collective-permute-start.15 = (bf16[4,288,512]{2,1,0:T(8,128)(2,1)}, bf16[4,288,512]{2,1,0:T(8,128)(2,1)}, u32[]{:S(2)}, u32[]{:S(2)}) collective-permute-start(bf16[4,288,512]{2,1,0:T(8,128)(2,1)} %all-to-all-done.3.mine_ref), channel_id=1, source_target_pairs={{0,4},{4,0},{8,12},{12,8},{16,20},{20,16},{24,28},{28,24},{1,5},{5... | collective-permute-start | bytes 3538952 | tf_op jit(solution)/shard_map/ppermute | solution.py:92
  177.1 27.0 %collective-permute-start.16 = (bf16[4,288,512]{2,1,0:T(8,128)(2,1)}, bf16[4,288,512]{2,1,0:T(8,128)(2,1)S(1)}, u32[]{:S(2)}, u32[]{:S(2)}) collective-permute-start(bf16[4,288,512]{2,1,0:T(8,128)(2,1)} %all-to-all-done.3.mine_ref), channel_id=1, source_target_pairs={{0,1},{1,0},{2,3},{3,2},{4,5},{5,4},{6,7},{7,6},{8,9},{9,8},{10,11... | collective-permute-start | bytes 3538952 | tf_op jit(solution)/shard_map/ppermute | solution.py:92
  177.1 28.0 %collective-permute-start.17 = (bf16[4,288,512]{2,1,0:T(8,128)(2,1)}, bf16[4,288,512]{2,1,0:T(8,128)(2,1)S(1)}, u32[]{:S(2)}, u32[]{:S(2)}) collective-permute-start(bf16[4,288,512]{2,1,0:T(8,128)(2,1)} %collective-permute-done.9.cross_ref), channel_id=1, source_target_pairs={{0,1},{1,0},{2,3},{3,2},{4,5},{5,4},{6,7},{7,6},{8,9},{9,8},{10,11... | collective-permute-start | bytes 3538952 | tf_op jit(solution)/shard_map/ppermute | solution.py:92
  207.4 38.2 %all-to-all-start.5 = ((bf16[4,288,640]{2,1,0:T(8,128)(2,1)}), bf16[4,288,640]{2,1,0:T(8,128)(2,1)S(1)}, u32[]{:S(2)}, u32[]{:S(2)}) async-start(bf16[4,288,640]{2,1,0:T(8,128)(2,1)} %pad_maximum_fusion.7), calls=%async_computation.5 | async-start | bytes 2949120 | tf_op jit(solution)/shard_map/all_to_all | solution.py:104
  212.4 26.0 %collective-permute-start.19 = (bf16[4,288,512]{2,1,0:T(8,128)(2,1)}, bf16[4,288,512]{2,1,0:T(8,128)(2,1)S(1)}, u32[]{:S(2)}, u32[]{:S(2)}) collective-permute-start(bf16[4,288,512]{2,1,0:T(8,128)(2,1)} %all-to-all-done.4.mine_ref), channel_id=1, source_target_pairs={{0,4},{4,0},{8,12},{12,8},{16,20},{20,16},{24,28},{28,24},{1,5},{5... | collective-permute-start | bytes 3538952 | tf_op jit(solution)/shard_map/ppermute | solution.py:92
  213.0 25.4 %collective-permute-start.20 = (bf16[4,288,512]{2,1,0:T(8,128)(2,1)}, bf16[4,288,512]{2,1,0:T(8,128)(2,1)S(1)}, u32[]{:S(2)}, u32[]{:S(2)}) collective-permute-start(bf16[4,288,512]{2,1,0:T(8,128)(2,1)} %all-to-all-done.4.mine_ref), channel_id=1, source_target_pairs={{0,1},{1,0},{2,3},{3,2},{4,5},{5,4},{6,7},{7,6},{8,9},{9,8},{10,11... | collective-permute-start | bytes 3538952 | tf_op jit(solution)/shard_map/ppermute | solution.py:92
  213.0 27.5 %collective-permute-start.21 = (bf16[4,288,512]{2,1,0:T(8,128)(2,1)}, bf16[4,288,512]{2,1,0:T(8,128)(2,1)S(1)}, u32[]{:S(2)}, u32[]{:S(2)}) collective-permute-start(bf16[4,288,512]{2,1,0:T(8,128)(2,1)} %collective-permute-done.15.cross_ref), channel_id=1, source_target_pairs={{0,1},{1,0},{2,3},{3,2},{4,5},{5,4},{6,7},{7,6},{8,9},{9,8},{10,11... | collective-permute-start | bytes 3538952 | tf_op jit(solution)/shard_map/ppermute | solution.py:92
  247.9 17.8 %collective-permute-start.25 = (bf16[160,2304]{1,0:T(8,128)(2,1)}, bf16[160,2304]{1,0:T(8,128)(2,1)}, u32[]{:S(2)}, u32[]{:S(2)}) collective-permute-start(bf16[160,2304]{1,0:T(8,128)(2,1)} %slice.935), channel_id=1, source_target_pairs={{0,2},{1,3},{2,0},{3,1},{4,6},{5,7},{6,4},{7,5},{8,10},{9,11},{10,... | collective-permute-start | bytes 2211848 | tf_op jit(solution)/shard_map/ppermute | solution.py:92
  249.7 41.3 %all-to-all-start.6 = ((bf16[4,288,640]{2,1,0:T(8,128)(2,1)}), bf16[4,288,640]{2,1,0:T(8,128)(2,1)S(1)}, u32[]{:S(2)}, u32[]{:S(2)}) async-start(bf16[4,288,640]{2,1,0:T(8,128)(2,1)} %pad_maximum_fusion.8), calls=%async_computation.6 | async-start | bytes 2949120 | tf_op jit(solution)/shard_map/all_to_all | solution.py:104
  255.8 33.0 %collective-permute-start.22 = (bf16[4,288,640]{2,1,0:T(8,128)(2,1)S(1)}, bf16[4,288,640]{2,1,0:T(8,128)(2,1)S(1)}, u32[]{:S(2)}, u32[]{:S(2)}) collective-permute-start(bf16[4,288,640]{2,1,0:T(8,128)(2,1)S(1)} %all-to-all-done.5.mine_ref), channel_id=1, source_target_pairs={{0,4},{4,0},{8,12},{12,8},{16,20},{20,16},{24,28},{28,24},{1,5},{5... | collective-permute-start | bytes 4423688 | tf_op jit(solution)/shard_map/ppermute | solution.py:92
  256.3 33.5 %collective-permute-start.23 = (bf16[4,288,640]{2,1,0:T(8,128)(2,1)S(1)}, bf16[4,288,640]{2,1,0:T(8,128)(2,1)S(1)}, u32[]{:S(2)}, u32[]{:S(2)}) collective-permute-start(bf16[4,288,640]{2,1,0:T(8,128)(2,1)S(1)} %all-to-all-done.5.mine_ref), channel_id=1, source_target_pairs={{0,1},{1,0},{2,3},{3,2},{4,5},{5,4},{6,7},{7,6},{8,9},{9,8},{10,11... | collective-permute-start | bytes 4423688 | tf_op jit(solution)/shard_map/ppermute | solution.py:92
  256.8 12.6 %collective-permute-start.24 = (bf16[4,288,512]{2,1,0:T(8,128)(2,1)S(1)}, bf16[4,288,512]{2,1,0:T(8,128)(2,1)S(1)}, u32[]{:S(2)}, u32[]{:S(2)}) collective-permute-start(bf16[4,288,512]{2,1,0:T(8,128)(2,1)S(1)} %copy-done.50), channel_id=1, source_target_pairs={{0,1},{1,0},{2,3},{3,2},{4,5},{5,4},{6,7},{7,6},{8,9},{9,8},{10,11... | collective-permute-start | bytes 3538952 | tf_op jit(solution)/shard_map/ppermute | solution.py:92
  294.2 39.8 %all-to-all-start.7 = ((bf16[4,288,640]{2,1,0:T(8,128)(2,1)}), bf16[4,288,640]{2,1,0:T(8,128)(2,1)}, u32[]{:S(2)}, u32[]{:S(2)}) async-start(bf16[4,288,640]{2,1,0:T(8,128)(2,1)} %pad_maximum_fusion.9), calls=%async_computation.7 | async-start | bytes 2949120 | tf_op jit(solution)/shard_map/all_to_all | solution.py:104
  298.9 31.7 %collective-permute-start.26 = (bf16[4,288,640]{2,1,0:T(8,128)(2,1)S(1)}, bf16[4,288,640]{2,1,0:T(8,128)(2,1)S(1)}, u32[]{:S(2)}, u32[]{:S(2)}) collective-permute-start(bf16[4,288,640]{2,1,0:T(8,128)(2,1)S(1)} %all-to-all-done.6.mine_ref), channel_id=1, source_target_pairs={{0,4},{4,0},{8,12},{12,8},{16,20},{20,16},{24,28},{28,24},{1,5},{5... | collective-permute-start | bytes 4423688 | tf_op jit(solution)/shard_map/ppermute | solution.py:92
  299.4 31.2 %collective-permute-start.27 = (bf16[4,288,640]{2,1,0:T(8,128)(2,1)S(1)}, bf16[4,288,640]{2,1,0:T(8,128)(2,1)S(1)}, u32[]{:S(2)}, u32[]{:S(2)}) collective-permute-start(bf16[4,288,640]{2,1,0:T(8,128)(2,1)S(1)} %all-to-all-done.6.mine_ref), channel_id=1, source_target_pairs={{0,1},{1,0},{2,3},{3,2},{4,5},{5,4},{6,7},{7,6},{8,9},{9,8},{10,11... | collective-permute-start | bytes 4423688 | tf_op jit(solution)/shard_map/ppermute | solution.py:92
  299.4 33.4 %collective-permute-start.28 = (bf16[4,288,640]{2,1,0:T(8,128)(2,1)}, bf16[4,288,640]{2,1,0:T(8,128)(2,1)S(1)}, u32[]{:S(2)}, u32[]{:S(2)}) collective-permute-start(bf16[4,288,640]{2,1,0:T(8,128)(2,1)} %copy-done.33), channel_id=1, source_target_pairs={{0,1},{1,0},{2,3},{3,2},{4,5},{5,4},{6,7},{7,6},{8,9},{9,8},{10,11... | collective-permute-start | bytes 4423688 | tf_op jit(solution)/shard_map/ppermute | solution.py:92
  300.0 18.6 %collective-permute-start.29 = (bf16[160,2304]{1,0:T(8,128)(2,1)}, bf16[160,2304]{1,0:T(8,128)(2,1)S(1)}, u32[]{:S(2)}, u32[]{:S(2)}) collective-permute-start(bf16[160,2304]{1,0:T(8,128)(2,1)} %multiply_convert_fusion), channel_id=1, source_target_pairs={{0,2},{1,3},{2,0},{3,1},{4,6},{5,7},{6,4},{7,5},{8,10},{9,11},{10,... | collective-permute-start | bytes 2211848 | tf_op jit(solution)/shard_map/ppermute | solution.py:92
  336.4 42.3 %all-to-all-start.8 = ((bf16[4,288,512]{2,1,0:T(8,128)(2,1)}), bf16[4,288,512]{2,1,0:T(8,128)(2,1)}, u32[]{:S(2)}, u32[]{:S(2)}) async-start(bf16[4,288,512]{2,1,0:T(8,128)(2,1)} %pad_maximum_fusion.15), calls=%async_computation.8 | async-start | bytes 2359296 | tf_op jit(solution)/shard_map/all_to_all | solution.py:104
  341.6 33.9 %collective-permute-start.30 = (bf16[4,288,640]{2,1,0:T(8,128)(2,1)}, bf16[4,288,640]{2,1,0:T(8,128)(2,1)}, u32[]{:S(2)}, u32[]{:S(2)}) collective-permute-start(bf16[4,288,640]{2,1,0:T(8,128)(2,1)} %all-to-all-done.7.mine_ref), channel_id=1, source_target_pairs={{0,4},{4,0},{8,12},{12,8},{16,20},{20,16},{24,28},{28,24},{1,5},{5... | collective-permute-start | bytes 4423688 | tf_op jit(solution)/shard_map/ppermute | solution.py:92
  342.2 33.3 %collective-permute-start.31 = (bf16[4,288,640]{2,1,0:T(8,128)(2,1)}, bf16[4,288,640]{2,1,0:T(8,128)(2,1)S(1)}, u32[]{:S(2)}, u32[]{:S(2)}) collective-permute-start(bf16[4,288,640]{2,1,0:T(8,128)(2,1)} %all-to-all-done.7.mine_ref), channel_id=1, source_target_pairs={{0,1},{1,0},{2,3},{3,2},{4,5},{5,4},{6,7},{7,6},{8,9},{9,8},{10,11... | collective-permute-start | bytes 4423688 | tf_op jit(solution)/shard_map/ppermute | solution.py:92
  342.3 35.2 %collective-permute-start.32 = (bf16[4,288,640]{2,1,0:T(8,128)(2,1)}, bf16[4,288,640]{2,1,0:T(8,128)(2,1)S(1)}, u32[]{:S(2)}, u32[]{:S(2)}) collective-permute-start(bf16[4,288,640]{2,1,0:T(8,128)(2,1)} %copy-done.37), channel_id=1, source_target_pairs={{0,1},{1,0},{2,3},{3,2},{4,5},{5,4},{6,7},{7,6},{8,9},{9,8},{10,11... | collective-permute-start | bytes 4423688 | tf_op jit(solution)/shard_map/ppermute | solution.py:92
  342.8 32.8 %collective-permute-start.33 = (bf16[160,2304]{1,0:T(8,128)(2,1)}, bf16[160,2304]{1,0:T(8,128)(2,1)S(1)}, u32[]{:S(2)}, u32[]{:S(2)}) collective-permute-start(bf16[160,2304]{1,0:T(8,128)(2,1)} %multiply_convert_fusion), channel_id=1, source_target_pairs={{0,8},{4,12},{8,0},{12,4},{16,24},{20,28},{24,16},{28,20},{1,9},{5... | collective-permute-start | bytes 2211848 | tf_op jit(solution)/shard_map/ppermute | solution.py:92
  378.7 16.7 %collective-permute-start.37 = (bf16[160,2304]{1,0:T(8,128)(2,1)}, bf16[160,2304]{1,0:T(8,128)(2,1)S(1)}, u32[]{:S(2)}, u32[]{:S(2)}) collective-permute-start(bf16[160,2304]{1,0:T(8,128)(2,1)} %copy-done.111), channel_id=1, source_target_pairs={{0,2},{1,3},{2,0},{3,1},{4,6},{5,7},{6,4},{7,5},{8,10},{9,11},{10,... | collective-permute-start | bytes 2211848 | tf_op jit(solution)/shard_map/ppermute | solution.py:92
  381.3 42.3 %collective-permute-start.36 = (bf16[4,288,640]{2,1,0:T(8,128)(2,1)}, bf16[4,288,640]{2,1,0:T(8,128)(2,1)}, u32[]{:S(2)}, u32[]{:S(2)}) collective-permute-start(bf16[4,288,640]{2,1,0:T(8,128)(2,1)} %collective-permute-done.30.cross_ref), channel_id=1, source_target_pairs={{0,1},{1,0},{2,3},{3,2},{4,5},{5,4},{6,7},{7,6},{8,9},{9,8},{10,11... | collective-permute-start | bytes 4423688 | tf_op jit(solution)/shard_map/ppermute | solution.py:92
  382.6 41.0 %collective-permute-start.34 = (bf16[4,288,512]{2,1,0:T(8,128)(2,1)}, bf16[4,288,512]{2,1,0:T(8,128)(2,1)}, u32[]{:S(2)}, u32[]{:S(2)}) collective-permute-start(bf16[4,288,512]{2,1,0:T(8,128)(2,1)} %all-to-all-done.8.mine_ref), channel_id=1, source_target_pairs={{0,4},{4,0},{8,12},{12,8},{16,20},{20,16},{24,28},{28,24},{1,5},{5... | collective-permute-start | bytes 3538952 | tf_op jit(solution)/shard_map/ppermute | solution.py:92
  383.2 40.4 %collective-permute-start.35 = (bf16[4,288,512]{2,1,0:T(8,128)(2,1)}, bf16[4,288,512]{2,1,0:T(8,128)(2,1)}, u32[]{:S(2)}, u32[]{:S(2)}) collective-permute-start(bf16[4,288,512]{2,1,0:T(8,128)(2,1)} %all-to-all-done.8.mine_ref), channel_id=1, source_target_pairs={{0,1},{1,0},{2,3},{3,2},{4,5},{5,4},{6,7},{7,6},{8,9},{9,8},{10,11... | collective-permute-start | bytes 3538952 | tf_op jit(solution)/shard_map/ppermute | solution.py:92
  423.6 15.6 %collective-permute-start.38 = (bf16[4,288,512]{2,1,0:T(8,128)(2,1)}, bf16[4,288,512]{2,1,0:T(8,128)(2,1)S(1)}, u32[]{:S(2)}, u32[]{:S(2)}) collective-permute-start(bf16[4,288,512]{2,1,0:T(8,128)(2,1)} %collective-permute-done.34.cross_ref), channel_id=1, source_target_pairs={{0,1},{1,0},{2,3},{3,2},{4,5},{5,4},{6,7},{7,6},{8,9},{9,8},{10,11... | collective-permute-start | bytes 3538952 | tf_op jit(solution)/shard_map/ppermute | solution.py:92
  450.4 17.6 %collective-permute-start.41 = (bf16[160,2304]{1,0:T(8,128)(2,1)S(1)}, bf16[160,2304]{1,0:T(8,128)(2,1)S(1)}, u32[]{:S(2)}, u32[]{:S(2)}) collective-permute-start(bf16[160,2304]{1,0:T(8,128)(2,1)S(1)} %pad_maximum_fusion.23), channel_id=1, source_target_pairs={{0,8},{4,12},{8,0},{12,4},{16,24},{20,28},{24,16},{28,20},{1,9},{5... | collective-permute-start | bytes 2211848 | tf_op jit(solution)/shard_map/ppermute | solution.py:92
  450.5 17.6 %collective-permute-start.39 = (bf16[160,2304]{1,0:T(8,128)(2,1)S(1)}, bf16[160,2304]{1,0:T(8,128)(2,1)S(1)}, u32[]{:S(2)}, u32[]{:S(2)}) collective-permute-start(bf16[160,2304]{1,0:T(8,128)(2,1)S(1)} %pad_maximum_fusion.22), channel_id=1, source_target_pairs={{0,2},{1,3},{2,0},{3,1},{4,6},{5,7},{6,4},{7,5},{8,10},{9,11},{10,... | collective-permute-start | bytes 2211848 | tf_op jit(solution)/shard_map/ppermute | solution.py:92
  480.6 15.5 %collective-permute-start.43 = (bf16[160,2304]{1,0:T(8,128)(2,1)}, bf16[160,2304]{1,0:T(8,128)(2,1)}, u32[]{:S(2)}, u32[]{:S(2)}) collective-permute-start(bf16[160,2304]{1,0:T(8,128)(2,1)} %get-tuple-element.346), channel_id=1, source_target_pairs={{0,2},{1,3},{2,0},{3,1},{4,6},{5,7},{6,4},{7,5},{8,10},{9,11},{10,... | collective-permute-start | bytes 2211848 | tf_op jit(solution)/shard_map/ppermute | solution.py:92
  482.2 16.8 %collective-permute-start.44 = (bf16[160,2304]{1,0:T(8,128)(2,1)}, bf16[160,2304]{1,0:T(8,128)(2,1)}, u32[]{:S(2)}, u32[]{:S(2)}) collective-permute-start(bf16[160,2304]{1,0:T(8,128)(2,1)} %get-tuple-element.346), channel_id=1, source_target_pairs={{0,8},{4,12},{8,0},{12,4},{16,24},{20,28},{24,16},{28,20},{1,9},{5... | collective-permute-start | bytes 2211848 | tf_op jit(solution)/shard_map/ppermute | solution.py:92
  570.6 13.0 %collective-permute-start.65 = (bf16[3,16,2304]{2,1,0:T(8,128)(2,1)S(1)}, bf16[3,16,2304]{2,1,0:T(8,128)(2,1)S(1)}, u32[]{:S(2)}, u32[]{:S(2)}) collective-permute-start(bf16[3,16,2304]{2,1,0:T(8,128)(2,1)S(1)} %fusion.56), channel_id=1, source_target_pairs={{0,8},{4,12},{8,0},{12,4},{16,24},{20,28},{24,16},{28,20},{1,9},{5... | collective-permute-start | bytes 663560 | tf_op jit(solution)/shard_map/ppermute | solution.py:92
  571.8 28.2 %collective-permute-start.47 = (bf16[160,2304]{1,0:T(8,128)(2,1)S(1)}, bf16[160,2304]{1,0:T(8,128)(2,1)S(1)}, u32[]{:S(2)}, u32[]{:S(2)}) collective-permute-start(bf16[160,2304]{1,0:T(8,128)(2,1)S(1)} %pad_maximum_fusion.24), channel_id=1, source_target_pairs={{0,2},{1,3},{2,0},{3,1},{4,6},{5,7},{6,4},{7,5},{8,10},{9,11},{10,... | collective-permute-start | bytes 2211848 | tf_op jit(solution)/shard_map/ppermute | solution.py:92
  572.8 29.3 %collective-permute-start.49 = (bf16[160,2304]{1,0:T(8,128)(2,1)S(1)}, bf16[160,2304]{1,0:T(8,128)(2,1)S(1)}, u32[]{:S(2)}, u32[]{:S(2)}) collective-permute-start(bf16[160,2304]{1,0:T(8,128)(2,1)S(1)} %pad_maximum_fusion.25), channel_id=1, source_target_pairs={{0,8},{4,12},{8,0},{12,4},{16,24},{20,28},{24,16},{28,20},{1,9},{5... | collective-permute-start | bytes 2211848 | tf_op jit(solution)/shard_map/ppermute | solution.py:92
  573.9 23.2 %collective-permute-start.74 = (bf16[1,96,1152]{2,1,0:T(8,128)(2,1)S(1)}, bf16[1,96,1152]{2,1,0:T(8,128)(2,1)S(1)}, u32[]{:S(2)}, u32[]{:S(2)}) collective-permute-start(bf16[1,96,1152]{2,1,0:T(8,128)(2,1)S(1)} %bitcast.304), channel_id=1, source_target_pairs={{0,16},{4,20},{8,24},{12,28},{16,0},{20,4},{24,8},{28,12},{1,17},{... | collective-permute-start | bytes 663560 | tf_op jit(solution)/shard_map/ppermute | solution.py:92
  597.2 13.9 %collective-permute-start.75 = (bf16[2,96,1152]{2,1,0:T(8,128)(2,1)S(1)}, bf16[2,96,1152]{2,1,0:T(8,128)(2,1)S(1)}, u32[]{:S(2)}, u32[]{:S(2)}) collective-permute-start(bf16[2,96,1152]{2,1,0:T(8,128)(2,1)S(1)} %pad_maximum_fusion.31), channel_id=1, source_target_pairs={{0,8},{4,12},{8,0},{12,4},{16,24},{20,28},{24,16},{28,20},{1,9},{5... | collective-permute-start | bytes 1327112 | tf_op jit(solution)/shard_map/ppermute | solution.py:92
  600.2 17.7 %collective-permute-start.48 = (bf16[80,2304]{1,0:T(8,128)(2,1)S(1)}, bf16[80,2304]{1,0:T(8,128)(2,1)S(1)}, u32[]{:S(2)}, u32[]{:S(2)}) collective-permute-start(bf16[80,2304]{1,0:T(8,128)(2,1)S(1)} %fusion.30), channel_id=1, source_target_pairs={{0,8},{4,12},{8,0},{12,4},{16,24},{20,28},{24,16},{28,20},{1,9},{5... | collective-permute-start | bytes 1105928 | tf_op jit(solution)/shard_map/ppermute | solution.py:92
  611.2 22.9 %collective-permute-start.76 = (bf16[4,96,1152]{2,1,0:T(8,128)(2,1)S(1)}, bf16[4,96,1152]{2,1,0:T(8,128)(2,1)S(1)}, u32[]{:S(2)}, u32[]{:S(2)}) collective-permute-start(bf16[4,96,1152]{2,1,0:T(8,128)(2,1)S(1)} %pad_maximum_fusion.19), channel_id=1, source_target_pairs={{0,4},{4,0},{8,12},{12,8},{16,20},{20,16},{24,28},{28,24},{1,5},{5... | collective-permute-start | bytes 2654216 | tf_op jit(solution)/shard_map/ppermute | solution.py:92
  632.9 24.4 %collective-permute-start.51 = (bf16[160,2304]{1,0:T(8,128)(2,1)}, bf16[160,2304]{1,0:T(8,128)(2,1)}, u32[]{:S(2)}, u32[]{:S(2)}) collective-permute-start(bf16[160,2304]{1,0:T(8,128)(2,1)} %subtract_convert_fusion), channel_id=1, source_target_pairs={{0,2},{1,3},{2,0},{3,1},{4,6},{5,7},{6,4},{7,5},{8,10},{9,11},{10,... | collective-permute-start | bytes 2211848 | tf_op jit(solution)/shard_map/ppermute | solution.py:92
  681.1 14.3 %collective-permute-start.52 = (bf16[320,1024]{1,0:T(8,128)(2,1)S(1)}, bf16[320,1024]{1,0:T(8,128)(2,1)S(1)}, u32[]{:S(2)}, u32[]{:S(2)}) collective-permute-start(bf16[320,1024]{1,0:T(8,128)(2,1)S(1)} %pad_maximum_fusion.27), channel_id=1, source_target_pairs={{0,1},{1,0},{2,3},{3,2},{4,5},{5,4},{6,7},{7,6},{8,9},{9,8},{10,11... | collective-permute-start | bytes 1966088 | tf_op jit(solution)/shard_map/ppermute | solution.py:92
  702.9 50.3 %collective-permute-start.53 = (bf16[160,2304]{1,0:T(8,128)(2,1)S(1)}, bf16[160,2304]{1,0:T(8,128)(2,1)S(1)}, u32[]{:S(2)}, u32[]{:S(2)}) collective-permute-start(bf16[160,2304]{1,0:T(8,128)(2,1)S(1)} %slice.934), channel_id=1, source_target_pairs={{0,2},{1,3},{2,0},{3,1},{4,6},{5,7},{6,4},{7,5},{8,10},{9,11},{10,... | collective-permute-start | bytes 2211848 | tf_op jit(solution)/shard_map/ppermute | solution.py:92
  705.2 47.7 %collective-permute-start.71 = (bf16[1,8,16,2304]{3,1,2,0:T(8,128)(2,1)S(1)}, bf16[1,8,16,2304]{3,1,2,0:T(8,128)(2,1)S(1)}, u32[]{:S(2)}, u32[]{:S(2)}) collective-permute-start(bf16[1,8,16,2304]{3,1,2,0:T(8,128)(2,1)S(1)} %fusion.1), channel_id=1, source_target_pairs={{0,2},{1,3},{2,0},{3,1},{4,6},{5,7},{6,4},{7,5},{8,10},{9,11},{10,... | collective-permute-start | bytes 1769480 | tf_op jit(solution)/shard_map/ppermute | solution.py:92
  706.6 29.4 %collective-permute-start.55 = (bf16[16,2304]{1,0:T(8,128)(2,1)S(1)}, bf16[16,2304]{1,0:T(8,128)(2,1)S(1)}, u32[]{:S(2)}, u32[]{:S(2)}) collective-permute-start(bf16[16,2304]{1,0:T(8,128)(2,1)S(1)} %fusion.70), channel_id=1, source_target_pairs={{0,2},{1,3},{2,0},{3,1},{4,6},{5,7},{6,4},{7,5},{8,10},{9,11},{10,... | collective-permute-start | bytes 221192 | tf_op jit(solution)/shard_map/ppermute | solution.py:92
  709.1 27.6 %collective-permute-start.63 = (bf16[2,16,1536]{2,1,0:T(8,128)(2,1)S(1)}, bf16[2,16,1536]{2,1,0:T(8,128)(2,1)S(1)}, u32[]{:S(2)}, u32[]{:S(2)}) collective-permute-start(bf16[2,16,1536]{2,1,0:T(8,128)(2,1)S(1)} %pad_maximum_fusion.45), channel_id=1, source_target_pairs={{0,8},{4,12},{8,0},{12,4},{16,24},{20,28},{24,16},{28,20},{1,9},{5... | collective-permute-start | bytes 294920 | tf_op jit(solution)/shard_map/ppermute | solution.py:92
  753.1 21.2 %collective-permute-start.72 = (bf16[2,8,16,2304]{3,1,2,0:T(8,128)(2,1)S(1)}, bf16[2,8,16,2304]{3,1,2,0:T(8,128)(2,1)S(1)}, u32[]{:S(2)}, u32[]{:S(2)}) collective-permute-start(bf16[2,8,16,2304]{3,1,2,0:T(8,128)(2,1)S(1)} %get-tuple-element.393), channel_id=1, source_target_pairs={{0,1},{1,0},{2,3},{3,2},{4,5},{5,4},{6,7},{7,6},{8,9},{9,8},{10,11... | collective-permute-start | bytes 3538952 | tf_op jit(solution)/shard_map/ppermute | solution.py:92
  760.6 13.5 %collective-permute-start.59 = (bf16[1,8,16,2304]{3,1,2,0:T(8,128)(2,1)S(1)}, bf16[1,8,16,2304]{3,1,2,0:T(8,128)(2,1)S(1)}, u32[]{:S(2)}, u32[]{:S(2)}) collective-permute-start(bf16[1,8,16,2304]{3,1,2,0:T(8,128)(2,1)S(1)} %fusion), channel_id=1, source_target_pairs={{0,2},{1,3},{2,0},{3,1},{4,6},{5,7},{6,4},{7,5},{8,10},{9,11},{10,... | collective-permute-start | bytes 1769480 | tf_op jit(solution)/shard_map/ppermute | solution.py:92
  (190 other events, 1477.8 us)

commit v3 on v2

--- a/solution.py
+++ b/solution.py
@@ -97,35 +97,45 @@
     return jax.tree.unflatten(tree, lax.optimization_barrier(flat))
 
 
-def along_z(blocks, columns_z):
-    kinds = blocks.shape[0]
+def along_z(sent, columns_z):
     lines = [[2 * z + x for z in range(columns_z)] for x in range(2)]
-    sent = jnp.concatenate([blocks] * (columns_z // kinds))
     return lax.all_to_all(sent, "dp", 0, 0, axis_index_groups=lines)
 
 
-def assemble(parts, place):
-    columns_z, rows, columns = parts[0].shape
-
-    def kernel(place_ref, mine_ref, cross_ref, core_ref, core_cross_ref, out_ref):
+def assemble(pieces, place):
+    columns_z, _, columns = pieces[0][0].shape
+    heights = [parts[0].shape[1] for parts in pieces]
+    rows = sum(heights)
+
+    def kernel(place_ref, *refs):
+        out_ref = refs[-1]
         my_x = place_ref[0]
-        out_ref[my_x, :, :columns] = mine_ref[0]
-        out_ref[my_x, :, columns:] = core_ref[0]
-        out_ref[1 - my_x, :, :columns] = cross_ref[0]
-        out_ref[1 - my_x, :, columns:] = core_cross_ref[0]
+        for i, height in enumerate(heights):
+            mine_ref, cross_ref, core_ref, core_cross_ref = refs[4 * i : 4 * i + 4]
+            here = pl.ds(sum(heights[:i]), height)
+            out_ref[my_x, here, :columns] = mine_ref[0]
+            out_ref[my_x, here, columns:] = core_ref[0]
+            out_ref[1 - my_x, here, :columns] = cross_ref[0]
+            out_ref[1 - my_x, here, columns:] = core_cross_ref[0]
 
     out = pl.pallas_call(
         kernel,
-        out_shape=jax.ShapeDtypeStruct((2 * columns_z, rows, 2 * columns), parts[0].dtype),
+        out_shape=jax.ShapeDtypeStruct((2 * columns_z, rows, 2 * columns), jnp.bfloat16),
         grid_spec=pltpu.PrefetchScalarGridSpec(
             num_scalar_prefetch=1,
             grid=(columns_z,),
-            in_specs=[pl.BlockSpec((1, rows, columns), lambda k, place_ref: (k, 0, 0))] * 4,
+            in_specs=[
+                pl.BlockSpec((1, height, columns), lambda k, place_ref: (k, 0, 0))
+                for height in heights
+                for _ in range(4)
+            ],
             out_specs=pl.BlockSpec((2, rows, 2 * columns), lambda k, place_ref: (k, 0, 0)),
         ),
         compiler_params=pltpu.CompilerParams(vmem_limit_bytes=32 << 20),
-        cost_estimate=TINY,
-    )(place, *parts)
+        cost_estimate=pl.CostEstimate(
+            flops=0, transcendentals=0, bytes_accessed=16 * columns_z * rows * columns
+        ),
+    )(place, *[part for parts in pieces for part in parts])
     return out.reshape(2 * columns_z * rows, 2 * columns)
 
 
@@ -317,110 +327,198 @@
     count, depth = rows.shape
     units, tile = w_gate.shape[1], 256
     half = inner.shape[1] // 2
-
-    def kernel(rows_ref, gate_w, up_w, inner_ref, gate_e, up_e, gate_ref, up_ref, hidden_ref):
-        inner_rows = inner_ref[...]
-        gate = fdot(rows_ref[...], gate_w[...]) + fdot(inner_rows[:, :half], gate_e[...])
-        up = fdot(rows_ref[...], up_w[...]) + fdot(inner_rows[:, half:], up_e[...])
-        bend = jnp.tanh(GELU_A * (gate + GELU_B * (gate * gate * gate)))
-        gate_ref[...] = gate
-        up_ref[...] = up
-        hidden_ref[...] = low(0.5 * gate * (1.0 + bend) * up)
-
-    whole = lambda array: pl.BlockSpec(array.shape, lambda j: (0, 0))
-    column = lambda array: pl.BlockSpec((array.shape[0], tile), lambda j: (0, j))
-    result = lambda dtype: jax.ShapeDtypeStruct((count, units), dtype)
-    return pl.pallas_call(
-        kernel,
-        out_shape=[result(jnp.float32), result(jnp.float32), result(jnp.bfloat16)],
-        grid=(units // tile,),
-        in_specs=[whole(rows), column(w_gate), column(w_up), whole(inner), column(e_gate),
-                  column(e_up)],
-        out_specs=[pl.BlockSpec((count, tile), lambda j: (0, j))] * 3,
-        compiler_params=pltpu.CompilerParams(vmem_limit_bytes=48 << 20),
-        cost_estimate=TINY,
-    )(rows, w_gate, w_up, inner, e_gate, e_up)
-
-
-def feed_forward_back(grad_rows, grad_inner, inner_t, grad_inner_t, s_gate_up, keep, chunks):
-    count, depth = grad_rows.shape
-    tile = 256
-    tiles = [chunk[0].shape[1] // tile for chunk in chunks]
-    firsts = [sum(tiles[:i]) for i in range(len(tiles))]
-    total = sum(tiles)
-    twice = grad_inner.shape[1]
-    each = len(chunks[0])
-
-    def kernel(grad_ref, inner_grad_ref, inner_t_ref, inner_grad_t_ref, s_ref, keep_ref, *refs):
-        ins, (rows_ref, inner_ref, units_ref, total_ref, sums_ref) = refs[:-5], refs[-5:]
-        step = pl.program_id(0)
-
-        @pl.when(step == 0)
-        def _():
-            total_ref[...] = jnp.zeros_like(total_ref)
-            sums_ref[...] = jnp.zeros_like(sums_ref)
-
-        def one(down, gate_w, up_w, gate_in, up_in, hidden, s_down, e_gate, e_up):
-            grad = fdot(grad_ref[...], down[...]) + fdot(inner_grad_ref[...], s_down[...])
-            gate, up = gate_in[...], up_in[...]
+    step = count // 4
+
+    def kernel(rows_ref, gate_w, up_w, inner_ref, gate_e, up_e, hidden_ref, gate_ref, up_ref):
+        for i in range(4):
+            here = slice(i * step, (i + 1) * step)
+            inner_rows = inner_ref[here]
+            gate = fdot(rows_ref[here], gate_w[...]) + fdot(inner_rows[:, :half], gate_e[...])
+            up = fdot(rows_ref[here], up_w[...]) + fdot(inner_rows[:, half:], up_e[...])
             square = gate * gate
             bend = jnp.tanh(GELU_A * gate * (1.0 + GELU_B * square))
             half_up = 0.5 * (1.0 + bend)
             slope = half_up + 0.5 * gate * (1.0 - bend * bend) * (
                 GELU_A * (1.0 + 3.0 * GELU_B * square)
             )
-            grad_gate = low(grad * up * slope)
-            grad_up = low(grad * (gate * half_up))
-            total_ref[...] += fdot(grad_gate, gate_w[...], ((1,), (1,))) + fdot(
-                grad_up, up_w[...], ((1,), (1,))
+            bent = gate * half_up
+            hidden_ref[here] = low(bent * up)
+            gate_ref[here] = low(up * slope)
+            up_ref[here] = low(bent)
+
+    whole = lambda array: pl.BlockSpec(array.shape, lambda j: (0, 0))
+    column = lambda array: pl.BlockSpec((array.shape[0], tile), lambda j: (0, j))
+    return pl.pallas_call(
+        kernel,
+        out_shape=[jax.ShapeDtypeStruct((count, units), jnp.bfloat16)] * 3,
+        grid=(units // tile,),
+        in_specs=[whole(rows), column(w_gate), column(w_up), whole(inner), column(e_gate),
+                  column(e_up)],
+        out_specs=[pl.BlockSpec((count, tile), lambda j: (0, j))] * 3,
+        compiler_params=pltpu.CompilerParams(vmem_limit_bytes=63 << 20),
+        cost_estimate=TINY,
+    )(rows, w_gate, w_up, inner, e_gate, e_up)
+
+
+def square_shapes(count, depth):
+    rows = count // 4
+    half = rows // 2
+    return [
+        jax.ShapeDtypeStruct((rows, depth), jnp.float32),
+        jax.ShapeDtypeStruct((half, depth), jnp.float32),
+        jax.ShapeDtypeStruct((half, depth), jnp.float32),
+        jax.ShapeDtypeStruct((rows, depth), jnp.bfloat16),
+        jax.ShapeDtypeStruct((rows, depth), jnp.bfloat16),
+    ]
+
+
+def store_square(values, refs):
+    rows = values.shape[0] // 4
+    half = rows // 2
+    mine_ref, y_ref, z_ref, send_y_ref, send_z_ref = refs
+    mine_ref[...] = values[:rows]
+    y_ref[...] = values[rows + half : 2 * rows]
+    z_ref[...] = values[2 * rows : 2 * rows + half]
+    send_y_ref[:half] = low(values[rows : rows + half])
+    send_y_ref[half:] = low(values[3 * rows : 3 * rows + half])
+    send_z_ref[:half] = low(values[2 * rows + half : 3 * rows])
+    send_z_ref[half:] = low(values[3 * rows + half :])
+
+
+def down_last(first, hidden, w_down_t):
+    count, depth = first.shape
+    tile = depth // 3
+
+    def kernel(first_ref, hidden_ref, weight_ref, *out_refs):
+        store_square(
+            first_ref[...] + fdot(hidden_ref[...], weight_ref[...], ((1,), (1,))), out_refs
+        )
+
+    shapes = square_shapes(count, depth)
+    return pl.pallas_call(
+        kernel,
+        out_shape=shapes,
+        grid=(depth // tile,),
+        in_specs=[
+            pl.BlockSpec((count, tile), lambda j: (0, j)),
+            pl.BlockSpec(hidden.shape, lambda j: (0, 0)),
+            pl.BlockSpec((tile, w_down_t.shape[1]), lambda j: (j, 0)),
+        ],
+        out_specs=[pl.BlockSpec((shape.shape[0], tile), lambda j: (0, j)) for shape in shapes],
+        compiler_params=pltpu.CompilerParams(vmem_limit_bytes=48 << 20),
+        cost_estimate=TINY,
+    )(first, hidden, w_down_t)
+
+
+def feed_forward_back(grad_rows, e_down, s_gate_up, keep, chunks):
+    count, depth = grad_rows.shape
+    tiles = [chunk[0].shape[1] // 2 for chunk in chunks]
+    columns = depth // 3
+    steps = []
+    for i, chunk in enumerate(chunks):
+        steps += [(i, j) for j in range(chunk[0].shape[1] // tiles[i])]
+    total = len(steps)
+    firsts = [steps.index((i, 0)) for i in range(len(chunks))]
+    counts = [chunk[0].shape[1] // tiles[i] for i, chunk in enumerate(chunks)]
+    starts = [sum(chunk[0].shape[1] for chunk in chunks[:i]) for i in range(len(chunks))]
+    width = sum(chunk[0].shape[1] for chunk in chunks)
+    twice = e_down.shape[0]
+    each = len(chunks[0])
+    parts = square_shapes(count, depth)
+
+    def kernel(grad_ref, e_down_ref, s_ref, keep_ref, *refs):
+        ins = refs[: each * len(chunks)]
+        out_refs = refs[each * len(chunks) :]
+        rows_refs = out_refs[: len(parts)]
+        inner_grad_ref, inner_ref, gates_ref, ups_ref, sums_ref = out_refs[len(parts) :]
+        step = pl.program_id(0)
+
+        @pl.when(step == 0)
+        def _():
+            inner_grad = fdot(grad_ref[...], e_down_ref[...], ((1,), (1,)))
+            inner_grad_ref[...] = low(inner_grad * keep_ref[:, :twice])
+
+        def one(place, begin, down, gate_in, up_in, s_down, e_gate, e_up, gate_w, up_w):
+            grad = fdot(grad_ref[...], down[...]) + fdot(inner_grad_ref[...], s_down[...])
+            grad_gate = low(grad * gate_in[...].astype(jnp.float32))
+            grad_up = low(grad * up_in[...].astype(jnp.float32))
+            gates_ref[:, place] = grad_gate
+            ups_ref[:, place] = grad_up
+            first = fdot(grad_gate, e_gate[...], ((1,), (1,)))
+            second = fdot(grad_up, e_up[...], ((1,), (1,)))
+            if begin:
+                sums_ref[:, :twice] = first
+                sums_ref[:, twice:] = second
+            else:
+                sums_ref[:, :twice] += first
+                sums_ref[:, twice:] += second
+
+        for k, (i, j) in enumerate(steps):
+            place = slice(starts[i] + j * tiles[i], starts[i] + (j + 1) * tiles[i])
+            pl.when(step == k)(
+                functools.partial(one, place, k == 0, *ins[i * each : (i + 1) * each])
             )
-            sums_ref[:, :twice] += fdot(grad_gate, e_gate[...], ((1,), (1,)))
-            sums_ref[:, twice:] += fdot(grad_up, e_up[...], ((1,), (1,)))
-            units_ref[:twice] = fdot(inner_t_ref[:twice], grad_gate)
-            units_ref[twice : 2 * twice] = fdot(inner_t_ref[twice:], grad_up)
-            units_ref[2 * twice :] = fdot(inner_grad_t_ref[...], hidden[...])
-
-        for i in range(len(chunks)):
-            within = (step >= firsts[i]) & (step < firsts[i] + tiles[i])
-            pl.when(within)(functools.partial(one, *ins[i * each : (i + 1) * each]))
 
         @pl.when(step == total - 1)
         def _():
-            kept = low(sums_ref[...] * keep_ref[...])
-            inner_ref[...] = kept
-            rows_ref[...] = low(total_ref[...] + fdot(kept, s_ref[...]))
-
-    whole = lambda array: pl.BlockSpec(array.shape, lambda j: (0, 0))
+            inner_ref[...] = low(sums_ref[...] * keep_ref[...])
+
+        @pl.when(step >= total)
+        def _():
+            rows = fdot(inner_ref[...], s_ref[...])
+            for i, chunk in enumerate(chunks):
+                gate_w, up_w = ins[(i + 1) * each - 2 : (i + 1) * each]
+                place = slice(starts[i], starts[i] + chunk[0].shape[1])
+                rows += fdot(gates_ref[:, place], gate_w[...], ((1,), (1,)))
+                rows += fdot(ups_ref[:, place], up_w[...], ((1,), (1,)))
+            store_square(rows, rows_refs)
+
+    once = pl.Buffered(1)
+    whole = lambda array: pl.BlockSpec(array.shape, lambda j: (0, 0), pipeline_mode=once)
+    second = lambda j: jnp.clip(j - total, 0, depth // columns - 1)
 
     def column(i, array):
         return pl.BlockSpec(
-            (array.shape[0], tile),
-            lambda j: (0, jnp.clip(j - firsts[i], 0, tiles[i] - 1)),
+            (array.shape[0], tiles[i]),
+            lambda j: (0, jnp.clip(j - firsts[i], 0, counts[i] - 1)),
         )
 
-    fixed = [grad_rows, grad_inner, inner_t, grad_inner_t, s_gate_up, keep]
+    def specs(i, chunk):
+        return [column(i, array) for array in chunk[:-2]] + [
+            pl.BlockSpec((columns, array.shape[1]), lambda j: (second(j), 0))
+            for array in chunk[-2:]
+        ]
+
     return pl.pallas_call(
         kernel,
-        out_shape=[
-            jax.ShapeDtypeStruct((count, depth), jnp.bfloat16),
+        out_shape=parts
+        + [
+            jax.ShapeDtypeStruct((count, twice), jnp.bfloat16),
             jax.ShapeDtypeStruct((count, 2 * twice), jnp.bfloat16),
-            jax.ShapeDtypeStruct((3 * twice, total * tile), jnp.float32),
-        ],
-        grid=(total,),
-        in_specs=[whole(array) for array in fixed]
-        + [column(i, array) for i, chunk in enumerate(chunks) for array in chunk],
+            jax.ShapeDtypeStruct((count, width), jnp.bfloat16),
+            jax.ShapeDtypeStruct((count, width), jnp.bfloat16),
+        ],
+        grid=(total + depth // columns,),
+        in_specs=[
+            whole(grad_rows),
+            whole(e_down),
+            pl.BlockSpec((s_gate_up.shape[0], columns), lambda j: (0, second(j))),
+            whole(keep),
+        ]
+        + [spec for i, chunk in enumerate(chunks) for spec in specs(i, chunk)],
         out_specs=[
-            pl.BlockSpec((count, depth), lambda j: (0, 0)),
+            pl.BlockSpec((part.shape[0], columns), lambda j: (0, second(j))) for part in parts
+        ]
+        + [
+            pl.BlockSpec((count, twice), lambda j: (0, 0)),
             pl.BlockSpec((count, 2 * twice), lambda j: (0, 0)),
-            pl.BlockSpec((3 * twice, tile), lambda j: (0, j)),
-        ],
-        scratch_shapes=[
-            pltpu.VMEM((count, depth), jnp.float32),
-            pltpu.VMEM((count, 2 * twice), jnp.float32),
-        ],
-        compiler_params=pltpu.CompilerParams(vmem_limit_bytes=60 << 20),
+            pl.BlockSpec((count, width), lambda j: (0, 0), pipeline_mode=once),
+            pl.BlockSpec((count, width), lambda j: (0, 0), pipeline_mode=once),
+        ],
+        scratch_shapes=[pltpu.VMEM((count, 2 * twice), jnp.float32)],
+        compiler_params=pltpu.CompilerParams(vmem_limit_bytes=63 << 20),
         cost_estimate=TINY,
-    )(*fixed, *[array for chunk in chunks for array in chunk])
+    )(grad_rows, e_down, s_gate_up, keep, *[array for chunk in chunks for array in chunk])
 
 
 def scatter_pair(part):
@@ -437,33 +535,123 @@
     half = own.shape[0] // 2
     from_y = flip(own, "tensor", 2)
     from_z = flip(own, "dp", 2)
-    diagonal = [flip(from_y[:half], "dp", 2), flip(from_z[half:], "tensor", 2)]
+    send_z, send_y = settle(from_y[:half], from_z[half:])
+    diagonal = [flip(send_z, "dp", 2), flip(send_y, "tensor", 2)]
     return jnp.concatenate([own, from_y, from_z] + diagonal)
 
 
-def scatter_square(part):
-    rows = part.shape[0] // 4
-    half = rows // 2
-    mine, to_y, to_z, to_zy = (part[i * rows : (i + 1) * rows] for i in range(4))
-    got_y = flip(low(jnp.concatenate([to_y[:half], to_zy[:half]])), "tensor", 2)
-    got_z = flip(low(jnp.concatenate([to_z[half:], to_zy[half:]])), "dp", 2)
-    got_y, got_z = got_y.astype(jnp.float32), got_z.astype(jnp.float32)
-    last_y = flip(low(to_y[half:] + got_z[half:]), "tensor", 2).astype(jnp.float32)
-    last_z = flip(low(to_z[:half] + got_y[half:]), "dp", 2).astype(jnp.float32)
+def sum_by_adapter(hots, gathered, shared, widths):
+    count, rows, columns = gathered.shape
+    adapters = hots.shape[1]
+    cuts = [0, shared] + [shared + sum(widths[: i + 1]) for i in range(len(widths))]
+
+    def kernel(hots_ref, gathered_ref, *out_refs):
+        for i, out_ref in enumerate(out_refs):
+            here = slice(cuts[i], cuts[i + 1])
+            for adapter in range(adapters):
+                total = 0.0
+                for entry in range(count):
+                    total += hots_ref[entry, adapter] * gathered_ref[entry, :, here].astype(
+                        jnp.float32
+                    )
+                out_ref[adapter] = total.astype(out_ref.dtype)
+
+    shapes = [jax.ShapeDtypeStruct((adapters, rows, shared), jnp.bfloat16)] + [
+        jax.ShapeDtypeStruct((adapters, rows, width), jnp.float32) for width in widths
+    ]
+    return pl.pallas_call(
+        kernel,
+        out_shape=shapes,
+        in_specs=[
+            pl.BlockSpec(memory_space=pltpu.SMEM),
+            pl.BlockSpec(gathered.shape, lambda: (0, 0, 0)),
+        ],
+        out_specs=[pl.BlockSpec(shape.shape, lambda: (0, 0, 0)) for shape in shapes],
+        compiler_params=pltpu.CompilerParams(vmem_limit_bytes=40 << 20),
+        cost_estimate=TINY,
+    )(hots, gathered)
+
+
+def sum_unit_grads(hots, gathered, kinds):
+    count, rows, columns = gathered.shape
+    rank = rows // kinds
+    adapters = hots.shape[2]
+
+    def kernel(hots_ref, gathered_ref, *out_refs):
+        for side in range(2):
+            for kind in range(kinds):
+                here = slice(kind * rank, (kind + 1) * rank)
+                for adapter in range(adapters):
+                    total = 0.0
+                    for entry in range(count):
+                        total += hots_ref[side, entry, adapter] * gathered_ref[
+                            entry, here
+                        ].astype(jnp.float32)
+                    out_refs[kind][adapter, :, side * columns : (side + 1) * columns] = total
+
+    return pl.pallas_call(
+        kernel,
+        out_shape=[jax.ShapeDtypeStruct((adapters, rank, 2 * columns), jnp.float32)] * kinds,
+        in_specs=[
+            pl.BlockSpec(memory_space=pltpu.SMEM),
+            pl.BlockSpec(gathered.shape, lambda: (0, 0, 0)),
+        ],
+        out_specs=[pl.BlockSpec((adapters, rank, 2 * columns), lambda: (0, 0, 0))] * kinds,
+        compiler_params=pltpu.CompilerParams(vmem_limit_bytes=48 << 20),
+        cost_estimate=TINY,
+    )(hots, gathered)
+
+
+def join_halves(core, mine, other, kinds):
+    adapters, rank, columns = mine.shape
+    half = columns // kinds
+
+    def kernel(core_ref, mine_ref, other_ref, *out_refs):
+        swap = core_ref[0] == 1
+        for kind in range(kinds):
+            here = slice(kind * half, (kind + 1) * half)
+            first = mine_ref[:, :, here].astype(jnp.float32)
+            second = other_ref[:, :, here].astype(jnp.float32)
+            out_refs[kind][:, :, :half] = jnp.where(swap, second, first)
+            out_refs[kind][:, :, half:] = jnp.where(swap, first, second)
+
+    return pl.pallas_call(
+        kernel,
+        out_shape=[jax.ShapeDtypeStruct((adapters, rank, 2 * half), jnp.float32)] * kinds,
+        in_specs=[pl.BlockSpec(memory_space=pltpu.SMEM)]
+        + [pl.BlockSpec(mine.shape, lambda: (0, 0, 0))] * 2,
+        out_specs=[pl.BlockSpec((adapters, rank, 2 * half), lambda: (0, 0, 0))] * kinds,
+        compiler_params=pltpu.CompilerParams(vmem_limit_bytes=48 << 20),
+        cost_estimate=TINY,
+    )(core, mine, other)
+
+
+def square_first(parts):
+    mine, to_y, to_z, send_y, send_z = parts
+    return (flip(send_y, "tensor", 2), flip(send_z, "dp", 2)), (mine, to_y, to_z)
+
+
+def square_last(first, rest):
+    got_y, got_z = (got.astype(jnp.float32) for got in first)
+    mine, to_y, to_z = rest
+    half = to_y.shape[0]
+    send_y, send_z = settle(low(to_y + got_z[half:]), low(to_z + got_y[half:]))
+    last_y = flip(send_y, "tensor", 2).astype(jnp.float32)
+    last_z = flip(send_z, "dp", 2).astype(jnp.float32)
     return jnp.concatenate(
         [mine[:half] + got_y[:half] + last_z, mine[half:] + got_z[:half] + last_y]
     )
 
 
-def gather_trees(values, trees):
-    values = values[None]
-    bits = [1 << b for b in range(1, trees.bit_length() - 1)][::-1] + [1]
-    for bit in bits:
-        values = jnp.concatenate([values, flip(values, "dp", bit)])
-    index = [0]
-    for bit in bits:
-        index += [i ^ bit for i in index]
-    return values, index
+def tree_bits(trees):
+    return [1 << b for b in range(1, trees.bit_length() - 1)][::-1] + [1]
+
+
+def tree_order(trees):
+    order = [0]
+    for bit in tree_bits(trees):
+        order += [i ^ bit for i in order]
+    return order
 
 
 def on_device(
@@ -527,6 +715,9 @@
         down_halves[:, :, :first_units],
         down_halves[:, :, first_units:],
     ]
+    waiting = [
+        jnp.concatenate([blocks] * (columns_z // blocks.shape[0])) for blocks in waiting
+    ]
     count = len(waiting)
     near, cross = {}, {}
 
@@ -563,28 +754,25 @@
         return values
 
     def matrix(*keys):
-        parts = [
-            jnp.concatenate([store[key] for key in keys], axis=1) if len(keys) > 1 else store[keys[0]]
-            for store in (near, cross, near_core, cross_core)
-        ]
-        return assemble(parts, place)
+        stores = (near, cross, near_core, cross_core)
+        return assemble([[store[key] for store in stores] for key in keys], place)
 
     transfers(0)
     own_rows = layer_input.astype(jnp.float32)
     normed = low(rms_scale(own_rows, norm_gain[0]))
-    normed_all = gather_pair(normed)
     near_ids = flip(adapter_ids, "dp", 2)
     labels = jnp.arange(ADAPTERS, dtype=jnp.int32)
     order = jnp.stack([my_part, my_part ^ 2, my_part ^ 1, my_part ^ 3]).astype(jnp.int32)
     visible, cos_rows, sin_rows = tree_tables(segment_ids, parent_segments[0], order)
-    row_count = normed_all.shape[0]
+    row_count = 2 * normed.shape[0]
     visible = low(visible[:row_count])
     cos_rows, sin_rows = cos_rows[:row_count], sin_rows[:row_count]
-    normed_all, near_ids, visible, cos_rows, sin_rows = close(
-        0, normed_all, near_ids, visible, cos_rows, sin_rows
+    normed, near_ids, visible, cos_rows, sin_rows = close(
+        0, normed, near_ids, visible, cos_rows, sin_rows
     )
 
     transfers(1)
+    normed_all = gather_pair(normed)
     picked = pick_adapters(
         jnp.concatenate([adapter_ids, near_ids, (my_z % 2).astype(jnp.int32)[None]]),
         [
@@ -620,15 +808,15 @@
     s_gate_up = jnp.concatenate(picked[8:12])
     e_down = jnp.concatenate(picked[12:14])
     ffn_mine = jnp.concatenate(picked[14:20])
-    inner_qkv = low(times_rows(normed_all, s_qkv))
-    attn_mine, e_output, s_gate_up, e_down, ffn_mine, s_qkv, inner_qkv = close(
-        1, attn_mine, e_output, s_gate_up, e_down, ffn_mine, s_qkv, inner_qkv
+    normed_all, attn_mine, e_output, s_gate_up, e_down, ffn_mine, s_qkv = close(
+        1, normed_all, attn_mine, e_output, s_gate_up, e_down, ffn_mine, s_qkv
     )
 
     transfers(2)
     attn_other = on_core(attn_mine)
     ffn_other = on_core(ffn_mine)
-    attn_other, ffn_other = close(2, attn_other, ffn_other)
+    inner_qkv = low(times_rows(normed_all, s_qkv))
+    attn_other, ffn_other, inner_qkv = close(2, attn_other, ffn_other, inner_qkv)
 
     transfers(3)
     heads_here = sum(widths)
@@ -646,15 +834,18 @@
         == jnp.concatenate([column_kind, column_kind])[None, :]
     )
     e_qkv = low(jnp.where(kind_mask, jnp.tile(beside(e_mine, e_other), (3, 1)), 0.0))
-    tree_ids, tree_index = gather_trees(adapter_ids, trees)
     units_a = beside(ffn_mine[:, :first_units], ffn_other[:, :first_units])
     units_b = beside(ffn_mine[:, first_units:], ffn_other[:, first_units:])
     adapters_ab = [
         [block[i * 2 * rank : (i + 1) * 2 * rank] for i in range(3)] for block in (units_a, units_b)
     ]
-    tree_ids, e_qkv, s_output, adapters_ab = close(3, tree_ids, e_qkv, s_output, adapters_ab)
-
+    e_qkv, s_output, adapters_ab = close(3, e_qkv, s_output, adapters_ab)
+
+    bits = tree_bits(trees)
+    tree_ids = adapter_ids
     transfers(4)
+    for bit in bits[:-2]:
+        tree_ids = jnp.concatenate([tree_ids, flip(tree_ids, "dp", bit)])
     full_qkv = matrix(0, 1)
     projected = project_heads(
         normed_all, full_qkv, inner_qkv, e_qkv, cos_rows, sin_rows, queries
@@ -662,39 +853,42 @@
     received = on_core(
         beside(projected[:, heads_here + starts[1] :], projected[:, starts[1] : heads_here])
     )
-    full_qkv, projected, received = close(4, full_qkv, projected, received)
+    full_qkv, projected, received, tree_ids = close(
+        4, full_qkv, projected, received, tree_ids
+    )
 
     transfers(5)
     full_out_t = matrix(2)
+    tree_ids = jnp.concatenate([tree_ids, flip(tree_ids, "dp", bits[-2])])
     mixed_heads = attend(projected, received, visible, queries)
     inner_output = low(times_rows(mixed_heads, s_output))
     attn_part = times_rows(mixed_heads, full_out_t) + product(inner_output, e_output)
-    mixed_heads, full_out_t, inner_output, attn_part = close(
-        5, mixed_heads, full_out_t, inner_output, attn_part
+    attended = scatter_pair(attn_part)
+    mixed_heads, full_out_t, inner_output, attended, tree_ids = close(
+        5, mixed_heads, full_out_t, inner_output, attended, tree_ids
     )
 
     transfers(6)
-    attended = scatter_pair(attn_part)
     full_gate_b = matrix(3)
     residual = own_rows + rms_scale(attended, norm_gain[1])
     normed_ffn = low(rms_scale(residual, norm_gain[2]))
-    residual, attended, normed_ffn, full_gate_b = close(
-        6, residual, attended, normed_ffn, full_gate_b
+    normed_y = flip(normed_ffn, "tensor", 2)
+    half_rows = normed_ffn.shape[0] // 2
+    normed_z_first = flip(normed_ffn[:half_rows], "dp", 2)
+    residual, normed_ffn, normed_y, normed_z_first, full_gate_b = close(
+        6, residual, normed_ffn, normed_y, normed_z_first, full_gate_b
     )
 
     transfers(7)
-    normed_y = flip(normed_ffn, "tensor", 2)
+    normed_z_last = flip(normed_ffn[half_rows:], "dp", 2)
     full_up_b = matrix(4)
-    normed_y, full_up_b = close(7, normed_y, full_up_b)
+    tree_ids = jnp.concatenate([tree_ids, flip(tree_ids, "dp", bits[-1])])
+    normed_z_last, full_up_b, tree_ids = close(7, normed_z_last, full_up_b, tree_ids)
 
     transfers(8)
-    normed_z = flip(normed_ffn, "dp", 2)
+    normed_z = jnp.concatenate([normed_z_first, normed_z_last])
+    normed_zy = flip(normed_z, "tensor", 2)
     full_gate_a = matrix(5)
-    normed_z, full_gate_a = close(8, normed_z, full_gate_a)
-
-    transfers(9)
-    normed_zy = flip(normed_z, "tensor", 2)
-    full_up_a = matrix(6)
     ffn_rows = jnp.concatenate([normed_ffn, normed_y, normed_z, normed_zy])
     block_rows = residual.shape[0]
     row_block = jnp.arange(4 * block_rows, dtype=jnp.int32) // block_rows
@@ -703,67 +897,123 @@
     keep_four = (row_near == rank_near).astype(jnp.float32)
     keep_two = keep_four[:, : 2 * rank]
     inner_gate_up = low(keep_four * times_rows(ffn_rows, s_gate_up))
-    chunk_out = [
-        gate_and_up(ffn_rows, full_gate, full_up, inner_gate_up, e_gate, e_up)
-        for full_gate, full_up, (e_gate, e_up, _) in (
-            (full_gate_a, full_up_a, adapters_ab[0]),
-            (full_gate_b, full_up_b, adapters_ab[1]),
-        )
-    ]
-    chunk_out, full_gate_a, full_up_a, full_gate_b, full_up_b = close(
-        9, chunk_out, full_gate_a, full_up_a, full_gate_b, full_up_b
-    )
-
-    cross_core[8] = on_core(cross[8])
-    full_down_a = matrix(7)
-    hidden = [parts[2] for parts in chunk_out]
+    chunk_b = gate_and_up(
+        ffn_rows, full_gate_b, full_up_b, inner_gate_up, adapters_ab[1][0], adapters_ab[1][1]
+    )
+    ffn_rows, inner_gate_up, chunk_b, full_gate_a = close(
+        8, ffn_rows, inner_gate_up, chunk_b, full_gate_a
+    )
+
+    transfers(9)
+    full_up_a = matrix(6)
+    chunk_a = gate_and_up(
+        ffn_rows, full_gate_a, full_up_a, inner_gate_up, adapters_ab[0][0], adapters_ab[0][1]
+    )
+    chunk_out = [chunk_a, chunk_b]
+    hidden = [parts[0] for parts in chunk_out]
     inner_down = low(
         keep_two
         * (times_rows(hidden[0], adapters_ab[0][2]) + times_rows(hidden[1], adapters_ab[1][2]))
     )
+    full_down_a = matrix(7)
     ffn_first = times_rows(hidden[0], full_down_a) + product(inner_down, e_down)
+    chunk_out, inner_down, ffn_first = close(9, chunk_out, inner_down, ffn_first)
+    hidden = [parts[0] for parts in chunk_out]
+
+    cross_core[8] = on_core(cross[8])
     full_down_b = matrix(8)
-    ffn_part = ffn_first + times_rows(hidden[1], full_down_b)
-    ffn_out = scatter_square(ffn_part)
+    ffn_out = square_last(*square_first(down_last(ffn_first, hidden[1], full_down_b)))
     layer_output = low(residual + rms_scale(ffn_out, norm_gain[3]))
 
     grad_out = cotangent.astype(jnp.float32)
     grad_ffn = gather_square(low(rms_back(ffn_out, norm_gain[3], grad_out)))
-    grad_inner_down = low(keep_two * times_rows(grad_ffn, e_down))
-    grad_normed_part, grad_inner_gate_up, grad_units = feed_forward_back(
+    *grad_normed_parts, grad_inner_down, grad_inner_gate_up, grad_gate, grad_up = feed_forward_back(
         grad_ffn,
-        grad_inner_down,
-        inner_gate_up.T,
-        grad_inner_down.T,
+        e_down,
         s_gate_up,
         keep_four,
         [
-            (full_down, full_gate, full_up, *parts, adapters[2], adapters[0], adapters[1])
+            (full_down, *parts[1:], adapters[2], adapters[0], adapters[1], full_gate, full_up)
             for full_down, full_gate, full_up, parts, adapters in (
                 (full_down_a, full_gate_a, full_up_a, chunk_out[0], adapters_ab[0]),
                 (full_down_b, full_gate_b, full_up_b, chunk_out[1], adapters_ab[1]),
             )
         ],
     )
-    grad_normed_ffn = scatter_square(grad_normed_part)
+    def from_other_core(mine, other):
+        return low(mine + on_core(low(other)).astype(jnp.float32))
+
+    parts_first, parts_rest = square_first(grad_normed_parts)
+    grad_shrink_down = jnp.concatenate(
+        [over_rows(grad_inner_down, units_of) for units_of in hidden], axis=1
+    )
+    inner_gate, inner_up = inner_gate_up[:, : 2 * rank], inner_gate_up[:, 2 * rank :]
+    grad_units = jnp.stack(
+        [
+            grads.reshape(2, rank, 2 * units)
+            for grads in (
+                over_rows(inner_gate, grad_gate),
+                over_rows(inner_up, grad_up),
+                grad_shrink_down,
+            )
+        ],
+        axis=1,
+    ).reshape(6 * rank, 2 * units)
+    rest = units - first_units
+    cuts = [0, first_units, 2 * first_units, 2 * first_units + rest, 2 * units]
+    quarters = [grad_units[:, cuts[i] : cuts[i + 1]] for i in range(4)]
+    mine, other = beside(quarters[0], quarters[2]), beside(quarters[1], quarters[3])
+    local = from_other_core(mine, other)
+    parts_first, local, grad_inner_gate_up, grad_ffn = settle(
+        parts_first, local, grad_inner_gate_up, grad_ffn
+    )
+    local_all = jnp.stack([local, flip(local, "dp", 1)])
     grad_expand_down = over_rows(inner_down, grad_ffn)
     grad_shrink_gate_up = over_rows(grad_inner_gate_up, ffn_rows)
-
+    grad_normed_ffn = square_last(parts_first, parts_rest)
     grad_resid = grad_out + rms_back(residual, norm_gain[2], grad_normed_ffn)
-    grad_attn = gather_pair(low(rms_back(attended, norm_gain[1], grad_resid)))
-
+    grad_attn_mine = low(rms_back(attended, norm_gain[1], grad_resid))
+    shared = jnp.concatenate([grad_shrink_gate_up, grad_expand_down]).reshape(3, 2, rank, -1)
+    grad_attn_mine, grad_resid, local_all, shared = settle(
+        grad_attn_mine, grad_resid, local_all, shared
+    )
+
+    def core_half(blocks):
+        half = blocks.shape[-1] // 2
+        kept = jnp.where(my_part % 2 == 1, blocks[..., half:], blocks[..., :half])
+        return jnp.concatenate([low(block) for block in kept], axis=1)
+
+    def with_bit(values, bit):
+        return jnp.concatenate([values, flip(values, "dp", bit)])
+
+    grad_attn = gather_pair(grad_attn_mine)
+    shared_near = flip(low(shared[:, 1]), "dp", 2)
+    bits = tree_bits(trees)
+    for bit in bits[:-2]:
+        local_all = with_bit(local_all, bit)
+    grad_attn, local_all, shared, shared_near = settle(grad_attn, local_all, shared, shared_near)
+
+    local_near = flip(local_all, "dp", bits[-2])
     grad_inner_output = low(times_rows(grad_attn, e_output))
-    grad_mixed = low(
-        product(grad_attn, full_out_t) + product(grad_inner_output, s_output)
-    )
+    grad_mixed = low(product(grad_attn, full_out_t) + product(grad_inner_output, s_output))
+    grad_queries, grad_pairs = attend_back(
+        projected, received, visible, grad_mixed, cos_rows, sin_rows, queries
+    )
+    pair = 2 * HEAD_WIDTH
+    to_core = low(beside(grad_pairs[row_count:, pair:], grad_pairs[row_count:, :pair]))
+    from_core = on_core(to_core)
+    shared = shared[:, 0] + shared_near.astype(jnp.float32)
+    shared = shared + on_core(low(shared)).astype(jnp.float32)
+    shared = shared + flip(low(shared), "tensor", 2).astype(jnp.float32)
+    shared_mine = core_half(shared)
+    from_core, grad_queries, grad_pairs, shared_mine = settle(
+        from_core, grad_queries, grad_pairs, shared_mine
+    )
+
+    shared_all = with_bit(shared_mine[None], 1)
     grad_expand_output = over_rows(inner_output, grad_attn)
     grad_shrink_output = over_rows(grad_inner_output, mixed_heads)
-    grad_queries, grad_pairs = attend_back(
-        projected, received, visible, grad_mixed, cos_rows, sin_rows, queries
-    )
-    pair = 2 * HEAD_WIDTH
-    to_core = low(beside(grad_pairs[row_count:, pair:], grad_pairs[row_count:, :pair]))
-    grad_pairs = grad_pairs[:row_count] + on_core(to_core).astype(jnp.float32)
+    grad_pairs = grad_pairs[:row_count] + from_core.astype(jnp.float32)
     grad_sides = []
     for side in range(2):
         keys_values = grad_pairs[:, side * pair : (side + 1) * pair]
@@ -775,85 +1025,91 @@
     grad_qkv = jnp.concatenate(grad_sides, axis=1)
     grad_inner_qkv = low(times_rows(grad_qkv, e_qkv))
     grad_expand_qkv = over_rows(inner_qkv, grad_qkv)
-    grad_shrink_qkv = over_rows(grad_inner_qkv, normed_all)
-    grad_normed = scatter_pair(
-        times_rows(grad_qkv, full_qkv) + product(grad_inner_qkv, s_qkv)
-    )
-    input_grad = grad_resid + rms_back(own_rows, norm_gain[0], grad_normed)
-
-    tree_ids = tree_ids.reshape(trees)
-    hot_near = low(tree_ids[:, None] == labels[None, :])
-
-    def by_adapter(hot, gathered):
-        return lax.dot_general(
-            hot, gathered, (((0,), (0,)), ((), ())), preferred_element_type=jnp.float32
-        )
-
-    def from_other_core(mine, other):
-        return low(mine + on_core(low(other)).astype(jnp.float32))
-
-    rest = units - first_units
-    cuts = [0, first_units, 2 * first_units, 2 * first_units + rest, 2 * units]
-    quarters = [grad_units[:, cuts[i] : cuts[i + 1]] for i in range(4)]
-    mine, other = beside(quarters[0], quarters[2]), beside(quarters[1], quarters[3])
-    local = from_other_core(mine, other)
-    local_all, _ = gather_trees(local, trees)
-    local_all = local_all.reshape(trees, 3, 2, rank, units)
-    same, crossed, same_hot, crossed_hot = [], [], [], []
-    where_is = {tree: i for i, tree in enumerate(tree_index)}
-    for j in range(trees):
-        for near in range(2):
-            target = (crossed if (j // 2) % 2 else same)
-            hots = (crossed_hot if (j // 2) % 2 else same_hot)
-            target.append(local_all[where_is[j], :, near])
-            hots.append(hot_near[where_is[j ^ (2 * near)]])
-    mine_sum = by_adapter(jnp.stack(same_hot), jnp.stack(same))
-    other_sum = by_adapter(jnp.stack(crossed_hot), jnp.stack(crossed))
-    low_half = jnp.where(odd, other_sum, mine_sum)
-    high_half = jnp.where(odd, mine_sum, other_sum)
-    both_halves = jnp.concatenate([low_half, high_half], axis=-1)
-    out_expand_gate, out_expand_up, out_shrink_down = (both_halves[:, i] for i in range(3))
-
-    def share(blocks):
-        blocks = low(blocks)
-        swapped = jnp.where(my_part % 2 == 1, blocks.reshape(2, 2, rank, -1)[:, ::-1], blocks.reshape(2, 2, rank, -1))
-        swapped = jnp.where(my_part // 2 == 1, swapped[::-1], swapped)
-        kept = swapped[:, 0].astype(jnp.float32) + on_core(swapped[:, 1]).astype(jnp.float32)
-        kept = kept[0] + flip(low(kept[1]), "tensor", 2).astype(jnp.float32)
-        gathered, _ = gather_trees(low(kept), trees)
-        total = low(by_adapter(hot_near, gathered))[None]
-        total = jnp.concatenate([total, flip(total, "tensor", 2)])
-        total = jnp.stack([total, on_core(total)], axis=1)
-        total = jnp.where(my_part // 2 == 1, total[::-1], total)
-        total = jnp.where(my_part % 2 == 1, total[:, ::-1], total)
-        return total.reshape((4,) + total.shape[2:]).astype(jnp.float32)
-
-    shared = jnp.concatenate([grad_shrink_gate_up, grad_expand_down]).reshape(3, 2, rank, -1)
-    shared = shared[:, 0] + flip(low(shared[:, 1]), "dp", 2).astype(jnp.float32)
-    shared = share(jnp.concatenate([shared, grad_expand_output[None]]))
-    out_shrink_gate, out_shrink_up, out_expand_down, out_expand_output = (
-        shared[i] for i in range(4)
-    )
-
+    last = jnp.concatenate(
+        [over_rows(grad_inner_qkv, normed_all), grad_expand_output]
+    ).reshape(4, rank, -1)
     pieces = []
     for side in range(2):
         for i in range(3):
             first = side * heads_here + starts[i]
             pieces.append(grad_expand_qkv[i * rank : (i + 1) * rank, first : first + widths[i]])
         pieces.append(grad_shrink_output[:, side * widths[0] : (side + 1) * widths[0]])
-    local = from_other_core(
+    local_attn = from_other_core(
         jnp.concatenate(pieces[:4], axis=1), jnp.concatenate(pieces[4:], axis=1)
     )
-    local_all, _ = gather_trees(local, trees)
-    local_all = by_adapter(hot_near, local_all)
-    out_expand_query, out_expand_key, out_expand_value = (
-        local_all[:, :, starts[i] : starts[i] + widths[i]] for i in range(3)
-    )
-    out_shrink_output = local_all[:, :, heads_here:]
-
-    shared = grad_shrink_qkv.reshape(3, rank, -1)
-    shared = share(jnp.concatenate([shared, jnp.zeros_like(shared[:1])]))
-    out_shrink_query, out_shrink_key, out_shrink_value = (shared[i] for i in range(3))
+    last = last + on_core(low(last)).astype(jnp.float32)
+    last, local_attn, grad_qkv, grad_inner_qkv, shared_all = settle(
+        last, local_attn, grad_qkv, grad_inner_qkv, shared_all
+    )
+
+    last_y = flip(low(last), "tensor", 2)
+    for bit in bits[:-2]:
+        shared_all = with_bit(shared_all, bit)
+    part = times_rows(grad_qkv, full_qkv) + product(grad_inner_qkv, s_qkv)
+    last_y, part, shared_all, local_near = settle(last_y, part, shared_all, local_near)
+
+    last_mine = beside(core_half(last + last_y.astype(jnp.float32)), local_attn)
+    last_all = lax.all_to_all(
+        jnp.broadcast_to(last_mine[None], (trees,) + last_mine.shape), "dp", 0, 0
+    )
+    from_y = flip(low(part[block_rows:]), "tensor", 2)
+    shared_all = with_bit(shared_all, bits[-2])
+    from_y, shared_all = settle(from_y, shared_all)
+    grad_normed = part[:block_rows] + from_y.astype(jnp.float32)
+    input_grad = grad_resid + rms_back(own_rows, norm_gain[0], grad_normed)
+    local_all = jnp.concatenate([local_all, local_near])
+
+    tree_ids = tree_ids.reshape(trees)
+    hot_near = (tree_ids[:, None] == labels[None, :]).astype(jnp.float32)
+    distances = my_tree ^ jnp.arange(trees, dtype=jnp.int32)
+    place_of = jnp.stack(
+        [jnp.asarray(tree_order(trees).index(j), jnp.int32) for j in range(trees)]
+    )
+    at = jnp.sum(
+        jnp.where(
+            distances[:, None] == jnp.arange(trees, dtype=jnp.int32)[None, :], place_of[None, :], 0
+        ),
+        axis=1,
+    )
+    hot_trees = jnp.sum(
+        jnp.where(
+            at[:, None, None] == jnp.arange(trees, dtype=jnp.int32)[None, :, None],
+            hot_near[None],
+            0.0,
+        ),
+        axis=1,
+    )
+
+    order_local = [0, 1]
+    for bit in bits[:-1]:
+        order_local += [i ^ bit for i in order_local]
+    ids_at = {tree: i for i, tree in enumerate(tree_order(trees))}
+    hots, crossing = [], []
+    for j in order_local:
+        for near_tree in range(2):
+            hots.append(hot_near[ids_at[j ^ (2 * near_tree)]])
+            crossing.append((j // 2) % 2)
+    hots = jnp.stack(hots)
+    parity = jnp.asarray(crossing, jnp.int32) ^ (my_z % 2).astype(jnp.int32)
+    local_all = local_all.reshape(2 * trees, 3 * rank, units)
+    hots = jnp.stack([jnp.where(parity[:, None] == side, hots, 0.0) for side in range(2)])
+    hots_local = jnp.stack([hot_near[ids_at[j]] for j in order_local])
+    out_expand_gate, out_expand_up, out_shrink_down = sum_unit_grads(hots, local_all, 3)
+    core = (my_part % 2).astype(jnp.int32)[None]
+    depth_half = s_qkv.shape[1] // 2
+    (sums,) = sum_by_adapter(hots_local, shared_all, 3 * depth_half, [])
+    out_shrink_gate, out_shrink_up, out_expand_down = join_halves(core, sums, on_core(sums), 3)
+    (last_all, input_grad, out_expand_gate, out_expand_up, out_shrink_down, out_shrink_gate,
+     out_shrink_up, out_expand_down) = settle(
+        last_all, input_grad, out_expand_gate, out_expand_up, out_shrink_down, out_shrink_gate,
+        out_shrink_up, out_expand_down,
+    )
+    sums, out_expand_query, out_expand_key, out_expand_value, out_shrink_output = sum_by_adapter(
+        hot_trees, last_all, 4 * depth_half, widths + widths[:1]
+    )
+    out_shrink_query, out_shrink_key, out_shrink_value, out_expand_output = join_halves(
+        core, sums, on_core(sums), 4
+    )
     return (
         layer_output,
         input_grad,

time: 794 us -> 677 us (0.85)
  waiting for transfers between devices: 341 us -> 265 us
  local copies, waits for them, and re-layouts: 119 us -> 83.2 us
  Pallas kernels: 112 us -> 132 us
  other arithmetic: 59.8 us -> 44.4 us
  matrix products: 48.9 us -> 35.3 us
    ppermute x77 -> x70, waiting for transfers between devices: 312 us -> 245 us  [flip(): return lax.ppermute(values, axis_name, [(i, i ^ bit) for i in range(size)])]
    another operation x24 -> x3, local copies, waits for them, and re-layouts: 22.7 us -> 0.14 us  [the longest x1 0.06 us: on_device(): jnp.stack([grads.reshape(2, rank, 2 * units) for grads in (over_rows(inne...]
    pallas_call x3 -> x9, Pallas kernels: 77.8 us -> 90.5 us  [the longest x1 40.4 us: feed_forward_back(): pl.pallas_call(kernel, out_shape=parts + [jax.ShapeDtypeStruct((count, tw...]
    all_to_all x9, waiting for transfers between devices: 28.9 us -> 19.4 us  [along_z(): return lax.all_to_all(sent, 'dp', 0, 0, axis_index_groups=lines)]
    concatenate x26 -> x19, other arithmetic: 21.6 us -> 12.6 us  [the longest x6 7.25 us: on_device(): jnp.concatenate([blocks] * (columns_z // blocks.shape[0]))]
    dot_general x12 -> x10, matrix products: 29.8 us -> 21.8 us  [times_rows(): lax.dot_general(former, latter, (((1,), (1,)), ((), ())), preferred_eleme...]
    unnamed x355 -> x287, local copies, waits for them, and re-layouts: 67.9 us -> 61.7 us
    ppermute x77 -> x70, starting transfers between devices: 57.7 us -> 56.6 us  [flip(): return lax.ppermute(values, axis_name, [(i, i ^ bit) for i in range(size)])]
  transfers between devices with their start and end apart: 86 -> 80, of which waited for: 40 -> 37; matrix products, arithmetic and copies ran while one was open for 16% -> 13% of each run, Pallas kernels for 7% -> 11%
where the time goes in v3:
time: 677 us; the launch traced here: 666 us
  waiting for transfers between devices  265 us (39%)
  Pallas kernels  132 us (19%)
  starting transfers between devices  103 us (15%)
  local copies, waits for them, and re-layouts  83.2 us (12%)
  other arithmetic  44.4 us (7%)
  matrix products  35.3 us (5%)
    ppermute x70, waiting for transfers between devices, flip(): return lax.ppermute(values, axis_name, [(i, i ^ bit) for i in range(size)])  245 us
    unnamed x287, local copies, waits for them, and re-layouts  61.7 us
    ppermute x70, starting transfers between devices, flip(): return lax.ppermute(values, axis_name, [(i, i ^ bit) for i in range(size)])  56.6 us
    all_to_all x9, starting transfers between devices, along_z(): return lax.all_to_all(sent, 'dp', 0, 0, axis_index_groups=lines)  42 us
    pallas_call x1, Pallas kernels, feed_forward_back(): pl.pallas_call(kernel, out_shape=parts + [jax.ShapeDtypeStruct((count, tw...  40.4 us
    pallas_call x2, Pallas kernels, gate_and_up(): pl.pallas_call(kernel, out_shape=[jax.ShapeDtypeStruct((count, units), jn...  25.9 us
    pallas_call x8, Pallas kernels, assemble(): pl.pallas_call(kernel, out_shape=jax.ShapeDtypeStruct((2 * columns_z, row...  22.6 us
    dot_general x10, matrix products, times_rows(): lax.dot_general(former, latter, (((1,), (1,)), ((), ())), preferred_eleme...  21.8 us
  transfers between devices with their start and end apart: 80, of which 37 were waited for; matrix products, arithmetic and copies ran while one was open for 13% of the time, Pallas kernels for 11%

profile of v3, /device:TPU:0, one launch (start us, length us, event | category | flops | bytes accessed | tf_op | source)
XLA Modules:
  0.0 666.5 jit_solution(13457357387975573900)
XLA Ops:
  5.4 6.5 all-to-all-start
  18.8 12.3 %collective-permute-done = s32[1]{0:T(128)} collective-permute-done((s32[1]{0:T(128)}, s32[1]{0:T(128)}, u32[]{:S(2)}, u32[]{:S(2)}) %collective-permute-start) | collective-permute-done | bytes 36 | tf_op jit(solution)/shard_map/ppermute | solution.py:92
  31.2 9.3 %all-to-all-done.refs_0_ = bf16[4,144,1024]{2,1,0:T(8,128)(2,1)S(1)} async-done(((bf16[4,144,1024]{2,1,0:T(8,128)(2,1)}), bf16[4,144,1024]{2,1,0:T(8,128)(2,1)S(1)}, u32[]{:S(2)}, u32[]{:S(2)}) %all-to-all-start) | async-done | bytes 1179680 | tf_op jit(solution)/shard_map/all_to_all | solution.py:102
  40.4 2.3 concatenate.173
  44.2 4.3 all-to-all-start.1
  51.3 2.9 shard_map.387
  69.8 8.3 %all-to-all-done.1.refs_4_ = bf16[4,144,1024]{2,1,0:T(8,128)(2,1)} async-done(((bf16[4,144,1024]{2,1,0:T(8,128)(2,1)}), bf16[4,144,1024]{2,1,0:T(8,128)(2,1)}, u32[]{:S(2)}, u32[]{:S(2)}) %all-to-all-start.1) | async-done | bytes 1179680 | tf_op jit(solution)/shard_map/all_to_all | solution.py:102
  80.1 3.5 all-to-all-start.2
  90.2 21.3 %collective-permute-done.4.refs_5_ = bf16[4,144,1024]{2,1,0:T(8,128)(2,1)S(1)} collective-permute-done((bf16[4,144,1024]{2,1,0:T(8,128)(2,1)}, bf16[4,144,1024]{2,1,0:T(8,128)(2,1)S(1)}, u32[]{:S(2)}, u32[]{:S(2)}) %collective-permute-start.4) | collective-permute-done | bytes 1179680 | tf_op jit(solution)/shard_map/ppermute | solution.py:92
  114.6 4.7 all-to-all-start.3
  128.6 18.6 %collective-permute-done.9.refs_1_ = bf16[4,288,512]{2,1,0:T(8,128)(2,1)} collective-permute-done((bf16[4,288,512]{2,1,0:T(8,128)(2,1)S(1)}, bf16[4,288,512]{2,1,0:T(8,128)(2,1)}, u32[]{:S(2)}, u32[]{:S(2)}) %collective-permute-start.9) | collective-permute-done | bytes 1179680 | tf_op jit(solution)/shard_map/ppermute | solution.py:92
  149.3 4.9 all-to-all-start.4
  160.3 3.0 shard_map.388
  163.4 6.5 shard_map.389.mine_ref
  170.2 3.0 collective-permute-start.16
  174.6 5.7 collective-permute-done.16
  182.4 3.8 all-to-all-start.5
  187.3 3.0 shard_map.390
  192.9 2.5 shard_map.391
  203.6 6.0 collective-permute-done.21
  209.7 5.3 collective-permute-done.20
  216.3 9.7 %collective-permute-done.17.refs_1_ = bf16[4,288,512]{2,1,0:T(8,128)(2,1)S(1)} collective-permute-done((bf16[4,288,512]{2,1,0:T(8,128)(2,1)}, bf16[4,288,512]{2,1,0:T(8,128)(2,1)S(1)}, u32[]{:S(2)}, u32[]{:S(2)}) %collective-permute-start.17) | collective-permute-done | bytes 1179680 | tf_op jit(solution)/shard_map/ppermute | solution.py:92
  228.5 4.9 all-to-all-start.6
  242.9 2.8 shard_map.392
  245.7 2.2 copy-done.2
  248.0 18.0 %collective-permute-done.26 = bf16[80,2304]{1,0:T(8,128)(2,1)S(1)} collective-permute-done((bf16[80,2304]{1,0:T(8,128)(2,1)S(1)}, bf16[80,2304]{1,0:T(8,128)(2,1)S(1)}, u32[]{:S(2)}, u32[]{:S(2)}) %collective-permute-start.26) | collective-permute-done | bytes 368672 | tf_op jit(solution)/shard_map/ppermute | solution.py:92
  269.1 4.3 all-to-all-start.7
  280.4 27.0 %collective-permute-done.31 = s32[4]{0:T(128)S(1)} collective-permute-done((s32[4]{0:T(128)S(1)}, s32[4]{0:T(128)S(1)}, u32[]{:S(2)}, u32[]{:S(2)}) %collective-permute-start.31) | collective-permute-done | bytes 48 | tf_op jit(solution)/shard_map/ppermute | solution.py:92
  308.0 2.3 shard_map.393
  317.8 5.1 all-to-all-start.8
  325.7 2.7 shard_map.395
  328.5 2.5 copy-done
  331.8 10.3 %collective-permute-done.35 = bf16[160,2304]{1,0:T(8,128)(2,1)S(1)} collective-permute-done((bf16[160,2304]{1,0:T(8,128)(2,1)S(1)}, bf16[160,2304]{1,0:T(8,128)(2,1)S(1)}, u32[]{:S(2)}, u32[]{:S(2)}) %collective-permute-start.35) | collective-permute-done | bytes 737312 | tf_op jit(solution)/shard_map/ppermute | solution.py:92
  343.0 3.4 fusion.15.inner_ref
  346.4 11.9 %shard_map.394 = (bf16[640,1024]{1,0:T(8,128)(2,1)}, bf16[640,1024]{1,0:T(8,128)(2,1)}, bf16[640,1024]{1,0:T(8,128)(2,1)}) custom-call(bf16[640,2304]{1,0:T(8,128)(2,1)} %constant_dynamic-update-slice_fusion.9.rows_ref, bf16[2304,1024]{1,0:T(8,128)(2,1)} %bitcast.159, bf16[2304,1024]{1,0:T(8,128)(2,1)} %bitcast.161, bf16[640,64]{1,0:T(8,128)(2,1)} %fusion.15.inner_ref, ...), custom_call_target="tpu_custom_call" | custom-call | flops 1 | bytes 1 | tf_op jit(solution)/shard_map/pallas_call | solution.py:351
  361.5 3.1 shard_map.396
  364.6 2.5 copy-done.1
  367.1 14.0 %shard_map.397 = (bf16[640,1280]{1,0:T(8,128)(2,1)}, bf16[640,1280]{1,0:T(8,128)(2,1)}, bf16[640,1280]{1,0:T(8,128)(2,1)}) custom-call(bf16[640,2304]{1,0:T(8,128)(2,1)} %constant_dynamic-update-slice_fusion.9.rows_ref, bf16[2304,1280]{1,0:T(8,128)(2,1)} %bitcast.155, bf16[2304,1280]{1,0:T(8,128)(2,1)} %bitcast.157, bf16[640,64]{1,0:T(8,128)(2,1)} %fusion.15.inner_ref, ...), custom_call_target="tpu_custom_call" | custom-call | flops 1 | bytes 1 | tf_op jit(solution)/shard_map/pallas_call | solution.py:351
  385.5 3.5 shard_map.398
  389.0 5.8 convolution_add_fusion.first_ref
  395.2 2.8 collective-permute-done.39.refs_3_
  397.9 2.8 shard_map.399
  402.9 6.7 %shard_map.400 = (f32[160,2304]{1,0:T(8,128)S(1)}, f32[80,2304]{1,0:T(8,128)S(1)}, f32[80,2304]{1,0:T(8,128)S(1)}, bf16[160,2304]{1,0:T(8,128)(2,1)S(1)}, bf16[160,2304]{1,0:T(8,128)(2,1)S(1)}) custom-call(f32[640,2304]{1,0:T(8,128)} %convolution_add_fusion.first_ref, bf16[640,1024]{1,0:T(8,128)(2,1)S(1)} %copy-done.11, bf16[2304,1024]{1,0:T(8,128)(2,1)} %bitcast.163), custom_call_target="tpu_custom_call" | custom-call | flops 1 | bytes 1 | tf_op jit(solution)/shard_map/pallas_call | solution.py:398
  412.2 16.4 %collective-permute-done.41 = bf16[160,2304]{1,0:T(8,128)(2,1)S(1)} collective-permute-done((bf16[160,2304]{1,0:T(8,128)(2,1)S(1)}, bf16[160,2304]{1,0:T(8,128)(2,1)S(1)}, u32[]{:S(2)}, u32[]{:S(2)}) %collective-permute-start.41) | collective-permute-done | bytes 737312 | tf_op jit(solution)/shard_map/ppermute | solution.py:92
  431.3 8.7 %collective-permute-done.42 = bf16[80,2304]{1,0:T(8,128)(2,1)S(1)} collective-permute-done((bf16[80,2304]{1,0:T(8,128)(2,1)S(1)}, bf16[80,2304]{1,0:T(8,128)(2,1)S(1)}, u32[]{:S(2)}, u32[]{:S(2)}) %collective-permute-start.42) | collective-permute-done | bytes 368672 | tf_op jit(solution)/shard_map/ppermute | solution.py:92
  446.3 13.6 %collective-permute-done.44 = bf16[160,2304]{1,0:T(8,128)(2,1)S(1)} collective-permute-done((bf16[160,2304]{1,0:T(8,128)(2,1)S(1)}, bf16[160,2304]{1,0:T(8,128)(2,1)S(1)}, u32[]{:S(2)}, u32[]{:S(2)}) %collective-permute-start.44) | collective-permute-done | bytes 737312 | tf_op jit(solution)/shard_map/ppermute | solution.py:92
  465.0 3.0 collective-permute-done.46
  469.7 40.4 %shard_map.401 = (f32[160,2304]{1,0:T(8,128)}, f32[80,2304]{1,0:T(8,128)}, f32[80,2304]{1,0:T(8,128)}, bf16[160,2304]{1,0:T(8,128)(2,1)}, bf16[160,2304]{1,0:T(8...) custom-call(bf16[640,2304]{1,0:T(8,128)(2,1)} %constant_dynamic-upda, ...), custom_call_target="tpu_custom_call" | custom-call | flops 1 | bytes 1 | tf_op jit(solution)/shard_map/pallas_call | solution.py:492
  521.8 10.4 %collective-permute-done.48 = bf16[160,2304]{1,0:T(8,128)(2,1)S(1)} collective-permute-done((bf16[160,2304]{1,0:T(8,128)(2,1)S(1)}, bf16[160,2304]{1,0:T(8,128)(2,1)S(1)}, u32[]{:S(2)}, u32[]{:S(2)}) %collective-permute-start.48) | collective-permute-done | bytes 737312 | tf_op jit(solution)/shard_map/ppermute | solution.py:92
  538.8 2.5 fusion.69
  550.8 2.3 collective-permute-start.55
  554.5 11.4 %collective-permute-done.55 = bf16[2,96,1152]{2,1,0:T(8,128)(2,1)S(1)} collective-permute-done((bf16[2,96,1152]{2,1,0:T(8,128)(2,1)S(1)}, bf16[2,96,1152]{2,1,0:T(8,128)(2,1)S(1)}, u32[]{:S(2)}, u32[]{:S(2)}) %collective-permute-start.55) | collective-permute-done | bytes 442400 | tf_op jit(solution)/shard_map/ppermute | solution.py:92
  569.6 6.3 shard_map.402
  581.4 5.9 collective-permute-done.59
  592.6 3.5 collective-permute-done.62
  598.4 2.6 collective-permute-start.64
  601.0 4.9 convolution_add_fusion.1
  605.9 4.6 collective-permute-done.64
  612.1 4.9 all-to-all-start.9
  622.7 7.9 %shard_map.403 = (f32[8,16,2304]{2,1,0:T(8,128)}, f32[8,16,2304]{2,1,0:T(8,128)}, f32[8,16,2304]{2,1,0:T(8,128)}) custom-call(f32[2,16,8]{2,1,0:T(8,128)S(1)} %pad_maximum_fusion.38.hots_ref, bf16[16,48,1152]{2,1,0:T(8,128)(2,1)S(1)} %bitcast.171), custom_call_target="tpu_custom_call" | custom-call | flops 1 | bytes 1 | tf_op jit(solution)/shard_map/pallas_call | solution.py:592
  630.7 20.0 %collective-permute-done.67 = bf16[4,16,3456]{2,1,0:T(8,128)(2,1)S(1)} collective-permute-done((bf16[4,16,3456]{2,1,0:T(8,128)(2,1)S(1)}, bf16[4,16,3456]{2,1,0:T(8,128)(2,1)S(1)}, u32[]{:S(2)}, u32[]{:S(2)}) %collective-permute-start.67) | collective-permute-done | bytes 442400 | tf_op jit(solution)/shard_map/ppermute | solution.py:92
  657.7 3.4 shard_map.406
  661.1 2.8 collective-permute-done.69.other_ref
  664.0 2.3 shard_map.407
  (612 shorter events, 199.0 us)
Async XLA Ops:
  5.4 35.0 %all-to-all-start = ((bf16[4,144,1024]{2,1,0:T(8,128)(2,1)}), bf16[4,144,1024]{2,1,0:T(8,128)(2,1)S(1)}, u32[]{:S(2)}, u32[]{:S(2)}) async-start(bf16[4,144,1024]{2,1,0:T(8,128)(2,1)} %concatenate.172), calls=%async_computation | async-start | bytes 2359296 | tf_op jit(solution)/shard_map/all_to_all | solution.py:102
  11.9 19.3 %collective-permute-start = (s32[1]{0:T(128)}, s32[1]{0:T(128)}, u32[]{:S(2)}, u32[]{:S(2)}) collective-permute-start(s32[1]{0:T(128)} %param.52), channel_id=1, source_target_pairs={{0,8},{4,12},{8,0},{12,4},{16,24},{20,28},{24,16},{28,20},{1,9},{5... | collective-permute-start | bytes 20 | tf_op jit(solution)/shard_map/ppermute | solution.py:92
  42.7 27.0 %collective-permute-start.1 = (bf16[4,144,1024]{2,1,0:T(8,128)(2,1)S(1)}, bf16[4,144,1024]{2,1,0:T(8,128)(2,1)}, u32[]{:S(2)}, u32[]{:S(2)}) collective-permute-start(bf16[4,144,1024]{2,1,0:T(8,128)(2,1)S(1)} %all-to-all-done.refs_0_), channel_id=1, source_target_pairs={{0,4},{4,0},{8,12},{12,8},{16,20},{20,16},{24,28},{28,24},{1,5},{5... | collective-permute-start | bytes 3538952 | tf_op jit(solution)/shard_map/ppermute | solution.py:92
  44.2 25.6 %collective-permute-start.2 = (bf16[4,144,1024]{2,1,0:T(8,128)(2,1)S(1)}, bf16[4,144,1024]{2,1,0:T(8,128)(2,1)}, u32[]{:S(2)}, u32[]{:S(2)}) collective-permute-start(bf16[4,144,1024]{2,1,0:T(8,128)(2,1)S(1)} %all-to-all-done.refs_0_), channel_id=1, source_target_pairs={{0,1},{1,0},{2,3},{3,2},{4,5},{5,4},{6,7},{7,6},{8,9},{9,8},{10,11... | collective-permute-start | bytes 3538952 | tf_op jit(solution)/shard_map/ppermute | solution.py:92
  44.2 33.8 %all-to-all-start.1 = ((bf16[4,144,1024]{2,1,0:T(8,128)(2,1)}), bf16[4,144,1024]{2,1,0:T(8,128)(2,1)}, u32[]{:S(2)}, u32[]{:S(2)}) async-start(bf16[4,144,1024]{2,1,0:T(8,128)(2,1)} %concatenate.173), calls=%async_computation.1 | async-start | bytes 2359296 | tf_op jit(solution)/shard_map/all_to_all | solution.py:102
  48.5 19.8 %collective-permute-start.3 = (bf16[160,2304]{1,0:T(8,128)(2,1)S(1)}, bf16[160,2304]{1,0:T(8,128)(2,1)}, u32[]{:S(2)}, u32[]{:S(2)}) collective-permute-start(bf16[160,2304]{1,0:T(8,128)(2,1)S(1)} %fusion.7), channel_id=1, source_target_pairs={{0,2},{1,3},{2,0},{3,1},{4,6},{5,7},{6,4},{7,5},{8,10},{9,11},{10,... | collective-permute-start | bytes 2211848 | tf_op jit(solution)/shard_map/ppermute | solution.py:92
  80.1 34.5 %all-to-all-start.2 = ((bf16[4,288,512]{2,1,0:T(8,128)(2,1)}), bf16[4,288,512]{2,1,0:T(8,128)(2,1)S(1)}, u32[]{:S(2)}, u32[]{:S(2)}) async-start(bf16[4,288,512]{2,1,0:T(8,128)(2,1)} %concatenate.174), calls=%async_computation.2 | async-start | bytes 2359296 | tf_op jit(solution)/shard_map/all_to_all | solution.py:102
  83.7 27.9 %collective-permute-start.4 = (bf16[4,144,1024]{2,1,0:T(8,128)(2,1)}, bf16[4,144,1024]{2,1,0:T(8,128)(2,1)S(1)}, u32[]{:S(2)}, u32[]{:S(2)}) collective-permute-start(bf16[4,144,1024]{2,1,0:T(8,128)(2,1)} %all-to-all-done.1.refs_4_), channel_id=1, source_target_pairs={{0,4},{4,0},{8,12},{12,8},{16,20},{20,16},{24,28},{28,24},{1,5},{5... | collective-permute-start | bytes 3538952 | tf_op jit(solution)/shard_map/ppermute | solution.py:92
  84.3 27.3 %collective-permute-start.5 = (bf16[4,144,1024]{2,1,0:T(8,128)(2,1)}, bf16[4,144,1024]{2,1,0:T(8,128)(2,1)S(1)}, u32[]{:S(2)}, u32[]{:S(2)}) collective-permute-start(bf16[4,144,1024]{2,1,0:T(8,128)(2,1)} %all-to-all-done.1.refs_4_), channel_id=1, source_target_pairs={{0,1},{1,0},{2,3},{3,2},{4,5},{5,4},{6,7},{7,6},{8,9},{9,8},{10,11... | collective-permute-start | bytes 3538952 | tf_op jit(solution)/shard_map/ppermute | solution.py:92
  84.3 29.3 %collective-permute-start.6 = (bf16[4,144,1024]{2,1,0:T(8,128)(2,1)}, bf16[4,144,1024]{2,1,0:T(8,128)(2,1)S(1)}, u32[]{:S(2)}, u32[]{:S(2)}) collective-permute-start(bf16[4,144,1024]{2,1,0:T(8,128)(2,1)} %collective-permute-done.1.refs_1_), channel_id=1, source_target_pairs={{0,1},{1,0},{2,3},{3,2},{4,5},{5,4},{6,7},{7,6},{8,9},{9,8},{10,11... | collective-permute-start | bytes 3538952 | tf_op jit(solution)/shard_map/ppermute | solution.py:92
  114.6 34.7 %all-to-all-start.3 = ((bf16[4,288,512]{2,1,0:T(8,128)(2,1)}), bf16[4,288,512]{2,1,0:T(8,128)(2,1)}, u32[]{:S(2)}, u32[]{:S(2)}) async-start(bf16[4,288,512]{2,1,0:T(8,128)(2,1)} %pad_maximum_fusion.7), calls=%async_computation.3 | async-start | bytes 2359296 | tf_op jit(solution)/shard_map/all_to_all | solution.py:102
  120.8 26.4 %collective-permute-start.9 = (bf16[4,288,512]{2,1,0:T(8,128)(2,1)S(1)}, bf16[4,288,512]{2,1,0:T(8,128)(2,1)}, u32[]{:S(2)}, u32[]{:S(2)}) collective-permute-start(bf16[4,288,512]{2,1,0:T(8,128)(2,1)S(1)} %all-to-all-done.2.refs_0_), channel_id=1, source_target_pairs={{0,4},{4,0},{8,12},{12,8},{16,20},{20,16},{24,28},{28,24},{1,5},{5... | collective-permute-start | bytes 3538952 | tf_op jit(solution)/shard_map/ppermute | solution.py:92
  121.4 25.8 %collective-permute-start.10 = (bf16[4,288,512]{2,1,0:T(8,128)(2,1)S(1)}, bf16[4,288,512]{2,1,0:T(8,128)(2,1)S(1)}, u32[]{:S(2)}, u32[]{:S(2)}) collective-permute-start(bf16[4,288,512]{2,1,0:T(8,128)(2,1)S(1)} %all-to-all-done.2.refs_0_), channel_id=1, source_target_pairs={{0,1},{1,0},{2,3},{3,2},{4,5},{5,4},{6,7},{7,6},{8,9},{9,8},{10,11... | collective-permute-start | bytes 3538952 | tf_op jit(solution)/shard_map/ppermute | solution.py:92
  121.4 26.9 %collective-permute-start.11 = (bf16[4,144,1024]{2,1,0:T(8,128)(2,1)S(1)}, bf16[4,144,1024]{2,1,0:T(8,128)(2,1)S(1)}, u32[]{:S(2)}, u32[]{:S(2)}) collective-permute-start(bf16[4,144,1024]{2,1,0:T(8,128)(2,1)S(1)} %copy-done.37), channel_id=1, source_target_pairs={{0,1},{1,0},{2,3},{3,2},{4,5},{5,4},{6,7},{7,6},{8,9},{9,8},{10,11... | collective-permute-start | bytes 3538952 | tf_op jit(solution)/shard_map/ppermute | solution.py:92
  149.3 33.1 %all-to-all-start.4 = ((bf16[4,288,512]{2,1,0:T(8,128)(2,1)}), bf16[4,288,512]{2,1,0:T(8,128)(2,1)}, u32[]{:S(2)}, u32[]{:S(2)}) async-start(bf16[4,288,512]{2,1,0:T(8,128)(2,1)} %pad_maximum_fusion.8), calls=%async_computation.4 | async-start | bytes 2359296 | tf_op jit(solution)/shard_map/all_to_all | solution.py:102
  154.2 28.2 %collective-permute-start.12 = (bf16[4,288,512]{2,1,0:T(8,128)(2,1)}, bf16[4,288,512]{2,1,0:T(8,128)(2,1)}, u32[]{:S(2)}, u32[]{:S(2)}) collective-permute-start(bf16[4,288,512]{2,1,0:T(8,128)(2,1)} %all-to-all-done.3.refs_0_), channel_id=1, source_target_pairs={{0,4},{4,0},{8,12},{12,8},{16,20},{20,16},{24,28},{28,24},{1,5},{5... | collective-permute-start | bytes 3538952 | tf_op jit(solution)/shard_map/ppermute | solution.py:92
  154.7 27.7 %collective-permute-start.13 = (bf16[4,288,512]{2,1,0:T(8,128)(2,1)}, bf16[4,288,512]{2,1,0:T(8,128)(2,1)}, u32[]{:S(2)}, u32[]{:S(2)}) collective-permute-start(bf16[4,288,512]{2,1,0:T(8,128)(2,1)} %all-to-all-done.3.refs_0_), channel_id=1, source_target_pairs={{0,1},{1,0},{2,3},{3,2},{4,5},{5,4},{6,7},{7,6},{8,9},{9,8},{10,11... | collective-permute-start | bytes 3538952 | tf_op jit(solution)/shard_map/ppermute | solution.py:92
  154.7 27.7 %collective-permute-start.14 = (bf16[4,288,512]{2,1,0:T(8,128)(2,1)}, bf16[4,288,512]{2,1,0:T(8,128)(2,1)}, u32[]{:S(2)}, u32[]{:S(2)}) collective-permute-start(bf16[4,288,512]{2,1,0:T(8,128)(2,1)} %collective-permute-done.9.refs_1_), channel_id=1, source_target_pairs={{0,1},{1,0},{2,3},{3,2},{4,5},{5,4},{6,7},{7,6},{8,9},{9,8},{10,11... | collective-permute-start | bytes 3538952 | tf_op jit(solution)/shard_map/ppermute | solution.py:92
  170.1 11.4 %collective-permute-start.15 = (bf16[320,1024]{1,0:T(8,128)(2,1)S(1)}, bf16[320,1024]{1,0:T(8,128)(2,1)S(1)}, u32[]{:S(2)}, u32[]{:S(2)}) collective-permute-start(bf16[320,1024]{1,0:T(8,128)(2,1)S(1)} %pad_maximum_fusion.17), channel_id=1, source_target_pairs={{0,1},{1,0},{2,3},{3,2},{4,5},{5,4},{6,7},{7,6},{8,9},{9,8},{10,11... | collective-permute-start | bytes 1966088 | tf_op jit(solution)/shard_map/ppermute | solution.py:92
  170.2 10.1 %collective-permute-start.16 = (s32[1]{0:T(128)}, s32[1]{0:T(128)}, u32[]{:S(2)}, u32[]{:S(2)}) collective-permute-start(s32[1]{0:T(128)} %param.52), channel_id=1, source_target_pairs={{0,16},{4,20},{8,24},{12,28},{16,0},{20,4},{24,8},{28,12},{1,17},{... | collective-permute-start | bytes 20 | tf_op jit(solution)/shard_map/ppermute | solution.py:92
  182.4 45.6 %all-to-all-start.5 = ((bf16[4,288,640]{2,1,0:T(8,128)(2,1)}), bf16[4,288,640]{2,1,0:T(8,128)(2,1)S(1)}, u32[]{:S(2)}, u32[]{:S(2)}) async-start(bf16[4,288,640]{2,1,0:T(8,128)(2,1)} %pad_maximum_fusion.2), calls=%async_computation.5 | async-start | bytes 2949120 | tf_op jit(solution)/shard_map/all_to_all | solution.py:102
  197.6 17.4 %collective-permute-start.20 = (bf16[160,2304]{1,0:T(8,128)(2,1)S(1)}, bf16[160,2304]{1,0:T(8,128)(2,1)S(1)}, u32[]{:S(2)}, u32[]{:S(2)}) collective-permute-start(bf16[160,2304]{1,0:T(8,128)(2,1)S(1)} %slice.644), channel_id=1, source_target_pairs={{0,2},{1,3},{2,0},{3,1},{4,6},{5,7},{6,4},{7,5},{8,10},{9,11},{10,... | collective-permute-start | bytes 2211848 | tf_op jit(solution)/shard_map/ppermute | solution.py:92
  199.2 26.8 %collective-permute-start.17 = (bf16[4,288,512]{2,1,0:T(8,128)(2,1)}, bf16[4,288,512]{2,1,0:T(8,128)(2,1)S(1)}, u32[]{:S(2)}, u32[]{:S(2)}) collective-permute-start(bf16[4,288,512]{2,1,0:T(8,128)(2,1)} %all-to-all-done.4.refs_0_), channel_id=1, source_target_pairs={{0,4},{4,0},{8,12},{12,8},{16,20},{20,16},{24,28},{28,24},{1,5},{5... | collective-permute-start | bytes 3538952 | tf_op jit(solution)/shard_map/ppermute | solution.py:92
  199.7 26.3 %collective-permute-start.18 = (bf16[4,288,512]{2,1,0:T(8,128)(2,1)}, bf16[4,288,512]{2,1,0:T(8,128)(2,1)S(1)}, u32[]{:S(2)}, u32[]{:S(2)}) collective-permute-start(bf16[4,288,512]{2,1,0:T(8,128)(2,1)} %all-to-all-done.4.refs_0_), channel_id=1, source_target_pairs={{0,1},{1,0},{2,3},{3,2},{4,5},{5,4},{6,7},{7,6},{8,9},{9,8},{10,11... | collective-permute-start | bytes 3538952 | tf_op jit(solution)/shard_map/ppermute | solution.py:92
  199.7 27.3 %collective-permute-start.19 = (bf16[4,288,512]{2,1,0:T(8,128)(2,1)}, bf16[4,288,512]{2,1,0:T(8,128)(2,1)S(1)}, u32[]{:S(2)}, u32[]{:S(2)}) collective-permute-start(bf16[4,288,512]{2,1,0:T(8,128)(2,1)} %collective-permute-done.12.refs_1_), channel_id=1, source_target_pairs={{0,1},{1,0},{2,3},{3,2},{4,5},{5,4},{6,7},{7,6},{8,9},{9,8},{10,11... | collective-permute-start | bytes 3538952 | tf_op jit(solution)/shard_map/ppermute | solution.py:92
  201.6 8.0 %collective-permute-start.21 = (s32[2]{0:T(128)S(1)}, s32[2]{0:T(128)S(1)}, u32[]{:S(2)}, u32[]{:S(2)}) collective-permute-start(s32[2]{0:T(128)S(1)} %copy-done.125), channel_id=1, source_target_pairs={{0,8},{4,12},{8,0},{12,4},{16,24},{20,28},{24,16},{28,20},{1,9},{5... | collective-permute-start | bytes 32 | tf_op jit(solution)/shard_map/ppermute | solution.py:92
  228.0 39.0 %collective-permute-start.22 = (bf16[4,288,640]{2,1,0:T(8,128)(2,1)S(1)}, bf16[4,288,640]{2,1,0:T(8,128)(2,1)}, u32[]{:S(2)}, u32[]{:S(2)}) collective-permute-start(bf16[4,288,640]{2,1,0:T(8,128)(2,1)S(1)} %all-to-all-done.5.refs_0_), channel_id=1, source_target_pairs={{0,4},{4,0},{8,12},{12,8},{16,20},{20,16},{24,28},{28,24},{1,5},{5... | collective-permute-start | bytes 4423688 | tf_op jit(solution)/shard_map/ppermute | solution.py:92
  228.5 38.8 %collective-permute-start.23 = (bf16[4,288,640]{2,1,0:T(8,128)(2,1)S(1)}, bf16[4,288,640]{2,1,0:T(8,128)(2,1)}, u32[]{:S(2)}, u32[]{:S(2)}) collective-permute-start(bf16[4,288,640]{2,1,0:T(8,128)(2,1)S(1)} %all-to-all-done.5.refs_0_), channel_id=1, source_target_pairs={{0,1},{1,0},{2,3},{3,2},{4,5},{5,4},{6,7},{7,6},{8,9},{9,8},{10,11... | collective-permute-start | bytes 4423688 | tf_op jit(solution)/shard_map/ppermute | solution.py:92
  228.5 40.5 %all-to-all-start.6 = ((bf16[4,288,640]{2,1,0:T(8,128)(2,1)}), bf16[4,288,640]{2,1,0:T(8,128)(2,1)}, u32[]{:S(2)}, u32[]{:S(2)}) async-start(bf16[4,288,640]{2,1,0:T(8,128)(2,1)} %pad_maximum_fusion.3), calls=%async_computation.6 | async-start | bytes 2949120 | tf_op jit(solution)/shard_map/all_to_all | solution.py:102
  233.5 32.5 %collective-permute-start.24 = (bf16[4,288,512]{2,1,0:T(8,128)(2,1)S(1)}, bf16[4,288,512]{2,1,0:T(8,128)(2,1)S(1)}, u32[]{:S(2)}, u32[]{:S(2)}) collective-permute-start(bf16[4,288,512]{2,1,0:T(8,128)(2,1)S(1)} %collective-permute-done.17.refs_1_), channel_id=1, source_target_pairs={{0,1},{1,0},{2,3},{3,2},{4,5},{5,4},{6,7},{7,6},{8,9},{9,8},{10,11... | collective-permute-start | bytes 3538952 | tf_op jit(solution)/shard_map/ppermute | solution.py:92
  237.8 28.2 %collective-permute-start.25 = (bf16[160,2304]{1,0:T(8,128)(2,1)S(1)}, bf16[160,2304]{1,0:T(8,128)(2,1)S(1)}, u32[]{:S(2)}, u32[]{:S(2)}) collective-permute-start(bf16[160,2304]{1,0:T(8,128)(2,1)S(1)} %multiply_convert_fusion), channel_id=1, source_target_pairs={{0,2},{1,3},{2,0},{3,1},{4,6},{5,7},{6,4},{7,5},{8,10},{9,11},{10,... | collective-permute-start | bytes 2211848 | tf_op jit(solution)/shard_map/ppermute | solution.py:92
  238.7 27.2 %collective-permute-start.26 = (bf16[80,2304]{1,0:T(8,128)(2,1)S(1)}, bf16[80,2304]{1,0:T(8,128)(2,1)S(1)}, u32[]{:S(2)}, u32[]{:S(2)}) collective-permute-start(bf16[80,2304]{1,0:T(8,128)(2,1)S(1)} %slice.462), channel_id=1, source_target_pairs={{0,8},{4,12},{8,0},{12,4},{16,24},{20,28},{24,16},{28,20},{1,9},{5... | collective-permute-start | bytes 1105928 | tf_op jit(solution)/shard_map/ppermute | solution.py:92
  269.1 47.2 %all-to-all-start.7 = ((bf16[4,288,640]{2,1,0:T(8,128)(2,1)}), bf16[4,288,640]{2,1,0:T(8,128)(2,1)}, u32[]{:S(2)}, u32[]{:S(2)}) async-start(bf16[4,288,640]{2,1,0:T(8,128)(2,1)} %pad_maximum_fusion.4), calls=%async_computation.7 | async-start | bytes 2949120 | tf_op jit(solution)/shard_map/all_to_all | solution.py:102
  273.4 39.9 %collective-permute-start.27 = (bf16[4,288,640]{2,1,0:T(8,128)(2,1)}, bf16[4,288,640]{2,1,0:T(8,128)(2,1)}, u32[]{:S(2)}, u32[]{:S(2)}) collective-permute-start(bf16[4,288,640]{2,1,0:T(8,128)(2,1)} %all-to-all-done.6.refs_0_), channel_id=1, source_target_pairs={{0,4},{4,0},{8,12},{12,8},{16,20},{20,16},{24,28},{28,24},{1,5},{5... | collective-permute-start | bytes 4423688 | tf_op jit(solution)/shard_map/ppermute | solution.py:92
  275.0 38.4 %collective-permute-start.28 = (bf16[4,288,640]{2,1,0:T(8,128)(2,1)}, bf16[4,288,640]{2,1,0:T(8,128)(2,1)S(1)}, u32[]{:S(2)}, u32[]{:S(2)}) collective-permute-start(bf16[4,288,640]{2,1,0:T(8,128)(2,1)} %all-to-all-done.6.refs_0_), channel_id=1, source_target_pairs={{0,1},{1,0},{2,3},{3,2},{4,5},{5,4},{6,7},{7,6},{8,9},{9,8},{10,11... | collective-permute-start | bytes 4423688 | tf_op jit(solution)/shard_map/ppermute | solution.py:92
  275.0 40.2 %collective-permute-start.29 = (bf16[4,288,640]{2,1,0:T(8,128)(2,1)}, bf16[4,288,640]{2,1,0:T(8,128)(2,1)S(1)}, u32[]{:S(2)}, u32[]{:S(2)}) collective-permute-start(bf16[4,288,640]{2,1,0:T(8,128)(2,1)} %collective-permute-done.22.refs_1_), channel_id=1, source_target_pairs={{0,1},{1,0},{2,3},{3,2},{4,5},{5,4},{6,7},{7,6},{8,9},{9,8},{10,11... | collective-permute-start | bytes 4423688 | tf_op jit(solution)/shard_map/ppermute | solution.py:92
  277.8 29.6 %collective-permute-start.31 = (s32[4]{0:T(128)S(1)}, s32[4]{0:T(128)S(1)}, u32[]{:S(2)}, u32[]{:S(2)}) collective-permute-start(s32[4]{0:T(128)S(1)} %pad_add_fusion.4), channel_id=1, source_target_pairs={{0,4},{4,0},{8,12},{12,8},{16,20},{20,16},{24,28},{28,24},{1,5},{5... | collective-permute-start | bytes 56 | tf_op jit(solution)/shard_map/ppermute | solution.py:92
  278.4 34.9 %collective-permute-start.30 = (bf16[80,2304]{1,0:T(8,128)(2,1)S(1)}, bf16[80,2304]{1,0:T(8,128)(2,1)S(1)}, u32[]{:S(2)}, u32[]{:S(2)}) collective-permute-start(bf16[80,2304]{1,0:T(8,128)(2,1)S(1)} %slice.375), channel_id=1, source_target_pairs={{0,8},{4,12},{8,0},{12,4},{16,24},{20,28},{24,16},{28,20},{1,9},{5... | collective-permute-start | bytes 1105928 | tf_op jit(solution)/shard_map/ppermute | solution.py:92
  316.3 42.1 %collective-permute-start.32 = (bf16[4,288,640]{2,1,0:T(8,128)(2,1)}, bf16[4,288,640]{2,1,0:T(8,128)(2,1)}, u32[]{:S(2)}, u32[]{:S(2)}) collective-permute-start(bf16[4,288,640]{2,1,0:T(8,128)(2,1)} %all-to-all-done.7.refs_0_), channel_id=1, source_target_pairs={{0,4},{4,0},{8,12},{12,8},{16,20},{20,16},{24,28},{28,24},{1,5},{5... | collective-permute-start | bytes 4423688 | tf_op jit(solution)/shard_map/ppermute | solution.py:92
  317.8 40.6 %collective-permute-start.33 = (bf16[4,288,640]{2,1,0:T(8,128)(2,1)}, bf16[4,288,640]{2,1,0:T(8,128)(2,1)}, u32[]{:S(2)}, u32[]{:S(2)}) collective-permute-start(bf16[4,288,640]{2,1,0:T(8,128)(2,1)} %all-to-all-done.7.refs_0_), channel_id=1, source_target_pairs={{0,1},{1,0},{2,3},{3,2},{4,5},{5,4},{6,7},{7,6},{8,9},{9,8},{10,11... | collective-permute-start | bytes 4423688 | tf_op jit(solution)/shard_map/ppermute | solution.py:92
  317.8 40.6 %all-to-all-start.8 = ((bf16[4,288,512]{2,1,0:T(8,128)(2,1)}), bf16[4,288,512]{2,1,0:T(8,128)(2,1)}, u32[]{:S(2)}, u32[]{:S(2)}) async-start(bf16[4,288,512]{2,1,0:T(8,128)(2,1)} %pad_maximum_fusion.9), calls=%async_computation.8 | async-start | bytes 2359296 | tf_op jit(solution)/shard_map/all_to_all | solution.py:102
  322.9 35.5 %collective-permute-start.34 = (bf16[4,288,640]{2,1,0:T(8,128)(2,1)}, bf16[4,288,640]{2,1,0:T(8,128)(2,1)}, u32[]{:S(2)}, u32[]{:S(2)}) collective-permute-start(bf16[4,288,640]{2,1,0:T(8,128)(2,1)} %collective-permute-done.27.refs_1_), channel_id=1, source_target_pairs={{0,1},{1,0},{2,3},{3,2},{4,5},{5,4},{6,7},{7,6},{8,9},{9,8},{10,11... | collective-permute-start | bytes 4423688 | tf_op jit(solution)/shard_map/ppermute | solution.py:92
  323.3 18.7 %collective-permute-start.35 = (bf16[160,2304]{1,0:T(8,128)(2,1)S(1)}, bf16[160,2304]{1,0:T(8,128)(2,1)S(1)}, u32[]{:S(2)}, u32[]{:S(2)}) collective-permute-start(bf16[160,2304]{1,0:T(8,128)(2,1)S(1)} %pad_maximum_fusion.16), channel_id=1, source_target_pairs={{0,2},{1,3},{2,0},{3,1},{4,6},{5,7},{6,4},{7,5},{8,10},{9,11},{10,... | collective-permute-start | bytes 2211848 | tf_op jit(solution)/shard_map/ppermute | solution.py:92
  358.4 27.1 %collective-permute-start.38 = (bf16[4,288,640]{2,1,0:T(8,128)(2,1)}, bf16[4,288,640]{2,1,0:T(8,128)(2,1)}, u32[]{:S(2)}, u32[]{:S(2)}) collective-permute-start(bf16[4,288,640]{2,1,0:T(8,128)(2,1)} %collective-permute-done.32.refs_1_), channel_id=1, source_target_pairs={{0,1},{1,0},{2,3},{3,2},{4,5},{5,4},{6,7},{7,6},{8,9},{9,8},{10,11... | collective-permute-start | bytes 4423688 | tf_op jit(solution)/shard_map/ppermute | solution.py:92
  359.4 35.4 %collective-permute-start.36 = (bf16[4,288,512]{2,1,0:T(8,128)(2,1)}, bf16[4,288,512]{2,1,0:T(8,128)(2,1)}, u32[]{:S(2)}, u32[]{:S(2)}) collective-permute-start(bf16[4,288,512]{2,1,0:T(8,128)(2,1)} %all-to-all-done.8.refs_0_), channel_id=1, source_target_pairs={{0,4},{4,0},{8,12},{12,8},{16,20},{20,16},{24,28},{28,24},{1,5},{5... | collective-permute-start | bytes 3538952 | tf_op jit(solution)/shard_map/ppermute | solution.py:92
  359.9 34.9 %collective-permute-start.37 = (bf16[4,288,512]{2,1,0:T(8,128)(2,1)}, bf16[4,288,512]{2,1,0:T(8,128)(2,1)}, u32[]{:S(2)}, u32[]{:S(2)}) collective-permute-start(bf16[4,288,512]{2,1,0:T(8,128)(2,1)} %all-to-all-done.8.refs_0_), channel_id=1, source_target_pairs={{0,1},{1,0},{2,3},{3,2},{4,5},{5,4},{6,7},{7,6},{8,9},{9,8},{10,11... | collective-permute-start | bytes 3538952 | tf_op jit(solution)/shard_map/ppermute | solution.py:92
  409.6 19.0 %collective-permute-start.41 = (bf16[160,2304]{1,0:T(8,128)(2,1)S(1)}, bf16[160,2304]{1,0:T(8,128)(2,1)S(1)}, u32[]{:S(2)}, u32[]{:S(2)}) collective-permute-start(bf16[160,2304]{1,0:T(8,128)(2,1)S(1)} %get-tuple-element.325), channel_id=1, source_target_pairs={{0,8},{4,12},{8,0},{12,4},{16,24},{20,28},{24,16},{28,20},{1,9},{5... | collective-permute-start | bytes 2211848 | tf_op jit(solution)/shard_map/ppermute | solution.py:92
  411.6 18.4 %collective-permute-start.40 = (bf16[160,2304]{1,0:T(8,128)(2,1)S(1)}, bf16[160,2304]{1,0:T(8,128)(2,1)S(1)}, u32[]{:S(2)}, u32[]{:S(2)}) collective-permute-start(bf16[160,2304]{1,0:T(8,128)(2,1)S(1)} %get-tuple-element.323), channel_id=1, source_target_pairs={{0,2},{1,3},{2,0},{3,1},{4,6},{5,7},{6,4},{7,5},{8,10},{9,11},{10,... | collective-permute-start | bytes 2211848 | tf_op jit(solution)/shard_map/ppermute | solution.py:92
  430.2 9.7 %collective-permute-start.42 = (bf16[80,2304]{1,0:T(8,128)(2,1)S(1)}, bf16[80,2304]{1,0:T(8,128)(2,1)S(1)}, u32[]{:S(2)}, u32[]{:S(2)}) collective-permute-start(bf16[80,2304]{1,0:T(8,128)(2,1)S(1)} %fusion.22), channel_id=1, source_target_pairs={{0,8},{4,12},{8,0},{12,4},{16,24},{20,28},{24,16},{28,20},{1,9},{5... | collective-permute-start | bytes 1105928 | tf_op jit(solution)/shard_map/ppermute | solution.py:92
  430.8 9.7 %collective-permute-start.43 = (bf16[80,2304]{1,0:T(8,128)(2,1)S(1)}, bf16[80,2304]{1,0:T(8,128)(2,1)S(1)}, u32[]{:S(2)}, u32[]{:S(2)}) collective-permute-start(bf16[80,2304]{1,0:T(8,128)(2,1)S(1)} %fusion.23), channel_id=1, source_target_pairs={{0,2},{1,3},{2,0},{3,1},{4,6},{5,7},{6,4},{7,5},{8,10},{9,11},{10,... | collective-permute-start | bytes 1105928 | tf_op jit(solution)/shard_map/ppermute | solution.py:92
  443.3 16.7 %collective-permute-start.44 = (bf16[160,2304]{1,0:T(8,128)(2,1)S(1)}, bf16[160,2304]{1,0:T(8,128)(2,1)S(1)}, u32[]{:S(2)}, u32[]{:S(2)}) collective-permute-start(bf16[160,2304]{1,0:T(8,128)(2,1)S(1)} %get-tuple-element.427), channel_id=1, source_target_pairs={{0,2},{1,3},{2,0},{3,1},{4,6},{5,7},{6,4},{7,5},{8,10},{9,11},{10,... | collective-permute-start | bytes 2211848 | tf_op jit(solution)/shard_map/ppermute | solution.py:92
  443.7 16.4 %collective-permute-start.45 = (bf16[160,2304]{1,0:T(8,128)(2,1)S(1)}, bf16[160,2304]{1,0:T(8,128)(2,1)S(1)}, u32[]{:S(2)}, u32[]{:S(2)}) collective-permute-start(bf16[160,2304]{1,0:T(8,128)(2,1)S(1)} %get-tuple-element.427), channel_id=1, source_target_pairs={{0,8},{4,12},{8,0},{12,4},{16,24},{20,28},{24,16},{28,20},{1,9},{5... | collective-permute-start | bytes 2211848 | tf_op jit(solution)/shard_map/ppermute | solution.py:92
  517.6 14.6 %collective-permute-start.48 = (bf16[160,2304]{1,0:T(8,128)(2,1)S(1)}, bf16[160,2304]{1,0:T(8,128)(2,1)S(1)}, u32[]{:S(2)}, u32[]{:S(2)}) collective-permute-start(bf16[160,2304]{1,0:T(8,128)(2,1)S(1)} %copy-done.124), channel_id=1, source_target_pairs={{0,2},{1,3},{2,0},{3,1},{4,6},{5,7},{6,4},{7,5},{8,10},{9,11},{10,... | collective-permute-start | bytes 2211848 | tf_op jit(solution)/shard_map/ppermute | solution.py:92
  519.4 15.0 %collective-permute-start.49 = (bf16[160,2304]{1,0:T(8,128)(2,1)S(1)}, bf16[160,2304]{1,0:T(8,128)(2,1)S(1)}, u32[]{:S(2)}, u32[]{:S(2)}) collective-permute-start(bf16[160,2304]{1,0:T(8,128)(2,1)S(1)} %copy-done.123), channel_id=1, source_target_pairs={{0,8},{4,12},{8,0},{12,4},{16,24},{20,28},{24,16},{28,20},{1,9},{5... | collective-permute-start | bytes 2211848 | tf_op jit(solution)/shard_map/ppermute | solution.py:92
  550.3 15.7 %collective-permute-start.54 = (bf16[160,2304]{1,0:T(8,128)(2,1)S(1)}, bf16[160,2304]{1,0:T(8,128)(2,1)S(1)}, u32[]{:S(2)}, u32[]{:S(2)}) collective-permute-start(bf16[160,2304]{1,0:T(8,128)(2,1)S(1)} %subtract_convert_fusion), channel_id=1, source_target_pairs={{0,2},{1,3},{2,0},{3,1},{4,6},{5,7},{6,4},{7,5},{8,10},{9,11},{10,... | collective-permute-start | bytes 2211848 | tf_op jit(solution)/shard_map/ppermute | solution.py:92
  550.8 15.1 %collective-permute-start.55 = (bf16[2,96,1152]{2,1,0:T(8,128)(2,1)S(1)}, bf16[2,96,1152]{2,1,0:T(8,128)(2,1)S(1)}, u32[]{:S(2)}, u32[]{:S(2)}) collective-permute-start(bf16[2,96,1152]{2,1,0:T(8,128)(2,1)S(1)} %pad_maximum_fusion.23), channel_id=1, source_target_pairs={{0,16},{4,20},{8,24},{12,28},{16,0},{20,4},{24,8},{28,12},{1,17},{... | collective-permute-start | bytes 1327112 | tf_op jit(solution)/shard_map/ppermute | solution.py:92
  553.2 12.9 %collective-permute-start.56 = (bf16[3,16,2304]{2,1,0:T(8,128)(2,1)S(1)}, bf16[3,16,2304]{2,1,0:T(8,128)(2,1)S(1)}, u32[]{:S(2)}, u32[]{:S(2)}) collective-permute-start(bf16[3,16,2304]{2,1,0:T(8,128)(2,1)S(1)} %fusion.29), channel_id=1, source_target_pairs={{0,8},{4,12},{8,0},{12,4},{16,24},{20,28},{24,16},{28,20},{1,9},{5... | collective-permute-start | bytes 663560 | tf_op jit(solution)/shard_map/ppermute | solution.py:92
  579.2 8.2 %collective-permute-start.57 = (bf16[320,1024]{1,0:T(8,128)(2,1)S(1)}, bf16[320,1024]{1,0:T(8,128)(2,1)S(1)}, u32[]{:S(2)}, u32[]{:S(2)}) collective-permute-start(bf16[320,1024]{1,0:T(8,128)(2,1)S(1)} %pad_maximum_fusion.18), channel_id=1, source_target_pairs={{0,1},{1,0},{2,3},{3,2},{4,5},{5,4},{6,7},{7,6},{8,9},{9,8},{10,11... | collective-permute-start | bytes 1966088 | tf_op jit(solution)/shard_map/ppermute | solution.py:92
  579.3 31.3 %collective-permute-start.65 = (bf16[4,96,1152]{2,1,0:T(8,128)(2,1)S(1)}, bf16[4,96,1152]{2,1,0:T(8,128)(2,1)}, u32[]{:S(2)}, u32[]{:S(2)}) collective-permute-start(bf16[4,96,1152]{2,1,0:T(8,128)(2,1)S(1)} %pad_maximum_fusion.12), channel_id=1, source_target_pairs={{0,8},{4,12},{8,0},{12,4},{16,24},{20,28},{24,16},{28,20},{1,9},{5... | collective-permute-start | bytes 2654216 | tf_op jit(solution)/shard_map/ppermute | solution.py:92
  596.3 14.3 %collective-permute-start.63 = (bf16[4,16,2304]{2,1,0:T(8,128)(2,1)S(1)}, bf16[4,16,2304]{2,1,0:T(8,128)(2,1)S(1)}, u32[]{:S(2)}, u32[]{:S(2)}) collective-permute-start(bf16[4,16,2304]{2,1,0:T(8,128)(2,1)S(1)} %convert_element_type.257), channel_id=1, source_target_pairs={{0,2},{1,3},{2,0},{3,1},{4,6},{5,7},{6,4},{7,5},{8,10},{9,11},{10,... | collective-permute-start | bytes 884744 | tf_op jit(solution)/shard_map/ppermute | solution.py:92
  598.4 12.1 %collective-permute-start.64 = (bf16[2,16,3456]{2,1,0:T(8,128)(2,1)S(1)}, bf16[2,16,3456]{2,1,0:T(8,128)(2,1)S(1)}, u32[]{:S(2)}, u32[]{:S(2)}) collective-permute-start(bf16[2,16,3456]{2,1,0:T(8,128)(2,1)S(1)} %pad_maximum_fusion.29), channel_id=1, source_target_pairs={{0,16},{4,20},{8,24},{12,28},{16,0},{20,4},{24,8},{28,12},{1,17},{... | collective-permute-start | bytes 663560 | tf_op jit(solution)/shard_map/ppermute | solution.py:92
  612.1 45.7 %all-to-all-start.9 = ((bf16[8,16,6144]{2,1,0:T(8,128)(2,1)}), bf16[8,16,6144]{2,1,0:T(8,128)(2,1)S(1)}, u32[]{:S(2)}, u32[]{:S(2)}) async-start(bf16[8,16,6144]{2,1,0:T(8,128)(2,1)} %broadcast_in_dim.243), calls=%async_computation.9 | async-start | bytes 3145728 | tf_op jit(solution)/shard_map/all_to_all | solution.py:1052
  617.1 33.6 %collective-permute-start.67 = (bf16[4,16,3456]{2,1,0:T(8,128)(2,1)S(1)}, bf16[4,16,3456]{2,1,0:T(8,128)(2,1)S(1)}, u32[]{:S(2)}, u32[]{:S(2)}) collective-permute-start(bf16[4,16,3456]{2,1,0:T(8,128)(2,1)S(1)} %pad_maximum_fusion.24), channel_id=1, source_target_pairs={{0,8},{4,12},{8,0},{12,4},{16,24},{20,28},{24,16},{28,20},{1,9},{5... | collective-permute-start | bytes 1327112 | tf_op jit(solution)/shard_map/ppermute | solution.py:92
  620.7 30.1 %collective-permute-start.66 = (bf16[160,2304]{1,0:T(8,128)(2,1)S(1)}, bf16[160,2304]{1,0:T(8,128)(2,1)S(1)}, u32[]{:S(2)}, u32[]{:S(2)}) collective-permute-start(bf16[160,2304]{1,0:T(8,128)(2,1)S(1)} %slice.643), channel_id=1, source_target_pairs={{0,2},{1,3},{2,0},{3,1},{4,6},{5,7},{6,4},{7,5},{8,10},{9,11},{10,... | collective-permute-start | bytes 2211848 | tf_op jit(solution)/shard_map/ppermute | solution.py:92
  (152 other events, 887.2 us)

commit v4 on v3

--- a/solution.py
+++ b/solution.py
@@ -437,8 +437,10 @@
         def _():
             inner_grad = fdot(grad_ref[...], e_down_ref[...], ((1,), (1,)))
             inner_grad_ref[...] = low(inner_grad * keep_ref[:, :twice])
-
-        def one(place, begin, down, gate_in, up_in, s_down, e_gate, e_up, gate_w, up_w):
+            sums_ref[...] = jnp.zeros_like(sums_ref)
+
+        def one(i, down, gate_in, up_in, s_down, e_gate, e_up, gate_w, up_w):
+            place = pl.ds(pl.multiple_of(starts[i] + (step - firsts[i]) * tiles[i], 128), tiles[i])
             grad = fdot(grad_ref[...], down[...]) + fdot(inner_grad_ref[...], s_down[...])
             grad_gate = low(grad * gate_in[...].astype(jnp.float32))
             grad_up = low(grad * up_in[...].astype(jnp.float32))
@@ -446,18 +448,12 @@
             ups_ref[:, place] = grad_up
             first = fdot(grad_gate, e_gate[...], ((1,), (1,)))
             second = fdot(grad_up, e_up[...], ((1,), (1,)))
-            if begin:
-                sums_ref[:, :twice] = first
-                sums_ref[:, twice:] = second
-            else:
-                sums_ref[:, :twice] += first
-                sums_ref[:, twice:] += second
-
-        for k, (i, j) in enumerate(steps):
-            place = slice(starts[i] + j * tiles[i], starts[i] + (j + 1) * tiles[i])
-            pl.when(step == k)(
-                functools.partial(one, place, k == 0, *ins[i * each : (i + 1) * each])
-            )
+            sums_ref[:, :twice] += first
+            sums_ref[:, twice:] += second
+
+        for i in range(len(chunks)):
+            within = (step >= firsts[i]) & (step < firsts[i] + counts[i])
+            pl.when(within)(functools.partial(one, i, *ins[i * each : (i + 1) * each]))
 
         @pl.when(step == total - 1)
         def _():
@@ -540,24 +536,23 @@
     return jnp.concatenate([own, from_y, from_z] + diagonal)
 
 
-def sum_by_adapter(hots, gathered, shared, widths):
+def sum_by_adapter(ids, gathered, shared, widths):
     count, rows, columns = gathered.shape
-    adapters = hots.shape[1]
     cuts = [0, shared] + [shared + sum(widths[: i + 1]) for i in range(len(widths))]
 
-    def kernel(hots_ref, gathered_ref, *out_refs):
-        for i, out_ref in enumerate(out_refs):
-            here = slice(cuts[i], cuts[i + 1])
-            for adapter in range(adapters):
-                total = 0.0
-                for entry in range(count):
-                    total += hots_ref[entry, adapter] * gathered_ref[entry, :, here].astype(
-                        jnp.float32
-                    )
-                out_ref[adapter] = total.astype(out_ref.dtype)
-
-    shapes = [jax.ShapeDtypeStruct((adapters, rows, shared), jnp.bfloat16)] + [
-        jax.ShapeDtypeStruct((adapters, rows, width), jnp.float32) for width in widths
+    def kernel(ids_ref, gathered_ref, *refs):
+        out_refs, total_ref = refs[:-1], refs[-1]
+        total_refs = [total_ref] + list(out_refs[1:])
+        for ref in total_refs:
+            ref[...] = jnp.zeros_like(ref)
+        for entry in range(count):
+            adapter = ids_ref[entry]
+            for i, ref in enumerate(total_refs):
+                ref[adapter] += gathered_ref[entry, :, cuts[i] : cuts[i + 1]].astype(jnp.float32)
+        out_refs[0][...] = low(total_ref[...])
+
+    shapes = [jax.ShapeDtypeStruct((ADAPTERS, rows, shared), jnp.bfloat16)] + [
+        jax.ShapeDtypeStruct((ADAPTERS, rows, width), jnp.float32) for width in widths
     ]
     return pl.pallas_call(
         kernel,
@@ -567,9 +562,10 @@
             pl.BlockSpec(gathered.shape, lambda: (0, 0, 0)),
         ],
         out_specs=[pl.BlockSpec(shape.shape, lambda: (0, 0, 0)) for shape in shapes],
+        scratch_shapes=[pltpu.VMEM((ADAPTERS, rows, shared), jnp.float32)],
         compiler_params=pltpu.CompilerParams(vmem_limit_bytes=40 << 20),
         cost_estimate=TINY,
-    )(hots, gathered)
+    )(ids, gathered)
 
 
 def sum_unit_grads(hots, gathered, kinds):
@@ -581,7 +577,9 @@
         for side in range(2):
             for kind in range(kinds):
                 here = slice(kind * rank, (kind + 1) * rank)
-                for adapter in range(adapters):
+
+                @pl.loop(0, adapters)
+                def _(adapter):
                     total = 0.0
                     for entry in range(count):
                         total += hots_ref[side, entry, adapter] * gathered_ref[
@@ -648,8 +646,9 @@
 
 
 def tree_order(trees):
+    bits = tree_bits(trees)
     order = [0]
-    for bit in tree_bits(trees):
+    for bit in bits[-1:] + bits[:-1]:
         order += [i ^ bit for i in order]
     return order
 
@@ -767,14 +766,17 @@
     row_count = 2 * normed.shape[0]
     visible = low(visible[:row_count])
     cos_rows, sin_rows = cos_rows[:row_count], sin_rows[:row_count]
-    normed, near_ids, visible, cos_rows, sin_rows = close(
-        0, normed, near_ids, visible, cos_rows, sin_rows
+    ids_parts = [adapter_ids, flip(adapter_ids, "dp", 1)]
+    normed, near_ids, visible, cos_rows, sin_rows, ids_parts = close(
+        0, normed, near_ids, visible, cos_rows, sin_rows, ids_parts
     )
 
     transfers(1)
     normed_all = gather_pair(normed)
+    picks = jnp.concatenate([adapter_ids, near_ids, (my_z % 2).astype(jnp.int32)[None]])
+    normed_all, picks = settle(normed_all, picks)
     picked = pick_adapters(
-        jnp.concatenate([adapter_ids, near_ids, (my_z % 2).astype(jnp.int32)[None]]),
+        picks,
         [
             (stack, False)
             for stack in (
@@ -808,15 +810,23 @@
     s_gate_up = jnp.concatenate(picked[8:12])
     e_down = jnp.concatenate(picked[12:14])
     ffn_mine = jnp.concatenate(picked[14:20])
-    normed_all, attn_mine, e_output, s_gate_up, e_down, ffn_mine, s_qkv = close(
-        1, normed_all, attn_mine, e_output, s_gate_up, e_down, ffn_mine, s_qkv
+    for bit in tree_bits(trees)[:-2]:
+        tree_ids = jnp.concatenate(ids_parts)
+        ids_parts = [tree_ids, flip(tree_ids, "dp", bit)]
+    normed_all, attn_mine, e_output, s_gate_up, e_down, ffn_mine, s_qkv, ids_parts = close(
+        1, normed_all, attn_mine, e_output, s_gate_up, e_down, ffn_mine, s_qkv, ids_parts
     )
 
     transfers(2)
     attn_other = on_core(attn_mine)
     ffn_other = on_core(ffn_mine)
     inner_qkv = low(times_rows(normed_all, s_qkv))
-    attn_other, ffn_other, inner_qkv = close(2, attn_other, ffn_other, inner_qkv)
+    tree_ids = jnp.concatenate(ids_parts)
+    ids_parts = [tree_ids, flip(tree_ids, "dp", 2)]
+    attn_other, ffn_other, inner_qkv, ids_parts = close(
+        2, attn_other, ffn_other, inner_qkv, ids_parts
+    )
+    tree_ids = jnp.concatenate(ids_parts)
 
     transfers(3)
     heads_here = sum(widths)
@@ -841,11 +851,7 @@
     ]
     e_qkv, s_output, adapters_ab = close(3, e_qkv, s_output, adapters_ab)
 
-    bits = tree_bits(trees)
-    tree_ids = adapter_ids
     transfers(4)
-    for bit in bits[:-2]:
-        tree_ids = jnp.concatenate([tree_ids, flip(tree_ids, "dp", bit)])
     full_qkv = matrix(0, 1)
     projected = project_heads(
         normed_all, full_qkv, inner_qkv, e_qkv, cos_rows, sin_rows, queries
@@ -853,19 +859,16 @@
     received = on_core(
         beside(projected[:, heads_here + starts[1] :], projected[:, starts[1] : heads_here])
     )
-    full_qkv, projected, received, tree_ids = close(
-        4, full_qkv, projected, received, tree_ids
-    )
+    full_qkv, projected, received = close(4, full_qkv, projected, received)
 
     transfers(5)
     full_out_t = matrix(2)
-    tree_ids = jnp.concatenate([tree_ids, flip(tree_ids, "dp", bits[-2])])
     mixed_heads = attend(projected, received, visible, queries)
     inner_output = low(times_rows(mixed_heads, s_output))
     attn_part = times_rows(mixed_heads, full_out_t) + product(inner_output, e_output)
     attended = scatter_pair(attn_part)
-    mixed_heads, full_out_t, inner_output, attended, tree_ids = close(
-        5, mixed_heads, full_out_t, inner_output, attended, tree_ids
+    mixed_heads, full_out_t, inner_output, attended = close(
+        5, mixed_heads, full_out_t, inner_output, attended
     )
 
     transfers(6)
@@ -882,14 +885,17 @@
     transfers(7)
     normed_z_last = flip(normed_ffn[half_rows:], "dp", 2)
     full_up_b = matrix(4)
-    tree_ids = jnp.concatenate([tree_ids, flip(tree_ids, "dp", bits[-1])])
-    normed_z_last, full_up_b, tree_ids = close(7, normed_z_last, full_up_b, tree_ids)
+    normed_zy_first = flip(normed_z_first, "tensor", 2)
+    normed_z_last, normed_zy_first, full_up_b = close(
+        7, normed_z_last, normed_zy_first, full_up_b
+    )
 
     transfers(8)
-    normed_z = jnp.concatenate([normed_z_first, normed_z_last])
-    normed_zy = flip(normed_z, "tensor", 2)
+    normed_zy_last = flip(normed_z_last, "tensor", 2)
     full_gate_a = matrix(5)
-    ffn_rows = jnp.concatenate([normed_ffn, normed_y, normed_z, normed_zy])
+    ffn_rows = jnp.concatenate(
+        [normed_ffn, normed_y, normed_z_first, normed_z_last, normed_zy_first, normed_zy_last]
+    )
     block_rows = residual.shape[0]
     row_block = jnp.arange(4 * block_rows, dtype=jnp.int32) // block_rows
     row_near = (row_block // 2)[:, None]
@@ -1010,7 +1016,9 @@
         from_core, grad_queries, grad_pairs, shared_mine
     )
 
-    shared_all = with_bit(shared_mine[None], 1)
+    shared_all = shared_mine[None]
+    for bit in bits[:-2]:
+        shared_all = with_bit(shared_all, bit)
     grad_expand_output = over_rows(inner_output, grad_attn)
     grad_shrink_output = over_rows(grad_inner_output, mixed_heads)
     grad_pairs = grad_pairs[:row_count] + from_core.astype(jnp.float32)
@@ -1043,8 +1051,7 @@
     )
 
     last_y = flip(low(last), "tensor", 2)
-    for bit in bits[:-2]:
-        shared_all = with_bit(shared_all, bit)
+    shared_all = with_bit(shared_all, bits[-2])
     part = times_rows(grad_qkv, full_qkv) + product(grad_inner_qkv, s_qkv)
     last_y, part, shared_all, local_near = settle(last_y, part, shared_all, local_near)
 
@@ -1053,7 +1060,7 @@
         jnp.broadcast_to(last_mine[None], (trees,) + last_mine.shape), "dp", 0, 0
     )
     from_y = flip(low(part[block_rows:]), "tensor", 2)
-    shared_all = with_bit(shared_all, bits[-2])
+    shared_all = with_bit(shared_all, 1)
     from_y, shared_all = settle(from_y, shared_all)
     grad_normed = part[:block_rows] + from_y.astype(jnp.float32)
     input_grad = grad_resid + rms_back(own_rows, norm_gain[0], grad_normed)
@@ -1071,15 +1078,12 @@
         ),
         axis=1,
     )
-    hot_trees = jnp.sum(
+    ids_trees = jnp.sum(
         jnp.where(
-            at[:, None, None] == jnp.arange(trees, dtype=jnp.int32)[None, :, None],
-            hot_near[None],
-            0.0,
+            at[:, None] == jnp.arange(trees, dtype=jnp.int32)[None, :], tree_ids[None, :], 0
         ),
         axis=1,
     )
-
     order_local = [0, 1]
     for bit in bits[:-1]:
         order_local += [i ^ bit for i in order_local]
@@ -1093,11 +1097,11 @@
     parity = jnp.asarray(crossing, jnp.int32) ^ (my_z % 2).astype(jnp.int32)
     local_all = local_all.reshape(2 * trees, 3 * rank, units)
     hots = jnp.stack([jnp.where(parity[:, None] == side, hots, 0.0) for side in range(2)])
-    hots_local = jnp.stack([hot_near[ids_at[j]] for j in order_local])
+    ids_shared = tree_ids.reshape(2, trees // 4, 2).transpose(2, 0, 1).reshape(trees)
     out_expand_gate, out_expand_up, out_shrink_down = sum_unit_grads(hots, local_all, 3)
     core = (my_part % 2).astype(jnp.int32)[None]
     depth_half = s_qkv.shape[1] // 2
-    (sums,) = sum_by_adapter(hots_local, shared_all, 3 * depth_half, [])
+    (sums,) = sum_by_adapter(ids_shared, shared_all, 3 * depth_half, [])
     out_shrink_gate, out_shrink_up, out_expand_down = join_halves(core, sums, on_core(sums), 3)
     (last_all, input_grad, out_expand_gate, out_expand_up, out_shrink_down, out_shrink_gate,
      out_shrink_up, out_expand_down) = settle(
@@ -1105,7 +1109,7 @@
         out_shrink_up, out_expand_down,
     )
     sums, out_expand_query, out_expand_key, out_expand_value, out_shrink_output = sum_by_adapter(
-        hot_trees, last_all, 4 * depth_half, widths + widths[:1]
+        ids_trees, last_all, 4 * depth_half, widths + widths[:1]
     )
     out_shrink_query, out_shrink_key, out_shrink_value, out_expand_output = join_halves(
         core, sums, on_core(sums), 4

time: 677 us -> 666 us (0.984)
  waiting for transfers between devices: 265 us -> 252 us
    ppermute x70 -> x71, waiting for transfers between devices: 245 us -> 221 us  [flip(): return lax.ppermute(values, axis_name, [(i, i ^ bit) for i in range(size)])]
    ppermute x70 -> x71, starting transfers between devices: 56.6 us -> 65.2 us  [flip(): return lax.ppermute(values, axis_name, [(i, i ^ bit) for i in range(size)])]
    all_to_all x9, waiting for transfers between devices: 19.4 us -> 27.7 us  [along_z(): return lax.all_to_all(sent, 'dp', 0, 0, axis_index_groups=lines)]
    unnamed x287 -> x312, local copies, waits for them, and re-layouts: 61.7 us -> 61.9 us
  transfers between devices with their start and end apart: 80 -> 81, of which waited for: 37 -> 39; matrix products, arithmetic and copies ran while one was open for 13% -> 15% of each run, Pallas kernels for 11% -> 12%
where the time goes in v4:
time: 666 us; the launch traced here: 657 us
  waiting for transfers between devices  252 us (38%)
  Pallas kernels  129 us (19%)
  starting transfers between devices  109 us (16%)
  local copies, waits for them, and re-layouts  84.2 us (13%)
  other arithmetic  44.5 us (7%)
  matrix products  34.4 us (5%)
    ppermute x71, waiting for transfers between devices, flip(): return lax.ppermute(values, axis_name, [(i, i ^ bit) for i in range(size)])  221 us
    ppermute x71, starting transfers between devices, flip(): return lax.ppermute(values, axis_name, [(i, i ^ bit) for i in range(size)])  65.2 us
    unnamed x312, local copies, waits for them, and re-layouts  61.9 us
    all_to_all x9, starting transfers between devices, along_z(): return lax.all_to_all(sent, 'dp', 0, 0, axis_index_groups=lines)  40 us
    pallas_call x1, Pallas kernels, feed_forward_back(): pl.pallas_call(kernel, out_shape=parts + [jax.ShapeDtypeStruct((count, tw...  39.1 us
    all_to_all x9, waiting for transfers between devices, along_z(): return lax.all_to_all(sent, 'dp', 0, 0, axis_index_groups=lines)  27.7 us
    pallas_call x2, Pallas kernels, gate_and_up(): pl.pallas_call(kernel, out_shape=[jax.ShapeDtypeStruct((count, units), jn...  26 us
    pallas_call x8, Pallas kernels, assemble(): pl.pallas_call(kernel, out_shape=jax.ShapeDtypeStruct((2 * columns_z, row...  22.7 us
  transfers between devices with their start and end apart: 81, of which 39 were waited for; matrix products, arithmetic and copies ran while one was open for 15% of the time, Pallas kernels for 12%

profile of v4, /device:TPU:0, one launch (start us, length us, event | category | flops | bytes accessed | tf_op | source)
XLA Modules:
  0.0 656.5 jit_solution(16480787719621471414)
XLA Ops:
  0.6 3.1 collective-permute-start
  10.0 4.0 all-to-all-start
  18.2 23.8 %all-to-all-done.refs_0_ = bf16[4,144,1024]{2,1,0:T(8,128)(2,1)S(1)} async-done(((bf16[4,144,1024]{2,1,0:T(8,128)(2,1)}), bf16[4,144,1024]{2,1,0:T(8,128)(2,1)S(1)}, u32[]{:S(2)}, u32[]{:S(2)}) %all-to-all-start) | async-done | bytes 1179680 | tf_op jit(solution)/shard_map/all_to_all | solution.py:102
  42.0 2.3 concatenate.176
  47.9 4.3 all-to-all-start.1
  53.4 8.5 %collective-permute-done.4 = bf16[160,2304]{1,0:T(8,128)(2,1)} collective-permute-done((bf16[160,2304]{1,0:T(8,128)(2,1)S(1)}, bf16[160,2304]{1,0:T(8,128)(2,1)}, u32[]{:S(2)}, u32[]{:S(2)}) %collective-permute-start.4) | collective-permute-done | bytes 737312 | tf_op jit(solution)/shard_map/ppermute | solution.py:92
  63.3 3.0 shard_map.387
  83.8 3.5 all-to-all-start.2
  95.0 11.7 %collective-permute-done.11 = s32[4]{0:T(128)} collective-permute-done((s32[4]{0:T(128)S(1)}, s32[4]{0:T(128)}, u32[]{:S(2)}, u32[]{:S(2)}) %collective-permute-start.11) | collective-permute-done | bytes 48 | tf_op jit(solution)/shard_map/ppermute | solution.py:92
  108.0 7.2 %collective-permute-done.6.refs_5_ = bf16[4,144,1024]{2,1,0:T(8,128)(2,1)S(1)} collective-permute-done((bf16[4,144,1024]{2,1,0:T(8,128)(2,1)}, bf16[4,144,1024]{2,1,0:T(8,128)(2,1)S(1)}, u32[]{:S(2)}, u32[]{:S(2)}) %collective-permute-start.6) | collective-permute-done | bytes 1179680 | tf_op jit(solution)/shard_map/ppermute | solution.py:92
  118.2 4.7 all-to-all-start.3
  133.3 17.7 %collective-permute-done.12.refs_1_ = bf16[4,288,512]{2,1,0:T(8,128)(2,1)} collective-permute-done((bf16[4,288,512]{2,1,0:T(8,128)(2,1)S(1)}, bf16[4,288,512]{2,1,0:T(8,128)(2,1)}, u32[]{:S(2)}, u32[]{:S(2)}) %collective-permute-start.12) | collective-permute-done | bytes 1179680 | tf_op jit(solution)/shard_map/ppermute | solution.py:92
  153.0 4.9 all-to-all-start.4
  165.0 3.0 shard_map.388
  168.0 6.5 shard_map.389.mine_ref
  178.6 4.6 collective-permute-done.15.refs_1_
  183.9 4.2 all-to-all-start.5
  189.2 3.0 shard_map.390
  194.8 2.5 shard_map.391
  203.5 13.1 %collective-permute-done.22 = bf16[160,2304]{1,0:T(8,128)(2,1)S(1)} collective-permute-done((bf16[160,2304]{1,0:T(8,128)(2,1)S(1)}, bf16[160,2304]{1,0:T(8,128)(2,1)S(1)}, u32[]{:S(2)}, u32[]{:S(2)}) %collective-permute-start.22) | collective-permute-done | bytes 737312 | tf_op jit(solution)/shard_map/ppermute | solution.py:92
  217.9 8.7 %collective-permute-done.19.refs_1_ = bf16[4,288,512]{2,1,0:T(8,128)(2,1)S(1)} collective-permute-done((bf16[4,288,512]{2,1,0:T(8,128)(2,1)}, bf16[4,288,512]{2,1,0:T(8,128)(2,1)S(1)}, u32[]{:S(2)}, u32[]{:S(2)}) %collective-permute-start.19) | collective-permute-done | bytes 1179680 | tf_op jit(solution)/shard_map/ppermute | solution.py:92
  231.6 4.9 all-to-all-start.6
  245.5 2.8 shard_map.392
  250.5 18.5 %collective-permute-done.27 = bf16[80,2304]{1,0:T(8,128)(2,1)S(1)} collective-permute-done((bf16[80,2304]{1,0:T(8,128)(2,1)S(1)}, bf16[80,2304]{1,0:T(8,128)(2,1)S(1)}, u32[]{:S(2)}, u32[]{:S(2)}) %collective-permute-start.27) | collective-permute-done | bytes 368672 | tf_op jit(solution)/shard_map/ppermute | solution.py:92
  272.2 4.3 all-to-all-start.7
  288.8 19.3 %collective-permute-done.31 = bf16[80,2304]{1,0:T(8,128)(2,1)S(1)} collective-permute-done((bf16[80,2304]{1,0:T(8,128)(2,1)S(1)}, bf16[80,2304]{1,0:T(8,128)(2,1)S(1)}, u32[]{:S(2)}, u32[]{:S(2)}) %collective-permute-start.31) | collective-permute-done | bytes 368672 | tf_op jit(solution)/shard_map/ppermute | solution.py:92
  308.1 2.3 collective-permute-done.28.refs_1_
  312.8 5.2 all-to-all-start.8
  323.1 2.8 shard_map.395
  325.9 2.5 copy-done
  332.1 3.4 fusion.15.inner_ref
  335.5 11.9 %shard_map.394 = (bf16[640,1024]{1,0:T(8,128)(2,1)}, bf16[640,1024]{1,0:T(8,128)(2,1)}, bf16[640,1024]{1,0:T(8,128)(2,1)}) custom-call(bf16[640,2304]{1,0:T(8,128)(2,1)} %constant_dynamic-update-slice_fusion.9.rows_ref, bf16[2304,1024]{1,0:T(8,128)(2,1)} %bitcast.161, bf16[2304,1024]{1,0:T(8,128)(2,1)} %bitcast.163, bf16[640,64]{1,0:T(8,128)(2,1)} %fusion.15.inner_ref, ...), custom_call_target="tpu_custom_call" | custom-call | flops 1 | bytes 1 | tf_op jit(solution)/shard_map/pallas_call | solution.py:351
  347.4 4.1 collective-permute-done.33.refs_1_
  354.6 3.1 shard_map.396
  357.7 2.4 copy-done.1
  360.2 14.0 %shard_map.397 = (bf16[640,1280]{1,0:T(8,128)(2,1)}, bf16[640,1280]{1,0:T(8,128)(2,1)}, bf16[640,1280]{1,0:T(8,128)(2,1)}) custom-call(bf16[640,2304]{1,0:T(8,128)(2,1)} %constant_dynamic-update-slice_fusion.9.rows_ref, bf16[2304,1280]{1,0:T(8,128)(2,1)} %bitcast.157, bf16[2304,1280]{1,0:T(8,128)(2,1)} %bitcast.159, bf16[640,64]{1,0:T(8,128)(2,1)} %fusion.15.inner_ref, ...), custom_call_target="tpu_custom_call" | custom-call | flops 1 | bytes 1 | tf_op jit(solution)/shard_map/pallas_call | solution.py:351
  378.7 3.5 shard_map.398
  382.2 5.8 convolution_add_fusion.first_ref
  388.4 2.8 collective-permute-done.40.refs_3_
  391.1 2.8 shard_map.399
  396.1 6.9 %shard_map.400 = (f32[160,2304]{1,0:T(8,128)S(1)}, f32[80,2304]{1,0:T(8,128)S(1)}, f32[80,2304]{1,0:T(8,128)S(1)}, bf16[160,2304]{1,0:T(8,128)(2,1)S(1)}, bf16[160,2304]{1,0:T(8,128)(2,1)S(1)}) custom-call(f32[640,2304]{1,0:T(8,128)} %convolution_add_fusion.first_ref, bf16[640,1024]{1,0:T(8,128)(2,1)S(1)} %copy-done.11, bf16[2304,1024]{1,0:T(8,128)(2,1)} %bitcast.165), custom_call_target="tpu_custom_call" | custom-call | flops 1 | bytes 1 | tf_op jit(solution)/shard_map/pallas_call | solution.py:398
  406.3 15.5 %collective-permute-done.41 = bf16[160,2304]{1,0:T(8,128)(2,1)S(1)} collective-permute-done((bf16[160,2304]{1,0:T(8,128)(2,1)S(1)}, bf16[160,2304]{1,0:T(8,128)(2,1)S(1)}, u32[]{:S(2)}, u32[]{:S(2)}) %collective-permute-start.41) | collective-permute-done | bytes 737312 | tf_op jit(solution)/shard_map/ppermute | solution.py:92
  425.4 7.4 %collective-permute-done.43 = bf16[80,2304]{1,0:T(8,128)(2,1)S(1)} collective-permute-done((bf16[80,2304]{1,0:T(8,128)(2,1)S(1)}, bf16[80,2304]{1,0:T(8,128)(2,1)S(1)}, u32[]{:S(2)}, u32[]{:S(2)}) %collective-permute-start.43) | collective-permute-done | bytes 368672 | tf_op jit(solution)/shard_map/ppermute | solution.py:92
  440.3 13.2 %collective-permute-done.45 = bf16[160,2304]{1,0:T(8,128)(2,1)S(1)} collective-permute-done((bf16[160,2304]{1,0:T(8,128)(2,1)S(1)}, bf16[160,2304]{1,0:T(8,128)(2,1)S(1)}, u32[]{:S(2)}, u32[]{:S(2)}) %collective-permute-start.45) | collective-permute-done | bytes 737312 | tf_op jit(solution)/shard_map/ppermute | solution.py:92
  458.0 4.2 collective-permute-done.47
  463.8 39.1 %shard_map.401 = (f32[160,2304]{1,0:T(8,128)}, f32[80,2304]{1,0:T(8,128)}, f32[80,2304]{1,0:T(8,128)}, bf16[160,2304]{1,0:T(8,128)(2,1)}, bf16[160,2304]{1,0:T(8...) custom-call(bf16[640,2304]{1,0:T(8,128)(2,1)} %constant_dynamic-upda, ...), custom_call_target="tpu_custom_call" | custom-call | flops 1 | bytes 1 | tf_op jit(solution)/shard_map/pallas_call | solution.py:488
  502.9 2.6 fusion.33
  513.1 10.7 %collective-permute-done.49 = bf16[160,2304]{1,0:T(8,128)(2,1)S(1)} collective-permute-done((bf16[160,2304]{1,0:T(8,128)(2,1)S(1)}, bf16[160,2304]{1,0:T(8,128)(2,1)S(1)}, u32[]{:S(2)}, u32[]{:S(2)}) %collective-permute-start.49) | collective-permute-done | bytes 737312 | tf_op jit(solution)/shard_map/ppermute | solution.py:92
  524.1 2.5 fusion.68
  532.6 4.5 collective-permute-done.52
  543.8 2.9 collective-permute-start.56
  549.1 11.0 %collective-permute-done.56 = bf16[2,96,1152]{2,1,0:T(8,128)(2,1)S(1)} collective-permute-done((bf16[2,96,1152]{2,1,0:T(8,128)(2,1)S(1)}, bf16[2,96,1152]{2,1,0:T(8,128)(2,1)S(1)}, u32[]{:S(2)}, u32[]{:S(2)}) %collective-permute-start.56) | collective-permute-done | bytes 442400 | tf_op jit(solution)/shard_map/ppermute | solution.py:92
  563.9 6.5 shard_map.402
  575.2 5.8 collective-permute-done.60
  583.6 3.0 collective-permute-start.63
  587.9 7.3 %collective-permute-done.63 = bf16[1,16,3456]{2,1,0:T(8,128)(2,1)S(1)} collective-permute-done((bf16[1,16,3456]{2,1,0:T(8,128)(2,1)S(1)}, bf16[1,16,3456]{2,1,0:T(8,128)(2,1)S(1)}, u32[]{:S(2)}, u32[]{:S(2)}) %collective-permute-start.63) | collective-permute-done | bytes 110624 | tf_op jit(solution)/shard_map/ppermute | solution.py:92
  595.3 3.8 collective-permute-start.65
  601.3 5.0 convolution_add_fusion.1
  609.5 3.6 all-to-all-start.9
  620.9 8.4 %shard_map.403 = (f32[8,16,2304]{2,1,0:T(8,128)}, f32[8,16,2304]{2,1,0:T(8,128)}, f32[8,16,2304]{2,1,0:T(8,128)}) custom-call(f32[2,16,8]{2,1,0:T(8,128)S(1)} %pad_maximum_fusion.37.hots_ref, bf16[16,48,1152]{2,1,0:T(8,128)(2,1)S(1)} %bitcast.173), custom_call_target="tpu_custom_call" | custom-call | flops 1 | bytes 1 | tf_op jit(solution)/shard_map/pallas_call | solution.py:590
  629.3 11.2 %collective-permute-done.68 = bf16[4,16,3456]{2,1,0:T(8,128)(2,1)S(1)} collective-permute-done((bf16[4,16,3456]{2,1,0:T(8,128)(2,1)S(1)}, bf16[4,16,3456]{2,1,0:T(8,128)(2,1)S(1)}, u32[]{:S(2)}, u32[]{:S(2)}) %collective-permute-start.68) | collective-permute-done | bytes 442400 | tf_op jit(solution)/shard_map/ppermute | solution.py:92
  646.5 2.6 all-to-all-done.9.gathered_ref
  650.9 2.8 collective-permute-done.70.other_ref
  653.8 2.3 shard_map.407
  (641 shorter events, 209.2 us)
Async XLA Ops:
  0.6 17.6 %collective-permute-start = (s32[1]{0:T(128)}, s32[1]{0:T(128)}, u32[]{:S(2)}, u32[]{:S(2)}) collective-permute-start(s32[1]{0:T(128)} %param.52), channel_id=1, source_target_pairs={{0,8},{4,12},{8,0},{12,4},{16,24},{20,28},{24,16},{28,20},{1,9},{5... | collective-permute-start | bytes 20 | tf_op jit(solution)/shard_map/ppermute | solution.py:92
  3.7 14.5 %collective-permute-start.1 = (s32[1]{0:T(128)}, s32[1]{0:T(128)}, u32[]{:S(2)}, u32[]{:S(2)}) collective-permute-start(s32[1]{0:T(128)} %param.52), channel_id=1, source_target_pairs={{0,4},{4,0},{8,12},{12,8},{16,20},{20,16},{24,28},{28,24},{1,5},{5... | collective-permute-start | bytes 20 | tf_op jit(solution)/shard_map/ppermute | solution.py:92
  10.0 32.0 %all-to-all-start = ((bf16[4,144,1024]{2,1,0:T(8,128)(2,1)}), bf16[4,144,1024]{2,1,0:T(8,128)(2,1)S(1)}, u32[]{:S(2)}, u32[]{:S(2)}) async-start(bf16[4,144,1024]{2,1,0:T(8,128)(2,1)} %concatenate.175), calls=%async_computation | async-start | bytes 2359296 | tf_op jit(solution)/shard_map/all_to_all | solution.py:102
  44.3 17.6 %collective-permute-start.4 = (bf16[160,2304]{1,0:T(8,128)(2,1)S(1)}, bf16[160,2304]{1,0:T(8,128)(2,1)}, u32[]{:S(2)}, u32[]{:S(2)}) collective-permute-start(bf16[160,2304]{1,0:T(8,128)(2,1)S(1)} %fusion.7), channel_id=1, source_target_pairs={{0,2},{1,3},{2,0},{3,1},{4,6},{5,7},{6,4},{7,5},{8,10},{9,11},{10,... | collective-permute-start | bytes 2211848 | tf_op jit(solution)/shard_map/ppermute | solution.py:92
  46.5 33.9 %collective-permute-start.2 = (bf16[4,144,1024]{2,1,0:T(8,128)(2,1)S(1)}, bf16[4,144,1024]{2,1,0:T(8,128)(2,1)}, u32[]{:S(2)}, u32[]{:S(2)}) collective-permute-start(bf16[4,144,1024]{2,1,0:T(8,128)(2,1)S(1)} %all-to-all-done.refs_0_), channel_id=1, source_target_pairs={{0,4},{4,0},{8,12},{12,8},{16,20},{20,16},{24,28},{28,24},{1,5},{5... | collective-permute-start | bytes 3538952 | tf_op jit(solution)/shard_map/ppermute | solution.py:92
  47.1 33.3 %collective-permute-start.3 = (bf16[4,144,1024]{2,1,0:T(8,128)(2,1)S(1)}, bf16[4,144,1024]{2,1,0:T(8,128)(2,1)}, u32[]{:S(2)}, u32[]{:S(2)}) collective-permute-start(bf16[4,144,1024]{2,1,0:T(8,128)(2,1)S(1)} %all-to-all-done.refs_0_), channel_id=1, source_target_pairs={{0,1},{1,0},{2,3},{3,2},{4,5},{5,4},{6,7},{7,6},{8,9},{9,8},{10,11... | collective-permute-start | bytes 3538952 | tf_op jit(solution)/shard_map/ppermute | solution.py:92
  47.8 32.5 %collective-permute-start.5 = (s32[2]{0:T(128)S(1)}, s32[2]{0:T(128)S(1)}, u32[]{:S(2)}, u32[]{:S(2)}) collective-permute-start(s32[2]{0:T(128)S(1)} %pad_add_fusion.3), channel_id=1, source_target_pairs={{0,16},{4,20},{8,24},{12,28},{16,0},{20,4},{24,8},{28,12},{1,17},{... | collective-permute-start | bytes 32 | tf_op jit(solution)/shard_map/ppermute | solution.py:92
  47.9 33.8 %all-to-all-start.1 = ((bf16[4,144,1024]{2,1,0:T(8,128)(2,1)}), bf16[4,144,1024]{2,1,0:T(8,128)(2,1)}, u32[]{:S(2)}, u32[]{:S(2)}) async-start(bf16[4,144,1024]{2,1,0:T(8,128)(2,1)} %concatenate.176), calls=%async_computation.1 | async-start | bytes 2359296 | tf_op jit(solution)/shard_map/all_to_all | solution.py:102
  83.8 34.5 %all-to-all-start.2 = ((bf16[4,288,512]{2,1,0:T(8,128)(2,1)}), bf16[4,288,512]{2,1,0:T(8,128)(2,1)S(1)}, u32[]{:S(2)}, u32[]{:S(2)}) async-start(bf16[4,288,512]{2,1,0:T(8,128)(2,1)} %concatenate.177), calls=%async_computation.2 | async-start | bytes 2359296 | tf_op jit(solution)/shard_map/all_to_all | solution.py:102
  87.3 27.9 %collective-permute-start.6 = (bf16[4,144,1024]{2,1,0:T(8,128)(2,1)}, bf16[4,144,1024]{2,1,0:T(8,128)(2,1)S(1)}, u32[]{:S(2)}, u32[]{:S(2)}) collective-permute-start(bf16[4,144,1024]{2,1,0:T(8,128)(2,1)} %all-to-all-done.1.refs_4_), channel_id=1, source_target_pairs={{0,4},{4,0},{8,12},{12,8},{16,20},{20,16},{24,28},{28,24},{1,5},{5... | collective-permute-start | bytes 3538952 | tf_op jit(solution)/shard_map/ppermute | solution.py:92
  88.9 26.3 %collective-permute-start.7 = (bf16[4,144,1024]{2,1,0:T(8,128)(2,1)}, bf16[4,144,1024]{2,1,0:T(8,128)(2,1)S(1)}, u32[]{:S(2)}, u32[]{:S(2)}) collective-permute-start(bf16[4,144,1024]{2,1,0:T(8,128)(2,1)} %all-to-all-done.1.refs_4_), channel_id=1, source_target_pairs={{0,1},{1,0},{2,3},{3,2},{4,5},{5,4},{6,7},{7,6},{8,9},{9,8},{10,11... | collective-permute-start | bytes 3538952 | tf_op jit(solution)/shard_map/ppermute | solution.py:92
  88.9 28.3 %collective-permute-start.8 = (bf16[4,144,1024]{2,1,0:T(8,128)(2,1)}, bf16[4,144,1024]{2,1,0:T(8,128)(2,1)S(1)}, u32[]{:S(2)}, u32[]{:S(2)}) collective-permute-start(bf16[4,144,1024]{2,1,0:T(8,128)(2,1)} %collective-permute-done.2.refs_1_), channel_id=1, source_target_pairs={{0,1},{1,0},{2,3},{3,2},{4,5},{5,4},{6,7},{7,6},{8,9},{9,8},{10,11... | collective-permute-start | bytes 3538952 | tf_op jit(solution)/shard_map/ppermute | solution.py:92
  93.1 13.6 %collective-permute-start.11 = (s32[4]{0:T(128)S(1)}, s32[4]{0:T(128)}, u32[]{:S(2)}, u32[]{:S(2)}) collective-permute-start(s32[4]{0:T(128)S(1)} %pad_add_fusion.4), channel_id=1, source_target_pairs={{0,8},{4,12},{8,0},{12,4},{16,24},{20,28},{24,16},{28,20},{1,9},{5... | collective-permute-start | bytes 56 | tf_op jit(solution)/shard_map/ppermute | solution.py:92
  95.0 13.0 %collective-permute-start.10 = (bf16[96,1152]{1,0:T(8,128)(2,1)}, bf16[96,1152]{1,0:T(8,128)(2,1)S(1)}, u32[]{:S(2)}, u32[]{:S(2)}) collective-permute-start(bf16[96,1152]{1,0:T(8,128)(2,1)} %constant_dynamic-update-slice_fusion.3), channel_id=1, source_target_pairs={{0,1},{1,0},{2,3},{3,2},{4,5},{5,4},{6,7},{7,6},{8,9},{9,8},{10,11... | collective-permute-start | bytes 663560 | tf_op jit(solution)/shard_map/ppermute | solution.py:92
  118.2 34.7 %all-to-all-start.3 = ((bf16[4,288,512]{2,1,0:T(8,128)(2,1)}), bf16[4,288,512]{2,1,0:T(8,128)(2,1)}, u32[]{:S(2)}, u32[]{:S(2)}) async-start(bf16[4,288,512]{2,1,0:T(8,128)(2,1)} %pad_maximum_fusion.7), calls=%async_computation.3 | async-start | bytes 2359296 | tf_op jit(solution)/shard_map/all_to_all | solution.py:102
  124.5 26.5 %collective-permute-start.12 = (bf16[4,288,512]{2,1,0:T(8,128)(2,1)S(1)}, bf16[4,288,512]{2,1,0:T(8,128)(2,1)}, u32[]{:S(2)}, u32[]{:S(2)}) collective-permute-start(bf16[4,288,512]{2,1,0:T(8,128)(2,1)S(1)} %all-to-all-done.2.refs_0_), channel_id=1, source_target_pairs={{0,4},{4,0},{8,12},{12,8},{16,20},{20,16},{24,28},{28,24},{1,5},{5... | collective-permute-start | bytes 3538952 | tf_op jit(solution)/shard_map/ppermute | solution.py:92
  126.0 24.9 %collective-permute-start.13 = (bf16[4,288,512]{2,1,0:T(8,128)(2,1)S(1)}, bf16[4,288,512]{2,1,0:T(8,128)(2,1)S(1)}, u32[]{:S(2)}, u32[]{:S(2)}) collective-permute-start(bf16[4,288,512]{2,1,0:T(8,128)(2,1)S(1)} %all-to-all-done.2.refs_0_), channel_id=1, source_target_pairs={{0,1},{1,0},{2,3},{3,2},{4,5},{5,4},{6,7},{7,6},{8,9},{9,8},{10,11... | collective-permute-start | bytes 3538952 | tf_op jit(solution)/shard_map/ppermute | solution.py:92
  126.1 25.9 %collective-permute-start.14 = (bf16[4,144,1024]{2,1,0:T(8,128)(2,1)S(1)}, bf16[4,144,1024]{2,1,0:T(8,128)(2,1)S(1)}, u32[]{:S(2)}, u32[]{:S(2)}) collective-permute-start(bf16[4,144,1024]{2,1,0:T(8,128)(2,1)S(1)} %copy-done.38), channel_id=1, source_target_pairs={{0,1},{1,0},{2,3},{3,2},{4,5},{5,4},{6,7},{7,6},{8,9},{9,8},{10,11... | collective-permute-start | bytes 3538952 | tf_op jit(solution)/shard_map/ppermute | solution.py:92
  153.0 30.9 %all-to-all-start.4 = ((bf16[4,288,512]{2,1,0:T(8,128)(2,1)}), bf16[4,288,512]{2,1,0:T(8,128)(2,1)}, u32[]{:S(2)}, u32[]{:S(2)}) async-start(bf16[4,288,512]{2,1,0:T(8,128)(2,1)} %pad_maximum_fusion.8), calls=%async_computation.4 | async-start | bytes 2359296 | tf_op jit(solution)/shard_map/all_to_all | solution.py:102
  157.9 25.3 %collective-permute-start.15 = (bf16[4,288,512]{2,1,0:T(8,128)(2,1)}, bf16[4,288,512]{2,1,0:T(8,128)(2,1)}, u32[]{:S(2)}, u32[]{:S(2)}) collective-permute-start(bf16[4,288,512]{2,1,0:T(8,128)(2,1)} %all-to-all-done.3.refs_0_), channel_id=1, source_target_pairs={{0,4},{4,0},{8,12},{12,8},{16,20},{20,16},{24,28},{28,24},{1,5},{5... | collective-permute-start | bytes 3538952 | tf_op jit(solution)/shard_map/ppermute | solution.py:92
  159.4 23.8 %collective-permute-start.16 = (bf16[4,288,512]{2,1,0:T(8,128)(2,1)}, bf16[4,288,512]{2,1,0:T(8,128)(2,1)}, u32[]{:S(2)}, u32[]{:S(2)}) collective-permute-start(bf16[4,288,512]{2,1,0:T(8,128)(2,1)} %all-to-all-done.3.refs_0_), channel_id=1, source_target_pairs={{0,1},{1,0},{2,3},{3,2},{4,5},{5,4},{6,7},{7,6},{8,9},{9,8},{10,11... | collective-permute-start | bytes 3538952 | tf_op jit(solution)/shard_map/ppermute | solution.py:92
  159.4 23.8 %collective-permute-start.17 = (bf16[4,288,512]{2,1,0:T(8,128)(2,1)}, bf16[4,288,512]{2,1,0:T(8,128)(2,1)}, u32[]{:S(2)}, u32[]{:S(2)}) collective-permute-start(bf16[4,288,512]{2,1,0:T(8,128)(2,1)} %collective-permute-done.12.refs_1_), channel_id=1, source_target_pairs={{0,1},{1,0},{2,3},{3,2},{4,5},{5,4},{6,7},{7,6},{8,9},{9,8},{10,11... | collective-permute-start | bytes 3538952 | tf_op jit(solution)/shard_map/ppermute | solution.py:92
  183.9 44.6 %all-to-all-start.5 = ((bf16[4,288,640]{2,1,0:T(8,128)(2,1)}), bf16[4,288,640]{2,1,0:T(8,128)(2,1)S(1)}, u32[]{:S(2)}, u32[]{:S(2)}) async-start(bf16[4,288,640]{2,1,0:T(8,128)(2,1)} %pad_maximum_fusion.2), calls=%async_computation.5 | async-start | bytes 2949120 | tf_op jit(solution)/shard_map/all_to_all | solution.py:102
  199.5 17.1 %collective-permute-start.22 = (bf16[160,2304]{1,0:T(8,128)(2,1)S(1)}, bf16[160,2304]{1,0:T(8,128)(2,1)S(1)}, u32[]{:S(2)}, u32[]{:S(2)}) collective-permute-start(bf16[160,2304]{1,0:T(8,128)(2,1)S(1)} %slice.636), channel_id=1, source_target_pairs={{0,2},{1,3},{2,0},{3,1},{4,6},{5,7},{6,4},{7,5},{8,10},{9,11},{10,... | collective-permute-start | bytes 2211848 | tf_op jit(solution)/shard_map/ppermute | solution.py:92
  200.1 26.5 %collective-permute-start.19 = (bf16[4,288,512]{2,1,0:T(8,128)(2,1)}, bf16[4,288,512]{2,1,0:T(8,128)(2,1)S(1)}, u32[]{:S(2)}, u32[]{:S(2)}) collective-permute-start(bf16[4,288,512]{2,1,0:T(8,128)(2,1)} %all-to-all-done.4.refs_0_), channel_id=1, source_target_pairs={{0,4},{4,0},{8,12},{12,8},{16,20},{20,16},{24,28},{28,24},{1,5},{5... | collective-permute-start | bytes 3538952 | tf_op jit(solution)/shard_map/ppermute | solution.py:92
  201.6 25.0 %collective-permute-start.20 = (bf16[4,288,512]{2,1,0:T(8,128)(2,1)}, bf16[4,288,512]{2,1,0:T(8,128)(2,1)S(1)}, u32[]{:S(2)}, u32[]{:S(2)}) collective-permute-start(bf16[4,288,512]{2,1,0:T(8,128)(2,1)} %all-to-all-done.4.refs_0_), channel_id=1, source_target_pairs={{0,1},{1,0},{2,3},{3,2},{4,5},{5,4},{6,7},{7,6},{8,9},{9,8},{10,11... | collective-permute-start | bytes 3538952 | tf_op jit(solution)/shard_map/ppermute | solution.py:92
  201.6 26.0 %collective-permute-start.21 = (bf16[4,288,512]{2,1,0:T(8,128)(2,1)}, bf16[4,288,512]{2,1,0:T(8,128)(2,1)S(1)}, u32[]{:S(2)}, u32[]{:S(2)}) collective-permute-start(bf16[4,288,512]{2,1,0:T(8,128)(2,1)} %collective-permute-done.15.refs_1_), channel_id=1, source_target_pairs={{0,1},{1,0},{2,3},{3,2},{4,5},{5,4},{6,7},{7,6},{8,9},{9,8},{10,11... | collective-permute-start | bytes 3538952 | tf_op jit(solution)/shard_map/ppermute | solution.py:92
  228.6 41.5 %collective-permute-start.23 = (bf16[4,288,640]{2,1,0:T(8,128)(2,1)S(1)}, bf16[4,288,640]{2,1,0:T(8,128)(2,1)}, u32[]{:S(2)}, u32[]{:S(2)}) collective-permute-start(bf16[4,288,640]{2,1,0:T(8,128)(2,1)S(1)} %all-to-all-done.5.refs_0_), channel_id=1, source_target_pairs={{0,4},{4,0},{8,12},{12,8},{16,20},{20,16},{24,28},{28,24},{1,5},{5... | collective-permute-start | bytes 4423688 | tf_op jit(solution)/shard_map/ppermute | solution.py:92
  230.1 40.3 %collective-permute-start.24 = (bf16[4,288,640]{2,1,0:T(8,128)(2,1)S(1)}, bf16[4,288,640]{2,1,0:T(8,128)(2,1)}, u32[]{:S(2)}, u32[]{:S(2)}) collective-permute-start(bf16[4,288,640]{2,1,0:T(8,128)(2,1)S(1)} %all-to-all-done.5.refs_0_), channel_id=1, source_target_pairs={{0,1},{1,0},{2,3},{3,2},{4,5},{5,4},{6,7},{7,6},{8,9},{9,8},{10,11... | collective-permute-start | bytes 4423688 | tf_op jit(solution)/shard_map/ppermute | solution.py:92
  231.6 40.6 %all-to-all-start.6 = ((bf16[4,288,640]{2,1,0:T(8,128)(2,1)}), bf16[4,288,640]{2,1,0:T(8,128)(2,1)}, u32[]{:S(2)}, u32[]{:S(2)}) async-start(bf16[4,288,640]{2,1,0:T(8,128)(2,1)} %pad_maximum_fusion.3), calls=%async_computation.6 | async-start | bytes 2949120 | tf_op jit(solution)/shard_map/all_to_all | solution.py:102
  237.1 32.0 %collective-permute-start.25 = (bf16[4,288,512]{2,1,0:T(8,128)(2,1)S(1)}, bf16[4,288,512]{2,1,0:T(8,128)(2,1)S(1)}, u32[]{:S(2)}, u32[]{:S(2)}) collective-permute-start(bf16[4,288,512]{2,1,0:T(8,128)(2,1)S(1)} %collective-permute-done.19.refs_1_), channel_id=1, source_target_pairs={{0,1},{1,0},{2,3},{3,2},{4,5},{5,4},{6,7},{7,6},{8,9},{9,8},{10,11... | collective-permute-start | bytes 3538952 | tf_op jit(solution)/shard_map/ppermute | solution.py:92
  239.6 29.4 %collective-permute-start.26 = (bf16[160,2304]{1,0:T(8,128)(2,1)S(1)}, bf16[160,2304]{1,0:T(8,128)(2,1)S(1)}, u32[]{:S(2)}, u32[]{:S(2)}) collective-permute-start(bf16[160,2304]{1,0:T(8,128)(2,1)S(1)} %multiply_convert_fusion), channel_id=1, source_target_pairs={{0,2},{1,3},{2,0},{3,1},{4,6},{5,7},{6,4},{7,5},{8,10},{9,11},{10,... | collective-permute-start | bytes 2211848 | tf_op jit(solution)/shard_map/ppermute | solution.py:92
  241.2 27.8 %collective-permute-start.27 = (bf16[80,2304]{1,0:T(8,128)(2,1)S(1)}, bf16[80,2304]{1,0:T(8,128)(2,1)S(1)}, u32[]{:S(2)}, u32[]{:S(2)}) collective-permute-start(bf16[80,2304]{1,0:T(8,128)(2,1)S(1)} %slice.454), channel_id=1, source_target_pairs={{0,8},{4,12},{8,0},{12,4},{16,24},{20,28},{24,16},{28,20},{1,9},{5... | collective-permute-start | bytes 1105928 | tf_op jit(solution)/shard_map/ppermute | solution.py:92
  272.2 40.6 %all-to-all-start.7 = ((bf16[4,288,640]{2,1,0:T(8,128)(2,1)}), bf16[4,288,640]{2,1,0:T(8,128)(2,1)}, u32[]{:S(2)}, u32[]{:S(2)}) async-start(bf16[4,288,640]{2,1,0:T(8,128)(2,1)} %pad_maximum_fusion.4), calls=%async_computation.7 | async-start | bytes 2949120 | tf_op jit(solution)/shard_map/all_to_all | solution.py:102
  276.5 34.0 %collective-permute-start.28 = (bf16[4,288,640]{2,1,0:T(8,128)(2,1)}, bf16[4,288,640]{2,1,0:T(8,128)(2,1)}, u32[]{:S(2)}, u32[]{:S(2)}) collective-permute-start(bf16[4,288,640]{2,1,0:T(8,128)(2,1)} %all-to-all-done.6.refs_0_), channel_id=1, source_target_pairs={{0,4},{4,0},{8,12},{12,8},{16,20},{20,16},{24,28},{28,24},{1,5},{5... | collective-permute-start | bytes 4423688 | tf_op jit(solution)/shard_map/ppermute | solution.py:92
  277.1 33.4 %collective-permute-start.29 = (bf16[4,288,640]{2,1,0:T(8,128)(2,1)}, bf16[4,288,640]{2,1,0:T(8,128)(2,1)S(1)}, u32[]{:S(2)}, u32[]{:S(2)}) collective-permute-start(bf16[4,288,640]{2,1,0:T(8,128)(2,1)} %all-to-all-done.6.refs_0_), channel_id=1, source_target_pairs={{0,1},{1,0},{2,3},{3,2},{4,5},{5,4},{6,7},{7,6},{8,9},{9,8},{10,11... | collective-permute-start | bytes 4423688 | tf_op jit(solution)/shard_map/ppermute | solution.py:92
  277.1 34.6 %collective-permute-start.30 = (bf16[4,288,640]{2,1,0:T(8,128)(2,1)}, bf16[4,288,640]{2,1,0:T(8,128)(2,1)S(1)}, u32[]{:S(2)}, u32[]{:S(2)}) collective-permute-start(bf16[4,288,640]{2,1,0:T(8,128)(2,1)} %collective-permute-done.23.refs_1_), channel_id=1, source_target_pairs={{0,1},{1,0},{2,3},{3,2},{4,5},{5,4},{6,7},{7,6},{8,9},{9,8},{10,11... | collective-permute-start | bytes 4423688 | tf_op jit(solution)/shard_map/ppermute | solution.py:92
  280.0 28.1 %collective-permute-start.31 = (bf16[80,2304]{1,0:T(8,128)(2,1)S(1)}, bf16[80,2304]{1,0:T(8,128)(2,1)S(1)}, u32[]{:S(2)}, u32[]{:S(2)}) collective-permute-start(bf16[80,2304]{1,0:T(8,128)(2,1)S(1)} %slice.367), channel_id=1, source_target_pairs={{0,8},{4,12},{8,0},{12,4},{16,24},{20,28},{24,16},{28,20},{1,9},{5... | collective-permute-start | bytes 1105928 | tf_op jit(solution)/shard_map/ppermute | solution.py:92
  282.0 26.1 %collective-permute-start.32 = (bf16[80,2304]{1,0:T(8,128)(2,1)S(1)}, bf16[80,2304]{1,0:T(8,128)(2,1)S(1)}, u32[]{:S(2)}, u32[]{:S(2)}) collective-permute-start(bf16[80,2304]{1,0:T(8,128)(2,1)S(1)} %copy-done.100), channel_id=1, source_target_pairs={{0,2},{1,3},{2,0},{3,1},{4,6},{5,7},{6,4},{7,5},{8,10},{9,11},{10,... | collective-permute-start | bytes 1105928 | tf_op jit(solution)/shard_map/ppermute | solution.py:92
  312.8 38.8 %all-to-all-start.8 = ((bf16[4,288,512]{2,1,0:T(8,128)(2,1)}), bf16[4,288,512]{2,1,0:T(8,128)(2,1)}, u32[]{:S(2)}, u32[]{:S(2)}) async-start(bf16[4,288,512]{2,1,0:T(8,128)(2,1)} %pad_maximum_fusion.9), calls=%async_computation.8 | async-start | bytes 2359296 | tf_op jit(solution)/shard_map/all_to_all | solution.py:102
  319.0 32.6 %collective-permute-start.33 = (bf16[4,288,640]{2,1,0:T(8,128)(2,1)}, bf16[4,288,640]{2,1,0:T(8,128)(2,1)}, u32[]{:S(2)}, u32[]{:S(2)}) collective-permute-start(bf16[4,288,640]{2,1,0:T(8,128)(2,1)} %all-to-all-done.7.refs_0_), channel_id=1, source_target_pairs={{0,4},{4,0},{8,12},{12,8},{16,20},{20,16},{24,28},{28,24},{1,5},{5... | collective-permute-start | bytes 4423688 | tf_op jit(solution)/shard_map/ppermute | solution.py:92
  319.5 32.0 %collective-permute-start.34 = (bf16[4,288,640]{2,1,0:T(8,128)(2,1)}, bf16[4,288,640]{2,1,0:T(8,128)(2,1)}, u32[]{:S(2)}, u32[]{:S(2)}) collective-permute-start(bf16[4,288,640]{2,1,0:T(8,128)(2,1)} %all-to-all-done.7.refs_0_), channel_id=1, source_target_pairs={{0,1},{1,0},{2,3},{3,2},{4,5},{5,4},{6,7},{7,6},{8,9},{9,8},{10,11... | collective-permute-start | bytes 4423688 | tf_op jit(solution)/shard_map/ppermute | solution.py:92
  319.5 32.0 %collective-permute-start.35 = (bf16[4,288,640]{2,1,0:T(8,128)(2,1)}, bf16[4,288,640]{2,1,0:T(8,128)(2,1)}, u32[]{:S(2)}, u32[]{:S(2)}) collective-permute-start(bf16[4,288,640]{2,1,0:T(8,128)(2,1)} %collective-permute-done.28.refs_1_), channel_id=1, source_target_pairs={{0,1},{1,0},{2,3},{3,2},{4,5},{5,4},{6,7},{7,6},{8,9},{9,8},{10,11... | collective-permute-start | bytes 4423688 | tf_op jit(solution)/shard_map/ppermute | solution.py:92
  320.8 10.5 %collective-permute-start.36 = (bf16[80,2304]{1,0:T(8,128)(2,1)S(1)}, bf16[80,2304]{1,0:T(8,128)(2,1)S(1)}, u32[]{:S(2)}, u32[]{:S(2)}) collective-permute-start(bf16[80,2304]{1,0:T(8,128)(2,1)S(1)} %copy-done.103), channel_id=1, source_target_pairs={{0,2},{1,3},{2,0},{3,1},{4,6},{5,7},{6,4},{7,5},{8,10},{9,11},{10,... | collective-permute-start | bytes 1105928 | tf_op jit(solution)/shard_map/ppermute | solution.py:92
  351.5 27.1 %collective-permute-start.39 = (bf16[4,288,640]{2,1,0:T(8,128)(2,1)}, bf16[4,288,640]{2,1,0:T(8,128)(2,1)}, u32[]{:S(2)}, u32[]{:S(2)}) collective-permute-start(bf16[4,288,640]{2,1,0:T(8,128)(2,1)} %collective-permute-done.33.refs_1_), channel_id=1, source_target_pairs={{0,1},{1,0},{2,3},{3,2},{4,5},{5,4},{6,7},{7,6},{8,9},{9,8},{10,11... | collective-permute-start | bytes 4423688 | tf_op jit(solution)/shard_map/ppermute | solution.py:92
  352.5 35.5 %collective-permute-start.37 = (bf16[4,288,512]{2,1,0:T(8,128)(2,1)}, bf16[4,288,512]{2,1,0:T(8,128)(2,1)}, u32[]{:S(2)}, u32[]{:S(2)}) collective-permute-start(bf16[4,288,512]{2,1,0:T(8,128)(2,1)} %all-to-all-done.8.refs_0_), channel_id=1, source_target_pairs={{0,4},{4,0},{8,12},{12,8},{16,20},{20,16},{24,28},{28,24},{1,5},{5... | collective-permute-start | bytes 3538952 | tf_op jit(solution)/shard_map/ppermute | solution.py:92
  353.0 35.0 %collective-permute-start.38 = (bf16[4,288,512]{2,1,0:T(8,128)(2,1)}, bf16[4,288,512]{2,1,0:T(8,128)(2,1)}, u32[]{:S(2)}, u32[]{:S(2)}) collective-permute-start(bf16[4,288,512]{2,1,0:T(8,128)(2,1)} %all-to-all-done.8.refs_0_), channel_id=1, source_target_pairs={{0,1},{1,0},{2,3},{3,2},{4,5},{5,4},{6,7},{7,6},{8,9},{9,8},{10,11... | collective-permute-start | bytes 3538952 | tf_op jit(solution)/shard_map/ppermute | solution.py:92
  403.0 18.8 %collective-permute-start.41 = (bf16[160,2304]{1,0:T(8,128)(2,1)S(1)}, bf16[160,2304]{1,0:T(8,128)(2,1)S(1)}, u32[]{:S(2)}, u32[]{:S(2)}) collective-permute-start(bf16[160,2304]{1,0:T(8,128)(2,1)S(1)} %get-tuple-element.334), channel_id=1, source_target_pairs={{0,2},{1,3},{2,0},{3,1},{4,6},{5,7},{6,4},{7,5},{8,10},{9,11},{10,... | collective-permute-start | bytes 2211848 | tf_op jit(solution)/shard_map/ppermute | solution.py:92
  404.6 18.4 %collective-permute-start.42 = (bf16[160,2304]{1,0:T(8,128)(2,1)S(1)}, bf16[160,2304]{1,0:T(8,128)(2,1)S(1)}, u32[]{:S(2)}, u32[]{:S(2)}) collective-permute-start(bf16[160,2304]{1,0:T(8,128)(2,1)S(1)} %get-tuple-element.336), channel_id=1, source_target_pairs={{0,8},{4,12},{8,0},{12,4},{16,24},{20,28},{24,16},{28,20},{1,9},{5... | collective-permute-start | bytes 2211848 | tf_op jit(solution)/shard_map/ppermute | solution.py:92
  423.1 9.7 %collective-permute-start.43 = (bf16[80,2304]{1,0:T(8,128)(2,1)S(1)}, bf16[80,2304]{1,0:T(8,128)(2,1)S(1)}, u32[]{:S(2)}, u32[]{:S(2)}) collective-permute-start(bf16[80,2304]{1,0:T(8,128)(2,1)S(1)} %fusion.22), channel_id=1, source_target_pairs={{0,8},{4,12},{8,0},{12,4},{16,24},{20,28},{24,16},{28,20},{1,9},{5... | collective-permute-start | bytes 1105928 | tf_op jit(solution)/shard_map/ppermute | solution.py:92
  437.1 16.4 %collective-permute-start.45 = (bf16[160,2304]{1,0:T(8,128)(2,1)S(1)}, bf16[160,2304]{1,0:T(8,128)(2,1)S(1)}, u32[]{:S(2)}, u32[]{:S(2)}) collective-permute-start(bf16[160,2304]{1,0:T(8,128)(2,1)S(1)} %get-tuple-element.439), channel_id=1, source_target_pairs={{0,2},{1,3},{2,0},{3,1},{4,6},{5,7},{6,4},{7,5},{8,10},{9,11},{10,... | collective-permute-start | bytes 2211848 | tf_op jit(solution)/shard_map/ppermute | solution.py:92
  437.9 16.6 %collective-permute-start.46 = (bf16[160,2304]{1,0:T(8,128)(2,1)S(1)}, bf16[160,2304]{1,0:T(8,128)(2,1)S(1)}, u32[]{:S(2)}, u32[]{:S(2)}) collective-permute-start(bf16[160,2304]{1,0:T(8,128)(2,1)S(1)} %get-tuple-element.439), channel_id=1, source_target_pairs={{0,8},{4,12},{8,0},{12,4},{16,24},{20,28},{24,16},{28,20},{1,9},{5... | collective-permute-start | bytes 2211848 | tf_op jit(solution)/shard_map/ppermute | solution.py:92
  509.2 14.6 %collective-permute-start.49 = (bf16[160,2304]{1,0:T(8,128)(2,1)S(1)}, bf16[160,2304]{1,0:T(8,128)(2,1)S(1)}, u32[]{:S(2)}, u32[]{:S(2)}) collective-permute-start(bf16[160,2304]{1,0:T(8,128)(2,1)S(1)} %copy-done.134), channel_id=1, source_target_pairs={{0,2},{1,3},{2,0},{3,1},{4,6},{5,7},{6,4},{7,5},{8,10},{9,11},{10,... | collective-permute-start | bytes 2211848 | tf_op jit(solution)/shard_map/ppermute | solution.py:92
  510.3 13.8 %collective-permute-start.50 = (bf16[160,2304]{1,0:T(8,128)(2,1)S(1)}, bf16[160,2304]{1,0:T(8,128)(2,1)S(1)}, u32[]{:S(2)}, u32[]{:S(2)}) collective-permute-start(bf16[160,2304]{1,0:T(8,128)(2,1)S(1)} %copy-done.133), channel_id=1, source_target_pairs={{0,8},{4,12},{8,0},{12,4},{16,24},{20,28},{24,16},{28,20},{1,9},{5... | collective-permute-start | bytes 2211848 | tf_op jit(solution)/shard_map/ppermute | solution.py:92
  543.8 16.3 %collective-permute-start.56 = (bf16[2,96,1152]{2,1,0:T(8,128)(2,1)S(1)}, bf16[2,96,1152]{2,1,0:T(8,128)(2,1)S(1)}, u32[]{:S(2)}, u32[]{:S(2)}) collective-permute-start(bf16[2,96,1152]{2,1,0:T(8,128)(2,1)S(1)} %pad_maximum_fusion.22), channel_id=1, source_target_pairs={{0,16},{4,20},{8,24},{12,28},{16,0},{20,4},{24,8},{28,12},{1,17},{... | collective-permute-start | bytes 1327112 | tf_op jit(solution)/shard_map/ppermute | solution.py:92
  546.7 13.5 %collective-permute-start.55 = (bf16[160,2304]{1,0:T(8,128)(2,1)S(1)}, bf16[160,2304]{1,0:T(8,128)(2,1)S(1)}, u32[]{:S(2)}, u32[]{:S(2)}) collective-permute-start(bf16[160,2304]{1,0:T(8,128)(2,1)S(1)} %subtract_convert_fusion), channel_id=1, source_target_pairs={{0,2},{1,3},{2,0},{3,1},{4,6},{5,7},{6,4},{7,5},{8,10},{9,11},{10,... | collective-permute-start | bytes 2211848 | tf_op jit(solution)/shard_map/ppermute | solution.py:92
  548.1 12.2 %collective-permute-start.57 = (bf16[3,16,2304]{2,1,0:T(8,128)(2,1)S(1)}, bf16[3,16,2304]{2,1,0:T(8,128)(2,1)S(1)}, u32[]{:S(2)}, u32[]{:S(2)}) collective-permute-start(bf16[3,16,2304]{2,1,0:T(8,128)(2,1)S(1)} %fusion.29), channel_id=1, source_target_pairs={{0,8},{4,12},{8,0},{12,4},{16,24},{20,28},{24,16},{28,20},{1,9},{5... | collective-permute-start | bytes 663560 | tf_op jit(solution)/shard_map/ppermute | solution.py:92
  563.8 9.6 %collective-permute-start.59 = (bf16[3,16,2304]{2,1,0:T(8,128)(2,1)S(1)}, bf16[3,16,2304]{2,1,0:T(8,128)(2,1)S(1)}, u32[]{:S(2)}, u32[]{:S(2)}) collective-permute-start(bf16[3,16,2304]{2,1,0:T(8,128)(2,1)S(1)} %fusion.35), channel_id=1, source_target_pairs={{0,1},{1,0},{2,3},{3,2},{4,5},{5,4},{6,7},{7,6},{8,9},{9,8},{10,11... | collective-permute-start | bytes 663560 | tf_op jit(solution)/shard_map/ppermute | solution.py:92
  573.4 32.9 %collective-permute-start.66 = (bf16[4,96,1152]{2,1,0:T(8,128)(2,1)S(1)}, bf16[4,96,1152]{2,1,0:T(8,128)(2,1)}, u32[]{:S(2)}, u32[]{:S(2)}) collective-permute-start(bf16[4,96,1152]{2,1,0:T(8,128)(2,1)S(1)} %pad_maximum_fusion.12), channel_id=1, source_target_pairs={{0,8},{4,12},{8,0},{12,4},{16,24},{20,28},{24,16},{28,20},{1,9},{5... | collective-permute-start | bytes 2654216 | tf_op jit(solution)/shard_map/ppermute | solution.py:92
  583.6 11.6 %collective-permute-start.63 = (bf16[1,16,3456]{2,1,0:T(8,128)(2,1)S(1)}, bf16[1,16,3456]{2,1,0:T(8,128)(2,1)S(1)}, u32[]{:S(2)}, u32[]{:S(2)}) collective-permute-start(bf16[1,16,3456]{2,1,0:T(8,128)(2,1)S(1)} %bitcast.191), channel_id=1, source_target_pairs={{0,16},{4,20},{8,24},{12,28},{16,0},{20,4},{24,8},{28,12},{1,17},{... | collective-permute-start | bytes 331784 | tf_op jit(solution)/shard_map/ppermute | solution.py:92
  595.3 10.9 %collective-permute-start.65 = (bf16[2,16,3456]{2,1,0:T(8,128)(2,1)S(1)}, bf16[2,16,3456]{2,1,0:T(8,128)(2,1)S(1)}, u32[]{:S(2)}, u32[]{:S(2)}) collective-permute-start(bf16[2,16,3456]{2,1,0:T(8,128)(2,1)S(1)} %pad_maximum_fusion.28), channel_id=1, source_target_pairs={{0,8},{4,12},{8,0},{12,4},{16,24},{20,28},{24,16},{28,20},{1,9},{5... | collective-permute-start | bytes 663560 | tf_op jit(solution)/shard_map/ppermute | solution.py:92
  609.5 39.5 %all-to-all-start.9 = ((bf16[8,16,6144]{2,1,0:T(8,128)(2,1)}), bf16[8,16,6144]{2,1,0:T(8,128)(2,1)S(1)}, u32[]{:S(2)}, u32[]{:S(2)}) async-start(bf16[8,16,6144]{2,1,0:T(8,128)(2,1)} %broadcast_in_dim.229), calls=%async_computation.9 | async-start | bytes 3145728 | tf_op jit(solution)/shard_map/all_to_all | solution.py:1059
  614.2 26.3 %collective-permute-start.68 = (bf16[4,16,3456]{2,1,0:T(8,128)(2,1)S(1)}, bf16[4,16,3456]{2,1,0:T(8,128)(2,1)S(1)}, u32[]{:S(2)}, u32[]{:S(2)}) collective-permute-start(bf16[4,16,3456]{2,1,0:T(8,128)(2,1)S(1)} %pad_maximum_fusion.23), channel_id=1, source_target_pairs={{0,4},{4,0},{8,12},{12,8},{16,20},{20,16},{24,28},{28,24},{1,5},{5... | collective-permute-start | bytes 1327112 | tf_op jit(solution)/shard_map/ppermute | solution.py:92
  618.0 22.6 %collective-permute-start.67 = (bf16[160,2304]{1,0:T(8,128)(2,1)S(1)}, bf16[160,2304]{1,0:T(8,128)(2,1)S(1)}, u32[]{:S(2)}, u32[]{:S(2)}) collective-permute-start(bf16[160,2304]{1,0:T(8,128)(2,1)S(1)} %slice.635), channel_id=1, source_target_pairs={{0,2},{1,3},{2,0},{3,1},{4,6},{5,7},{6,4},{7,5},{8,10},{9,11},{10,... | collective-permute-start | bytes 2211848 | tf_op jit(solution)/shard_map/ppermute | solution.py:92
  (165 other events, 1058.3 us)

commit v5 on v4

--- a/solution.py
+++ b/solution.py
@@ -272,7 +272,8 @@
     count = projected.shape[0]
     wide, pair = (queries + 2) * HEAD_WIDTH, 2 * HEAD_WIDTH
 
-    def kernel(mine_ref, got_ref, visible_ref, grad_ref, cos_ref, sin_ref, query_ref, pair_ref):
+    def kernel(mine_ref, got_ref, visible_ref, grad_ref, cos_ref, sin_ref, *out_refs):
+        query_ref, pair_ref, send_ref = out_refs
         first = queries * HEAD_WIDTH
         mine = mine_ref[:, first:]
         got = got_ref[...]
@@ -291,15 +292,18 @@
             grad_query = fdot(grad_scores, keys) * HEAD_WIDTH ** (-0.5)
             query_ref[:, columns] = low(turn(grad_query, cos_ref[...], -sin_ref[...]))
             grad_keys = grad_keys + fdot(grad_scores, query, ((0,), (0,)))
-        pair_ref[:, :HEAD_WIDTH] = grad_keys
-        pair_ref[:, HEAD_WIDTH:] = grad_values
+        pair_ref[:, :HEAD_WIDTH] = grad_keys[:count]
+        pair_ref[:, HEAD_WIDTH:] = grad_values[:count]
+        send_ref[:, :HEAD_WIDTH] = low(grad_keys[count:])
+        send_ref[:, HEAD_WIDTH:] = low(grad_values[count:])
 
     whole = lambda array: pl.BlockSpec(array.shape, lambda j: (0, 0))
     return pl.pallas_call(
         kernel,
         out_shape=[
             jax.ShapeDtypeStruct((count, 2 * queries * HEAD_WIDTH), jnp.bfloat16),
-            jax.ShapeDtypeStruct((2 * count, 2 * pair), jnp.float32),
+            jax.ShapeDtypeStruct((count, 2 * pair), jnp.float32),
+            jax.ShapeDtypeStruct((count, 2 * pair), jnp.bfloat16),
         ],
         grid=(2,),
         in_specs=[
@@ -312,7 +316,8 @@
         ],
         out_specs=[
             pl.BlockSpec((count, queries * HEAD_WIDTH), lambda j: (0, j)),
-            pl.BlockSpec((2 * count, pair), lambda j: (0, j)),
+            pl.BlockSpec((count, pair), lambda j: (0, j)),
+            pl.BlockSpec((count, pair), lambda j: (0, 1 - j)),
         ],
         compiler_params=pltpu.CompilerParams(vmem_limit_bytes=48 << 20),
         cost_estimate=TINY,
@@ -698,14 +703,17 @@
     def on_core(values):
         return flip(values, "tensor", 1)
 
-    w_qkv = jnp.concatenate([w_query, w_key, w_value], axis=1)
-    cut = w_qkv.shape[0] // 2 // 16 * 16
+    cut = w_query.shape[0] // 2 // 16 * 16
+    qkv_parts = [
+        jnp.concatenate([weight[rows] for weight in (w_query, w_key, w_value)], axis=1)
+        for rows in (slice(0, cut), slice(cut, None))
+    ]
     gate_halves, up_halves, down_halves = halves(w_gate), halves(w_up), halves(w_down.T)
     units = gate_halves.shape[2]
     first_units = (units // 128 + 1) // 2 * 128
     waiting = [
-        w_qkv[None, :cut],
-        w_qkv[None, cut:],
+        qkv_parts[0][None],
+        qkv_parts[1][None],
         w_output.T[None],
         gate_halves[:, :, first_units:],
         up_halves[:, :, first_units:],
@@ -1002,11 +1010,10 @@
     local_near = flip(local_all, "dp", bits[-2])
     grad_inner_output = low(times_rows(grad_attn, e_output))
     grad_mixed = low(product(grad_attn, full_out_t) + product(grad_inner_output, s_output))
-    grad_queries, grad_pairs = attend_back(
+    grad_queries, grad_pairs, to_core = attend_back(
         projected, received, visible, grad_mixed, cos_rows, sin_rows, queries
     )
     pair = 2 * HEAD_WIDTH
-    to_core = low(beside(grad_pairs[row_count:, pair:], grad_pairs[row_count:, :pair]))
     from_core = on_core(to_core)
     shared = shared[:, 0] + shared_near.astype(jnp.float32)
     shared = shared + on_core(low(shared)).astype(jnp.float32)
@@ -1021,7 +1028,7 @@
         shared_all = with_bit(shared_all, bit)
     grad_expand_output = over_rows(inner_output, grad_attn)
     grad_shrink_output = over_rows(grad_inner_output, mixed_heads)
-    grad_pairs = grad_pairs[:row_count] + from_core.astype(jnp.float32)
+    grad_pairs = grad_pairs + from_core.astype(jnp.float32)
     grad_sides = []
     for side in range(2):
         keys_values = grad_pairs[:, side * pair : (side + 1) * pair]

time: 666 us -> 661 us (level)
    unnamed x312 -> x308, local copies, waits for them, and re-layouts: 61.9 us -> 59.9 us
  transfers between devices with their start and end apart: 81 -> 81, of which waited for: 39 -> 39; matrix products, arithmetic and copies ran while one was open for 15% -> 14% of each run, Pallas kernels for 12% -> 12%
where the time goes in v5:
time: 661 us; the launch traced here: 652 us
  waiting for transfers between devices  252 us (38%)
  Pallas kernels  128 us (19%)
  starting transfers between devices  109 us (16%)
  local copies, waits for them, and re-layouts  82.6 us (12%)
  other arithmetic  42 us (6%)
  matrix products  34.3 us (5%)
    ppermute x71, waiting for transfers between devices, flip(): return lax.ppermute(values, axis_name, [(i, i ^ bit) for i in range(size)])  222 us
    ppermute x71, starting transfers between devices, flip(): return lax.ppermute(values, axis_name, [(i, i ^ bit) for i in range(size)])  65.7 us
    unnamed x308, local copies, waits for them, and re-layouts  59.9 us
    all_to_all x9, starting transfers between devices, along_z(): return lax.all_to_all(sent, 'dp', 0, 0, axis_index_groups=lines)  40.1 us
    pallas_call x1, Pallas kernels, feed_forward_back(): pl.pallas_call(kernel, out_shape=parts + [jax.ShapeDtypeStruct((count, tw...  39.2 us
    all_to_all x9, waiting for transfers between devices, along_z(): return lax.all_to_all(sent, 'dp', 0, 0, axis_index_groups=lines)  26.9 us
    pallas_call x2, Pallas kernels, gate_and_up(): pl.pallas_call(kernel, out_shape=[jax.ShapeDtypeStruct((count, units), jn...  26 us
    pallas_call x8, Pallas kernels, assemble(): pl.pallas_call(kernel, out_shape=jax.ShapeDtypeStruct((2 * columns_z, row...  22.7 us
  transfers between devices with their start and end apart: 81, of which 39 were waited for; matrix products, arithmetic and copies ran while one was open for 14% of the time, Pallas kernels for 12%

profile of v5, /device:TPU:0, one launch (start us, length us, event | category | flops | bytes accessed | tf_op | source)
XLA Modules:
  0.0 651.9 jit_solution(5553456189008313199)
XLA Ops:
  0.6 3.1 collective-permute-start
  8.5 4.0 all-to-all-start
  17.4 23.0 %all-to-all-done.refs_0_ = bf16[4,144,1024]{2,1,0:T(8,128)(2,1)S(1)} async-done(((bf16[4,144,1024]{2,1,0:T(8,128)(2,1)}), bf16[4,144,1024]{2,1,0:T(8,128)(2,1)S(1)}, u32[]{:S(2)}, u32[]{:S(2)}) %all-to-all-start) | async-done | bytes 1179680 | tf_op jit(solution)/shard_map/all_to_all | solution.py:102
  40.4 2.3 concatenate.176
  46.3 4.3 all-to-all-start.1
  51.7 8.6 %collective-permute-done.4 = bf16[160,2304]{1,0:T(8,128)(2,1)} collective-permute-done((bf16[160,2304]{1,0:T(8,128)(2,1)S(1)}, bf16[160,2304]{1,0:T(8,128)(2,1)}, u32[]{:S(2)}, u32[]{:S(2)}) %collective-permute-start.4) | collective-permute-done | bytes 737312 | tf_op jit(solution)/shard_map/ppermute | solution.py:92
  61.7 3.0 shard_map.387
  82.2 3.5 all-to-all-start.2
  93.4 11.7 %collective-permute-done.11 = s32[4]{0:T(128)} collective-permute-done((s32[4]{0:T(128)S(1)}, s32[4]{0:T(128)}, u32[]{:S(2)}, u32[]{:S(2)}) %collective-permute-start.11) | collective-permute-done | bytes 48 | tf_op jit(solution)/shard_map/ppermute | solution.py:92
  106.4 7.2 %collective-permute-done.6.refs_5_ = bf16[4,144,1024]{2,1,0:T(8,128)(2,1)S(1)} collective-permute-done((bf16[4,144,1024]{2,1,0:T(8,128)(2,1)}, bf16[4,144,1024]{2,1,0:T(8,128)(2,1)S(1)}, u32[]{:S(2)}, u32[]{:S(2)}) %collective-permute-start.6) | collective-permute-done | bytes 1179680 | tf_op jit(solution)/shard_map/ppermute | solution.py:92
  116.6 4.7 all-to-all-start.3
  131.7 17.6 %collective-permute-done.12.refs_1_ = bf16[4,288,512]{2,1,0:T(8,128)(2,1)} collective-permute-done((bf16[4,288,512]{2,1,0:T(8,128)(2,1)S(1)}, bf16[4,288,512]{2,1,0:T(8,128)(2,1)}, u32[]{:S(2)}, u32[]{:S(2)}) %collective-permute-start.12) | collective-permute-done | bytes 1179680 | tf_op jit(solution)/shard_map/ppermute | solution.py:92
  151.4 4.9 all-to-all-start.4
  163.3 3.0 shard_map.388
  166.4 6.5 %shard_map.389.mine_ref = bf16[320,2048]{1,0:T(8,128)(2,1)S(1)} custom-call(bf16[320,2304]{1,0:T(8,128)(2,1)S(1)} %pad_maximum_fusion.1.rows_ref, bf16[2304,2048]{1,0:T(8,128)(2,1)S(1)} %bitcast.167, bf16[320,48]{1,0:T(8,128)(2,1)S(1)} %copy-done.46, bf16[48,2048]{1,0:T(8,128)(2,1)S(1)} %copy-done.23, f32[320,128]{1,0:T(8,128)S(1)} %get-tuple-element.269.cosine_ref.cos_ref, ...), custom_call_target="tpu_custom_call" | custom-call | flops 1 | bytes 1 | tf_op jit(solution)/shard_map/pallas_call | solution.py:215
  177.0 4.6 collective-permute-done.15.refs_1_
  182.3 4.2 all-to-all-start.5
  187.6 3.0 shard_map.390
  193.2 2.5 shard_map.391
  201.9 13.1 %collective-permute-done.22 = bf16[160,2304]{1,0:T(8,128)(2,1)S(1)} collective-permute-done((bf16[160,2304]{1,0:T(8,128)(2,1)S(1)}, bf16[160,2304]{1,0:T(8,128)(2,1)S(1)}, u32[]{:S(2)}, u32[]{:S(2)}) %collective-permute-start.22) | collective-permute-done | bytes 737312 | tf_op jit(solution)/shard_map/ppermute | solution.py:92
  216.3 8.7 %collective-permute-done.19.refs_1_ = bf16[4,288,512]{2,1,0:T(8,128)(2,1)S(1)} collective-permute-done((bf16[4,288,512]{2,1,0:T(8,128)(2,1)}, bf16[4,288,512]{2,1,0:T(8,128)(2,1)S(1)}, u32[]{:S(2)}, u32[]{:S(2)}) %collective-permute-start.19) | collective-permute-done | bytes 1179680 | tf_op jit(solution)/shard_map/ppermute | solution.py:92
  230.0 4.9 all-to-all-start.6
  243.9 2.8 shard_map.392
  249.0 18.4 %collective-permute-done.27 = bf16[80,2304]{1,0:T(8,128)(2,1)S(1)} collective-permute-done((bf16[80,2304]{1,0:T(8,128)(2,1)S(1)}, bf16[80,2304]{1,0:T(8,128)(2,1)S(1)}, u32[]{:S(2)}, u32[]{:S(2)}) %collective-permute-start.27) | collective-permute-done | bytes 368672 | tf_op jit(solution)/shard_map/ppermute | solution.py:92
  270.6 4.3 all-to-all-start.7
  287.2 19.3 %collective-permute-done.31 = bf16[80,2304]{1,0:T(8,128)(2,1)S(1)} collective-permute-done((bf16[80,2304]{1,0:T(8,128)(2,1)S(1)}, bf16[80,2304]{1,0:T(8,128)(2,1)S(1)}, u32[]{:S(2)}, u32[]{:S(2)}) %collective-permute-start.31) | collective-permute-done | bytes 368672 | tf_op jit(solution)/shard_map/ppermute | solution.py:92
  306.5 2.3 collective-permute-done.28.refs_1_
  311.2 5.2 all-to-all-start.8
  321.5 2.8 shard_map.395
  324.3 2.5 copy-done
  330.5 3.4 fusion.15.inner_ref
  333.9 11.9 %shard_map.394 = (bf16[640,1024]{1,0:T(8,128)(2,1)}, bf16[640,1024]{1,0:T(8,128)(2,1)}, bf16[640,1024]{1,0:T(8,128)(2,1)}) custom-call(bf16[640,2304]{1,0:T(8,128)(2,1)} %constant_dynamic-update-slice_fusion.6.rows_ref, bf16[2304,1024]{1,0:T(8,128)(2,1)} %bitcast.161, bf16[2304,1024]{1,0:T(8,128)(2,1)} %bitcast.163, bf16[640,64]{1,0:T(8,128)(2,1)} %fusion.15.inner_ref, ...), custom_call_target="tpu_custom_call" | custom-call | flops 1 | bytes 1 | tf_op jit(solution)/shard_map/pallas_call | solution.py:356
  345.8 4.1 collective-permute-done.33.refs_1_
  353.0 3.1 shard_map.396
  356.1 2.4 copy-done.1
  358.5 14.0 %shard_map.397 = (bf16[640,1280]{1,0:T(8,128)(2,1)}, bf16[640,1280]{1,0:T(8,128)(2,1)}, bf16[640,1280]{1,0:T(8,128)(2,1)}) custom-call(bf16[640,2304]{1,0:T(8,128)(2,1)} %constant_dynamic-update-slice_fusion.6.rows_ref, bf16[2304,1280]{1,0:T(8,128)(2,1)} %bitcast.157, bf16[2304,1280]{1,0:T(8,128)(2,1)} %bitcast.159, bf16[640,64]{1,0:T(8,128)(2,1)} %fusion.15.inner_ref, ...), custom_call_target="tpu_custom_call" | custom-call | flops 1 | bytes 1 | tf_op jit(solution)/shard_map/pallas_call | solution.py:356
  377.0 3.5 shard_map.398
  380.5 5.8 convolution_add_fusion.first_ref
  386.7 2.8 collective-permute-done.40.refs_3_
  389.5 2.8 shard_map.399
  394.5 6.9 %shard_map.400 = (f32[160,2304]{1,0:T(8,128)S(1)}, f32[80,2304]{1,0:T(8,128)S(1)}, f32[80,2304]{1,0:T(8,128)S(1)}, bf16[160,2304]{1,0:T(8,128)(2,1)S(1)}, bf16[160,2304]{1,0:T(8,128)(2,1)S(1)}) custom-call(f32[640,2304]{1,0:T(8,128)} %convolution_add_fusion.first_ref, bf16[640,1024]{1,0:T(8,128)(2,1)S(1)} %copy-done.11, bf16[2304,1024]{1,0:T(8,128)(2,1)} %bitcast.165), custom_call_target="tpu_custom_call" | custom-call | flops 1 | bytes 1 | tf_op jit(solution)/shard_map/pallas_call | solution.py:403
  404.6 15.5 %collective-permute-done.41 = bf16[160,2304]{1,0:T(8,128)(2,1)S(1)} collective-permute-done((bf16[160,2304]{1,0:T(8,128)(2,1)S(1)}, bf16[160,2304]{1,0:T(8,128)(2,1)S(1)}, u32[]{:S(2)}, u32[]{:S(2)}) %collective-permute-start.41) | collective-permute-done | bytes 737312 | tf_op jit(solution)/shard_map/ppermute | solution.py:92
  423.8 7.5 %collective-permute-done.43 = bf16[80,2304]{1,0:T(8,128)(2,1)S(1)} collective-permute-done((bf16[80,2304]{1,0:T(8,128)(2,1)S(1)}, bf16[80,2304]{1,0:T(8,128)(2,1)S(1)}, u32[]{:S(2)}, u32[]{:S(2)}) %collective-permute-start.43) | collective-permute-done | bytes 368672 | tf_op jit(solution)/shard_map/ppermute | solution.py:92
  438.7 13.2 %collective-permute-done.45 = bf16[160,2304]{1,0:T(8,128)(2,1)S(1)} collective-permute-done((bf16[160,2304]{1,0:T(8,128)(2,1)S(1)}, bf16[160,2304]{1,0:T(8,128)(2,1)S(1)}, u32[]{:S(2)}, u32[]{:S(2)}) %collective-permute-start.45) | collective-permute-done | bytes 737312 | tf_op jit(solution)/shard_map/ppermute | solution.py:92
  456.4 4.2 collective-permute-done.47
  462.1 39.2 %shard_map.401 = (f32[160,2304]{1,0:T(8,128)}, f32[80,2304]{1,0:T(8,128)}, f32[80,2304]{1,0:T(8,128)}, bf16[160,2304]{1,0:T(8,128)(2,1)}, bf16[160,2304]{1,0:T(8...) custom-call(bf16[640,2304]{1,0:T(8,128)(2,1)} %constant_dynamic-upda, ...), custom_call_target="tpu_custom_call" | custom-call | flops 1 | bytes 1 | tf_op jit(solution)/shard_map/pallas_call | solution.py:493
  501.3 2.6 fusion.33
  511.5 10.6 %collective-permute-done.49 = bf16[160,2304]{1,0:T(8,128)(2,1)S(1)} collective-permute-done((bf16[160,2304]{1,0:T(8,128)(2,1)S(1)}, bf16[160,2304]{1,0:T(8,128)(2,1)S(1)}, u32[]{:S(2)}, u32[]{:S(2)}) %collective-permute-start.49) | collective-permute-done | bytes 737312 | tf_op jit(solution)/shard_map/ppermute | solution.py:92
  522.5 2.5 fusion.69
  531.0 4.5 collective-permute-done.52
  542.2 2.9 collective-permute-start.56
  547.6 10.9 %collective-permute-done.56 = bf16[2,96,1152]{2,1,0:T(8,128)(2,1)S(1)} collective-permute-done((bf16[2,96,1152]{2,1,0:T(8,128)(2,1)S(1)}, bf16[2,96,1152]{2,1,0:T(8,128)(2,1)S(1)}, u32[]{:S(2)}, u32[]{:S(2)}) %collective-permute-start.56) | collective-permute-done | bytes 442400 | tf_op jit(solution)/shard_map/ppermute | solution.py:92
  562.2 5.6 shard_map.402
  570.5 5.6 collective-permute-done.60
  578.8 3.2 collective-permute-start.63
  583.3 7.1 %collective-permute-done.63 = bf16[1,16,3456]{2,1,0:T(8,128)(2,1)S(1)} collective-permute-done((bf16[1,16,3456]{2,1,0:T(8,128)(2,1)S(1)}, bf16[1,16,3456]{2,1,0:T(8,128)(2,1)S(1)}, u32[]{:S(2)}, u32[]{:S(2)}) %collective-permute-start.63) | collective-permute-done | bytes 110624 | tf_op jit(solution)/shard_map/ppermute | solution.py:92
  590.5 3.9 collective-permute-start.65
  596.6 4.9 convolution_add_fusion.1
  604.9 3.6 all-to-all-start.9
  615.1 8.4 %shard_map.403 = (f32[8,16,2304]{2,1,0:T(8,128)}, f32[8,16,2304]{2,1,0:T(8,128)}, f32[8,16,2304]{2,1,0:T(8,128)}) custom-call(f32[2,16,8]{2,1,0:T(8,128)S(1)} %pad_maximum_fusion.38.hots_ref, bf16[16,48,1152]{2,1,0:T(8,128)(2,1)S(1)} %bitcast.173), custom_call_target="tpu_custom_call" | custom-call | flops 1 | bytes 1 | tf_op jit(solution)/shard_map/pallas_call | solution.py:595
  623.5 12.3 %collective-permute-done.68 = bf16[4,16,3456]{2,1,0:T(8,128)(2,1)S(1)} collective-permute-done((bf16[4,16,3456]{2,1,0:T(8,128)(2,1)S(1)}, bf16[4,16,3456]{2,1,0:T(8,128)(2,1)S(1)}, u32[]{:S(2)}, u32[]{:S(2)}) %collective-permute-start.68) | collective-permute-done | bytes 442400 | tf_op jit(solution)/shard_map/ppermute | solution.py:92
  641.8 2.6 all-to-all-done.9.gathered_ref
  646.2 2.8 collective-permute-done.70.other_ref
  649.1 2.3 shard_map.407
  (637 shorter events, 205.3 us)
Async XLA Ops:
  0.6 16.8 %collective-permute-start = (s32[1]{0:T(128)}, s32[1]{0:T(128)}, u32[]{:S(2)}, u32[]{:S(2)}) collective-permute-start(s32[1]{0:T(128)} %param.52), channel_id=1, source_target_pairs={{0,8},{4,12},{8,0},{12,4},{16,24},{20,28},{24,16},{28,20},{1,9},{5... | collective-permute-start | bytes 20 | tf_op jit(solution)/shard_map/ppermute | solution.py:92
  3.7 13.7 %collective-permute-start.1 = (s32[1]{0:T(128)}, s32[1]{0:T(128)}, u32[]{:S(2)}, u32[]{:S(2)}) collective-permute-start(s32[1]{0:T(128)} %param.52), channel_id=1, source_target_pairs={{0,4},{4,0},{8,12},{12,8},{16,20},{20,16},{24,28},{28,24},{1,5},{5... | collective-permute-start | bytes 20 | tf_op jit(solution)/shard_map/ppermute | solution.py:92
  8.5 32.0 %all-to-all-start = ((bf16[4,144,1024]{2,1,0:T(8,128)(2,1)}), bf16[4,144,1024]{2,1,0:T(8,128)(2,1)S(1)}, u32[]{:S(2)}, u32[]{:S(2)}) async-start(bf16[4,144,1024]{2,1,0:T(8,128)(2,1)} %concatenate.174), calls=%async_computation | async-start | bytes 2359296 | tf_op jit(solution)/shard_map/all_to_all | solution.py:102
  42.7 17.5 %collective-permute-start.4 = (bf16[160,2304]{1,0:T(8,128)(2,1)S(1)}, bf16[160,2304]{1,0:T(8,128)(2,1)}, u32[]{:S(2)}, u32[]{:S(2)}) collective-permute-start(bf16[160,2304]{1,0:T(8,128)(2,1)S(1)} %fusion.7), channel_id=1, source_target_pairs={{0,2},{1,3},{2,0},{3,1},{4,6},{5,7},{6,4},{7,5},{8,10},{9,11},{10,... | collective-permute-start | bytes 2211848 | tf_op jit(solution)/shard_map/ppermute | solution.py:92
  44.9 33.9 %collective-permute-start.2 = (bf16[4,144,1024]{2,1,0:T(8,128)(2,1)S(1)}, bf16[4,144,1024]{2,1,0:T(8,128)(2,1)}, u32[]{:S(2)}, u32[]{:S(2)}) collective-permute-start(bf16[4,144,1024]{2,1,0:T(8,128)(2,1)S(1)} %all-to-all-done.refs_0_), channel_id=1, source_target_pairs={{0,4},{4,0},{8,12},{12,8},{16,20},{20,16},{24,28},{28,24},{1,5},{5... | collective-permute-start | bytes 3538952 | tf_op jit(solution)/shard_map/ppermute | solution.py:92
  45.5 33.3 %collective-permute-start.3 = (bf16[4,144,1024]{2,1,0:T(8,128)(2,1)S(1)}, bf16[4,144,1024]{2,1,0:T(8,128)(2,1)}, u32[]{:S(2)}, u32[]{:S(2)}) collective-permute-start(bf16[4,144,1024]{2,1,0:T(8,128)(2,1)S(1)} %all-to-all-done.refs_0_), channel_id=1, source_target_pairs={{0,1},{1,0},{2,3},{3,2},{4,5},{5,4},{6,7},{7,6},{8,9},{9,8},{10,11... | collective-permute-start | bytes 3538952 | tf_op jit(solution)/shard_map/ppermute | solution.py:92
  46.2 32.6 %collective-permute-start.5 = (s32[2]{0:T(128)S(1)}, s32[2]{0:T(128)S(1)}, u32[]{:S(2)}, u32[]{:S(2)}) collective-permute-start(s32[2]{0:T(128)S(1)} %pad_add_fusion.3), channel_id=1, source_target_pairs={{0,16},{4,20},{8,24},{12,28},{16,0},{20,4},{24,8},{28,12},{1,17},{... | collective-permute-start | bytes 32 | tf_op jit(solution)/shard_map/ppermute | solution.py:92
  46.3 33.8 %all-to-all-start.1 = ((bf16[4,144,1024]{2,1,0:T(8,128)(2,1)}), bf16[4,144,1024]{2,1,0:T(8,128)(2,1)}, u32[]{:S(2)}, u32[]{:S(2)}) async-start(bf16[4,144,1024]{2,1,0:T(8,128)(2,1)} %concatenate.176), calls=%async_computation.1 | async-start | bytes 2359296 | tf_op jit(solution)/shard_map/all_to_all | solution.py:102
  82.2 34.5 %all-to-all-start.2 = ((bf16[4,288,512]{2,1,0:T(8,128)(2,1)}), bf16[4,288,512]{2,1,0:T(8,128)(2,1)S(1)}, u32[]{:S(2)}, u32[]{:S(2)}) async-start(bf16[4,288,512]{2,1,0:T(8,128)(2,1)} %concatenate.177), calls=%async_computation.2 | async-start | bytes 2359296 | tf_op jit(solution)/shard_map/all_to_all | solution.py:102
  85.7 27.9 %collective-permute-start.6 = (bf16[4,144,1024]{2,1,0:T(8,128)(2,1)}, bf16[4,144,1024]{2,1,0:T(8,128)(2,1)S(1)}, u32[]{:S(2)}, u32[]{:S(2)}) collective-permute-start(bf16[4,144,1024]{2,1,0:T(8,128)(2,1)} %all-to-all-done.1.refs_4_), channel_id=1, source_target_pairs={{0,4},{4,0},{8,12},{12,8},{16,20},{20,16},{24,28},{28,24},{1,5},{5... | collective-permute-start | bytes 3538952 | tf_op jit(solution)/shard_map/ppermute | solution.py:92
  87.3 26.3 %collective-permute-start.7 = (bf16[4,144,1024]{2,1,0:T(8,128)(2,1)}, bf16[4,144,1024]{2,1,0:T(8,128)(2,1)S(1)}, u32[]{:S(2)}, u32[]{:S(2)}) collective-permute-start(bf16[4,144,1024]{2,1,0:T(8,128)(2,1)} %all-to-all-done.1.refs_4_), channel_id=1, source_target_pairs={{0,1},{1,0},{2,3},{3,2},{4,5},{5,4},{6,7},{7,6},{8,9},{9,8},{10,11... | collective-permute-start | bytes 3538952 | tf_op jit(solution)/shard_map/ppermute | solution.py:92
  87.3 28.3 %collective-permute-start.8 = (bf16[4,144,1024]{2,1,0:T(8,128)(2,1)}, bf16[4,144,1024]{2,1,0:T(8,128)(2,1)S(1)}, u32[]{:S(2)}, u32[]{:S(2)}) collective-permute-start(bf16[4,144,1024]{2,1,0:T(8,128)(2,1)} %collective-permute-done.2.refs_1_), channel_id=1, source_target_pairs={{0,1},{1,0},{2,3},{3,2},{4,5},{5,4},{6,7},{7,6},{8,9},{9,8},{10,11... | collective-permute-start | bytes 3538952 | tf_op jit(solution)/shard_map/ppermute | solution.py:92
  91.5 13.6 %collective-permute-start.11 = (s32[4]{0:T(128)S(1)}, s32[4]{0:T(128)}, u32[]{:S(2)}, u32[]{:S(2)}) collective-permute-start(s32[4]{0:T(128)S(1)} %pad_add_fusion.4), channel_id=1, source_target_pairs={{0,8},{4,12},{8,0},{12,4},{16,24},{20,28},{24,16},{28,20},{1,9},{5... | collective-permute-start | bytes 56 | tf_op jit(solution)/shard_map/ppermute | solution.py:92
  93.4 13.0 %collective-permute-start.10 = (bf16[96,1152]{1,0:T(8,128)(2,1)}, bf16[96,1152]{1,0:T(8,128)(2,1)S(1)}, u32[]{:S(2)}, u32[]{:S(2)}) collective-permute-start(bf16[96,1152]{1,0:T(8,128)(2,1)} %constant_dynamic-update-slice_fusion), channel_id=1, source_target_pairs={{0,1},{1,0},{2,3},{3,2},{4,5},{5,4},{6,7},{7,6},{8,9},{9,8},{10,11... | collective-permute-start | bytes 663560 | tf_op jit(solution)/shard_map/ppermute | solution.py:92
  116.6 34.7 %all-to-all-start.3 = ((bf16[4,288,512]{2,1,0:T(8,128)(2,1)}), bf16[4,288,512]{2,1,0:T(8,128)(2,1)}, u32[]{:S(2)}, u32[]{:S(2)}) async-start(bf16[4,288,512]{2,1,0:T(8,128)(2,1)} %pad_maximum_fusion.7), calls=%async_computation.3 | async-start | bytes 2359296 | tf_op jit(solution)/shard_map/all_to_all | solution.py:102
  122.9 26.4 %collective-permute-start.12 = (bf16[4,288,512]{2,1,0:T(8,128)(2,1)S(1)}, bf16[4,288,512]{2,1,0:T(8,128)(2,1)}, u32[]{:S(2)}, u32[]{:S(2)}) collective-permute-start(bf16[4,288,512]{2,1,0:T(8,128)(2,1)S(1)} %all-to-all-done.2.refs_0_), channel_id=1, source_target_pairs={{0,4},{4,0},{8,12},{12,8},{16,20},{20,16},{24,28},{28,24},{1,5},{5... | collective-permute-start | bytes 3538952 | tf_op jit(solution)/shard_map/ppermute | solution.py:92
  124.4 24.9 %collective-permute-start.13 = (bf16[4,288,512]{2,1,0:T(8,128)(2,1)S(1)}, bf16[4,288,512]{2,1,0:T(8,128)(2,1)S(1)}, u32[]{:S(2)}, u32[]{:S(2)}) collective-permute-start(bf16[4,288,512]{2,1,0:T(8,128)(2,1)S(1)} %all-to-all-done.2.refs_0_), channel_id=1, source_target_pairs={{0,1},{1,0},{2,3},{3,2},{4,5},{5,4},{6,7},{7,6},{8,9},{9,8},{10,11... | collective-permute-start | bytes 3538952 | tf_op jit(solution)/shard_map/ppermute | solution.py:92
  124.4 25.9 %collective-permute-start.14 = (bf16[4,144,1024]{2,1,0:T(8,128)(2,1)S(1)}, bf16[4,144,1024]{2,1,0:T(8,128)(2,1)S(1)}, u32[]{:S(2)}, u32[]{:S(2)}) collective-permute-start(bf16[4,144,1024]{2,1,0:T(8,128)(2,1)S(1)} %copy-done.38), channel_id=1, source_target_pairs={{0,1},{1,0},{2,3},{3,2},{4,5},{5,4},{6,7},{7,6},{8,9},{9,8},{10,11... | collective-permute-start | bytes 3538952 | tf_op jit(solution)/shard_map/ppermute | solution.py:92
  151.4 30.9 %all-to-all-start.4 = ((bf16[4,288,512]{2,1,0:T(8,128)(2,1)}), bf16[4,288,512]{2,1,0:T(8,128)(2,1)}, u32[]{:S(2)}, u32[]{:S(2)}) async-start(bf16[4,288,512]{2,1,0:T(8,128)(2,1)} %pad_maximum_fusion.8), calls=%async_computation.4 | async-start | bytes 2359296 | tf_op jit(solution)/shard_map/all_to_all | solution.py:102
  156.2 25.3 %collective-permute-start.15 = (bf16[4,288,512]{2,1,0:T(8,128)(2,1)}, bf16[4,288,512]{2,1,0:T(8,128)(2,1)}, u32[]{:S(2)}, u32[]{:S(2)}) collective-permute-start(bf16[4,288,512]{2,1,0:T(8,128)(2,1)} %all-to-all-done.3.refs_0_), channel_id=1, source_target_pairs={{0,4},{4,0},{8,12},{12,8},{16,20},{20,16},{24,28},{28,24},{1,5},{5... | collective-permute-start | bytes 3538952 | tf_op jit(solution)/shard_map/ppermute | solution.py:92
  157.7 23.8 %collective-permute-start.16 = (bf16[4,288,512]{2,1,0:T(8,128)(2,1)}, bf16[4,288,512]{2,1,0:T(8,128)(2,1)}, u32[]{:S(2)}, u32[]{:S(2)}) collective-permute-start(bf16[4,288,512]{2,1,0:T(8,128)(2,1)} %all-to-all-done.3.refs_0_), channel_id=1, source_target_pairs={{0,1},{1,0},{2,3},{3,2},{4,5},{5,4},{6,7},{7,6},{8,9},{9,8},{10,11... | collective-permute-start | bytes 3538952 | tf_op jit(solution)/shard_map/ppermute | solution.py:92
  157.7 23.8 %collective-permute-start.17 = (bf16[4,288,512]{2,1,0:T(8,128)(2,1)}, bf16[4,288,512]{2,1,0:T(8,128)(2,1)}, u32[]{:S(2)}, u32[]{:S(2)}) collective-permute-start(bf16[4,288,512]{2,1,0:T(8,128)(2,1)} %collective-permute-done.12.refs_1_), channel_id=1, source_target_pairs={{0,1},{1,0},{2,3},{3,2},{4,5},{5,4},{6,7},{7,6},{8,9},{9,8},{10,11... | collective-permute-start | bytes 3538952 | tf_op jit(solution)/shard_map/ppermute | solution.py:92
  182.3 44.6 %all-to-all-start.5 = ((bf16[4,288,640]{2,1,0:T(8,128)(2,1)}), bf16[4,288,640]{2,1,0:T(8,128)(2,1)S(1)}, u32[]{:S(2)}, u32[]{:S(2)}) async-start(bf16[4,288,640]{2,1,0:T(8,128)(2,1)} %pad_maximum_fusion.2), calls=%async_computation.5 | async-start | bytes 2949120 | tf_op jit(solution)/shard_map/all_to_all | solution.py:102
  197.9 17.1 %collective-permute-start.22 = (bf16[160,2304]{1,0:T(8,128)(2,1)S(1)}, bf16[160,2304]{1,0:T(8,128)(2,1)S(1)}, u32[]{:S(2)}, u32[]{:S(2)}) collective-permute-start(bf16[160,2304]{1,0:T(8,128)(2,1)S(1)} %slice.633), channel_id=1, source_target_pairs={{0,2},{1,3},{2,0},{3,1},{4,6},{5,7},{6,4},{7,5},{8,10},{9,11},{10,... | collective-permute-start | bytes 2211848 | tf_op jit(solution)/shard_map/ppermute | solution.py:92
  198.4 26.5 %collective-permute-start.19 = (bf16[4,288,512]{2,1,0:T(8,128)(2,1)}, bf16[4,288,512]{2,1,0:T(8,128)(2,1)S(1)}, u32[]{:S(2)}, u32[]{:S(2)}) collective-permute-start(bf16[4,288,512]{2,1,0:T(8,128)(2,1)} %all-to-all-done.4.refs_0_), channel_id=1, source_target_pairs={{0,4},{4,0},{8,12},{12,8},{16,20},{20,16},{24,28},{28,24},{1,5},{5... | collective-permute-start | bytes 3538952 | tf_op jit(solution)/shard_map/ppermute | solution.py:92
  199.9 25.0 %collective-permute-start.20 = (bf16[4,288,512]{2,1,0:T(8,128)(2,1)}, bf16[4,288,512]{2,1,0:T(8,128)(2,1)S(1)}, u32[]{:S(2)}, u32[]{:S(2)}) collective-permute-start(bf16[4,288,512]{2,1,0:T(8,128)(2,1)} %all-to-all-done.4.refs_0_), channel_id=1, source_target_pairs={{0,1},{1,0},{2,3},{3,2},{4,5},{5,4},{6,7},{7,6},{8,9},{9,8},{10,11... | collective-permute-start | bytes 3538952 | tf_op jit(solution)/shard_map/ppermute | solution.py:92
  199.9 26.0 %collective-permute-start.21 = (bf16[4,288,512]{2,1,0:T(8,128)(2,1)}, bf16[4,288,512]{2,1,0:T(8,128)(2,1)S(1)}, u32[]{:S(2)}, u32[]{:S(2)}) collective-permute-start(bf16[4,288,512]{2,1,0:T(8,128)(2,1)} %collective-permute-done.15.refs_1_), channel_id=1, source_target_pairs={{0,1},{1,0},{2,3},{3,2},{4,5},{5,4},{6,7},{7,6},{8,9},{9,8},{10,11... | collective-permute-start | bytes 3538952 | tf_op jit(solution)/shard_map/ppermute | solution.py:92
  227.0 41.5 %collective-permute-start.23 = (bf16[4,288,640]{2,1,0:T(8,128)(2,1)S(1)}, bf16[4,288,640]{2,1,0:T(8,128)(2,1)}, u32[]{:S(2)}, u32[]{:S(2)}) collective-permute-start(bf16[4,288,640]{2,1,0:T(8,128)(2,1)S(1)} %all-to-all-done.5.refs_0_), channel_id=1, source_target_pairs={{0,4},{4,0},{8,12},{12,8},{16,20},{20,16},{24,28},{28,24},{1,5},{5... | collective-permute-start | bytes 4423688 | tf_op jit(solution)/shard_map/ppermute | solution.py:92
  228.4 40.3 %collective-permute-start.24 = (bf16[4,288,640]{2,1,0:T(8,128)(2,1)S(1)}, bf16[4,288,640]{2,1,0:T(8,128)(2,1)}, u32[]{:S(2)}, u32[]{:S(2)}) collective-permute-start(bf16[4,288,640]{2,1,0:T(8,128)(2,1)S(1)} %all-to-all-done.5.refs_0_), channel_id=1, source_target_pairs={{0,1},{1,0},{2,3},{3,2},{4,5},{5,4},{6,7},{7,6},{8,9},{9,8},{10,11... | collective-permute-start | bytes 4423688 | tf_op jit(solution)/shard_map/ppermute | solution.py:92
  230.0 40.6 %all-to-all-start.6 = ((bf16[4,288,640]{2,1,0:T(8,128)(2,1)}), bf16[4,288,640]{2,1,0:T(8,128)(2,1)}, u32[]{:S(2)}, u32[]{:S(2)}) async-start(bf16[4,288,640]{2,1,0:T(8,128)(2,1)} %pad_maximum_fusion.3), calls=%async_computation.6 | async-start | bytes 2949120 | tf_op jit(solution)/shard_map/all_to_all | solution.py:102
  235.5 31.9 %collective-permute-start.25 = (bf16[4,288,512]{2,1,0:T(8,128)(2,1)S(1)}, bf16[4,288,512]{2,1,0:T(8,128)(2,1)S(1)}, u32[]{:S(2)}, u32[]{:S(2)}) collective-permute-start(bf16[4,288,512]{2,1,0:T(8,128)(2,1)S(1)} %collective-permute-done.19.refs_1_), channel_id=1, source_target_pairs={{0,1},{1,0},{2,3},{3,2},{4,5},{5,4},{6,7},{7,6},{8,9},{9,8},{10,11... | collective-permute-start | bytes 3538952 | tf_op jit(solution)/shard_map/ppermute | solution.py:92
  238.0 29.4 %collective-permute-start.26 = (bf16[160,2304]{1,0:T(8,128)(2,1)S(1)}, bf16[160,2304]{1,0:T(8,128)(2,1)S(1)}, u32[]{:S(2)}, u32[]{:S(2)}) collective-permute-start(bf16[160,2304]{1,0:T(8,128)(2,1)S(1)} %multiply_convert_fusion), channel_id=1, source_target_pairs={{0,2},{1,3},{2,0},{3,1},{4,6},{5,7},{6,4},{7,5},{8,10},{9,11},{10,... | collective-permute-start | bytes 2211848 | tf_op jit(solution)/shard_map/ppermute | solution.py:92
  239.6 27.8 %collective-permute-start.27 = (bf16[80,2304]{1,0:T(8,128)(2,1)S(1)}, bf16[80,2304]{1,0:T(8,128)(2,1)S(1)}, u32[]{:S(2)}, u32[]{:S(2)}) collective-permute-start(bf16[80,2304]{1,0:T(8,128)(2,1)S(1)} %slice.454), channel_id=1, source_target_pairs={{0,8},{4,12},{8,0},{12,4},{16,24},{20,28},{24,16},{28,20},{1,9},{5... | collective-permute-start | bytes 1105928 | tf_op jit(solution)/shard_map/ppermute | solution.py:92
  270.6 40.6 %all-to-all-start.7 = ((bf16[4,288,640]{2,1,0:T(8,128)(2,1)}), bf16[4,288,640]{2,1,0:T(8,128)(2,1)}, u32[]{:S(2)}, u32[]{:S(2)}) async-start(bf16[4,288,640]{2,1,0:T(8,128)(2,1)} %pad_maximum_fusion.4), calls=%async_computation.7 | async-start | bytes 2949120 | tf_op jit(solution)/shard_map/all_to_all | solution.py:102
  274.9 34.0 %collective-permute-start.28 = (bf16[4,288,640]{2,1,0:T(8,128)(2,1)}, bf16[4,288,640]{2,1,0:T(8,128)(2,1)}, u32[]{:S(2)}, u32[]{:S(2)}) collective-permute-start(bf16[4,288,640]{2,1,0:T(8,128)(2,1)} %all-to-all-done.6.refs_0_), channel_id=1, source_target_pairs={{0,4},{4,0},{8,12},{12,8},{16,20},{20,16},{24,28},{28,24},{1,5},{5... | collective-permute-start | bytes 4423688 | tf_op jit(solution)/shard_map/ppermute | solution.py:92
  275.5 33.4 %collective-permute-start.29 = (bf16[4,288,640]{2,1,0:T(8,128)(2,1)}, bf16[4,288,640]{2,1,0:T(8,128)(2,1)S(1)}, u32[]{:S(2)}, u32[]{:S(2)}) collective-permute-start(bf16[4,288,640]{2,1,0:T(8,128)(2,1)} %all-to-all-done.6.refs_0_), channel_id=1, source_target_pairs={{0,1},{1,0},{2,3},{3,2},{4,5},{5,4},{6,7},{7,6},{8,9},{9,8},{10,11... | collective-permute-start | bytes 4423688 | tf_op jit(solution)/shard_map/ppermute | solution.py:92
  275.5 34.6 %collective-permute-start.30 = (bf16[4,288,640]{2,1,0:T(8,128)(2,1)}, bf16[4,288,640]{2,1,0:T(8,128)(2,1)S(1)}, u32[]{:S(2)}, u32[]{:S(2)}) collective-permute-start(bf16[4,288,640]{2,1,0:T(8,128)(2,1)} %collective-permute-done.23.refs_1_), channel_id=1, source_target_pairs={{0,1},{1,0},{2,3},{3,2},{4,5},{5,4},{6,7},{7,6},{8,9},{9,8},{10,11... | collective-permute-start | bytes 4423688 | tf_op jit(solution)/shard_map/ppermute | solution.py:92
  278.4 28.1 %collective-permute-start.31 = (bf16[80,2304]{1,0:T(8,128)(2,1)S(1)}, bf16[80,2304]{1,0:T(8,128)(2,1)S(1)}, u32[]{:S(2)}, u32[]{:S(2)}) collective-permute-start(bf16[80,2304]{1,0:T(8,128)(2,1)S(1)} %slice.372), channel_id=1, source_target_pairs={{0,8},{4,12},{8,0},{12,4},{16,24},{20,28},{24,16},{28,20},{1,9},{5... | collective-permute-start | bytes 1105928 | tf_op jit(solution)/shard_map/ppermute | solution.py:92
  280.4 26.1 %collective-permute-start.32 = (bf16[80,2304]{1,0:T(8,128)(2,1)S(1)}, bf16[80,2304]{1,0:T(8,128)(2,1)S(1)}, u32[]{:S(2)}, u32[]{:S(2)}) collective-permute-start(bf16[80,2304]{1,0:T(8,128)(2,1)S(1)} %copy-done.99), channel_id=1, source_target_pairs={{0,2},{1,3},{2,0},{3,1},{4,6},{5,7},{6,4},{7,5},{8,10},{9,11},{10,... | collective-permute-start | bytes 1105928 | tf_op jit(solution)/shard_map/ppermute | solution.py:92
  311.2 38.8 %all-to-all-start.8 = ((bf16[4,288,512]{2,1,0:T(8,128)(2,1)}), bf16[4,288,512]{2,1,0:T(8,128)(2,1)}, u32[]{:S(2)}, u32[]{:S(2)}) async-start(bf16[4,288,512]{2,1,0:T(8,128)(2,1)} %pad_maximum_fusion.9), calls=%async_computation.8 | async-start | bytes 2359296 | tf_op jit(solution)/shard_map/all_to_all | solution.py:102
  317.4 32.6 %collective-permute-start.33 = (bf16[4,288,640]{2,1,0:T(8,128)(2,1)}, bf16[4,288,640]{2,1,0:T(8,128)(2,1)}, u32[]{:S(2)}, u32[]{:S(2)}) collective-permute-start(bf16[4,288,640]{2,1,0:T(8,128)(2,1)} %all-to-all-done.7.refs_0_), channel_id=1, source_target_pairs={{0,4},{4,0},{8,12},{12,8},{16,20},{20,16},{24,28},{28,24},{1,5},{5... | collective-permute-start | bytes 4423688 | tf_op jit(solution)/shard_map/ppermute | solution.py:92
  317.9 32.0 %collective-permute-start.34 = (bf16[4,288,640]{2,1,0:T(8,128)(2,1)}, bf16[4,288,640]{2,1,0:T(8,128)(2,1)}, u32[]{:S(2)}, u32[]{:S(2)}) collective-permute-start(bf16[4,288,640]{2,1,0:T(8,128)(2,1)} %all-to-all-done.7.refs_0_), channel_id=1, source_target_pairs={{0,1},{1,0},{2,3},{3,2},{4,5},{5,4},{6,7},{7,6},{8,9},{9,8},{10,11... | collective-permute-start | bytes 4423688 | tf_op jit(solution)/shard_map/ppermute | solution.py:92
  317.9 32.0 %collective-permute-start.35 = (bf16[4,288,640]{2,1,0:T(8,128)(2,1)}, bf16[4,288,640]{2,1,0:T(8,128)(2,1)}, u32[]{:S(2)}, u32[]{:S(2)}) collective-permute-start(bf16[4,288,640]{2,1,0:T(8,128)(2,1)} %collective-permute-done.28.refs_1_), channel_id=1, source_target_pairs={{0,1},{1,0},{2,3},{3,2},{4,5},{5,4},{6,7},{7,6},{8,9},{9,8},{10,11... | collective-permute-start | bytes 4423688 | tf_op jit(solution)/shard_map/ppermute | solution.py:92
  319.2 10.5 %collective-permute-start.36 = (bf16[80,2304]{1,0:T(8,128)(2,1)S(1)}, bf16[80,2304]{1,0:T(8,128)(2,1)S(1)}, u32[]{:S(2)}, u32[]{:S(2)}) collective-permute-start(bf16[80,2304]{1,0:T(8,128)(2,1)S(1)} %copy-done.102), channel_id=1, source_target_pairs={{0,2},{1,3},{2,0},{3,1},{4,6},{5,7},{6,4},{7,5},{8,10},{9,11},{10,... | collective-permute-start | bytes 1105928 | tf_op jit(solution)/shard_map/ppermute | solution.py:92
  349.9 27.1 %collective-permute-start.39 = (bf16[4,288,640]{2,1,0:T(8,128)(2,1)}, bf16[4,288,640]{2,1,0:T(8,128)(2,1)}, u32[]{:S(2)}, u32[]{:S(2)}) collective-permute-start(bf16[4,288,640]{2,1,0:T(8,128)(2,1)} %collective-permute-done.33.refs_1_), channel_id=1, source_target_pairs={{0,1},{1,0},{2,3},{3,2},{4,5},{5,4},{6,7},{7,6},{8,9},{9,8},{10,11... | collective-permute-start | bytes 4423688 | tf_op jit(solution)/shard_map/ppermute | solution.py:92
  350.9 35.5 %collective-permute-start.37 = (bf16[4,288,512]{2,1,0:T(8,128)(2,1)}, bf16[4,288,512]{2,1,0:T(8,128)(2,1)}, u32[]{:S(2)}, u32[]{:S(2)}) collective-permute-start(bf16[4,288,512]{2,1,0:T(8,128)(2,1)} %all-to-all-done.8.refs_0_), channel_id=1, source_target_pairs={{0,4},{4,0},{8,12},{12,8},{16,20},{20,16},{24,28},{28,24},{1,5},{5... | collective-permute-start | bytes 3538952 | tf_op jit(solution)/shard_map/ppermute | solution.py:92
  351.4 34.9 %collective-permute-start.38 = (bf16[4,288,512]{2,1,0:T(8,128)(2,1)}, bf16[4,288,512]{2,1,0:T(8,128)(2,1)}, u32[]{:S(2)}, u32[]{:S(2)}) collective-permute-start(bf16[4,288,512]{2,1,0:T(8,128)(2,1)} %all-to-all-done.8.refs_0_), channel_id=1, source_target_pairs={{0,1},{1,0},{2,3},{3,2},{4,5},{5,4},{6,7},{7,6},{8,9},{9,8},{10,11... | collective-permute-start | bytes 3538952 | tf_op jit(solution)/shard_map/ppermute | solution.py:92
  401.3 18.7 %collective-permute-start.41 = (bf16[160,2304]{1,0:T(8,128)(2,1)S(1)}, bf16[160,2304]{1,0:T(8,128)(2,1)S(1)}, u32[]{:S(2)}, u32[]{:S(2)}) collective-permute-start(bf16[160,2304]{1,0:T(8,128)(2,1)S(1)} %get-tuple-element.335), channel_id=1, source_target_pairs={{0,2},{1,3},{2,0},{3,1},{4,6},{5,7},{6,4},{7,5},{8,10},{9,11},{10,... | collective-permute-start | bytes 2211848 | tf_op jit(solution)/shard_map/ppermute | solution.py:92
  402.9 18.4 %collective-permute-start.42 = (bf16[160,2304]{1,0:T(8,128)(2,1)S(1)}, bf16[160,2304]{1,0:T(8,128)(2,1)S(1)}, u32[]{:S(2)}, u32[]{:S(2)}) collective-permute-start(bf16[160,2304]{1,0:T(8,128)(2,1)S(1)} %get-tuple-element.337), channel_id=1, source_target_pairs={{0,8},{4,12},{8,0},{12,4},{16,24},{20,28},{24,16},{28,20},{1,9},{5... | collective-permute-start | bytes 2211848 | tf_op jit(solution)/shard_map/ppermute | solution.py:92
  421.5 9.7 %collective-permute-start.43 = (bf16[80,2304]{1,0:T(8,128)(2,1)S(1)}, bf16[80,2304]{1,0:T(8,128)(2,1)S(1)}, u32[]{:S(2)}, u32[]{:S(2)}) collective-permute-start(bf16[80,2304]{1,0:T(8,128)(2,1)S(1)} %fusion.22), channel_id=1, source_target_pairs={{0,8},{4,12},{8,0},{12,4},{16,24},{20,28},{24,16},{28,20},{1,9},{5... | collective-permute-start | bytes 1105928 | tf_op jit(solution)/shard_map/ppermute | solution.py:92
  423.3 9.4 %collective-permute-start.44 = (bf16[80,2304]{1,0:T(8,128)(2,1)S(1)}, bf16[80,2304]{1,0:T(8,128)(2,1)S(1)}, u32[]{:S(2)}, u32[]{:S(2)}) collective-permute-start(bf16[80,2304]{1,0:T(8,128)(2,1)S(1)} %fusion.23), channel_id=1, source_target_pairs={{0,2},{1,3},{2,0},{3,1},{4,6},{5,7},{6,4},{7,5},{8,10},{9,11},{10,... | collective-permute-start | bytes 1105928 | tf_op jit(solution)/shard_map/ppermute | solution.py:92
  435.5 16.4 %collective-permute-start.45 = (bf16[160,2304]{1,0:T(8,128)(2,1)S(1)}, bf16[160,2304]{1,0:T(8,128)(2,1)S(1)}, u32[]{:S(2)}, u32[]{:S(2)}) collective-permute-start(bf16[160,2304]{1,0:T(8,128)(2,1)S(1)} %get-tuple-element.441), channel_id=1, source_target_pairs={{0,2},{1,3},{2,0},{3,1},{4,6},{5,7},{6,4},{7,5},{8,10},{9,11},{10,... | collective-permute-start | bytes 2211848 | tf_op jit(solution)/shard_map/ppermute | solution.py:92
  436.3 16.6 %collective-permute-start.46 = (bf16[160,2304]{1,0:T(8,128)(2,1)S(1)}, bf16[160,2304]{1,0:T(8,128)(2,1)S(1)}, u32[]{:S(2)}, u32[]{:S(2)}) collective-permute-start(bf16[160,2304]{1,0:T(8,128)(2,1)S(1)} %get-tuple-element.441), channel_id=1, source_target_pairs={{0,8},{4,12},{8,0},{12,4},{16,24},{20,28},{24,16},{28,20},{1,9},{5... | collective-permute-start | bytes 2211848 | tf_op jit(solution)/shard_map/ppermute | solution.py:92
  507.6 14.6 %collective-permute-start.49 = (bf16[160,2304]{1,0:T(8,128)(2,1)S(1)}, bf16[160,2304]{1,0:T(8,128)(2,1)S(1)}, u32[]{:S(2)}, u32[]{:S(2)}) collective-permute-start(bf16[160,2304]{1,0:T(8,128)(2,1)S(1)} %copy-done.133), channel_id=1, source_target_pairs={{0,2},{1,3},{2,0},{3,1},{4,6},{5,7},{6,4},{7,5},{8,10},{9,11},{10,... | collective-permute-start | bytes 2211848 | tf_op jit(solution)/shard_map/ppermute | solution.py:92
  508.7 13.8 %collective-permute-start.50 = (bf16[160,2304]{1,0:T(8,128)(2,1)S(1)}, bf16[160,2304]{1,0:T(8,128)(2,1)S(1)}, u32[]{:S(2)}, u32[]{:S(2)}) collective-permute-start(bf16[160,2304]{1,0:T(8,128)(2,1)S(1)} %copy-done.132), channel_id=1, source_target_pairs={{0,8},{4,12},{8,0},{12,4},{16,24},{20,28},{24,16},{28,20},{1,9},{5... | collective-permute-start | bytes 2211848 | tf_op jit(solution)/shard_map/ppermute | solution.py:92
  542.2 16.2 %collective-permute-start.56 = (bf16[2,96,1152]{2,1,0:T(8,128)(2,1)S(1)}, bf16[2,96,1152]{2,1,0:T(8,128)(2,1)S(1)}, u32[]{:S(2)}, u32[]{:S(2)}) collective-permute-start(bf16[2,96,1152]{2,1,0:T(8,128)(2,1)S(1)} %pad_maximum_fusion.21), channel_id=1, source_target_pairs={{0,16},{4,20},{8,24},{12,28},{16,0},{20,4},{24,8},{28,12},{1,17},{... | collective-permute-start | bytes 1327112 | tf_op jit(solution)/shard_map/ppermute | solution.py:92
  545.1 13.5 %collective-permute-start.55 = (bf16[160,2304]{1,0:T(8,128)(2,1)S(1)}, bf16[160,2304]{1,0:T(8,128)(2,1)S(1)}, u32[]{:S(2)}, u32[]{:S(2)}) collective-permute-start(bf16[160,2304]{1,0:T(8,128)(2,1)S(1)} %subtract_convert_fusion), channel_id=1, source_target_pairs={{0,2},{1,3},{2,0},{3,1},{4,6},{5,7},{6,4},{7,5},{8,10},{9,11},{10,... | collective-permute-start | bytes 2211848 | tf_op jit(solution)/shard_map/ppermute | solution.py:92
  546.5 12.2 %collective-permute-start.57 = (bf16[3,16,2304]{2,1,0:T(8,128)(2,1)S(1)}, bf16[3,16,2304]{2,1,0:T(8,128)(2,1)S(1)}, u32[]{:S(2)}, u32[]{:S(2)}) collective-permute-start(bf16[3,16,2304]{2,1,0:T(8,128)(2,1)S(1)} %fusion.29), channel_id=1, source_target_pairs={{0,8},{4,12},{8,0},{12,4},{16,24},{20,28},{24,16},{28,20},{1,9},{5... | collective-permute-start | bytes 663560 | tf_op jit(solution)/shard_map/ppermute | solution.py:92
  568.6 33.0 %collective-permute-start.66 = (bf16[4,96,1152]{2,1,0:T(8,128)(2,1)S(1)}, bf16[4,96,1152]{2,1,0:T(8,128)(2,1)S(1)}, u32[]{:S(2)}, u32[]{:S(2)}) collective-permute-start(bf16[4,96,1152]{2,1,0:T(8,128)(2,1)S(1)} %pad_maximum_fusion.12), channel_id=1, source_target_pairs={{0,8},{4,12},{8,0},{12,4},{16,24},{20,28},{24,16},{28,20},{1,9},{5... | collective-permute-start | bytes 2654216 | tf_op jit(solution)/shard_map/ppermute | solution.py:92
  578.8 11.6 %collective-permute-start.63 = (bf16[1,16,3456]{2,1,0:T(8,128)(2,1)S(1)}, bf16[1,16,3456]{2,1,0:T(8,128)(2,1)S(1)}, u32[]{:S(2)}, u32[]{:S(2)}) collective-permute-start(bf16[1,16,3456]{2,1,0:T(8,128)(2,1)S(1)} %bitcast.191), channel_id=1, source_target_pairs={{0,16},{4,20},{8,24},{12,28},{16,0},{20,4},{24,8},{28,12},{1,17},{... | collective-permute-start | bytes 331784 | tf_op jit(solution)/shard_map/ppermute | solution.py:92
  590.5 11.0 %collective-permute-start.65 = (bf16[2,16,3456]{2,1,0:T(8,128)(2,1)S(1)}, bf16[2,16,3456]{2,1,0:T(8,128)(2,1)S(1)}, u32[]{:S(2)}, u32[]{:S(2)}) collective-permute-start(bf16[2,16,3456]{2,1,0:T(8,128)(2,1)S(1)} %pad_maximum_fusion.29), channel_id=1, source_target_pairs={{0,8},{4,12},{8,0},{12,4},{16,24},{20,28},{24,16},{28,20},{1,9},{5... | collective-permute-start | bytes 663560 | tf_op jit(solution)/shard_map/ppermute | solution.py:92
  604.9 39.5 %all-to-all-start.9 = ((bf16[8,16,6144]{2,1,0:T(8,128)(2,1)}), bf16[8,16,6144]{2,1,0:T(8,128)(2,1)S(1)}, u32[]{:S(2)}, u32[]{:S(2)}) async-start(bf16[8,16,6144]{2,1,0:T(8,128)(2,1)} %broadcast_in_dim.229), calls=%async_computation.9 | async-start | bytes 3145728 | tf_op jit(solution)/shard_map/all_to_all | solution.py:1066
  609.5 26.4 %collective-permute-start.68 = (bf16[4,16,3456]{2,1,0:T(8,128)(2,1)S(1)}, bf16[4,16,3456]{2,1,0:T(8,128)(2,1)S(1)}, u32[]{:S(2)}, u32[]{:S(2)}) collective-permute-start(bf16[4,16,3456]{2,1,0:T(8,128)(2,1)S(1)} %pad_maximum_fusion.22), channel_id=1, source_target_pairs={{0,4},{4,0},{8,12},{12,8},{16,20},{20,16},{24,28},{28,24},{1,5},{5... | collective-permute-start | bytes 1327112 | tf_op jit(solution)/shard_map/ppermute | solution.py:92
  613.3 22.6 %collective-permute-start.67 = (bf16[160,2304]{1,0:T(8,128)(2,1)S(1)}, bf16[160,2304]{1,0:T(8,128)(2,1)S(1)}, u32[]{:S(2)}, u32[]{:S(2)}) collective-permute-start(bf16[160,2304]{1,0:T(8,128)(2,1)S(1)} %slice.632), channel_id=1, source_target_pairs={{0,2},{1,3},{2,0},{3,1},{4,6},{5,7},{6,4},{7,5},{8,10},{9,11},{10,... | collective-permute-start | bytes 2211848 | tf_op jit(solution)/shard_map/ppermute | solution.py:92
  (164 other events, 1020.4 us)

commit v6 on v5

--- a/solution.py
+++ b/solution.py
@@ -767,14 +767,15 @@
     transfers(0)
     own_rows = layer_input.astype(jnp.float32)
     normed = low(rms_scale(own_rows, norm_gain[0]))
-    near_ids = flip(adapter_ids, "dp", 2)
+    normed, late_ids = settle(normed, adapter_ids)
+    near_ids = flip(late_ids, "dp", 2)
     labels = jnp.arange(ADAPTERS, dtype=jnp.int32)
     order = jnp.stack([my_part, my_part ^ 2, my_part ^ 1, my_part ^ 3]).astype(jnp.int32)
     visible, cos_rows, sin_rows = tree_tables(segment_ids, parent_segments[0], order)
     row_count = 2 * normed.shape[0]
     visible = low(visible[:row_count])
     cos_rows, sin_rows = cos_rows[:row_count], sin_rows[:row_count]
-    ids_parts = [adapter_ids, flip(adapter_ids, "dp", 1)]
+    ids_parts = [late_ids, flip(late_ids, "dp", 1)]
     normed, near_ids, visible, cos_rows, sin_rows, ids_parts = close(
         0, normed, near_ids, visible, cos_rows, sin_rows, ids_parts
     )

time: 661 us -> 663 us (level)
    unnamed x308 -> x310, local copies, waits for them, and re-layouts: 59.9 us -> 59.9 us
  transfers between devices with their start and end apart: 81 -> 81, of which waited for: 39 -> 39; matrix products, arithmetic and copies ran while one was open for 14% -> 13% of each run, Pallas kernels for 12% -> 12%
where the time goes in v6:
time: 663 us; the launch traced here: 654 us
  waiting for transfers between devices  254 us (38%)
  Pallas kernels  128 us (19%)
  starting transfers between devices  109 us (16%)
  local copies, waits for them, and re-layouts  79.6 us (12%)
  other arithmetic  44.3 us (7%)
  matrix products  34.3 us (5%)
    ppermute x71, waiting for transfers between devices, flip(): return lax.ppermute(values, axis_name, [(i, i ^ bit) for i in range(size)])  222 us
    ppermute x71, starting transfers between devices, flip(): return lax.ppermute(values, axis_name, [(i, i ^ bit) for i in range(size)])  65.6 us
    unnamed x310, local copies, waits for them, and re-layouts  59.9 us
    all_to_all x9, starting transfers between devices, along_z(): return lax.all_to_all(sent, 'dp', 0, 0, axis_index_groups=lines)  40 us
    pallas_call x1, Pallas kernels, feed_forward_back(): pl.pallas_call(kernel, out_shape=parts + [jax.ShapeDtypeStruct((count, tw...  39.1 us
    all_to_all x9, waiting for transfers between devices, along_z(): return lax.all_to_all(sent, 'dp', 0, 0, axis_index_groups=lines)  29.3 us
    pallas_call x2, Pallas kernels, gate_and_up(): pl.pallas_call(kernel, out_shape=[jax.ShapeDtypeStruct((count, units), jn...  26 us
    pallas_call x8, Pallas kernels, assemble(): pl.pallas_call(kernel, out_shape=jax.ShapeDtypeStruct((2 * columns_z, row...  22.7 us
  transfers between devices with their start and end apart: 81, of which 39 were waited for; matrix products, arithmetic and copies ran while one was open for 13% of the time, Pallas kernels for 12%

profile of v6, /device:TPU:0, one launch (start us, length us, event | category | flops | bytes accessed | tf_op | source)
XLA Modules:
  0.0 653.6 jit_solution(12797568356915299912)
XLA Ops:
  5.4 3.1 collective-permute-start
  11.3 4.0 all-to-all-start
  17.8 25.5 %all-to-all-done.refs_0_ = bf16[4,144,1024]{2,1,0:T(8,128)(2,1)S(1)} async-done(((bf16[4,144,1024]{2,1,0:T(8,128)(2,1)}), bf16[4,144,1024]{2,1,0:T(8,128)(2,1)S(1)}, u32[]{:S(2)}, u32[]{:S(2)}) %all-to-all-start) | async-done | bytes 1179680 | tf_op jit(solution)/shard_map/all_to_all | solution.py:102
  48.0 4.3 all-to-all-start.1
  53.5 8.6 %collective-permute-done.4 = bf16[160,2304]{1,0:T(8,128)(2,1)} collective-permute-done((bf16[160,2304]{1,0:T(8,128)(2,1)S(1)}, bf16[160,2304]{1,0:T(8,128)(2,1)}, u32[]{:S(2)}, u32[]{:S(2)}) %collective-permute-start.4) | collective-permute-done | bytes 737312 | tf_op jit(solution)/shard_map/ppermute | solution.py:92
  63.5 3.0 shard_map.387
  84.0 3.5 all-to-all-start.2
  95.2 11.7 %collective-permute-done.11 = s32[4]{0:T(128)} collective-permute-done((s32[4]{0:T(128)S(1)}, s32[4]{0:T(128)}, u32[]{:S(2)}, u32[]{:S(2)}) %collective-permute-start.11) | collective-permute-done | bytes 48 | tf_op jit(solution)/shard_map/ppermute | solution.py:92
  108.2 7.2 %collective-permute-done.6.refs_5_ = bf16[4,144,1024]{2,1,0:T(8,128)(2,1)S(1)} collective-permute-done((bf16[4,144,1024]{2,1,0:T(8,128)(2,1)}, bf16[4,144,1024]{2,1,0:T(8,128)(2,1)S(1)}, u32[]{:S(2)}, u32[]{:S(2)}) %collective-permute-start.6) | collective-permute-done | bytes 1179680 | tf_op jit(solution)/shard_map/ppermute | solution.py:92
  118.4 4.7 all-to-all-start.3
  133.5 17.7 %collective-permute-done.12.refs_1_ = bf16[4,288,512]{2,1,0:T(8,128)(2,1)} collective-permute-done((bf16[4,288,512]{2,1,0:T(8,128)(2,1)S(1)}, bf16[4,288,512]{2,1,0:T(8,128)(2,1)}, u32[]{:S(2)}, u32[]{:S(2)}) %collective-permute-start.12) | collective-permute-done | bytes 1179680 | tf_op jit(solution)/shard_map/ppermute | solution.py:92
  153.2 4.9 all-to-all-start.4
  165.1 3.0 shard_map.388
  168.2 6.5 %shard_map.389.mine_ref = bf16[320,2048]{1,0:T(8,128)(2,1)S(1)} custom-call(bf16[320,2304]{1,0:T(8,128)(2,1)S(1)} %pad_maximum_fusion.1.rows_ref, bf16[2304,2048]{1,0:T(8,128)(2,1)S(1)} %bitcast.167, bf16[320,48]{1,0:T(8,128)(2,1)S(1)} %copy-done.46, bf16[48,2048]{1,0:T(8,128)(2,1)S(1)} %copy-done.23, f32[320,128]{1,0:T(8,128)S(1)} %get-tuple-element.273.cosine_ref.cos_ref, ...), custom_call_target="tpu_custom_call" | custom-call | flops 1 | bytes 1 | tf_op jit(solution)/shard_map/pallas_call | solution.py:215
  178.7 4.6 collective-permute-done.15.refs_1_
  184.1 4.2 all-to-all-start.5
  189.4 3.0 shard_map.390
  194.9 2.5 shard_map.391
  203.7 13.1 %collective-permute-done.22 = bf16[160,2304]{1,0:T(8,128)(2,1)S(1)} collective-permute-done((bf16[160,2304]{1,0:T(8,128)(2,1)S(1)}, bf16[160,2304]{1,0:T(8,128)(2,1)S(1)}, u32[]{:S(2)}, u32[]{:S(2)}) %collective-permute-start.22) | collective-permute-done | bytes 737312 | tf_op jit(solution)/shard_map/ppermute | solution.py:92
  218.0 8.7 %collective-permute-done.19.refs_1_ = bf16[4,288,512]{2,1,0:T(8,128)(2,1)S(1)} collective-permute-done((bf16[4,288,512]{2,1,0:T(8,128)(2,1)}, bf16[4,288,512]{2,1,0:T(8,128)(2,1)S(1)}, u32[]{:S(2)}, u32[]{:S(2)}) %collective-permute-start.19) | collective-permute-done | bytes 1179680 | tf_op jit(solution)/shard_map/ppermute | solution.py:92
  231.8 4.9 all-to-all-start.6
  245.6 2.8 shard_map.392
  250.7 18.5 %collective-permute-done.27 = bf16[80,2304]{1,0:T(8,128)(2,1)S(1)} collective-permute-done((bf16[80,2304]{1,0:T(8,128)(2,1)S(1)}, bf16[80,2304]{1,0:T(8,128)(2,1)S(1)}, u32[]{:S(2)}, u32[]{:S(2)}) %collective-permute-start.27) | collective-permute-done | bytes 368672 | tf_op jit(solution)/shard_map/ppermute | solution.py:92
  272.3 4.3 all-to-all-start.7
  283.7 2.3 shard_map.393
  289.0 19.3 %collective-permute-done.31 = bf16[80,2304]{1,0:T(8,128)(2,1)S(1)} collective-permute-done((bf16[80,2304]{1,0:T(8,128)(2,1)S(1)}, bf16[80,2304]{1,0:T(8,128)(2,1)S(1)}, u32[]{:S(2)}, u32[]{:S(2)}) %collective-permute-start.31) | collective-permute-done | bytes 368672 | tf_op jit(solution)/shard_map/ppermute | solution.py:92
  308.3 2.3 collective-permute-done.28.refs_1_
  312.9 5.2 all-to-all-start.8
  323.3 2.8 shard_map.395
  326.1 2.5 copy-done
  332.2 3.4 fusion.15.inner_ref
  335.6 11.9 %shard_map.394 = (bf16[640,1024]{1,0:T(8,128)(2,1)}, bf16[640,1024]{1,0:T(8,128)(2,1)}, bf16[640,1024]{1,0:T(8,128)(2,1)}) custom-call(bf16[640,2304]{1,0:T(8,128)(2,1)} %constant_dynamic-update-slice_fusion.6.rows_ref, bf16[2304,1024]{1,0:T(8,128)(2,1)} %bitcast.161, bf16[2304,1024]{1,0:T(8,128)(2,1)} %bitcast.163, bf16[640,64]{1,0:T(8,128)(2,1)} %fusion.15.inner_ref, ...), custom_call_target="tpu_custom_call" | custom-call | flops 1 | bytes 1 | tf_op jit(solution)/shard_map/pallas_call | solution.py:356
  347.6 4.1 collective-permute-done.33.refs_1_
  354.8 3.1 shard_map.396
  357.9 2.4 copy-done.1
  360.3 14.0 %shard_map.397 = (bf16[640,1280]{1,0:T(8,128)(2,1)}, bf16[640,1280]{1,0:T(8,128)(2,1)}, bf16[640,1280]{1,0:T(8,128)(2,1)}) custom-call(bf16[640,2304]{1,0:T(8,128)(2,1)} %constant_dynamic-update-slice_fusion.6.rows_ref, bf16[2304,1280]{1,0:T(8,128)(2,1)} %bitcast.157, bf16[2304,1280]{1,0:T(8,128)(2,1)} %bitcast.159, bf16[640,64]{1,0:T(8,128)(2,1)} %fusion.15.inner_ref, ...), custom_call_target="tpu_custom_call" | custom-call | flops 1 | bytes 1 | tf_op jit(solution)/shard_map/pallas_call | solution.py:356
  378.9 3.5 shard_map.398
  382.3 5.8 convolution_add_fusion.first_ref
  388.5 2.8 collective-permute-done.40.refs_3_
  391.3 2.8 shard_map.399
  396.3 6.8 %shard_map.400 = (f32[160,2304]{1,0:T(8,128)S(1)}, f32[80,2304]{1,0:T(8,128)S(1)}, f32[80,2304]{1,0:T(8,128)S(1)}, bf16[160,2304]{1,0:T(8,128)(2,1)S(1)}, bf16[160,2304]{1,0:T(8,128)(2,1)S(1)}) custom-call(f32[640,2304]{1,0:T(8,128)} %convolution_add_fusion.first_ref, bf16[640,1024]{1,0:T(8,128)(2,1)S(1)} %copy-done.11, bf16[2304,1024]{1,0:T(8,128)(2,1)} %bitcast.165), custom_call_target="tpu_custom_call" | custom-call | flops 1 | bytes 1 | tf_op jit(solution)/shard_map/pallas_call | solution.py:403
  406.4 15.5 %collective-permute-done.41 = bf16[160,2304]{1,0:T(8,128)(2,1)S(1)} collective-permute-done((bf16[160,2304]{1,0:T(8,128)(2,1)S(1)}, bf16[160,2304]{1,0:T(8,128)(2,1)S(1)}, u32[]{:S(2)}, u32[]{:S(2)}) %collective-permute-start.41) | collective-permute-done | bytes 737312 | tf_op jit(solution)/shard_map/ppermute | solution.py:92
  425.6 7.5 %collective-permute-done.43 = bf16[80,2304]{1,0:T(8,128)(2,1)S(1)} collective-permute-done((bf16[80,2304]{1,0:T(8,128)(2,1)S(1)}, bf16[80,2304]{1,0:T(8,128)(2,1)S(1)}, u32[]{:S(2)}, u32[]{:S(2)}) %collective-permute-start.43) | collective-permute-done | bytes 368672 | tf_op jit(solution)/shard_map/ppermute | solution.py:92
  440.4 13.2 %collective-permute-done.45 = bf16[160,2304]{1,0:T(8,128)(2,1)S(1)} collective-permute-done((bf16[160,2304]{1,0:T(8,128)(2,1)S(1)}, bf16[160,2304]{1,0:T(8,128)(2,1)S(1)}, u32[]{:S(2)}, u32[]{:S(2)}) %collective-permute-start.45) | collective-permute-done | bytes 737312 | tf_op jit(solution)/shard_map/ppermute | solution.py:92
  458.2 4.2 collective-permute-done.47
  463.9 39.1 %shard_map.401 = (f32[160,2304]{1,0:T(8,128)}, f32[80,2304]{1,0:T(8,128)}, f32[80,2304]{1,0:T(8,128)}, bf16[160,2304]{1,0:T(8,128)(2,1)}, bf16[160,2304]{1,0:T(8...) custom-call(bf16[640,2304]{1,0:T(8,128)(2,1)} %constant_dynamic-upda, ...), custom_call_target="tpu_custom_call" | custom-call | flops 1 | bytes 1 | tf_op jit(solution)/shard_map/pallas_call | solution.py:493
  503.1 2.6 fusion.33
  513.3 10.6 %collective-permute-done.49 = bf16[160,2304]{1,0:T(8,128)(2,1)S(1)} collective-permute-done((bf16[160,2304]{1,0:T(8,128)(2,1)S(1)}, bf16[160,2304]{1,0:T(8,128)(2,1)S(1)}, u32[]{:S(2)}, u32[]{:S(2)}) %collective-permute-start.49) | collective-permute-done | bytes 737312 | tf_op jit(solution)/shard_map/ppermute | solution.py:92
  524.2 2.5 fusion.69
  532.7 4.6 collective-permute-done.52
  544.0 2.9 collective-permute-start.56
  549.3 10.9 %collective-permute-done.56 = bf16[2,96,1152]{2,1,0:T(8,128)(2,1)S(1)} collective-permute-done((bf16[2,96,1152]{2,1,0:T(8,128)(2,1)S(1)}, bf16[2,96,1152]{2,1,0:T(8,128)(2,1)S(1)}, u32[]{:S(2)}, u32[]{:S(2)}) %collective-permute-start.56) | collective-permute-done | bytes 442400 | tf_op jit(solution)/shard_map/ppermute | solution.py:92
  564.0 5.6 shard_map.402
  572.3 5.7 collective-permute-done.60
  580.6 3.1 collective-permute-start.63
  585.0 7.2 %collective-permute-done.63 = bf16[1,16,3456]{2,1,0:T(8,128)(2,1)S(1)} collective-permute-done((bf16[1,16,3456]{2,1,0:T(8,128)(2,1)S(1)}, bf16[1,16,3456]{2,1,0:T(8,128)(2,1)S(1)}, u32[]{:S(2)}, u32[]{:S(2)}) %collective-permute-start.63) | collective-permute-done | bytes 110624 | tf_op jit(solution)/shard_map/ppermute | solution.py:92
  592.3 3.9 collective-permute-start.65
  598.4 4.9 convolution_add_fusion.1
  606.6 3.6 all-to-all-start.9
  616.8 8.4 %shard_map.403 = (f32[8,16,2304]{2,1,0:T(8,128)}, f32[8,16,2304]{2,1,0:T(8,128)}, f32[8,16,2304]{2,1,0:T(8,128)}) custom-call(f32[2,16,8]{2,1,0:T(8,128)S(1)} %pad_maximum_fusion.38.hots_ref, bf16[16,48,1152]{2,1,0:T(8,128)(2,1)S(1)} %bitcast.173), custom_call_target="tpu_custom_call" | custom-call | flops 1 | bytes 1 | tf_op jit(solution)/shard_map/pallas_call | solution.py:595
  625.2 12.4 %collective-permute-done.68 = bf16[4,16,3456]{2,1,0:T(8,128)(2,1)S(1)} collective-permute-done((bf16[4,16,3456]{2,1,0:T(8,128)(2,1)S(1)}, bf16[4,16,3456]{2,1,0:T(8,128)(2,1)S(1)}, u32[]{:S(2)}, u32[]{:S(2)}) %collective-permute-start.68) | collective-permute-done | bytes 442400 | tf_op jit(solution)/shard_map/ppermute | solution.py:92
  643.6 2.6 all-to-all-done.9.gathered_ref
  648.0 2.8 collective-permute-done.70.other_ref
  650.8 2.3 shard_map.407
  (639 shorter events, 204.5 us)
Async XLA Ops:
  5.4 12.4 %collective-permute-start = (s32[1]{0:T(128)}, s32[1]{0:T(128)}, u32[]{:S(2)}, u32[]{:S(2)}) collective-permute-start(s32[1]{0:T(128)} %param.52), channel_id=1, source_target_pairs={{0,8},{4,12},{8,0},{12,4},{16,24},{20,28},{24,16},{28,20},{1,9},{5... | collective-permute-start | bytes 20 | tf_op jit(solution)/shard_map/ppermute | solution.py:92
  8.5 9.3 %collective-permute-start.1 = (s32[1]{0:T(128)}, s32[1]{0:T(128)}, u32[]{:S(2)}, u32[]{:S(2)}) collective-permute-start(s32[1]{0:T(128)} %param.52), channel_id=1, source_target_pairs={{0,4},{4,0},{8,12},{12,8},{16,20},{20,16},{24,28},{28,24},{1,5},{5... | collective-permute-start | bytes 20 | tf_op jit(solution)/shard_map/ppermute | solution.py:92
  11.3 32.0 %all-to-all-start = ((bf16[4,144,1024]{2,1,0:T(8,128)(2,1)}), bf16[4,144,1024]{2,1,0:T(8,128)(2,1)S(1)}, u32[]{:S(2)}, u32[]{:S(2)}) async-start(bf16[4,144,1024]{2,1,0:T(8,128)(2,1)} %concatenate.174), calls=%async_computation | async-start | bytes 2359296 | tf_op jit(solution)/shard_map/all_to_all | solution.py:102
  44.5 17.5 %collective-permute-start.4 = (bf16[160,2304]{1,0:T(8,128)(2,1)S(1)}, bf16[160,2304]{1,0:T(8,128)(2,1)}, u32[]{:S(2)}, u32[]{:S(2)}) collective-permute-start(bf16[160,2304]{1,0:T(8,128)(2,1)S(1)} %fusion.7), channel_id=1, source_target_pairs={{0,2},{1,3},{2,0},{3,1},{4,6},{5,7},{6,4},{7,5},{8,10},{9,11},{10,... | collective-permute-start | bytes 2211848 | tf_op jit(solution)/shard_map/ppermute | solution.py:92
  46.7 33.9 %collective-permute-start.2 = (bf16[4,144,1024]{2,1,0:T(8,128)(2,1)S(1)}, bf16[4,144,1024]{2,1,0:T(8,128)(2,1)}, u32[]{:S(2)}, u32[]{:S(2)}) collective-permute-start(bf16[4,144,1024]{2,1,0:T(8,128)(2,1)S(1)} %all-to-all-done.refs_0_), channel_id=1, source_target_pairs={{0,4},{4,0},{8,12},{12,8},{16,20},{20,16},{24,28},{28,24},{1,5},{5... | collective-permute-start | bytes 3538952 | tf_op jit(solution)/shard_map/ppermute | solution.py:92
  47.3 33.3 %collective-permute-start.3 = (bf16[4,144,1024]{2,1,0:T(8,128)(2,1)S(1)}, bf16[4,144,1024]{2,1,0:T(8,128)(2,1)}, u32[]{:S(2)}, u32[]{:S(2)}) collective-permute-start(bf16[4,144,1024]{2,1,0:T(8,128)(2,1)S(1)} %all-to-all-done.refs_0_), channel_id=1, source_target_pairs={{0,1},{1,0},{2,3},{3,2},{4,5},{5,4},{6,7},{7,6},{8,9},{9,8},{10,11... | collective-permute-start | bytes 3538952 | tf_op jit(solution)/shard_map/ppermute | solution.py:92
  48.0 32.6 %collective-permute-start.5 = (s32[2]{0:T(128)S(1)}, s32[2]{0:T(128)S(1)}, u32[]{:S(2)}, u32[]{:S(2)}) collective-permute-start(s32[2]{0:T(128)S(1)} %pad_add_fusion.3), channel_id=1, source_target_pairs={{0,16},{4,20},{8,24},{12,28},{16,0},{20,4},{24,8},{28,12},{1,17},{... | collective-permute-start | bytes 32 | tf_op jit(solution)/shard_map/ppermute | solution.py:92
  48.0 33.8 %all-to-all-start.1 = ((bf16[4,144,1024]{2,1,0:T(8,128)(2,1)}), bf16[4,144,1024]{2,1,0:T(8,128)(2,1)}, u32[]{:S(2)}, u32[]{:S(2)}) async-start(bf16[4,144,1024]{2,1,0:T(8,128)(2,1)} %concatenate.176), calls=%async_computation.1 | async-start | bytes 2359296 | tf_op jit(solution)/shard_map/all_to_all | solution.py:102
  84.0 34.5 %all-to-all-start.2 = ((bf16[4,288,512]{2,1,0:T(8,128)(2,1)}), bf16[4,288,512]{2,1,0:T(8,128)(2,1)S(1)}, u32[]{:S(2)}, u32[]{:S(2)}) async-start(bf16[4,288,512]{2,1,0:T(8,128)(2,1)} %concatenate.177), calls=%async_computation.2 | async-start | bytes 2359296 | tf_op jit(solution)/shard_map/all_to_all | solution.py:102
  87.5 27.9 %collective-permute-start.6 = (bf16[4,144,1024]{2,1,0:T(8,128)(2,1)}, bf16[4,144,1024]{2,1,0:T(8,128)(2,1)S(1)}, u32[]{:S(2)}, u32[]{:S(2)}) collective-permute-start(bf16[4,144,1024]{2,1,0:T(8,128)(2,1)} %all-to-all-done.1.refs_4_), channel_id=1, source_target_pairs={{0,4},{4,0},{8,12},{12,8},{16,20},{20,16},{24,28},{28,24},{1,5},{5... | collective-permute-start | bytes 3538952 | tf_op jit(solution)/shard_map/ppermute | solution.py:92
  89.0 26.3 %collective-permute-start.7 = (bf16[4,144,1024]{2,1,0:T(8,128)(2,1)}, bf16[4,144,1024]{2,1,0:T(8,128)(2,1)S(1)}, u32[]{:S(2)}, u32[]{:S(2)}) collective-permute-start(bf16[4,144,1024]{2,1,0:T(8,128)(2,1)} %all-to-all-done.1.refs_4_), channel_id=1, source_target_pairs={{0,1},{1,0},{2,3},{3,2},{4,5},{5,4},{6,7},{7,6},{8,9},{9,8},{10,11... | collective-permute-start | bytes 3538952 | tf_op jit(solution)/shard_map/ppermute | solution.py:92
  89.0 28.3 %collective-permute-start.8 = (bf16[4,144,1024]{2,1,0:T(8,128)(2,1)}, bf16[4,144,1024]{2,1,0:T(8,128)(2,1)S(1)}, u32[]{:S(2)}, u32[]{:S(2)}) collective-permute-start(bf16[4,144,1024]{2,1,0:T(8,128)(2,1)} %collective-permute-done.2.refs_1_), channel_id=1, source_target_pairs={{0,1},{1,0},{2,3},{3,2},{4,5},{5,4},{6,7},{7,6},{8,9},{9,8},{10,11... | collective-permute-start | bytes 3538952 | tf_op jit(solution)/shard_map/ppermute | solution.py:92
  93.3 13.6 %collective-permute-start.11 = (s32[4]{0:T(128)S(1)}, s32[4]{0:T(128)}, u32[]{:S(2)}, u32[]{:S(2)}) collective-permute-start(s32[4]{0:T(128)S(1)} %pad_add_fusion.4), channel_id=1, source_target_pairs={{0,8},{4,12},{8,0},{12,4},{16,24},{20,28},{24,16},{28,20},{1,9},{5... | collective-permute-start | bytes 56 | tf_op jit(solution)/shard_map/ppermute | solution.py:92
  95.2 13.0 %collective-permute-start.10 = (bf16[96,1152]{1,0:T(8,128)(2,1)}, bf16[96,1152]{1,0:T(8,128)(2,1)S(1)}, u32[]{:S(2)}, u32[]{:S(2)}) collective-permute-start(bf16[96,1152]{1,0:T(8,128)(2,1)} %constant_dynamic-update-slice_fusion), channel_id=1, source_target_pairs={{0,1},{1,0},{2,3},{3,2},{4,5},{5,4},{6,7},{7,6},{8,9},{9,8},{10,11... | collective-permute-start | bytes 663560 | tf_op jit(solution)/shard_map/ppermute | solution.py:92
  118.4 34.7 %all-to-all-start.3 = ((bf16[4,288,512]{2,1,0:T(8,128)(2,1)}), bf16[4,288,512]{2,1,0:T(8,128)(2,1)}, u32[]{:S(2)}, u32[]{:S(2)}) async-start(bf16[4,288,512]{2,1,0:T(8,128)(2,1)} %pad_maximum_fusion.7), calls=%async_computation.3 | async-start | bytes 2359296 | tf_op jit(solution)/shard_map/all_to_all | solution.py:102
  124.7 26.5 %collective-permute-start.12 = (bf16[4,288,512]{2,1,0:T(8,128)(2,1)S(1)}, bf16[4,288,512]{2,1,0:T(8,128)(2,1)}, u32[]{:S(2)}, u32[]{:S(2)}) collective-permute-start(bf16[4,288,512]{2,1,0:T(8,128)(2,1)S(1)} %all-to-all-done.2.refs_0_), channel_id=1, source_target_pairs={{0,4},{4,0},{8,12},{12,8},{16,20},{20,16},{24,28},{28,24},{1,5},{5... | collective-permute-start | bytes 3538952 | tf_op jit(solution)/shard_map/ppermute | solution.py:92
  126.2 24.9 %collective-permute-start.13 = (bf16[4,288,512]{2,1,0:T(8,128)(2,1)S(1)}, bf16[4,288,512]{2,1,0:T(8,128)(2,1)S(1)}, u32[]{:S(2)}, u32[]{:S(2)}) collective-permute-start(bf16[4,288,512]{2,1,0:T(8,128)(2,1)S(1)} %all-to-all-done.2.refs_0_), channel_id=1, source_target_pairs={{0,1},{1,0},{2,3},{3,2},{4,5},{5,4},{6,7},{7,6},{8,9},{9,8},{10,11... | collective-permute-start | bytes 3538952 | tf_op jit(solution)/shard_map/ppermute | solution.py:92
  126.2 25.9 %collective-permute-start.14 = (bf16[4,144,1024]{2,1,0:T(8,128)(2,1)S(1)}, bf16[4,144,1024]{2,1,0:T(8,128)(2,1)S(1)}, u32[]{:S(2)}, u32[]{:S(2)}) collective-permute-start(bf16[4,144,1024]{2,1,0:T(8,128)(2,1)S(1)} %copy-done.38), channel_id=1, source_target_pairs={{0,1},{1,0},{2,3},{3,2},{4,5},{5,4},{6,7},{7,6},{8,9},{9,8},{10,11... | collective-permute-start | bytes 3538952 | tf_op jit(solution)/shard_map/ppermute | solution.py:92
  153.2 30.9 %all-to-all-start.4 = ((bf16[4,288,512]{2,1,0:T(8,128)(2,1)}), bf16[4,288,512]{2,1,0:T(8,128)(2,1)}, u32[]{:S(2)}, u32[]{:S(2)}) async-start(bf16[4,288,512]{2,1,0:T(8,128)(2,1)} %pad_maximum_fusion.8), calls=%async_computation.4 | async-start | bytes 2359296 | tf_op jit(solution)/shard_map/all_to_all | solution.py:102
  158.0 25.3 %collective-permute-start.15 = (bf16[4,288,512]{2,1,0:T(8,128)(2,1)}, bf16[4,288,512]{2,1,0:T(8,128)(2,1)}, u32[]{:S(2)}, u32[]{:S(2)}) collective-permute-start(bf16[4,288,512]{2,1,0:T(8,128)(2,1)} %all-to-all-done.3.refs_0_), channel_id=1, source_target_pairs={{0,4},{4,0},{8,12},{12,8},{16,20},{20,16},{24,28},{28,24},{1,5},{5... | collective-permute-start | bytes 3538952 | tf_op jit(solution)/shard_map/ppermute | solution.py:92
  159.5 23.8 %collective-permute-start.16 = (bf16[4,288,512]{2,1,0:T(8,128)(2,1)}, bf16[4,288,512]{2,1,0:T(8,128)(2,1)}, u32[]{:S(2)}, u32[]{:S(2)}) collective-permute-start(bf16[4,288,512]{2,1,0:T(8,128)(2,1)} %all-to-all-done.3.refs_0_), channel_id=1, source_target_pairs={{0,1},{1,0},{2,3},{3,2},{4,5},{5,4},{6,7},{7,6},{8,9},{9,8},{10,11... | collective-permute-start | bytes 3538952 | tf_op jit(solution)/shard_map/ppermute | solution.py:92
  159.5 23.8 %collective-permute-start.17 = (bf16[4,288,512]{2,1,0:T(8,128)(2,1)}, bf16[4,288,512]{2,1,0:T(8,128)(2,1)}, u32[]{:S(2)}, u32[]{:S(2)}) collective-permute-start(bf16[4,288,512]{2,1,0:T(8,128)(2,1)} %collective-permute-done.12.refs_1_), channel_id=1, source_target_pairs={{0,1},{1,0},{2,3},{3,2},{4,5},{5,4},{6,7},{7,6},{8,9},{9,8},{10,11... | collective-permute-start | bytes 3538952 | tf_op jit(solution)/shard_map/ppermute | solution.py:92
  184.1 44.6 %all-to-all-start.5 = ((bf16[4,288,640]{2,1,0:T(8,128)(2,1)}), bf16[4,288,640]{2,1,0:T(8,128)(2,1)S(1)}, u32[]{:S(2)}, u32[]{:S(2)}) async-start(bf16[4,288,640]{2,1,0:T(8,128)(2,1)} %pad_maximum_fusion.2), calls=%async_computation.5 | async-start | bytes 2949120 | tf_op jit(solution)/shard_map/all_to_all | solution.py:102
  199.7 17.1 %collective-permute-start.22 = (bf16[160,2304]{1,0:T(8,128)(2,1)S(1)}, bf16[160,2304]{1,0:T(8,128)(2,1)S(1)}, u32[]{:S(2)}, u32[]{:S(2)}) collective-permute-start(bf16[160,2304]{1,0:T(8,128)(2,1)S(1)} %slice.633), channel_id=1, source_target_pairs={{0,2},{1,3},{2,0},{3,1},{4,6},{5,7},{6,4},{7,5},{8,10},{9,11},{10,... | collective-permute-start | bytes 2211848 | tf_op jit(solution)/shard_map/ppermute | solution.py:92
  200.2 26.5 %collective-permute-start.19 = (bf16[4,288,512]{2,1,0:T(8,128)(2,1)}, bf16[4,288,512]{2,1,0:T(8,128)(2,1)S(1)}, u32[]{:S(2)}, u32[]{:S(2)}) collective-permute-start(bf16[4,288,512]{2,1,0:T(8,128)(2,1)} %all-to-all-done.4.refs_0_), channel_id=1, source_target_pairs={{0,4},{4,0},{8,12},{12,8},{16,20},{20,16},{24,28},{28,24},{1,5},{5... | collective-permute-start | bytes 3538952 | tf_op jit(solution)/shard_map/ppermute | solution.py:92
  201.7 25.0 %collective-permute-start.20 = (bf16[4,288,512]{2,1,0:T(8,128)(2,1)}, bf16[4,288,512]{2,1,0:T(8,128)(2,1)S(1)}, u32[]{:S(2)}, u32[]{:S(2)}) collective-permute-start(bf16[4,288,512]{2,1,0:T(8,128)(2,1)} %all-to-all-done.4.refs_0_), channel_id=1, source_target_pairs={{0,1},{1,0},{2,3},{3,2},{4,5},{5,4},{6,7},{7,6},{8,9},{9,8},{10,11... | collective-permute-start | bytes 3538952 | tf_op jit(solution)/shard_map/ppermute | solution.py:92
  201.7 26.0 %collective-permute-start.21 = (bf16[4,288,512]{2,1,0:T(8,128)(2,1)}, bf16[4,288,512]{2,1,0:T(8,128)(2,1)S(1)}, u32[]{:S(2)}, u32[]{:S(2)}) collective-permute-start(bf16[4,288,512]{2,1,0:T(8,128)(2,1)} %collective-permute-done.15.refs_1_), channel_id=1, source_target_pairs={{0,1},{1,0},{2,3},{3,2},{4,5},{5,4},{6,7},{7,6},{8,9},{9,8},{10,11... | collective-permute-start | bytes 3538952 | tf_op jit(solution)/shard_map/ppermute | solution.py:92
  228.7 41.5 %collective-permute-start.23 = (bf16[4,288,640]{2,1,0:T(8,128)(2,1)S(1)}, bf16[4,288,640]{2,1,0:T(8,128)(2,1)}, u32[]{:S(2)}, u32[]{:S(2)}) collective-permute-start(bf16[4,288,640]{2,1,0:T(8,128)(2,1)S(1)} %all-to-all-done.5.refs_0_), channel_id=1, source_target_pairs={{0,4},{4,0},{8,12},{12,8},{16,20},{20,16},{24,28},{28,24},{1,5},{5... | collective-permute-start | bytes 4423688 | tf_op jit(solution)/shard_map/ppermute | solution.py:92
  230.2 40.3 %collective-permute-start.24 = (bf16[4,288,640]{2,1,0:T(8,128)(2,1)S(1)}, bf16[4,288,640]{2,1,0:T(8,128)(2,1)}, u32[]{:S(2)}, u32[]{:S(2)}) collective-permute-start(bf16[4,288,640]{2,1,0:T(8,128)(2,1)S(1)} %all-to-all-done.5.refs_0_), channel_id=1, source_target_pairs={{0,1},{1,0},{2,3},{3,2},{4,5},{5,4},{6,7},{7,6},{8,9},{9,8},{10,11... | collective-permute-start | bytes 4423688 | tf_op jit(solution)/shard_map/ppermute | solution.py:92
  231.8 40.6 %all-to-all-start.6 = ((bf16[4,288,640]{2,1,0:T(8,128)(2,1)}), bf16[4,288,640]{2,1,0:T(8,128)(2,1)}, u32[]{:S(2)}, u32[]{:S(2)}) async-start(bf16[4,288,640]{2,1,0:T(8,128)(2,1)} %pad_maximum_fusion.3), calls=%async_computation.6 | async-start | bytes 2949120 | tf_op jit(solution)/shard_map/all_to_all | solution.py:102
  237.2 32.0 %collective-permute-start.25 = (bf16[4,288,512]{2,1,0:T(8,128)(2,1)S(1)}, bf16[4,288,512]{2,1,0:T(8,128)(2,1)S(1)}, u32[]{:S(2)}, u32[]{:S(2)}) collective-permute-start(bf16[4,288,512]{2,1,0:T(8,128)(2,1)S(1)} %collective-permute-done.19.refs_1_), channel_id=1, source_target_pairs={{0,1},{1,0},{2,3},{3,2},{4,5},{5,4},{6,7},{7,6},{8,9},{9,8},{10,11... | collective-permute-start | bytes 3538952 | tf_op jit(solution)/shard_map/ppermute | solution.py:92
  239.7 29.4 %collective-permute-start.26 = (bf16[160,2304]{1,0:T(8,128)(2,1)S(1)}, bf16[160,2304]{1,0:T(8,128)(2,1)S(1)}, u32[]{:S(2)}, u32[]{:S(2)}) collective-permute-start(bf16[160,2304]{1,0:T(8,128)(2,1)S(1)} %multiply_convert_fusion), channel_id=1, source_target_pairs={{0,2},{1,3},{2,0},{3,1},{4,6},{5,7},{6,4},{7,5},{8,10},{9,11},{10,... | collective-permute-start | bytes 2211848 | tf_op jit(solution)/shard_map/ppermute | solution.py:92
  241.4 27.8 %collective-permute-start.27 = (bf16[80,2304]{1,0:T(8,128)(2,1)S(1)}, bf16[80,2304]{1,0:T(8,128)(2,1)S(1)}, u32[]{:S(2)}, u32[]{:S(2)}) collective-permute-start(bf16[80,2304]{1,0:T(8,128)(2,1)S(1)} %slice.454), channel_id=1, source_target_pairs={{0,8},{4,12},{8,0},{12,4},{16,24},{20,28},{24,16},{28,20},{1,9},{5... | collective-permute-start | bytes 1105928 | tf_op jit(solution)/shard_map/ppermute | solution.py:92
  272.3 40.6 %all-to-all-start.7 = ((bf16[4,288,640]{2,1,0:T(8,128)(2,1)}), bf16[4,288,640]{2,1,0:T(8,128)(2,1)}, u32[]{:S(2)}, u32[]{:S(2)}) async-start(bf16[4,288,640]{2,1,0:T(8,128)(2,1)} %pad_maximum_fusion.4), calls=%async_computation.7 | async-start | bytes 2949120 | tf_op jit(solution)/shard_map/all_to_all | solution.py:102
  276.7 34.0 %collective-permute-start.28 = (bf16[4,288,640]{2,1,0:T(8,128)(2,1)}, bf16[4,288,640]{2,1,0:T(8,128)(2,1)}, u32[]{:S(2)}, u32[]{:S(2)}) collective-permute-start(bf16[4,288,640]{2,1,0:T(8,128)(2,1)} %all-to-all-done.6.refs_0_), channel_id=1, source_target_pairs={{0,4},{4,0},{8,12},{12,8},{16,20},{20,16},{24,28},{28,24},{1,5},{5... | collective-permute-start | bytes 4423688 | tf_op jit(solution)/shard_map/ppermute | solution.py:92
  277.3 33.4 %collective-permute-start.29 = (bf16[4,288,640]{2,1,0:T(8,128)(2,1)}, bf16[4,288,640]{2,1,0:T(8,128)(2,1)S(1)}, u32[]{:S(2)}, u32[]{:S(2)}) collective-permute-start(bf16[4,288,640]{2,1,0:T(8,128)(2,1)} %all-to-all-done.6.refs_0_), channel_id=1, source_target_pairs={{0,1},{1,0},{2,3},{3,2},{4,5},{5,4},{6,7},{7,6},{8,9},{9,8},{10,11... | collective-permute-start | bytes 4423688 | tf_op jit(solution)/shard_map/ppermute | solution.py:92
  277.3 34.6 %collective-permute-start.30 = (bf16[4,288,640]{2,1,0:T(8,128)(2,1)}, bf16[4,288,640]{2,1,0:T(8,128)(2,1)S(1)}, u32[]{:S(2)}, u32[]{:S(2)}) collective-permute-start(bf16[4,288,640]{2,1,0:T(8,128)(2,1)} %collective-permute-done.23.refs_1_), channel_id=1, source_target_pairs={{0,1},{1,0},{2,3},{3,2},{4,5},{5,4},{6,7},{7,6},{8,9},{9,8},{10,11... | collective-permute-start | bytes 4423688 | tf_op jit(solution)/shard_map/ppermute | solution.py:92
  280.2 28.1 %collective-permute-start.31 = (bf16[80,2304]{1,0:T(8,128)(2,1)S(1)}, bf16[80,2304]{1,0:T(8,128)(2,1)S(1)}, u32[]{:S(2)}, u32[]{:S(2)}) collective-permute-start(bf16[80,2304]{1,0:T(8,128)(2,1)S(1)} %slice.372), channel_id=1, source_target_pairs={{0,8},{4,12},{8,0},{12,4},{16,24},{20,28},{24,16},{28,20},{1,9},{5... | collective-permute-start | bytes 1105928 | tf_op jit(solution)/shard_map/ppermute | solution.py:92
  282.2 26.1 %collective-permute-start.32 = (bf16[80,2304]{1,0:T(8,128)(2,1)S(1)}, bf16[80,2304]{1,0:T(8,128)(2,1)S(1)}, u32[]{:S(2)}, u32[]{:S(2)}) collective-permute-start(bf16[80,2304]{1,0:T(8,128)(2,1)S(1)} %copy-done.98), channel_id=1, source_target_pairs={{0,2},{1,3},{2,0},{3,1},{4,6},{5,7},{6,4},{7,5},{8,10},{9,11},{10,... | collective-permute-start | bytes 1105928 | tf_op jit(solution)/shard_map/ppermute | solution.py:92
  312.9 38.8 %all-to-all-start.8 = ((bf16[4,288,512]{2,1,0:T(8,128)(2,1)}), bf16[4,288,512]{2,1,0:T(8,128)(2,1)}, u32[]{:S(2)}, u32[]{:S(2)}) async-start(bf16[4,288,512]{2,1,0:T(8,128)(2,1)} %pad_maximum_fusion.9), calls=%async_computation.8 | async-start | bytes 2359296 | tf_op jit(solution)/shard_map/all_to_all | solution.py:102
  319.1 32.6 %collective-permute-start.33 = (bf16[4,288,640]{2,1,0:T(8,128)(2,1)}, bf16[4,288,640]{2,1,0:T(8,128)(2,1)}, u32[]{:S(2)}, u32[]{:S(2)}) collective-permute-start(bf16[4,288,640]{2,1,0:T(8,128)(2,1)} %all-to-all-done.7.refs_0_), channel_id=1, source_target_pairs={{0,4},{4,0},{8,12},{12,8},{16,20},{20,16},{24,28},{28,24},{1,5},{5... | collective-permute-start | bytes 4423688 | tf_op jit(solution)/shard_map/ppermute | solution.py:92
  319.7 32.0 %collective-permute-start.34 = (bf16[4,288,640]{2,1,0:T(8,128)(2,1)}, bf16[4,288,640]{2,1,0:T(8,128)(2,1)}, u32[]{:S(2)}, u32[]{:S(2)}) collective-permute-start(bf16[4,288,640]{2,1,0:T(8,128)(2,1)} %all-to-all-done.7.refs_0_), channel_id=1, source_target_pairs={{0,1},{1,0},{2,3},{3,2},{4,5},{5,4},{6,7},{7,6},{8,9},{9,8},{10,11... | collective-permute-start | bytes 4423688 | tf_op jit(solution)/shard_map/ppermute | solution.py:92
  319.7 32.0 %collective-permute-start.35 = (bf16[4,288,640]{2,1,0:T(8,128)(2,1)}, bf16[4,288,640]{2,1,0:T(8,128)(2,1)}, u32[]{:S(2)}, u32[]{:S(2)}) collective-permute-start(bf16[4,288,640]{2,1,0:T(8,128)(2,1)} %collective-permute-done.28.refs_1_), channel_id=1, source_target_pairs={{0,1},{1,0},{2,3},{3,2},{4,5},{5,4},{6,7},{7,6},{8,9},{9,8},{10,11... | collective-permute-start | bytes 4423688 | tf_op jit(solution)/shard_map/ppermute | solution.py:92
  320.9 10.5 %collective-permute-start.36 = (bf16[80,2304]{1,0:T(8,128)(2,1)S(1)}, bf16[80,2304]{1,0:T(8,128)(2,1)S(1)}, u32[]{:S(2)}, u32[]{:S(2)}) collective-permute-start(bf16[80,2304]{1,0:T(8,128)(2,1)S(1)} %copy-done.101), channel_id=1, source_target_pairs={{0,2},{1,3},{2,0},{3,1},{4,6},{5,7},{6,4},{7,5},{8,10},{9,11},{10,... | collective-permute-start | bytes 1105928 | tf_op jit(solution)/shard_map/ppermute | solution.py:92
  351.7 27.1 %collective-permute-start.39 = (bf16[4,288,640]{2,1,0:T(8,128)(2,1)}, bf16[4,288,640]{2,1,0:T(8,128)(2,1)}, u32[]{:S(2)}, u32[]{:S(2)}) collective-permute-start(bf16[4,288,640]{2,1,0:T(8,128)(2,1)} %collective-permute-done.33.refs_1_), channel_id=1, source_target_pairs={{0,1},{1,0},{2,3},{3,2},{4,5},{5,4},{6,7},{7,6},{8,9},{9,8},{10,11... | collective-permute-start | bytes 4423688 | tf_op jit(solution)/shard_map/ppermute | solution.py:92
  352.7 35.5 %collective-permute-start.37 = (bf16[4,288,512]{2,1,0:T(8,128)(2,1)}, bf16[4,288,512]{2,1,0:T(8,128)(2,1)}, u32[]{:S(2)}, u32[]{:S(2)}) collective-permute-start(bf16[4,288,512]{2,1,0:T(8,128)(2,1)} %all-to-all-done.8.refs_0_), channel_id=1, source_target_pairs={{0,4},{4,0},{8,12},{12,8},{16,20},{20,16},{24,28},{28,24},{1,5},{5... | collective-permute-start | bytes 3538952 | tf_op jit(solution)/shard_map/ppermute | solution.py:92
  353.2 35.0 %collective-permute-start.38 = (bf16[4,288,512]{2,1,0:T(8,128)(2,1)}, bf16[4,288,512]{2,1,0:T(8,128)(2,1)}, u32[]{:S(2)}, u32[]{:S(2)}) collective-permute-start(bf16[4,288,512]{2,1,0:T(8,128)(2,1)} %all-to-all-done.8.refs_0_), channel_id=1, source_target_pairs={{0,1},{1,0},{2,3},{3,2},{4,5},{5,4},{6,7},{7,6},{8,9},{9,8},{10,11... | collective-permute-start | bytes 3538952 | tf_op jit(solution)/shard_map/ppermute | solution.py:92
  403.1 18.7 %collective-permute-start.41 = (bf16[160,2304]{1,0:T(8,128)(2,1)S(1)}, bf16[160,2304]{1,0:T(8,128)(2,1)S(1)}, u32[]{:S(2)}, u32[]{:S(2)}) collective-permute-start(bf16[160,2304]{1,0:T(8,128)(2,1)S(1)} %get-tuple-element.339), channel_id=1, source_target_pairs={{0,2},{1,3},{2,0},{3,1},{4,6},{5,7},{6,4},{7,5},{8,10},{9,11},{10,... | collective-permute-start | bytes 2211848 | tf_op jit(solution)/shard_map/ppermute | solution.py:92
  404.7 18.4 %collective-permute-start.42 = (bf16[160,2304]{1,0:T(8,128)(2,1)S(1)}, bf16[160,2304]{1,0:T(8,128)(2,1)S(1)}, u32[]{:S(2)}, u32[]{:S(2)}) collective-permute-start(bf16[160,2304]{1,0:T(8,128)(2,1)S(1)} %get-tuple-element.341), channel_id=1, source_target_pairs={{0,8},{4,12},{8,0},{12,4},{16,24},{20,28},{24,16},{28,20},{1,9},{5... | collective-permute-start | bytes 2211848 | tf_op jit(solution)/shard_map/ppermute | solution.py:92
  423.3 9.7 %collective-permute-start.43 = (bf16[80,2304]{1,0:T(8,128)(2,1)S(1)}, bf16[80,2304]{1,0:T(8,128)(2,1)S(1)}, u32[]{:S(2)}, u32[]{:S(2)}) collective-permute-start(bf16[80,2304]{1,0:T(8,128)(2,1)S(1)} %fusion.22), channel_id=1, source_target_pairs={{0,8},{4,12},{8,0},{12,4},{16,24},{20,28},{24,16},{28,20},{1,9},{5... | collective-permute-start | bytes 1105928 | tf_op jit(solution)/shard_map/ppermute | solution.py:92
  425.1 9.4 %collective-permute-start.44 = (bf16[80,2304]{1,0:T(8,128)(2,1)S(1)}, bf16[80,2304]{1,0:T(8,128)(2,1)S(1)}, u32[]{:S(2)}, u32[]{:S(2)}) collective-permute-start(bf16[80,2304]{1,0:T(8,128)(2,1)S(1)} %fusion.23), channel_id=1, source_target_pairs={{0,2},{1,3},{2,0},{3,1},{4,6},{5,7},{6,4},{7,5},{8,10},{9,11},{10,... | collective-permute-start | bytes 1105928 | tf_op jit(solution)/shard_map/ppermute | solution.py:92
  437.3 16.4 %collective-permute-start.45 = (bf16[160,2304]{1,0:T(8,128)(2,1)S(1)}, bf16[160,2304]{1,0:T(8,128)(2,1)S(1)}, u32[]{:S(2)}, u32[]{:S(2)}) collective-permute-start(bf16[160,2304]{1,0:T(8,128)(2,1)S(1)} %get-tuple-element.445), channel_id=1, source_target_pairs={{0,2},{1,3},{2,0},{3,1},{4,6},{5,7},{6,4},{7,5},{8,10},{9,11},{10,... | collective-permute-start | bytes 2211848 | tf_op jit(solution)/shard_map/ppermute | solution.py:92
  438.1 16.6 %collective-permute-start.46 = (bf16[160,2304]{1,0:T(8,128)(2,1)S(1)}, bf16[160,2304]{1,0:T(8,128)(2,1)S(1)}, u32[]{:S(2)}, u32[]{:S(2)}) collective-permute-start(bf16[160,2304]{1,0:T(8,128)(2,1)S(1)} %get-tuple-element.445), channel_id=1, source_target_pairs={{0,8},{4,12},{8,0},{12,4},{16,24},{20,28},{24,16},{28,20},{1,9},{5... | collective-permute-start | bytes 2211848 | tf_op jit(solution)/shard_map/ppermute | solution.py:92
  509.3 14.6 %collective-permute-start.49 = (bf16[160,2304]{1,0:T(8,128)(2,1)S(1)}, bf16[160,2304]{1,0:T(8,128)(2,1)S(1)}, u32[]{:S(2)}, u32[]{:S(2)}) collective-permute-start(bf16[160,2304]{1,0:T(8,128)(2,1)S(1)} %copy-done.134), channel_id=1, source_target_pairs={{0,2},{1,3},{2,0},{3,1},{4,6},{5,7},{6,4},{7,5},{8,10},{9,11},{10,... | collective-permute-start | bytes 2211848 | tf_op jit(solution)/shard_map/ppermute | solution.py:92
  510.4 13.8 %collective-permute-start.50 = (bf16[160,2304]{1,0:T(8,128)(2,1)S(1)}, bf16[160,2304]{1,0:T(8,128)(2,1)S(1)}, u32[]{:S(2)}, u32[]{:S(2)}) collective-permute-start(bf16[160,2304]{1,0:T(8,128)(2,1)S(1)} %copy-done.133), channel_id=1, source_target_pairs={{0,8},{4,12},{8,0},{12,4},{16,24},{20,28},{24,16},{28,20},{1,9},{5... | collective-permute-start | bytes 2211848 | tf_op jit(solution)/shard_map/ppermute | solution.py:92
  544.0 16.3 %collective-permute-start.56 = (bf16[2,96,1152]{2,1,0:T(8,128)(2,1)S(1)}, bf16[2,96,1152]{2,1,0:T(8,128)(2,1)S(1)}, u32[]{:S(2)}, u32[]{:S(2)}) collective-permute-start(bf16[2,96,1152]{2,1,0:T(8,128)(2,1)S(1)} %pad_maximum_fusion.21), channel_id=1, source_target_pairs={{0,16},{4,20},{8,24},{12,28},{16,0},{20,4},{24,8},{28,12},{1,17},{... | collective-permute-start | bytes 1327112 | tf_op jit(solution)/shard_map/ppermute | solution.py:92
  546.9 13.5 %collective-permute-start.55 = (bf16[160,2304]{1,0:T(8,128)(2,1)S(1)}, bf16[160,2304]{1,0:T(8,128)(2,1)S(1)}, u32[]{:S(2)}, u32[]{:S(2)}) collective-permute-start(bf16[160,2304]{1,0:T(8,128)(2,1)S(1)} %subtract_convert_fusion), channel_id=1, source_target_pairs={{0,2},{1,3},{2,0},{3,1},{4,6},{5,7},{6,4},{7,5},{8,10},{9,11},{10,... | collective-permute-start | bytes 2211848 | tf_op jit(solution)/shard_map/ppermute | solution.py:92
  548.3 12.2 %collective-permute-start.57 = (bf16[3,16,2304]{2,1,0:T(8,128)(2,1)S(1)}, bf16[3,16,2304]{2,1,0:T(8,128)(2,1)S(1)}, u32[]{:S(2)}, u32[]{:S(2)}) collective-permute-start(bf16[3,16,2304]{2,1,0:T(8,128)(2,1)S(1)} %fusion.29), channel_id=1, source_target_pairs={{0,8},{4,12},{8,0},{12,4},{16,24},{20,28},{24,16},{28,20},{1,9},{5... | collective-permute-start | bytes 663560 | tf_op jit(solution)/shard_map/ppermute | solution.py:92
  570.4 33.0 %collective-permute-start.66 = (bf16[4,96,1152]{2,1,0:T(8,128)(2,1)S(1)}, bf16[4,96,1152]{2,1,0:T(8,128)(2,1)S(1)}, u32[]{:S(2)}, u32[]{:S(2)}) collective-permute-start(bf16[4,96,1152]{2,1,0:T(8,128)(2,1)S(1)} %pad_maximum_fusion.12), channel_id=1, source_target_pairs={{0,8},{4,12},{8,0},{12,4},{16,24},{20,28},{24,16},{28,20},{1,9},{5... | collective-permute-start | bytes 2654216 | tf_op jit(solution)/shard_map/ppermute | solution.py:92
  580.6 11.6 %collective-permute-start.63 = (bf16[1,16,3456]{2,1,0:T(8,128)(2,1)S(1)}, bf16[1,16,3456]{2,1,0:T(8,128)(2,1)S(1)}, u32[]{:S(2)}, u32[]{:S(2)}) collective-permute-start(bf16[1,16,3456]{2,1,0:T(8,128)(2,1)S(1)} %bitcast.191), channel_id=1, source_target_pairs={{0,16},{4,20},{8,24},{12,28},{16,0},{20,4},{24,8},{28,12},{1,17},{... | collective-permute-start | bytes 331784 | tf_op jit(solution)/shard_map/ppermute | solution.py:92
  592.3 11.0 %collective-permute-start.65 = (bf16[2,16,3456]{2,1,0:T(8,128)(2,1)S(1)}, bf16[2,16,3456]{2,1,0:T(8,128)(2,1)S(1)}, u32[]{:S(2)}, u32[]{:S(2)}) collective-permute-start(bf16[2,16,3456]{2,1,0:T(8,128)(2,1)S(1)} %pad_maximum_fusion.29), channel_id=1, source_target_pairs={{0,8},{4,12},{8,0},{12,4},{16,24},{20,28},{24,16},{28,20},{1,9},{5... | collective-permute-start | bytes 663560 | tf_op jit(solution)/shard_map/ppermute | solution.py:92
  606.6 39.5 %all-to-all-start.9 = ((bf16[8,16,6144]{2,1,0:T(8,128)(2,1)}), bf16[8,16,6144]{2,1,0:T(8,128)(2,1)S(1)}, u32[]{:S(2)}, u32[]{:S(2)}) async-start(bf16[8,16,6144]{2,1,0:T(8,128)(2,1)} %broadcast_in_dim.229), calls=%async_computation.9 | async-start | bytes 3145728 | tf_op jit(solution)/shard_map/all_to_all | solution.py:1067
  611.2 26.4 %collective-permute-start.68 = (bf16[4,16,3456]{2,1,0:T(8,128)(2,1)S(1)}, bf16[4,16,3456]{2,1,0:T(8,128)(2,1)S(1)}, u32[]{:S(2)}, u32[]{:S(2)}) collective-permute-start(bf16[4,16,3456]{2,1,0:T(8,128)(2,1)S(1)} %pad_maximum_fusion.22), channel_id=1, source_target_pairs={{0,4},{4,0},{8,12},{12,8},{16,20},{20,16},{24,28},{28,24},{1,5},{5... | collective-permute-start | bytes 1327112 | tf_op jit(solution)/shard_map/ppermute | solution.py:92
  615.1 22.6 %collective-permute-start.67 = (bf16[160,2304]{1,0:T(8,128)(2,1)S(1)}, bf16[160,2304]{1,0:T(8,128)(2,1)S(1)}, u32[]{:S(2)}, u32[]{:S(2)}) collective-permute-start(bf16[160,2304]{1,0:T(8,128)(2,1)S(1)} %slice.632), channel_id=1, source_target_pairs={{0,2},{1,3},{2,0},{3,1},{4,6},{5,7},{6,4},{7,5},{8,10},{9,11},{10,... | collective-permute-start | bytes 2211848 | tf_op jit(solution)/shard_map/ppermute | solution.py:92
  (165 other events, 1031.0 us)
